TPU v7x, 256 devices: a whole 4x4x8 slice. The times are simulated.
256 devices in a mesh: ent: 64 (over z, x, core), basis: 4 (over y).
Axes of the slice: x: 4, y: 4, z: 8, core: 2. Of those that a mesh axis runs over, the one named last changes fastest.
Arguments:
- entity_rows: bfloat16 [32768, 256], P('ent'), may hold values from -6 to 6
- self_weight: bfloat16 [256, 256], replicated, may hold values from -0.375 to 0.375
- bases: bfloat16 [32, 256, 256], P('basis'), may hold values from -0.375 to 0.375
- coefficients: float32 [1315, 32], P(None, 'basis'), may hold values from -1 to 1
- send_block: int32 [64, 64, 2], P('ent'), may hold values from 0 to 3
- edge_rel: int32 [64, 64, 2], P('ent'), may hold values from 0 to 1314
- edge_dst: int32 [64, 64, 2], P(None, 'ent'), may hold values from 0 to 3
- edge_count: int32 [64, 64, 2], P(None, 'ent'), may hold values from 0 to 128, as said below
- cotangent: bfloat16 [32768, 256], P('ent'), may hold values from -0.75 to 0.75
Outputs:
- activation: bfloat16 [32768, 256], P('ent', 'basis')
- basis_grad: float32 [32, 256, 256], P('basis', 'ent')
- coef_grad: float32 [1315, 32], P(None, 'basis')
- entity_grad: bfloat16 [32768, 256], P('ent', 'basis')
Inputs may be any that keep to these rules, and one draw needn't show every extreme that they name: `edge_count`: 0 marks an empty slot; every draw has slots with all 128 rows live.
All inputs are finite; a program needn't handle non-finite values.
Results may differ from a plain program's by a relative error of at most 0.015.
Values may be sent and summed in bfloat16 or wider, within the bound.
No kernel may reach another device: no remote copies, remote signals or barrier semaphores. Data moves between devices by JAX's collectives and lax.ppermute only.
A program may use at most 128 MiB of HBM per device.

v0:
```python
import jax
import jax.numpy as jnp
from jax import lax
from jax.sharding import PartitionSpec as P

BLK = 128


def silu_parts(values):
    logistic = jax.nn.sigmoid(values)
    return (values * logistic, logistic * (1.0 + values * (1.0 - logistic)))


def local(
    entity_rows,
    self_weight,
    bases,
    coefficients,
    send_block,
    edge_rel,
    edge_dst,
    edge_count,
    cotangent,
):
    peers = lax.axis_size("ent")
    groups = lax.axis_size("basis")
    group_index = lax.axis_index("basis")
    ent_dev, feature_width = entity_rows.shape
    block_count = ent_dev // BLK
    share_width = feature_width // groups
    own_bases = bases.shape[0]
    col_start = group_index * share_width
    blocks = entity_rows.reshape(block_count, BLK, feature_width)
    outgoing = jnp.take(blocks, send_block[0], axis=0)
    outgoing_rel = edge_rel[0]
    incoming, rel_in = (
        lax.all_to_all(outgoing, "ent", split_axis=0, concat_axis=0, tiled=True),
        lax.all_to_all(outgoing_rel, "ent", split_axis=0, concat_axis=0, tiled=True),
    )
    slot_count = peers * incoming.shape[1]
    dst_local = edge_dst[:, 0, :]
    row_iota = lax.broadcasted_iota(jnp.int32, (1, 1, BLK), 2)
    live_rows = row_iota < edge_count[:, 0, :][:, :, None]
    incoming = jnp.where(live_rows[..., None], incoming, jnp.zeros((), jnp.bfloat16))
    coef_bf = coefficients.astype(jnp.bfloat16)
    in_weights = jnp.take(coef_bf, rel_in.reshape(slot_count), axis=0)
    block_iota = lax.broadcasted_iota(jnp.int32, (1, block_count), 1)
    target_hot = (dst_local.reshape(slot_count)[:, None] == block_iota).astype(jnp.bfloat16)
    spread = (target_hot[:, :, None] * in_weights[:, None, :]).reshape(
        slot_count, block_count * own_bases
    )
    flat_in = incoming.reshape(slot_count, BLK * feature_width)
    messages = lax.dot_general(
        spread, flat_in, (((0,), (0,)), ((), ())), preferred_element_type=jnp.float32
    )
    messages = messages.astype(jnp.bfloat16).reshape(block_count, own_bases, BLK, feature_width)
    partial_sum = jnp.einsum(
        "kbrd,bde->kre", messages, bases, preferred_element_type=jnp.float32
    ).reshape(ent_dev, feature_width)
    aggregate = lax.psum(partial_sum, "basis")
    pre_act = jnp.dot(entity_rows, self_weight, preferred_element_type=jnp.float32) + aggregate
    activated, slope_value = silu_parts(pre_act)
    pre_grad = (cotangent.astype(jnp.float32) * slope_value).astype(jnp.bfloat16)
    activation = lax.dynamic_slice_in_dim(activated, col_start, share_width, 1).astype(jnp.bfloat16)
    grad_blocks = pre_grad.reshape(block_count, BLK, feature_width)
    basis_term = jnp.einsum(
        "kbrd,kre->bde", messages, grad_blocks, preferred_element_type=jnp.float32
    )
    basis_grad = lax.psum_scatter(basis_term, "ent", scatter_dimension=1, tiled=True)
    back_blocks = jnp.take(grad_blocks, dst_local, axis=0)
    back_blocks = jnp.where(live_rows[..., None], back_blocks, jnp.zeros((), jnp.bfloat16))
    returned_in = lax.all_to_all(back_blocks, "ent", split_axis=0, concat_axis=0, tiled=True)
    src_local = send_block[0].reshape(slot_count)
    rel_local = edge_rel[0].reshape(slot_count)
    out_weights = jnp.take(coef_bf, rel_local, axis=0)
    source_hot = (src_local[:, None] == block_iota).astype(jnp.bfloat16)
    spread_back = (source_hot[:, :, None] * out_weights[:, None, :]).reshape(
        slot_count, block_count * own_bases
    )
    flat_back = returned_in.reshape(slot_count, BLK * feature_width)
    returned = lax.dot_general(
        spread_back, flat_back, (((0,), (0,)), ((), ())), preferred_element_type=jnp.float32
    )
    returned = returned.astype(jnp.bfloat16).reshape(block_count, own_bases, BLK, feature_width)
    back_partial = jnp.einsum(
        "kbre,bde->krd", returned, bases, preferred_element_type=jnp.float32
    ).reshape(ent_dev, feature_width)
    back_share = lax.psum_scatter(
        back_partial.astype(jnp.bfloat16), "basis", scatter_dimension=1, tiled=True
    ).astype(jnp.float32)
    weight_rows = lax.dynamic_slice_in_dim(self_weight, col_start, share_width, 0)
    self_part = lax.dot_general(
        pre_grad, weight_rows, (((1,), (1,)), ((), ())), preferred_element_type=jnp.float32
    )
    entity_grad = (self_part + back_share).astype(jnp.bfloat16)
    projected = jnp.einsum(
        "nd,bde->bne", entity_rows, bases, preferred_element_type=jnp.float32
    ).astype(jnp.bfloat16)
    proj_flat = projected.reshape(own_bases * block_count, BLK * feature_width)
    scores = lax.dot_general(
        flat_back, proj_flat, (((1,), (1,)), ((), ())), preferred_element_type=jnp.float32
    )
    scores = scores.reshape(slot_count, own_bases, block_count)
    per_slot = jnp.sum(scores * source_hot.astype(jnp.float32)[:, None, :], axis=2)
    relation_iota = lax.broadcasted_iota(jnp.int32, (1, coefficients.shape[0]), 1)
    relation_hot = (rel_local[:, None] == relation_iota).astype(jnp.float32)
    coef_term = lax.dot_general(
        relation_hot,
        per_slot,
        (((0,), (0,)), ((), ())),
        precision=lax.Precision.HIGHEST,
        preferred_element_type=jnp.float32,
    )
    coef_grad = lax.psum(coef_term, "ent")
    return (activation, basis_grad, coef_grad, entity_grad)


def solution(mesh):
    placed = (
        P("ent", None),
        P(),
        P("basis", None, None),
        P(None, "basis"),
        P("ent", None, None),
        P("ent", None, None),
        P(None, "ent", None),
        P(None, "ent", None),
        P("ent", None),
    )
    return jax.shard_map(
        local,
        mesh=mesh,
        in_specs=placed,
        out_specs=(P("ent", "basis"), P("basis", "ent", None), P(None, "basis"), P("ent", "basis")),
        check_vma=False,
    )
```

profile of v0, /device:TPU:1, one launch (start us, length us, event | category | flops | bytes accessed | tf_op | source)
XLA Modules:
  0.0 817.3 jit_solution(8115167516258157078)
XLA Ops:
  7.2 1.5 copy.69
  8.7 13.0 %all-to-all-start = ((s32[64,1,2]{2,1,0:T(1,128)}), s32[64,1,2]{2,1,0:T(1,128)S(1)}, u32[]{:S(2)}, u32[]{:S(2)}) async-start(s32[64,1,2]{2,1,0:T(1,128)} %copy.69), calls=%async_computation | async-start | bytes 65536 | tf_op jit(solution)/shard_map/all_to_all | solution.py:38
  23.4 7.4 gather_fusion.1
  30.8 7.4 broadcast_select_fusion
  38.3 10.7 %all-to-all-start.1 = ((bf16[64,2,128,256]{3,2,1,0:T(8,128)(2,1)}), bf16[64,2,128,256]{3,2,1,0:T(8,128)(2,1)}, u32[]{:S(2)}, u32[]{:S(2)}) async-start(bf16[64,2,128,256]{3,2,1,0:T(8,128)(2,1)} %broadcast_select_fusion), calls=%async_computation.1 | async-start | bytes 16777216 | tf_op jit(solution)/shard_map/all_to_all | solution.py:37
  52.2 179.1 %all-to-all-done.1 = bf16[64,2,128,256]{3,2,1,0:T(8,128)(2,1)} async-done(((bf16[64,2,128,256]{3,2,1,0:T(8,128)(2,1)}), bf16[64,2,128,256]{3,2,1,0:T(8,128)(2,1)}, u32[]{:S(2)}, u32[]{:S(2)}) %all-to-all-start.1) | async-done | bytes 8388640 | tf_op jit(solution)/shard_map/all_to_all | solution.py:37
  231.3 8.0 broadcast_select_fusion.1
  239.3 12.3 %copy.94 = bf16[16,8,128,256]{3,1,2,0:T(8,128)(2,1)} copy(bf16[16,8,128,256]{3,2,1,0:T(8,128)(2,1)} %bitcast.74) | data formatting | bytes 16777216
  251.7 4.7 convolution_convert_fusion.1
  256.3 1.3 copy-done.2
  258.2 1.5 convolution_bitcast_fusion.2
  260.1 47.0 %all-reduce.2.cloned.1.call-done = f32[512,256]{1,0:T(8,128)} async-done(((f32[512,256]{1,0:T(8,128)}), f32[512,256]{1,0:T(8,128)}) %all-reduce.2.cloned.1.call-update) | async-done | bytes 524304 | tf_op jit(solution)/shard_map/psum | solution.py:60
  307.1 2.4 multiply_convert_fusion
  309.5 6.4 gather_fusion.2
  315.9 8.0 select_select_fusion
  323.9 12.7 %all-to-all-start.2 = ((bf16[64,2,128,256]{3,2,1,0:T(8,128)(2,1)}), bf16[64,2,128,256]{3,2,1,0:T(8,128)(2,1)}, u32[]{:S(2)}, u32[]{:S(2)}) async-start(bf16[64,2,128,256]{3,2,1,0:T(8,128)(2,1)} %select_select_fusion), calls=%async_computation.3 | async-start | bytes 16777216 | tf_op jit(solution)/shard_map/all_to_all | solution.py:72
  336.7 4.8 copy.89
  341.5 3.6 convolution_bitcast_fusion
  346.6 2.1 convert_bitcast_fusion
  348.7 2.8 copy.82
  351.6 2.8 dot_general.47
  354.4 1.2 fusion.12
  356.3 149.1 %reduce-scatter.3.cloned.1.call-done = f32[8,4,256]{2,0,1:T(8,128)} async-done(((f32[8,256,256]{2,0,1:T(8,128)}), f32[8,4,256]{2,0,1:T(8,128)}) %reduce-scatter.3.cloned.1.call-update) | async-done | bytes 32784 | tf_op jit(solution)/shard_map/reduce_scatter | solution.py:69
  505.4 1.4 copy.88
  506.8 18.5 %all-to-all-done.2 = bf16[64,2,128,256]{3,2,1,0:T(8,128)(2,1)} async-done(((bf16[64,2,128,256]{3,2,1,0:T(8,128)(2,1)}), bf16[64,2,128,256]{3,2,1,0:T(8,128)(2,1)}, u32[]{:S(2)}, u32[]{:S(2)}) %all-to-all-start.2) | async-done | bytes 8388640 | tf_op jit(solution)/shard_map/all_to_all | solution.py:72
  525.4 12.4 %copy.95 = bf16[16,8,128,256]{3,1,2,0:T(8,128)(2,1)} copy(bf16[16,8,128,256]{3,2,1,0:T(8,128)(2,1)} %bitcast.31) | data formatting | bytes 16777216
  537.7 4.6 convolution_convert_fusion
  542.8 1.4 fusion.2
  544.3 13.6 %reshape.216 = bf16[128,32768,1]{1,0,2:T(8,128)(2,1)} reshape(bf16[64,2,128,256]{3,2,1,0:T(8,128)(2,1)} %all-to-all-done.2) | data formatting | bytes 16777216 | tf_op jit(solution)/shard_map/reshape | solution.py:80
  557.9 6.2 fusion.7
  564.6 244.5 %psum.15 = f32[1315,8]{0,1:T(8,128)} all-reduce(f32[1315,8]{0,1:T(8,128)S(1)} %fusion.10), channel_id=1, replica_groups=mesh['ent'=64,'basis'=4] {'ent'}, use_global_device_ids=true, to_apply=%region_3.6 | all-reduce | flops 10520 | bytes 84160 | tf_op jit(solution)/shard_map/psum | solution.py:114
  809.0 1.7 fusion.3
  (69 shorter events, 8.9 us)
Async XLA Ops:
  7.2 251.0 %copy-start = (bf16[8,256,256]{2,1,0:T(8,128)(2,1)S(1)}, bf16[8,256,256]{2,1,0:T(8,128)(2,1)}, u32[]{:S(2)}) copy-start(bf16[8,256,256]{2,1,0:T(8,128)(2,1)} %param.15) | copy-start | bytes 3145732
  8.7 29.6 %all-to-all-start = ((s32[64,1,2]{2,1,0:T(1,128)}), s32[64,1,2]{2,1,0:T(1,128)S(1)}, u32[]{:S(2)}, u32[]{:S(2)}) async-start(s32[64,1,2]{2,1,0:T(1,128)} %copy.69), calls=%async_computation | async-start | bytes 65536 | tf_op jit(solution)/shard_map/all_to_all | solution.py:38
  38.3 10.9 %copy-start.5 = (s32[64,1,2]{0,2,1:T(2,128)S(1)}, s32[64,1,2]{0,2,1:T(2,128)}, u32[]{:S(2)}) copy-start(s32[64,1,2]{0,2,1:T(2,128)} %param.19) | copy-start | bytes 1540
  38.3 11.0 %copy-start.9 = (s32[64,1,2]{0,2,1:T(2,128)S(1)}, s32[64,1,2]{0,2,1:T(2,128)}, u32[]{:S(2)}) copy-start(s32[64,1,2]{0,2,1:T(2,128)} %param.20) | copy-start | bytes 1540
  38.3 11.2 %copy-start.4 = (f32[1315,8]{0,1:T(8,128)S(1)}, f32[1315,8]{0,1:T(8,128)}, u32[]{:S(2)}) copy-start(f32[1315,8]{0,1:T(8,128)} %param.16) | copy-start | bytes 126244
  38.3 193.0 %all-to-all-start.1 = ((bf16[64,2,128,256]{3,2,1,0:T(8,128)(2,1)}), bf16[64,2,128,256]{3,2,1,0:T(8,128)(2,1)}, u32[]{:S(2)}, u32[]{:S(2)}) async-start(bf16[64,2,128,256]{3,2,1,0:T(8,128)(2,1)} %broadcast_select_fusion), calls=%async_computation.1 | async-start | bytes 16777216 | tf_op jit(solution)/shard_map/all_to_all | solution.py:37
  48.9 258.1 %all-reduce.2.cloned.1.call-start = ((), (), s32[]{:S(2)}) async-start(), calls=%async_computation.5 | async-start | bytes 1048576 | tf_op jit(solution)/shard_map/psum | solution.py:60
  251.7 55.4 %copy-start.1 = (bf16[512,256]{1,0:T(8,128)(2,1)S(1)}, bf16[512,256]{1,0:T(8,128)(2,1)}, u32[]{:S(2)}) copy-start(bf16[512,256]{1,0:T(8,128)(2,1)} %param.13) | copy-start | bytes 786436
  251.7 55.4 %copy-start.7 = (bf16[256,256]{1,0:T(8,128)(2,1)S(1)}, bf16[256,256]{1,0:T(8,128)(2,1)}, u32[]{:S(2)}) copy-start(bf16[256,256]{1,0:T(8,128)(2,1)} %param.14) | copy-start | bytes 393220
  251.7 55.4 %copy-start.10 = (bf16[512,256]{1,0:T(8,128)(2,1)S(1)}, bf16[512,256]{1,0:T(8,128)(2,1)}, u32[]{:S(2)}) copy-start(bf16[512,256]{1,0:T(8,128)(2,1)} %param.21) | copy-start | bytes 786436
  256.3 1.3 copy-start.2
  323.9 201.4 %all-to-all-start.2 = ((bf16[64,2,128,256]{3,2,1,0:T(8,128)(2,1)}), bf16[64,2,128,256]{3,2,1,0:T(8,128)(2,1)}, u32[]{:S(2)}, u32[]{:S(2)}) async-start(bf16[64,2,128,256]{3,2,1,0:T(8,128)(2,1)} %select_select_fusion), calls=%async_computation.3 | async-start | bytes 16777216 | tf_op jit(solution)/shard_map/all_to_all | solution.py:72
  336.6 8.6 %copy-start.8 = (s32[1,64,2]{1,2,0:T(2,128)S(1)}, s32[1,64,2]{1,2,0:T(2,128)}, u32[]{:S(2)}) copy-start(s32[1,64,2]{1,2,0:T(2,128)} %param.18) | copy-start | bytes 1540
  336.6 8.7 %copy-start.6 = (s32[1,64,2]{1,2,0:T(2,128)S(1)}, s32[1,64,2]{1,2,0:T(2,128)}, u32[]{:S(2)}) copy-start(s32[1,64,2]{1,2,0:T(2,128)} %param.17) | copy-start | bytes 1540
  336.7 168.8 %reduce-scatter.3.cloned.1.call-start = ((), (), s32[]{:S(2)}) async-start(), calls=%async_computation.6 | async-start | bytes 2129920 | tf_op jit(solution)/shard_map/reduce_scatter | solution.py:69
  345.2 463.9 %reduce-scatter.5.cloned.1.call-start = ((), (), s32[]{:S(2)}) async-start(), calls=%async_computation.7 | async-start | bytes 327680 | tf_op jit(solution)/shard_map/reduce_scatter | solution.py:88
  544.3 13.6 %copy-start.3 = (bf16[8,4,32768]{2,1,0:T(4,128)(2,1)S(1)}, bf16[8,4,32768]{2,1,0:T(4,128)(2,1)}, u32[]{:S(2)}) copy-start(bf16[8,4,32768]{2,1,0:T(4,128)(2,1)} %dot_general.47) | copy-start | bytes 6291460
Sparse Core Ops, SparseCore 0:
  259.8 47.1 all-reduce.1
  345.3 160.1 reduce-scatter.2
  544.4 20.7 reduce-scatter.4
where the time goes:
time: 822 us; the launch traced here: 817 us
  waiting for transfers between devices  394 us (48%)
  blocking collectives  244 us (30%)
  local copies, waits for them, and re-layouts  72.4 us (9%)
  starting transfers between devices  36.6 us (4%)
  matrix products  28.7 us (3%)
  other arithmetic  27.2 us (3%)
  between operations  14 us (2%)
    psum x1, blocking collectives, local(): coef_grad = lax.psum(coef_term, 'ent')  244 us
    all_to_all x1, waiting for transfers between devices, local(): lax.all_to_all(outgoing, 'ent', split_axis=0, concat_axis=0, tiled=True)  179 us
    reduce_scatter x1, waiting for transfers between devices, local(): lax.psum_scatter(basis_term, 'ent', scatter_dimension=1, tiled=True)  149 us
    psum x1, waiting for transfers between devices, local(): aggregate = lax.psum(partial_sum, 'basis')  47 us
    unnamed x30, local copies, waits for them, and re-layouts  28.7 us
    all_to_all x1, waiting for transfers between devices, local(): lax.all_to_all(back_blocks, 'ent', split_axis=0, concat_axis=0, tiled=True)  18.5 us
  transfers between devices with their start and end apart: 6, of which 4 were waited for; matrix products, arithmetic and copies ran while one was open for 7% of the time, Pallas kernels for 0%

commit v1 on v0

v1 whole, which is shorter than its diff:
```python
import functools

import jax
import jax.numpy as jnp
from jax import lax
from jax.experimental import pallas as pl
from jax.experimental.pallas import tpu as pltpu
from jax.sharding import PartitionSpec as P

BLK = 128
BF = jnp.bfloat16
F32 = jnp.float32
NT = (((1,), (1,)), ((), ()))
TN = (((0,), (0,)), ((), ()))
LIMIT = 56 * 1024 * 1024
VM = pl.BlockSpec(memory_space=pltpu.VMEM)
SM = pl.BlockSpec(memory_space=pltpu.SMEM)


def call(body, outs, ins, scratch=()):
    return pl.pallas_call(
        body,
        out_shape=outs,
        in_specs=ins,
        out_specs=jax.tree.map(lambda _: VM, outs),
        scratch_shapes=list(scratch),
        compiler_params=pltpu.CompilerParams(vmem_limit_bytes=LIMIT),
    )


def take_body(share, idx_ref, g_ref, ent_ref, out_ref):
    first = g_ref[0] * share
    for s in range(out_ref.shape[0]):
        row = pl.multiple_of(idx_ref[s] * BLK + first, share)
        out_ref[s] = ent_ref[pl.ds(row, share), :]


def get(ref, at):
    return jnp.concatenate([ref[h, at, :] for h in range(ref.shape[0])], axis=1)


def put(ref, at, value):
    for h in range(ref.shape[0]):
        ref[h, at, :] = value[:, h * 128 : (h + 1) * 128]


def rows_scratch(rows, width):
    return pltpu.VMEM((width // 128, rows, 128), F32)


def slot_weights(table_ref, rel_ref, block_ref, nblk, base_rows, pad):
    chunks = (table_ref.shape[1] - base_rows) // pad
    width = table_ref.shape[2]
    slots = rel_ref.shape[1]
    groups = table_ref.shape[0]
    rel = rel_ref[...]
    parts = [jnp.zeros((pad, slots), F32) for _ in range(groups)]
    for j in range(chunks):
        ids = lax.broadcasted_iota(jnp.int32, (width, slots), 0) + j * width
        hot = jnp.where(ids == rel, 1.0, 0.0).astype(BF)
        for g in range(groups):
            rows = table_ref[g, pl.ds(base_rows + j * pad, pad), :]
            parts[g] += jnp.dot(rows, hot, preferred_element_type=F32)
    coef = jnp.concatenate([p[:8] for p in parts], axis=0)
    blk = block_ref[...]
    return jnp.concatenate([jnp.where(blk == n, coef, 0.0) for n in range(nblk)], axis=0)


def spread(x_ref, w, cnt_ref, first, xf, mf, xr_ref):
    slots = cnt_ref.shape[1]
    share = x_ref.shape[0] // slots
    step = 512

    def widen(i, c):
        at = pl.ds(pl.multiple_of(i * step, step), step)
        put(xf, at, x_ref[at, :].astype(F32))
        return c

    lax.fori_loop(0, x_ref.shape[0] // step, widen, 0)
    cnt = cnt_ref[...]

    def one(k, c):
        at = pl.ds(k, slots, stride=share)
        xk = get(xf, at).astype(BF)
        if xr_ref is not None:
            xr_ref[k] = xk
        wk = jnp.where(cnt > first + k, w, 0.0).astype(BF)
        put(mf, pl.ds(k, w.shape[0], stride=share), jnp.dot(wk, xk, preferred_element_type=F32))
        return c

    lax.fori_loop(0, share, one, 0, unroll=4)


def rows_of(mf, base, nbase, nblk, share):
    return jnp.concatenate(
        [get(mf, pl.ds((n * nbase + base) * share, share)) for n in range(nblk)], axis=0
    )


def own_rows(ref, first, nblk, share):
    return jnp.concatenate(
        [ref[pl.ds(pl.multiple_of(n * BLK + first, share), share), :] for n in range(nblk)], axis=0
    )


def fwd_body(
    nbase, nblk, pad, g_ref, dst_ref, x_ref, rel_ref, dstv_ref, cnt_ref, table_ref, ent_ref, sw_ref,
    cot_ref, y_ref, back_ref, xr_ref, pg_ref, xf, mf,
):
    groups = y_ref.shape[0]
    own = nbase // groups
    width = table_ref.shape[2]
    share = BLK // groups
    first = g_ref[0] * share
    w = slot_weights(table_ref, rel_ref, dstv_ref, nblk, own * width, pad)
    spread(x_ref, w, cnt_ref, first, xf, mf, xr_ref)
    acc = jnp.dot(own_rows(ent_ref, first, nblk, share), sw_ref[...], preferred_element_type=F32)
    for b in range(nbase):
        mb = rows_of(mf, b, nbase, nblk, share).astype(BF)
        y_ref[b // own, b % own] = mb
        acc += jnp.dot(mb, table_ref[b // own, pl.ds((b % own) * width, width), :], preferred_element_type=F32)
    s = jax.nn.sigmoid(acc)
    act = (acc * s).astype(BF)
    cot = own_rows(cot_ref, first, nblk, share).astype(F32)
    pg = (cot * (s * (1.0 + acc * (1.0 - s)))).astype(BF)
    pg_ref[...] = pg
    for g in range(groups):
        y_ref[g, own] = pg
        y_ref[g, own + 1] = act
    for i in range(back_ref.shape[0]):
        back_ref[i] = pg_ref[pl.ds(pl.multiple_of(dst_ref[i] * share, share), share), :]


def score_body(
    nbase, nblk, g_ref, xr_ref, pg_ref, dstv_ref, cnt_ref, relf_ref, table_ref, out_ref, pf
):
    groups = table_ref.shape[0]
    own = nbase // groups
    width = table_ref.shape[2]
    share = xr_ref.shape[0]
    slots = xr_ref.shape[1]
    first = g_ref[0] * share
    pg = pg_ref[...]
    for b in range(nbase):
        base = table_ref[b // own, pl.ds((b % own) * width, width), :]
        p = lax.dot_general(pg, base, NT, preferred_element_type=F32)
        for n in range(nblk):
            put(pf, pl.ds((n * nbase + b) * share, share), p[n * share : (n + 1) * share])
    cnt = cnt_ref[...]

    def one(k, acc):
        pk = get(pf, pl.ds(k, nblk * nbase, stride=share)).astype(BF)
        t = lax.dot_general(pk, xr_ref[k], NT, preferred_element_type=F32)
        return acc + jnp.where(cnt > first + k, t, 0.0)

    acc = lax.fori_loop(0, share, one, jnp.zeros((nblk * nbase, slots), F32), unroll=4)
    blk = dstv_ref[...]
    total = jnp.zeros((nbase, slots), F32)
    for n in range(nblk):
        total += jnp.where(blk == n, acc[n * nbase : (n + 1) * nbase], 0.0)
    for g in range(groups):
        out_ref[g] = total[g * own : (g + 1) * own]


def bwd_body(
    nbase, nblk, pad, g_ref, x_ref, rel_ref, srcv_ref, cnt_ref, table_ref, pg_ref, sw_ref, out_ref, xf, mf
):
    groups = table_ref.shape[0]
    own = nbase // groups
    width = table_ref.shape[2]
    share = BLK // groups
    first = g_ref[0] * share
    w = slot_weights(table_ref, rel_ref, srcv_ref, nblk, own * width, pad)
    spread(x_ref, w, cnt_ref, first, xf, mf, None)
    acc = lax.dot_general(pg_ref[...], sw_ref[...], NT, preferred_element_type=F32)
    for b in range(nbase):
        mb = rows_of(mf, b, nbase, nblk, share).astype(BF)
        base = table_ref[b // own, pl.ds((b % own) * width, width), :]
        acc += lax.dot_general(mb, base, NT, preferred_element_type=F32)
    cols = width // groups
    for g in range(groups):
        out_ref[g] = acc[:, g * cols : (g + 1) * cols].astype(BF)


def basis_body(peers, y_ref, out_ref, tmp, outf):
    groups = y_ref.shape[0]
    own = y_ref.shape[1] - 2
    width = y_ref.shape[3]
    deep = width // peers
    pg = jnp.concatenate([y_ref[g, own] for g in range(groups)], axis=0)
    for b in range(own):
        m = jnp.concatenate([y_ref[g, b] for g in range(groups)], axis=0)
        put(tmp, pl.ds(0, width), lax.dot_general(m, pg, TN, preferred_element_type=F32))
        for d in range(deep):
            put(outf, pl.ds(b * deep + d, peers, stride=own * deep), get(tmp, pl.ds(d, peers, stride=deep)))
    out_ref[...] = get(outf, pl.ds(0, out_ref.shape[0])).astype(BF)


def coef_body(own, in_ref, out_ref):
    peers, _, slots = in_ref.shape
    wide = out_ref.shape[1]

    def one(p, acc):
        blk = in_ref[p]
        score = blk[:own]
        rel = blk[own : own + 1].astype(jnp.int32)
        high = score.astype(BF)
        low = (score - high.astype(F32)).astype(BF)
        ids = lax.broadcasted_iota(jnp.int32, (wide, slots), 0)
        hot = jnp.where(ids == rel, 1.0, 0.0).astype(BF)
        both = jnp.concatenate([high.astype(F32), low.astype(F32)], axis=0).astype(BF)
        return acc + lax.dot_general(both, hot, NT, preferred_element_type=F32)

    acc = lax.fori_loop(0, peers, one, jnp.zeros((2 * own, wide), F32))
    out_ref[...] = acc[:own] + acc[own:]


def local(
    entity_rows,
    self_weight,
    bases,
    coefficients,
    send_block,
    edge_rel,
    edge_dst,
    edge_count,
    cotangent,
):
    peers = lax.axis_size("ent")
    groups = lax.axis_size("basis")
    ent_dev, width = entity_rows.shape
    nblk = ent_dev // BLK
    own = bases.shape[0]
    nbase = own * groups
    relations = coefficients.shape[0]
    cap = send_block.shape[2]
    slots = peers * cap
    share = BLK // groups
    pad = 16
    group = lax.axis_index("basis")
    g = group.reshape(1).astype(jnp.int32)

    src = send_block[0].reshape(slots)
    dst = edge_dst[:, 0, :].reshape(slots)
    rel_out = edge_rel[0].reshape(1, slots)
    cnt_in = edge_count[:, 0, :].reshape(1, slots)

    outgoing = call(
        functools.partial(take_body, share),
        jax.ShapeDtypeStruct((slots, share, width), BF),
        [SM, SM, VM],
    )(src, g, entity_rows)
    incoming = lax.all_to_all(
        outgoing.reshape(peers, cap * share, width), "ent", split_axis=0, concat_axis=0, tiled=True
    )
    notes = jnp.concatenate([edge_rel[0], edge_count[:, 0, :]], axis=1)
    notes = lax.all_to_all(notes, "ent", split_axis=0, concat_axis=0, tiled=True)
    rel_in = notes[:, :cap].reshape(1, slots)
    cnt_out = notes[:, cap:].reshape(1, slots)

    chunks = -(-relations // width)
    coef = jnp.pad(coefficients.astype(BF).T, ((0, pad - own), (0, chunks * width - relations)))
    coef = coef.reshape(pad, chunks, width).transpose(1, 0, 2).reshape(chunks * pad, width)
    table = lax.all_gather(
        jnp.concatenate([bases.reshape(own * width, width), coef], axis=0), "basis"
    )

    dstv, srcv = dst.reshape(1, slots), src.reshape(1, slots)
    y, back, xr, pg = call(
        functools.partial(fwd_body, nbase, nblk, pad),
        (
            jax.ShapeDtypeStruct((groups, own + 2, nblk * share, width), BF),
            jax.ShapeDtypeStruct((slots, share, width), BF),
            jax.ShapeDtypeStruct((share, slots, width), BF),
            jax.ShapeDtypeStruct((nblk * share, width), BF),
        ),
        [SM, SM] + [VM] * 8,
        [rows_scratch(slots * share, width), rows_scratch(nblk * nbase * share, width)],
    )(
        g, dst, incoming.reshape(slots * share, width), rel_in, dstv, cnt_in, table,
        entity_rows, self_weight, cotangent,
    )

    returned = lax.all_to_all(
        back.reshape(peers, cap * share, width), "ent", split_axis=0, concat_axis=0, tiled=True
    )
    shared = lax.all_to_all(y, "basis", split_axis=0, concat_axis=0, tiled=True)

    score = call(
        functools.partial(score_body, nbase, nblk),
        jax.ShapeDtypeStruct((groups, own, slots), F32),
        [SM] + [VM] * 6,
        [rows_scratch(nblk * nbase * share, width)],
    )(g, xr, pg, dstv, cnt_in, rel_in, table)
    score = lax.all_to_all(score, "basis", split_axis=0, concat_axis=0, tiled=True)
    score = jnp.concatenate(
        [jnp.sum(score, axis=0), jnp.broadcast_to(rel_in.astype(F32), (8, slots))], axis=0
    )
    scores = lax.all_to_all(
        jnp.broadcast_to(score[None], (peers,) + score.shape), "ent", split_axis=0, concat_axis=0, tiled=True
    )
    wide = -(-relations // 128) * 128
    coef_grad = call(
        functools.partial(coef_body, own), jax.ShapeDtypeStruct((own, wide), F32), [VM]
    )(scores)[:, :relations].T

    activation = lax.dynamic_slice_in_dim(shared[:, own + 1], group * (width // groups), width // groups, 2)
    activation = activation.reshape(groups, nblk, share, width // groups).transpose(1, 0, 2, 3)
    activation = activation.reshape(ent_dev, width // groups)

    deep = width // peers
    term = call(
        functools.partial(basis_body, peers),
        jax.ShapeDtypeStruct((peers * own * deep, width), BF),
        [VM],
        [rows_scratch(width, width), rows_scratch(peers * own * deep, width)],
    )(shared)
    term = lax.all_to_all(
        term.reshape(peers, own * deep, width), "ent", split_axis=0, concat_axis=0, tiled=True
    )
    basis_grad = jnp.sum(term.astype(F32), axis=0).reshape(own, deep, width)

    grad = call(
        functools.partial(bwd_body, nbase, nblk, pad),
        jax.ShapeDtypeStruct((groups, nblk * share, width // groups), BF),
        [SM] + [VM] * 7,
        [rows_scratch(slots * share, width), rows_scratch(nblk * nbase * share, width)],
    )(g, returned.reshape(slots * share, width), rel_out, srcv, cnt_out, table, pg, self_weight)
    grad = lax.all_to_all(grad, "basis", split_axis=0, concat_axis=0, tiled=True)
    grad = grad.reshape(groups, nblk, share, width // groups).transpose(1, 0, 2, 3)
    entity_grad = grad.reshape(ent_dev, width // groups)
    return (activation, basis_grad, coef_grad, entity_grad)


def solution(mesh):
    placed = (
        P("ent", None),
        P(),
        P("basis", None, None),
        P(None, "basis"),
        P("ent", None, None),
        P("ent", None, None),
        P(None, "ent", None),
        P(None, "ent", None),
        P("ent", None),
    )
    return jax.shard_map(
        local,
        mesh=mesh,
        in_specs=placed,
        out_specs=(P("ent", "basis"), P("basis", "ent", None), P(None, "basis"), P("ent", "basis")),
        check_vma=False,
    )
```

time: 822 us -> 293 us (0.36)
  waiting for transfers between devices: 394 us -> 105 us
  blocking collectives: 244 us -> 61.1 us
  local copies, waits for them, and re-layouts: 72.4 us -> 13.4 us
  Pallas kernels: 0 us -> 56 us
  matrix products: 28.7 us -> 0 us
  other arithmetic: 27.2 us -> 3.33 us
    psum x1 -> x0, blocking collectives: 244 us -> none  [local(): coef_grad = lax.psum(coef_term, 'ent')]
    reduce_scatter x2 -> x0, waiting for transfers between devices: 149 us -> none  [the longest x1 149 us: local(): lax.psum_scatter(basis_term, 'ent', scatter_dimension=1, tiled=True)]
    all_to_all x3 -> x6, waiting for transfers between devices: 198 us -> 105 us  [the longest x1 46.8 us: local(): lax.all_to_all(outgoing.reshape(peers, cap * share, width), 'ent', split_...]
    all_to_all x0 -> x2, blocking collectives: none -> 61.1 us  [the longest x1 34.9 us: local(): shared = lax.all_to_all(y, 'basis', split_axis=0, concat_axis=0, tiled=True)]
    pallas_call x0 -> x6, Pallas kernels: none -> 56 us  [the longest x1 16 us: local(): call(functools.partial(coef_body, own), jax.ShapeDtypeStruct((own, wide),...]
    psum x1 -> x0, waiting for transfers between devices: 47 us -> none  [local(): aggregate = lax.psum(partial_sum, 'basis')]
    dot_general x10 -> x0, matrix products: 28.7 us -> none  [the longest x1 6.23 us: local(): lax.dot_general(flat_back, proj_flat, (((1,), (1,)), ((), ())), preferred...]
    unnamed x30 -> x20, local copies, waits for them, and re-layouts: 28.7 us -> 3.19 us
  transfers between devices with their start and end apart: 6 -> 7, of which waited for: 4 -> 5; matrix products, arithmetic and copies ran while one was open for 7% -> 4% of each run, Pallas kernels for 0% -> 12%
where the time goes in v1:
time: 293 us; the launch traced here: 292 us
  waiting for transfers between devices  105 us (36%)
  blocking collectives  61.1 us (21%)
  Pallas kernels  56 us (19%)
  starting transfers between devices  38.6 us (13%)
  between operations  14.2 us (5%)
  local copies, waits for them, and re-layouts  13.4 us (5%)
  other arithmetic  3.33 us (1%)
    all_to_all x1, waiting for transfers between devices, local(): lax.all_to_all(outgoing.reshape(peers, cap * share, width), 'ent', split_...  46.8 us
    all_to_all x1, waiting for transfers between devices, local(): lax.all_to_all(back.reshape(peers, cap * share, width), 'ent', split_axis...  44.9 us
    all_to_all x1, blocking collectives, local(): shared = lax.all_to_all(y, 'basis', split_axis=0, concat_axis=0, tiled=True)  34.9 us
    all_to_all x1, blocking collectives, local(): lax.all_to_all(jnp.broadcast_to(score[None], (peers,) + score.shape), 'en...  26.2 us
    pallas_call x1, Pallas kernels, local(): call(functools.partial(coef_body, own), jax.ShapeDtypeStruct((own, wide),...  16 us
    all_to_all x1, starting transfers between devices, local(): lax.all_to_all(notes, 'ent', split_axis=0, concat_axis=0, tiled=True)  13 us
    pallas_call x1, Pallas kernels, local(): call(functools.partial(fwd_body, nbase, nblk, pad), (jax.ShapeDtypeStruct...  12.9 us
    pallas_call x1, Pallas kernels, local(): call(functools.partial(bwd_body, nbase, nblk, pad), jax.ShapeDtypeStruct(...  11.3 us
  transfers between devices with their start and end apart: 7, of which 5 were waited for; matrix products, arithmetic and copies ran while one was open for 4% of the time, Pallas kernels for 12%

profile of v1, /device:TPU:1, one launch (start us, length us, event | category | flops | bytes accessed | tf_op | source)
XLA Modules:
  0.0 292.1 jit_solution(14242725981416414583)
XLA Ops:
  7.2 0.8 convert_bitcast_fusion
  8.1 2.3 pad_maximum_fusion
  10.5 0.7 copy.66
  11.2 13.0 %all-to-all-start.1 = ((s32[64,1,4]{2,1,0:T(1,128)}), s32[64,1,4]{2,1,0:T(1,128)S(1)}, u32[]{:S(2)}, u32[]{:S(2)}) async-start(s32[64,1,4]{2,1,0:T(1,128)} %copy.66), calls=%async_computation.1 | async-start | bytes 65536 | tf_op jit(solution)/shard_map/all_to_all | solution.py:257
  24.3 0.7 reshape_squeeze.13.idx_ref
  24.9 2.6 shard_map.120
  27.5 6.0 %all-to-all-done.1 = s32[64,1,4]{2,1,0:T(1,128)S(1)} async-done(((s32[64,1,4]{2,1,0:T(1,128)}), s32[64,1,4]{2,1,0:T(1,128)S(1)}, u32[]{:S(2)}, u32[]{:S(2)}) %all-to-all-start.1) | async-done | bytes 1056 | tf_op jit(solution)/shard_map/all_to_all | solution.py:257
  33.5 4.9 %all-to-all-start = ((bf16[64,64,256]{2,1,0:T(8,128)(2,1)}), bf16[64,64,256]{2,1,0:T(8,128)(2,1)S(1)}, u32[]{:S(2)}, u32[]{:S(2)}) async-start(bf16[64,64,256]{2,1,0:T(8,128)(2,1)} %bitcast.37), calls=%async_computation | async-start | bytes 4194304 | tf_op jit(solution)/shard_map/all_to_all | solution.py:253
  38.5 0.7 reshape_reshape_squeeze.6.dstv_ref
  39.9 0.7 reshape_squeeze.14.cnt_ref
  41.3 46.8 %all-to-all-done = bf16[64,64,256]{2,1,0:T(8,128)(2,1)S(1)} async-done(((bf16[64,64,256]{2,1,0:T(8,128)(2,1)}), bf16[64,64,256]{2,1,0:T(8,128)(2,1)S(1)}, u32[]{:S(2)}, u32[]{:S(2)}) %all-to-all-start) | async-done | bytes 2097184 | tf_op jit(solution)/shard_map/all_to_all | solution.py:253
  88.1 1.3 copy-done.1
  89.5 12.9 %shard_map.121 = (bf16[4,10,128,256]{3,2,1,0:T(8,128)(2,1)}, bf16[128,32,256]{2,1,0:T(8,128)(2,1)}, bf16[32,128,256]{2,1,0:T(8,128)(2,1)}, bf16[128,256]{1,0:T(8,128)(2,1)}) custom-call(s32[1]{0:T(128)} %bitcast.g_ref, s32[128]{0:T(128)} %reshape_squeeze.12.dst_ref, bf16[4096,256]{1,0:T(8,128)(2,1)} %bitcast.38, s32[1,128]{1,0:T(1,128)} %reshape.72.rel_ref.relf_ref, ...), custom_call_target="tpu_custom_call" | custom-call | tf_op jit(solution)/shard_map/pallas_call | solution.py:269
  102.4 8.5 %shard_map.123 = f32[4,8,128]{2,1,0:T(8,128)} custom-call(s32[1]{0:T(128)} %bitcast.g_ref, bf16[32,128,256]{2,1,0:T(8,128)(2,1)} %get-tuple-element.9.xr_ref, bf16[128,256]{1,0:T(8,128)(2,1)} %get-tuple-element.10.pg_ref, s32[1,128]{1,0:T(1,128)} %reshape_reshape_squeeze.6.dstv_ref, s32[1,128]{1,0:T(1,128)} %reshape_squeeze.14.cnt_ref, ...), custom_call_target="tpu_custom_call" | custom-call | tf_op jit(solution)/shard_map/pallas_call | solution.py:289
  110.9 4.2 %all-to-all-start.4 = ((f32[4,8,128]{2,1,0:T(8,128)}), f32[4,8,128]{2,1,0:T(8,128)S(1)}, u32[]{:S(2)}, u32[]{:S(2)}) async-start(f32[4,8,128]{2,1,0:T(8,128)} %shard_map.123), calls=%async_computation.4 | async-start | bytes 32768 | tf_op jit(solution)/shard_map/all_to_all | solution.py:295
  115.2 4.1 %all-to-all-done.4 = f32[4,8,128]{2,1,0:T(8,128)S(1)} async-done(((f32[4,8,128]{2,1,0:T(8,128)}), f32[4,8,128]{2,1,0:T(8,128)S(1)}, u32[]{:S(2)}, u32[]{:S(2)}) %all-to-all-start.4) | async-done | bytes 16416 | tf_op jit(solution)/shard_map/all_to_all | solution.py:295
  119.3 26.2 %all_to_all.47.in_ref = f32[64,16,128]{2,1,0:T(8,128)} all-to-all(f32[64,16,128]{2,1,0:T(8,128)S(1)} %broadcast_in_dim.5), channel_id=1, replica_groups=mesh['ent'=64,'basis'=4] {'ent'}, dimensions={0} | all-to-all | bytes 1048576 | tf_op jit(solution)/shard_map/all_to_all | solution.py:299
  145.5 34.9 %all_to_all.48.y_ref = bf16[4,10,128,256]{3,2,1,0:T(8,128)(2,1)} all-to-all(bf16[4,10,128,256]{3,2,1,0:T(8,128)(2,1)S(1)} %copy-done.2), channel_id=1, replica_groups=mesh['ent'=64,'basis'=4] {'basis'}, dimensions={0} | all-to-all | bytes 5242880 | tf_op jit(solution)/shard_map/all_to_all | solution.py:287
  180.4 6.2 %all-to-all-start.6 = ((bf16[64,64,256]{2,1,0:T(8,128)(2,1)}), bf16[64,64,256]{2,1,0:T(8,128)(2,1)S(1)}, u32[]{:S(2)}, u32[]{:S(2)}) async-start(bf16[64,64,256]{2,1,0:T(8,128)(2,1)} %bitcast.40), calls=%async_computation.6 | async-start | bytes 4194304 | tf_op jit(solution)/shard_map/all_to_all | solution.py:284
  186.6 4.8 %shard_map.122 = bf16[2048,256]{1,0:T(8,128)(2,1)} custom-call(bf16[4,10,128,256]{3,2,1,0:T(8,128)(2,1)} %all_to_all.48.y_ref), custom_call_target="tpu_custom_call" | custom-call | tf_op jit(solution)/shard_map/pallas_call | solution.py:312
  191.4 44.9 %all-to-all-done.6 = bf16[64,64,256]{2,1,0:T(8,128)(2,1)S(1)} async-done(((bf16[64,64,256]{2,1,0:T(8,128)(2,1)}), bf16[64,64,256]{2,1,0:T(8,128)(2,1)S(1)}, u32[]{:S(2)}, u32[]{:S(2)}) %all-to-all-start.6) | async-done | bytes 2097184 | tf_op jit(solution)/shard_map/all_to_all | solution.py:284
  236.3 7.0 %all-to-all-start.3 = ((bf16[64,32,256]{2,1,0:T(8,128)(2,1)}), bf16[64,32,256]{2,1,0:T(8,128)(2,1)S(1)}, u32[]{:S(2)}, u32[]{:S(2)}) async-start(bf16[64,32,256]{2,1,0:T(8,128)(2,1)} %bitcast.39), calls=%async_computation.3 | async-start | bytes 2097152 | tf_op jit(solution)/shard_map/all_to_all | solution.py:318
  243.3 0.7 reshape_reshape_squeeze.7.srcv_ref
  244.7 0.7 reshape.82.cnt_ref
  245.5 16.0 %shard_map.124 = f32[8,1408]{1,0:T(8,128)} custom-call(f32[64,16,128]{2,1,0:T(8,128)} %all_to_all.47.in_ref), custom_call_target="tpu_custom_call" | custom-call | tf_op jit(solution)/shard_map/pallas_call | solution.py:303
  261.4 1.4 slice_bitcast_fusion
  263.0 0.7 copy.76
  263.7 11.3 %shard_map.125 = bf16[4,128,64]{2,1,0:T(8,128)(2,1)} custom-call(s32[1]{0:T(128)} %bitcast.g_ref, bf16[4096,256]{1,0:T(8,128)(2,1)} %bitcast.36, s32[1,128]{1,0:T(1,128)} %reshape_squeeze.15.rel_ref, s32[1,128]{1,0:T(1,128)} %reshape_reshape_squeeze.7.srcv_ref, s32[1,128]{1,0:T(1,128)} %reshape.82.cnt_ref, bf16[4,2144,256]{2,1,0:T(8,128)(2,1)} %bitcast.35, ...), custom_call_target="tpu_custom_call" | custom-call | tf_op jit(solution)/shard_map/pallas_call | solution.py:323
  275.0 1.6 copy.73
  276.7 3.3 %all-to-all-start.7 = ((bf16[4,128,64]{1,2,0:T(8,128)(2,1)}), bf16[4,128,64]{1,2,0:T(8,128)(2,1)S(1)}, u32[]{:S(2)}, u32[]{:S(2)}) async-start(bf16[4,128,64]{1,2,0:T(8,128)(2,1)} %copy.73), calls=%async_computation.7 | async-start | bytes 131072 | tf_op jit(solution)/shard_map/all_to_all | solution.py:329
  280.8 3.6 %all-to-all-done.7 = bf16[4,128,64]{1,2,0:T(8,128)(2,1)S(1)} async-done(((bf16[4,128,64]{1,2,0:T(8,128)(2,1)}), bf16[4,128,64]{1,2,0:T(8,128)(2,1)S(1)}, u32[]{:S(2)}, u32[]{:S(2)}) %all-to-all-start.7) | async-done | bytes 65568 | tf_op jit(solution)/shard_map/all_to_all | solution.py:329
  284.5 0.7 copy.77
  (42 shorter events, 3.8 us)
Async XLA Ops:
  7.2 3.3 %copy-start.4 = (s32[1,64,2]{1,2,0:T(2,128)S(1)}, s32[1,64,2]{1,2,0:T(2,128)}, u32[]{:S(2)}) copy-start(s32[1,64,2]{1,2,0:T(2,128)} %param.14) | copy-start | bytes 1540
  7.2 3.3 %copy-start.3 = (s32[64,1,2]{0,2,1:T(2,128)S(1)}, s32[64,1,2]{0,2,1:T(2,128)}, u32[]{:S(2)}) copy-start(s32[64,1,2]{0,2,1:T(2,128)} %param.16) | copy-start | bytes 1540
  7.2 17.0 %copy-start.5 = (s32[1,64,2]{1,2,0:T(2,128)S(1)}, s32[1,64,2]{1,2,0:T(2,128)}, u32[]{:S(2)}) copy-start(s32[1,64,2]{1,2,0:T(2,128)} %param.13) | copy-start | bytes 1540
  7.2 80.9 %all-gather.3.cloned.1.call-start = ((), (), s32[]{:S(2)}) async-start(), calls=%async_computation.8 | async-start | bytes 5488640 | tf_op jit(solution)/shard_map/all_gather | solution.py:264
  11.2 22.3 %all-to-all-start.1 = ((s32[64,1,4]{2,1,0:T(1,128)}), s32[64,1,4]{2,1,0:T(1,128)S(1)}, u32[]{:S(2)}, u32[]{:S(2)}) async-start(s32[64,1,4]{2,1,0:T(1,128)} %copy.66), calls=%async_computation.1 | async-start | bytes 65536 | tf_op jit(solution)/shard_map/all_to_all | solution.py:257
  33.5 4.9 %copy-start.6 = (s32[64,1,2]{0,2,1:T(2,128)S(1)}, s32[64,1,2]{0,2,1:T(2,128)}, u32[]{:S(2)}) copy-start(s32[64,1,2]{0,2,1:T(2,128)} %param.15) | copy-start | bytes 1540
  33.5 54.6 %all-to-all-start = ((bf16[64,64,256]{2,1,0:T(8,128)(2,1)}), bf16[64,64,256]{2,1,0:T(8,128)(2,1)S(1)}, u32[]{:S(2)}, u32[]{:S(2)}) async-start(bf16[64,64,256]{2,1,0:T(8,128)(2,1)} %bitcast.37), calls=%async_computation | async-start | bytes 4194304 | tf_op jit(solution)/shard_map/all_to_all | solution.py:253
  88.1 1.3 copy-start.1
  102.4 43.1 %copy-start.2 = (bf16[4,10,128,256]{3,2,1,0:T(8,128)(2,1)S(1)}, bf16[4,10,128,256]{3,2,1,0:T(8,128)(2,1)}, u32[]{:S(2)}) copy-start(bf16[4,10,128,256]{3,2,1,0:T(8,128)(2,1)} %get-tuple-element.8) | copy-start | bytes 7864324
  110.9 8.4 %all-to-all-start.4 = ((f32[4,8,128]{2,1,0:T(8,128)}), f32[4,8,128]{2,1,0:T(8,128)S(1)}, u32[]{:S(2)}, u32[]{:S(2)}) async-start(f32[4,8,128]{2,1,0:T(8,128)} %shard_map.123), calls=%async_computation.4 | async-start | bytes 32768 | tf_op jit(solution)/shard_map/all_to_all | solution.py:295
  180.4 55.9 %all-to-all-start.6 = ((bf16[64,64,256]{2,1,0:T(8,128)(2,1)}), bf16[64,64,256]{2,1,0:T(8,128)(2,1)S(1)}, u32[]{:S(2)}, u32[]{:S(2)}) async-start(bf16[64,64,256]{2,1,0:T(8,128)(2,1)} %bitcast.40), calls=%async_computation.6 | async-start | bytes 4194304 | tf_op jit(solution)/shard_map/all_to_all | solution.py:284
  191.4 71.5 %slice-start = ((bf16[4,10,128,256]{3,2,1,0:T(8,128)(2,1)}), bf16[4,1,128,256]{3,2,1,0:T(8,128)(2,1)S(1)}, s32[]{:S(2)}) async-start(bf16[4,10,128,256]{3,2,1,0:T(8,128)(2,1)} %all_to_all.48.y_ref), calls=%async_computation.9 | async-start | bytes 524288 | tf_op jit(solution)/shard_map/slice | solution.py:307
  236.3 27.4 %copy-start = (bf16[64,64,256]{2,1,0:T(8,128)(2,1)}, bf16[64,64,256]{2,1,0:T(8,128)(2,1)S(1)}, u32[]{:S(2)}) copy-start(bf16[64,64,256]{2,1,0:T(8,128)(2,1)S(1)} %all-to-all-done.6) | copy-start | bytes 6291460
  236.3 40.4 %all-to-all-start.3 = ((bf16[64,32,256]{2,1,0:T(8,128)(2,1)}), bf16[64,32,256]{2,1,0:T(8,128)(2,1)S(1)}, u32[]{:S(2)}, u32[]{:S(2)}) async-start(bf16[64,32,256]{2,1,0:T(8,128)(2,1)} %bitcast.39), calls=%async_computation.3 | async-start | bytes 2097152 | tf_op jit(solution)/shard_map/all_to_all | solution.py:318
  276.7 7.7 %all-to-all-start.7 = ((bf16[4,128,64]{1,2,0:T(8,128)(2,1)}), bf16[4,128,64]{1,2,0:T(8,128)(2,1)S(1)}, u32[]{:S(2)}, u32[]{:S(2)}) async-start(bf16[4,128,64]{1,2,0:T(8,128)(2,1)} %copy.73), calls=%async_computation.7 | async-start | bytes 131072 | tf_op jit(solution)/shard_map/all_to_all | solution.py:329
Sparse Core Ops, SparseCore 0:
  10.6 56.2 all-gather.2

commit v2 on v0

v2 whole, which is shorter than its diff:
```python
import functools

import jax
import jax.numpy as jnp
from jax import lax
from jax.experimental import pallas as pl
from jax.experimental.pallas import tpu as pltpu
from jax.sharding import PartitionSpec as P

BLK = 128
LANES = 128
NX = 4
NC = 2
BF = jnp.bfloat16
F32 = jnp.float32
NT = (((1,), (1,)), ((), ()))
TN = (((0,), (0,)), ((), ()))
MIB = 1024 * 1024
VM = pl.BlockSpec(memory_space=pltpu.VMEM)
SM = pl.BlockSpec(memory_space=pltpu.SMEM)


def call(body, outs, ins, scratch=(), limit=16):
    return pl.pallas_call(
        body,
        out_shape=outs,
        in_specs=ins,
        out_specs=jax.tree.map(lambda _: VM, outs),
        scratch_shapes=list(scratch),
        compiler_params=pltpu.CompilerParams(vmem_limit_bytes=limit * MIB),
    )


def bf(*shape):
    return jax.ShapeDtypeStruct(shape, BF)


def get(ref, at):
    return jnp.concatenate([ref[h, at, :] for h in range(ref.shape[0])], axis=1)


def put(ref, at, value):
    for h in range(ref.shape[0]):
        ref[h, at, :] = value[:, h * LANES : (h + 1) * LANES]


def rows_scratch(rows, width):
    return pltpu.VMEM((width // LANES, rows, LANES), F32)


def turn(i, r, n):
    return lax.rem(i + r + n, n)


def aligned(i, size):
    return pl.ds(pl.multiple_of(i * size, size), size)


def digits(value):
    high = value.astype(BF)
    return high, (value - high.astype(F32)).astype(BF)


def take_body(share, pos_ref, idx_ref, rel_ref, ent_ref, out_ref):
    first = pos_ref[0] * share
    cap = idx_ref.shape[2]
    halves = ent_ref.shape[1] // LANES
    lane = lax.broadcasted_iota(jnp.int32, (8, LANES), 1)
    for q in range(out_ref.shape[0]):
        note = jnp.zeros((8, LANES), jnp.int32)
        for c in range(cap):
            row = pl.multiple_of(idx_ref[0, q, c] * BLK + first, share)
            block = ent_ref[pl.ds(row, share), :]
            for h in range(halves):
                out_ref[q, pl.ds((c * halves + h) * share, share), :] = block[:, h * LANES : (h + 1) * LANES]
            rel = rel_ref[0, q, c]
            note = jnp.where(lane == 2 * c, rel >> 8, note)
            note = jnp.where(lane == 2 * c + 1, rel & 255, note)
        out_ref[q, pl.ds(cap * halves * share, 8), :] = note.astype(F32).astype(BF)


def slot_weights(own, pos_ref, coef_refs, rel, blk, nblk, cs):
    groups = len(coef_refs)
    rows, width = coef_refs[0].shape
    chunks = rows // 16
    slots = rel.shape[1]
    parts = [jnp.zeros((16, slots), F32) for _ in coef_refs]
    for j in range(chunks):
        ids = lax.broadcasted_iota(jnp.int32, (width, slots), 0) + j * width
        hot = jnp.where(ids == rel, 1.0, 0.0).astype(BF)
        for r, ref in enumerate(coef_refs):
            parts[r] += jnp.dot(ref[pl.ds(j * 16, 16), :], hot, preferred_element_type=F32)
    for r in range(groups):
        cs[turn(pos_ref[0], -r, groups)] = parts[r][:own]
    coef = cs[...].reshape(groups * own, slots)
    return jnp.concatenate([jnp.where(blk == n, coef, 0.0) for n in range(nblk)], axis=0)


def widen(x_ref, xf):
    step = 512

    def some(i, c):
        at = aligned(i, step)
        xf[at, :] = x_ref[at, :].astype(F32)
        return c

    lax.fori_loop(0, x_ref.shape[0] // step, some, 0, unroll=2 if x_ref.shape[0] % 1024 == 0 else 1)


def slot_rows(xf, peers, cap, halves, share, k):
    per = xf.shape[0] // peers
    return jnp.concatenate(
        [
            jnp.concatenate(
                [xf[pl.ds((c * halves + h) * share + k, peers, stride=per), :] for h in range(halves)], axis=1
            )
            for c in range(cap)
        ],
        axis=0,
    )


def rows_of(mf, base, nbase, nblk, share):
    return jnp.concatenate([get(mf, aligned(n * nbase + base, share)) for n in range(nblk)], axis=0)


def own_rows(ref, first, nblk, share):
    return jnp.concatenate(
        [ref[pl.ds(pl.multiple_of(n * BLK + first, share), share), :] for n in range(nblk)], axis=0
    )


def fwd_body(
    cap, nblk, own, pos_ref, dst_ref, count_ref, x_ref, dstv_ref, cnt_ref, c0, c1, c2, c3, table_ref, ent_ref,
    sw_ref, cot_ref, y0, y1, y2, y3, back_ref, xr_ref, pg_ref, rel_ref, xf, mf, cs, at_ref,
):
    groups = table_ref.shape[0]
    nbase = groups * own
    width = table_ref.shape[2]
    halves = width // LANES
    share = BLK // groups
    peers = back_ref.shape[0]
    per = xf.shape[0] // peers
    first = pos_ref[0] * share
    widen(x_ref, xf)
    notes = xf[pl.ds(cap * halves * share, peers, stride=per), :].astype(BF)
    lane = lax.broadcasted_iota(jnp.int32, (8, LANES), 1)
    line = lax.broadcasted_iota(jnp.int32, (8, LANES), 0)
    pick = jnp.where(lane == 2 * line, 256.0, jnp.where(lane == 2 * line + 1, 1.0, 0.0)).astype(BF)
    rels = lax.dot_general(pick, notes, NT, preferred_element_type=F32).astype(jnp.int32)
    rel = jnp.concatenate([rels[c : c + 1] for c in range(cap)], axis=1)
    rel_ref[...] = rel
    w = slot_weights(own, pos_ref, (c0, c1, c2, c3), rel, dstv_ref[...], nblk, cs)
    cnt = cnt_ref[...]

    def one(k, c):
        xk = slot_rows(xf, peers, cap, halves, share, k).astype(BF)
        xr_ref[k] = xk
        wk = jnp.where(cnt > first + k, w, 0.0).astype(BF)
        put(mf, pl.ds(k, w.shape[0], stride=share), jnp.dot(wk, xk, preferred_element_type=F32))
        return c

    lax.fori_loop(0, share, one, 0, unroll=4)
    acc = jnp.dot(own_rows(ent_ref, first, nblk, share), sw_ref[...], preferred_element_type=F32)
    ys = (y0, y1, y2, y3)
    rows = nblk * share
    for r, y in enumerate(ys):
        group = turn(pos_ref[0], r, groups)
        for b in range(own):
            mb = rows_of(mf, group * own + b, nbase, nblk, share).astype(BF)
            y[pl.ds(b * rows, rows), :] = mb
            acc += jnp.dot(mb, table_ref[group, pl.ds(b * width, width), :], preferred_element_type=F32)
    s = jax.nn.sigmoid(acc)
    at_ref[...] = (acc * s).T
    cot = own_rows(cot_ref, first, nblk, share).astype(F32)
    pg = (cot * (s * (1.0 + acc * (1.0 - s)))).astype(BF)
    pg_ref[...] = pg
    cols = width // groups
    for r, y in enumerate(ys):
        y[pl.ds(own * rows, rows), :] = pg
        group = turn(pos_ref[0], r, groups)
        act = at_ref[aligned(group, cols), :].astype(BF)
        half = cols // halves
        for h in range(halves):
            y[pl.ds((own + 1) * rows, half), h * LANES : (h + 1) * LANES] = act[h * half : (h + 1) * half]
    k_of = lax.broadcasted_iota(jnp.int32, (share, width), 0) + first
    for q in range(peers):
        for c in range(cap):
            block = pg_ref[aligned(dst_ref[q, 0, c], share), :]
            block = jnp.where(k_of < count_ref[q, 0, c], block.astype(F32), 0.0).astype(BF)
            for h in range(halves):
                back_ref[q, pl.ds((c * halves + h) * share, share), :] = block[:, h * LANES : (h + 1) * LANES]


def score_body(nblk, own, pos_ref, xr_ref, pg_ref, dstv_ref, cnt_ref, table_ref, s0, s1, s2, s3, pf, ts):
    groups = table_ref.shape[0]
    nbase = groups * own
    width = table_ref.shape[2]
    share, slots = xr_ref.shape[:2]
    first = pos_ref[0] * share
    pg = pg_ref[...]
    for b in range(nbase):
        base = table_ref[b // own, pl.ds((b % own) * width, width), :]
        p = lax.dot_general(pg, base, NT, preferred_element_type=F32)
        for n in range(nblk):
            put(pf, pl.ds((n * nbase + b) * share, share), p[n * share : (n + 1) * share])
    cnt = cnt_ref[...]

    def one(k, acc):
        pk = get(pf, pl.ds(k, nblk * nbase, stride=share)).astype(BF)
        t = lax.dot_general(pk, xr_ref[k], NT, preferred_element_type=F32)
        return acc + jnp.where(cnt > first + k, t, 0.0)

    acc = lax.fori_loop(0, share, one, jnp.zeros((nblk * nbase, slots), F32), unroll=4)
    blk = dstv_ref[...]
    total = jnp.zeros((nbase, slots), F32)
    for n in range(nblk):
        total += jnp.where(blk == n, acc[n * nbase : (n + 1) * nbase], 0.0)
    ts[...] = total
    for r, out in enumerate((s0, s1, s2, s3)):
        out[...] = ts[aligned(turn(pos_ref[0], r, groups), own), :]


def coef_body(rel_ref, s0, s1, s2, s3, out_ref):
    own, slots = s0.shape
    width = out_ref.shape[1]
    chunks = out_ref.shape[0] // (2 * own)
    high, low = digits((s0[...] + s1[...]) + (s2[...] + s3[...]))
    both = jnp.concatenate([high.astype(F32), low.astype(F32)], axis=0).astype(BF)
    rel = rel_ref[...]
    parts = []
    for j in range(chunks):
        ids = lax.broadcasted_iota(jnp.int32, (width, slots), 0) + j * width
        hot = jnp.where(ids == rel, 1.0, 0.0).astype(BF)
        t = lax.dot_general(both, hot, NT, preferred_element_type=F32)
        parts.append(t[:own] + t[own:])
    pack(out_ref, 0, jnp.concatenate(parts, axis=0))


def pack(ref, at, value):
    high, low = digits(value)
    n = value.shape[0]
    ref[pl.ds(at, n), :] = high
    ref[pl.ds(at + n, n), :] = low


def unpack(ref, at, n):
    return ref[pl.ds(at, n), :].astype(F32) + ref[pl.ds(at + n, n), :].astype(F32)


def basis_body(own, rows, peers, pos_ref, y0, y1, y2, y3, coef_ref, keep_ref, send_ref, tmp, outf):
    ys = (y0, y1, y2, y3)
    width = y0.shape[1]
    part = keep_ref.shape[0]
    each = part // NX
    deep = part * NC // (own * peers)
    nz = each // (own * deep)
    pg = jnp.concatenate([y[pl.ds(own * rows, rows), :] for y in ys], axis=0)
    for b in range(own):
        m = jnp.concatenate([y[pl.ds(b * rows, rows), :] for y in ys], axis=0)
        put(tmp, pl.ds(0, width), lax.dot_general(m, pg, TN, preferred_element_type=F32))
        for c in range(NC):
            for x in range(NX):
                for d in range(deep):
                    put(
                        outf,
                        pl.ds((c * NX + x) * each + b * deep + d, nz, stride=own * deep),
                        get(tmp, pl.ds((x * NC + c) * deep + d, nz, stride=NX * NC * deep)),
                    )
    keep_ref[...] = get(outf, aligned(pos_ref[1], part)).astype(BF)
    send_ref[pl.ds(0, part), :] = get(outf, aligned(1 - pos_ref[1], part)).astype(BF)
    send_ref[pl.ds(part, coef_ref.shape[0]), :] = coef_ref[...]


def core_body(pos_ref, keep_ref, got_ref, coef_ref, o0, o1, o2, o3, sums):
    part = keep_ref.shape[0]
    each = part // NX
    n = coef_ref.shape[0] // 2
    sums[...] = keep_ref[...].astype(F32) + got_ref[pl.ds(0, part), :].astype(F32)
    coef = unpack(coef_ref, 0, n) + unpack(got_ref, part, n)
    for r, out in enumerate((o0, o1, o2, o3)):
        out[pl.ds(0, each), :] = sums[aligned(turn(pos_ref[2], r, NX), each), :].astype(BF)
        pack(out, each, coef)


def x_body(nz, *refs):
    pos_ref, i0, i1, i2, i3 = refs[:5]
    outs = refs[5 : 5 + nz]
    sums, order = refs[5 + nz :]
    n = order.shape[1]
    each = i0.shape[0] - 2 * n
    last = each // nz
    sums[...] = sum(i[pl.ds(0, each), :].astype(F32) for i in (i0, i1, i2, i3))
    for r, i in enumerate((i0, i1, i2, i3)):
        order[turn(pos_ref[2], -r, NX)] = unpack(i, each, n)
    coef = (order[0] + order[1]) + (order[2] + order[3])
    for r, out in enumerate(outs):
        out[pl.ds(0, last), :] = sums[aligned(turn(pos_ref[3], r, nz), last), :].astype(BF)
        pack(out, last, coef)


def z_body(nz, own, *refs):
    pos_ref = refs[0]
    ins = refs[1 : 1 + nz]
    basis_ref, coef_ref, order = refs[1 + nz :]
    n = order.shape[1]
    last = basis_ref.shape[0]
    width = basis_ref.shape[1]
    basis_ref[...] = sum(i[pl.ds(0, last), :].astype(F32) for i in ins)
    for r, i in enumerate(ins):
        order[turn(pos_ref[3], -r, nz)] = unpack(i, last, n)
    coef = order[0]
    for r in range(1, nz):
        coef = coef + order[r]
    relations = coef_ref.shape[1]
    for j in range(n // own):
        size = min(width, relations - j * width)
        coef_ref[:, pl.ds(j * width, size)] = coef[j * own : (j + 1) * own, :size]


def bwd_body(
    cap, nblk, own, pos_ref, x_ref, rel_ref, srcv_ref, c0, c1, c2, c3, table_ref, pg_ref, sw_ref,
    o0, o1, o2, o3, xf, mf, cs, at_ref,
):
    groups = table_ref.shape[0]
    nbase = groups * own
    width = table_ref.shape[2]
    halves = width // LANES
    share = BLK // groups
    peers = rel_ref.shape[1] // cap
    w = slot_weights(own, pos_ref, (c0, c1, c2, c3), rel_ref[...], srcv_ref[...], nblk, cs).astype(BF)
    widen(x_ref, xf)

    def one(k, c):
        xk = slot_rows(xf, peers, cap, halves, share, k).astype(BF)
        put(mf, pl.ds(k, w.shape[0], stride=share), jnp.dot(w, xk, preferred_element_type=F32))
        return c

    lax.fori_loop(0, share, one, 0, unroll=4)
    acc = lax.dot_general(pg_ref[...], sw_ref[...], NT, preferred_element_type=F32)
    for b in range(nbase):
        mb = rows_of(mf, b, nbase, nblk, share).astype(BF)
        base = table_ref[b // own, pl.ds((b % own) * width, width), :]
        acc += lax.dot_general(mb, base, NT, preferred_element_type=F32)
    at_ref[...] = acc.T
    cols = width // groups
    for r, out in enumerate((o0, o1, o2, o3)):
        out[...] = at_ref[aligned(turn(pos_ref[0], r, groups), cols), :].astype(BF)


def join_body(nblk, row, pos_ref, i0, i1, i2, i3, out_ref, order):
    cols = out_ref.shape[0]
    share = BLK // 4
    for r, i in enumerate((i0, i1, i2, i3)):
        if row is None:
            piece = i[...]
        else:
            half = cols * LANES // i.shape[1]
            piece = jnp.concatenate(
                [i[pl.ds(row, half), h * LANES : (h + 1) * LANES] for h in range(i.shape[1] // LANES)], axis=0
            )
        order[turn(pos_ref[0], -r, 4)] = piece.astype(F32)
    for n in range(nblk):
        whole = jnp.concatenate([order[g][:, n * share : (n + 1) * share] for g in range(4)], axis=1)
        out_ref[:, n * BLK : (n + 1) * BLK] = whole.astype(BF)


def local(
    entity_rows,
    self_weight,
    bases,
    coefficients,
    send_block,
    edge_rel,
    edge_dst,
    edge_count,
    cotangent,
):
    peers = lax.axis_size("ent")
    groups = lax.axis_size("basis")
    ent_dev, width = entity_rows.shape
    nblk = ent_dev // BLK
    own = bases.shape[0]
    nbase = own * groups
    relations = coefficients.shape[0]
    cap = send_block.shape[2]
    slots = peers * cap
    share = BLK // groups
    halves = width // LANES
    nz = peers // (NX * NC)
    rows = nblk * share
    me = lax.axis_index("ent")
    pos = jnp.stack([lax.axis_index("basis"), me % NC, (me // NC) % NX, me // (NC * NX)]).astype(jnp.int32)

    def over_y(r, value):
        return lax.ppermute(value, "basis", [(i, (i + r) % groups) for i in range(groups)])

    def over_c(value):
        return lax.ppermute(value, "ent", [(i, i ^ 1) for i in range(peers)])

    def over_x(r, value):
        pairs = [(i, i - NC * ((i // NC) % NX) + NC * (((i // NC) + r) % NX)) for i in range(peers)]
        return lax.ppermute(value, "ent", pairs)

    def over_z(r, value):
        return lax.ppermute(value, "ent", [(i, (i + r * NC * NX) % peers) for i in range(peers)])

    def lines(value):
        return value.reshape(peers, cap).T.reshape(1, slots)

    dstv, srcv = lines(edge_dst), lines(send_block)
    cnt_in, rel_out = lines(edge_count), lines(edge_rel)

    per = cap * halves * share
    outgoing = call(functools.partial(take_body, share), bf(peers, per + 8, LANES), [SM, SM, SM, VM])(
        pos, send_block, edge_rel, entity_rows
    )
    incoming = lax.all_to_all(outgoing, "ent", split_axis=0, concat_axis=0, tiled=True)

    table = lax.all_gather(bases.reshape(own * width, width), "basis")
    chunks = -(-relations // width)
    coef = jnp.pad(coefficients.astype(BF).T, ((0, 16 - own), (0, chunks * width - relations)))
    coef = coef.reshape(16, chunks, width).transpose(1, 0, 2).reshape(chunks * 16, width)
    coefs = [coef] + [over_y(r, coef) for r in range(1, groups)]

    sides = [
        rows_scratch(nblk * nbase * share, width),
        pltpu.VMEM((groups, own, slots), F32),
        pltpu.VMEM((width, rows), F32),
    ]
    *ys, back, xr, pg, rel_in = call(
        functools.partial(fwd_body, cap, nblk, own),
        (
            *[bf((own + 1) * rows + share, width) for _ in range(groups)],
            bf(peers, per, LANES),
            bf(share, slots, width),
            bf(rows, width),
            jax.ShapeDtypeStruct((1, slots), jnp.int32),
        ),
        [SM] * 3 + [VM] * 11,
        [pltpu.VMEM((peers * (per + 8), LANES), F32), *sides],
        limit=28,
    )(
        pos, edge_dst, edge_count, incoming.reshape(peers * (per + 8), LANES), dstv, cnt_in, *coefs, table,
        entity_rows, self_weight, cotangent,
    )

    returned = lax.all_to_all(back, "ent", split_axis=0, concat_axis=0, tiled=True)
    ys = [ys[0]] + [over_y(r, ys[r]) for r in range(1, groups)]

    scores = call(
        functools.partial(score_body, nblk, own),
        tuple(jax.ShapeDtypeStruct((own, slots), F32) for _ in range(groups)),
        [SM] + [VM] * 5,
        [rows_scratch(nblk * nbase * share, width), pltpu.VMEM((nbase, slots), F32)],
    )(pos, xr, pg, dstv, cnt_in, table)
    scores = [scores[0]] + [over_y(r, scores[r]) for r in range(1, groups)]
    lot = chunks * own
    coef_part = call(coef_body, bf(2 * lot, width), [VM] * 5)(rel_in, *scores)

    part = peers * (own * width // peers) // NC
    keep, send = call(
        functools.partial(basis_body, own, rows, peers),
        (bf(part, width), bf(part + 2 * lot, width)),
        [SM] + [VM] * 5,
        [rows_scratch(width, width), rows_scratch(NC * part, width)],
    )(pos, *ys, coef_part)
    got = over_c(send)
    each = part // NX
    outs = call(
        core_body,
        tuple(bf(each + 2 * lot, width) for _ in range(NX)),
        [SM] + [VM] * 3,
        [pltpu.VMEM((part, width), F32)],
    )(pos, keep, got, coef_part)
    ins = [outs[0]] + [over_x(r, outs[r]) for r in range(1, NX)]
    last = each // nz
    outs = call(
        functools.partial(x_body, nz),
        tuple(bf(last + 2 * lot, width) for _ in range(nz)),
        [SM] + [VM] * NX,
        [pltpu.VMEM((each, width), F32), pltpu.VMEM((NX, lot, width), F32)],
    )(pos, *ins)
    ins = [outs[0]] + [over_z(r, outs[r]) for r in range(1, nz)]
    basis_grad, coef_grad = call(
        functools.partial(z_body, nz, own),
        (jax.ShapeDtypeStruct((last, width), F32), jax.ShapeDtypeStruct((own, relations), F32)),
        [SM] + [VM] * nz,
        [pltpu.VMEM((nz, lot, width), F32)],
    )(pos, *ins)

    cols = width // groups

    def join(row, pieces):
        return call(
            functools.partial(join_body, nblk, row),
            bf(cols, ent_dev),
            [SM] + [VM] * groups,
            [pltpu.VMEM((groups, cols, rows), F32)],
        )(pos, *pieces).T

    activation = join((own + 1) * rows, ys)

    grads = call(
        functools.partial(bwd_body, cap, nblk, own),
        tuple(bf(cols, rows) for _ in range(groups)),
        [SM] + [VM] * 10,
        [pltpu.VMEM((peers * per, LANES), F32), *sides],
        limit=20,
    )(pos, returned.reshape(peers * per, LANES), rel_out, srcv, *coefs, table, pg, self_weight)
    grads = [grads[0]] + [over_y(r, grads[r]) for r in range(1, groups)]
    entity_grad = join(None, grads)
    return (activation, basis_grad.reshape(own, width // peers, width), coef_grad.T, entity_grad)


def solution(mesh):
    placed = (
        P("ent", None),
        P(),
        P("basis", None, None),
        P(None, "basis"),
        P("ent", None, None),
        P("ent", None, None),
        P(None, "ent", None),
        P(None, "ent", None),
        P("ent", None),
    )
    return jax.shard_map(
        local,
        mesh=mesh,
        in_specs=placed,
        out_specs=(P("ent", "basis"), P("basis", "ent", None), P(None, "basis"), P("ent", "basis")),
        check_vma=False,
    )
```

time: 822 us -> 218 us (0.27)
  waiting for transfers between devices: 394 us -> 67.9 us
  blocking collectives: 244 us -> 0 us
  local copies, waits for them, and re-layouts: 72.4 us -> 35.8 us
  Pallas kernels: 0 us -> 35.7 us
  matrix products: 28.7 us -> 0 us
  other arithmetic: 27.2 us -> 0.08 us
  starting transfers between devices: 36.6 us -> 60.9 us
    psum x1 -> x0, blocking collectives: 244 us -> none  [local(): coef_grad = lax.psum(coef_term, 'ent')]
    reduce_scatter x2 -> x0, waiting for transfers between devices: 149 us -> none  [the longest x1 149 us: local(): lax.psum_scatter(basis_term, 'ent', scatter_dimension=1, tiled=True)]
    all_to_all x1, waiting for transfers between devices: 179 us -> 43.2 us  [local(): lax.all_to_all(outgoing, 'ent', split_axis=0, concat_axis=0, tiled=True)]
    psum x1 -> x0, waiting for transfers between devices: 47 us -> none  [local(): aggregate = lax.psum(partial_sum, 'basis')]
    ppermute x0 -> x23, starting transfers between devices: none -> 40.6 us  [the longest x12 19.3 us: over_y(): lax.ppermute(value, 'basis', [(i, (i + r) % groups) for i in range(groups)])]
    pallas_call x0 -> x11, Pallas kernels: none -> 35.7 us  [the longest x1 8.75 us: local(): call(functools.partial(bwd_body, cap, nblk, own), tuple((bf(cols, rows) f...]
    dot_general x10 -> x0, matrix products: 28.7 us -> none  [the longest x1 6.23 us: local(): lax.dot_general(flat_back, proj_flat, (((1,), (1,)), ((), ())), preferred...]
    select_n x8 -> x0, other arithmetic: 24.4 us -> none  [the longest x1 8.05 us: local(): jnp.where(live_rows[..., None], back_blocks, jnp.zeros((), jnp.bfloat16))]
  transfers between devices with their start and end apart: 6 -> 26, of which waited for: 4 -> 7; matrix products, arithmetic and copies ran while one was open for 7% -> 3% of each run, Pallas kernels for 0% -> 12%
where the time goes in v2:
time: 218 us; the launch traced here: 215 us
  waiting for transfers between devices  67.9 us (31%)
  starting transfers between devices  60.9 us (28%)
  local copies, waits for them, and re-layouts  35.8 us (16%)
  Pallas kernels  35.7 us (16%)
  between operations  14.4 us (7%)
    all_to_all x1, waiting for transfers between devices, local(): lax.all_to_all(outgoing, 'ent', split_axis=0, concat_axis=0, tiled=True)  43.2 us
    unnamed x100, local copies, waits for them, and re-layouts  31.3 us
    ppermute x12, starting transfers between devices, over_y(): lax.ppermute(value, 'basis', [(i, (i + r) % groups) for i in range(groups)])  19.3 us
    ppermute x7, starting transfers between devices, over_z(): lax.ppermute(value, 'ent', [(i, (i + r * NC * NX) % peers) for i in range...  14.1 us
    ppermute x12, waiting for transfers between devices, over_y(): lax.ppermute(value, 'basis', [(i, (i + r) % groups) for i in range(groups)])  13.4 us
    all_to_all x1, starting transfers between devices, local(): lax.all_to_all(outgoing, 'ent', split_axis=0, concat_axis=0, tiled=True)  13.1 us
    ppermute x3, waiting for transfers between devices, over_x(): return lax.ppermute(value, 'ent', pairs)  9.06 us
    pallas_call x1, Pallas kernels, local(): call(functools.partial(bwd_body, cap, nblk, own), tuple((bf(cols, rows) f...  8.75 us
  transfers between devices with their start and end apart: 26, of which 7 were waited for; matrix products, arithmetic and copies ran while one was open for 3% of the time, Pallas kernels for 12%

profile of v2, /device:TPU:1, one launch (start us, length us, event | category | flops | bytes accessed | tf_op | source)
XLA Modules:
  0.0 214.6 jit_solution(13222074833213311108)
XLA Ops:
  10.5 2.1 shard_map.120
  14.6 13.1 %all-to-all-start = ((bf16[64,136,128]{2,1,0:T(8,128)(2,1)}), bf16[64,136,128]{2,1,0:T(8,128)(2,1)S(1)}, u32[]{:S(2)}, u32[]{:S(2)}) async-start(bf16[64,136,128]{2,1,0:T(8,128)(2,1)} %copy-done.3), calls=%async_computation | async-start | bytes 4456448 | tf_op jit(solution)/shard_map/all_to_all | solution.py:418
  29.2 2.6 %collective-permute-start.1 = (bf16[96,256]{1,0:T(8,128)(2,1)S(1)}, bf16[96,256]{1,0:T(8,128)(2,1)S(1)}, u32[]{:S(2)}, u32[]{:S(2)}) collective-permute-start(bf16[96,256]{1,0:T(8,128)(2,1)S(1)} %bitcast.29), channel_id=1, source_target_pairs={{0,2},{1,3},{2,0},{3,1},{4,6},{5,7},{6,4},{7,5},{8,10},{9,11},{10,... | collective-permute-start | bytes 147464 | tf_op jit(solution)/shard_map/ppermute | solution.py:396
  34.3 2.7 %collective-permute-done.1.c2 = bf16[96,256]{1,0:T(8,128)(2,1)S(1)} collective-permute-done((bf16[96,256]{1,0:T(8,128)(2,1)S(1)}, bf16[96,256]{1,0:T(8,128)(2,1)S(1)}, u32[]{:S(2)}, u32[]{:S(2)}) %collective-permute-start.1) | collective-permute-done | bytes 49184 | tf_op jit(solution)/shard_map/ppermute | solution.py:396
  37.0 43.2 %all-to-all-done = bf16[64,136,128]{2,1,0:T(8,128)(2,1)S(1)} async-done(((bf16[64,136,128]{2,1,0:T(8,128)(2,1)}), bf16[64,136,128]{2,1,0:T(8,128)(2,1)S(1)}, u32[]{:S(2)}, u32[]{:S(2)}) %all-to-all-start) | async-done | bytes 2228256 | tf_op jit(solution)/shard_map/all_to_all | solution.py:418
  80.2 2.2 %copy-done = bf16[4,2048,256]{2,1,0:T(8,128)(2,1)S(1)} copy-done((bf16[4,2048,256]{2,1,0:T(8,128)(2,1)S(1)}, bf16[4,2048,256]{2,1,0:T(8,128)(2,1)}, u32[]{:S(2)}) %copy-start) | copy-done | bytes 4194328
  85.3 8.7 %shard_map.121 = (bf16[1184,256]{1,0:T(8,128)(2,1)S(1)}, bf16[1184,256]{1,0:T(8,128)(2,1)S(1)}, bf16[1184,256]{1,0:T(8,128)(2,1)S(1)}, bf16[1184,256]{1,0:T(8,12...) custom-call(s32[4]{0:T(128)S(1)} %copy-done.28, ...), custom_call_target="tpu_custom_call" | custom-call | tf_op jit(solution)/shard_map/pallas_call | solution.py:431
  95.3 1.4 copy-done.9
  99.8 7.1 %all-to-all-start.1 = ((bf16[64,128,128]{2,1,0:T(8,128)(2,1)}), bf16[64,128,128]{2,1,0:T(8,128)(2,1)S(1)}, u32[]{:S(2)}, u32[]{:S(2)}) async-start(bf16[64,128,128]{2,1,0:T(8,128)(2,1)} %copy-done.8), calls=%async_computation.1 | async-start | bytes 4194304 | tf_op jit(solution)/shard_map/all_to_all | solution.py:448
  108.2 2.6 %collective-permute-start.4 = (bf16[1184,256]{1,0:T(8,128)(2,1)}, bf16[1184,256]{1,0:T(8,128)(2,1)S(1)}, u32[]{:S(2)}, u32[]{:S(2)}) collective-permute-start(bf16[1184,256]{1,0:T(8,128)(2,1)} %copy-done.43), channel_id=1, source_target_pairs={{0,2},{1,3},{2,0},{3,1},{4,6},{5,7},{6,4},{7,5},{8,10},{9,11},{10,... | collective-permute-start | bytes 1818632 | tf_op jit(solution)/shard_map/ppermute | solution.py:396
  111.9 2.2 %copy-done.1 = bf16[4,2048,256]{2,1,0:T(8,128)(2,1)S(1)} copy-done((bf16[4,2048,256]{2,1,0:T(8,128)(2,1)S(1)}, bf16[4,2048,256]{2,1,0:T(8,128)(2,1)}, u32[]{:S(2)}) %copy-start.1) | copy-done | bytes 4194328
  114.1 1.6 copy-done.10
  117.7 5.3 %shard_map.123 = (f32[8,128]{1,0:T(8,128)S(1)}, f32[8,128]{1,0:T(8,128)S(1)}, f32[8,128]{1,0:T(8,128)S(1)}, f32[8,128]{1,0:T(8,128)S(1)}) custom-call(s32[4]{0:T(128)S(1)} %copy-done.29, bf16[32,128,256]{2,1,0:T(8,128)(2,1)S(1)} %copy-done.10, bf16[128,256]{1,0:T(8,128)(2,1)S(1)} %get-tuple-element.42.pg_ref, s32[1,128]{1,0:T(1,128)S(1)} %copy-done.35, ...), custom_call_target="tpu_custom_call" | custom-call | tf_op jit(solution)/shard_map/pallas_call | solution.py:451
  124.3 9.9 %collective-permute-done.6.s1 = f32[8,128]{1,0:T(8,128)S(1)} collective-permute-done((f32[8,128]{1,0:T(8,128)S(1)}, f32[8,128]{1,0:T(8,128)S(1)}, u32[]{:S(2)}, u32[]{:S(2)}) %collective-permute-start.6) | collective-permute-done | bytes 4128 | tf_op jit(solution)/shard_map/ppermute | solution.py:396
  134.2 3.6 %collective-permute-start.8 = (f32[8,128]{1,0:T(8,128)S(1)}, f32[8,128]{1,0:T(8,128)S(1)}, u32[]{:S(2)}, u32[]{:S(2)}) collective-permute-start(f32[8,128]{1,0:T(8,128)S(1)} %get-tuple-element.46), channel_id=1, source_target_pairs={{0,3},{1,0},{2,1},{3,2},{4,7},{5,4},{6,5},{7,6},{8,11},{9,8},{10,9... | collective-permute-start | bytes 12296 | tf_op jit(solution)/shard_map/ppermute | solution.py:396
  138.8 4.1 %shard_map.125 = (bf16[1024,256]{1,0:T(8,128)(2,1)S(1)}, bf16[1120,256]{1,0:T(8,128)(2,1)S(1)}) custom-call(s32[4]{0:T(128)S(1)} %copy-done.29, bf16[1184,256]{1,0:T(8,128)(2,1)S(1)} %get-tuple-element.36.i0.y0, bf16[1184,256]{1,0:T(8,128)(2,1)S(1)} %collective-permute-done.3.i1.y1, bf16[1184,256]{1,0:T(8,128)(2,1)S(1)} %collective-permute-done.4.i2.y2, ...), custom_call_target="tpu_custom_call" | custom-call | tf_op jit(solution)/shard_map/pallas_call | solution.py:462
  143.8 2.2 %collective-permute-start.9 = (bf16[1120,256]{1,0:T(8,128)(2,1)S(1)}, bf16[1120,256]{1,0:T(8,128)(2,1)S(1)}, u32[]{:S(2)}, u32[]{:S(2)}) collective-permute-start(bf16[1120,256]{1,0:T(8,128)(2,1)S(1)} %get-tuple-element.48), channel_id=1, source_target_pairs={{0,4},{4,0},{8,12},{12,8},{16,20},{20,16},{24,28},{28,24},{32,36},... | collective-permute-start | bytes 1720328 | tf_op jit(solution)/shard_map/ppermute | solution.py:399
  146.0 1.6 collective-permute-done.9.got_ref
  148.4 1.5 collective-permute-start.10
  149.9 2.4 %collective-permute-start.11 = (bf16[352,256]{1,0:T(8,128)(2,1)S(1)}, bf16[352,256]{1,0:T(8,128)(2,1)S(1)}, u32[]{:S(2)}, u32[]{:S(2)}) collective-permute-start(bf16[352,256]{1,0:T(8,128)(2,1)S(1)} %get-tuple-element.51), channel_id=1, source_target_pairs={{0,16},{4,20},{8,24},{12,28},{16,0},{20,4},{24,8},{28,12},{32,48},... | collective-permute-start | bytes 540680 | tf_op jit(solution)/shard_map/ppermute | solution.py:403
  153.4 3.4 %collective-permute-done.10.refs_2_ = bf16[352,256]{1,0:T(8,128)(2,1)S(1)} collective-permute-done((bf16[352,256]{1,0:T(8,128)(2,1)S(1)}, bf16[352,256]{1,0:T(8,128)(2,1)S(1)}, u32[]{:S(2)}, u32[]{:S(2)}) %collective-permute-start.10) | collective-permute-done | bytes 180256 | tf_op jit(solution)/shard_map/ppermute | solution.py:403
  156.9 5.6 %collective-permute-done.11.refs_3_ = bf16[352,256]{1,0:T(8,128)(2,1)S(1)} collective-permute-done((bf16[352,256]{1,0:T(8,128)(2,1)S(1)}, bf16[352,256]{1,0:T(8,128)(2,1)S(1)}, u32[]{:S(2)}, u32[]{:S(2)}) %collective-permute-start.11) | collective-permute-done | bytes 180256 | tf_op jit(solution)/shard_map/ppermute | solution.py:403
  162.5 1.4 shard_map.127
  165.4 1.8 collective-permute-start.14
  167.2 2.3 %collective-permute-start.15 = (bf16[128,256]{1,0:T(8,128)(2,1)}, bf16[128,256]{1,0:T(8,128)(2,1)}, u32[]{:S(2)}, u32[]{:S(2)}) collective-permute-start(bf16[128,256]{1,0:T(8,128)(2,1)} %get-tuple-element.56), channel_id=1, source_target_pairs={{0,96},{4,100},{8,104},{12,108},{16,112},{20,116},{24,120},{28,124... | collective-permute-start | bytes 196616 | tf_op jit(solution)/shard_map/ppermute | solution.py:406
  169.5 2.1 collective-permute-start.16
  171.5 2.6 %collective-permute-start.17 = (bf16[128,256]{1,0:T(8,128)(2,1)}, bf16[128,256]{1,0:T(8,128)(2,1)}, u32[]{:S(2)}, u32[]{:S(2)}) collective-permute-start(bf16[128,256]{1,0:T(8,128)(2,1)} %get-tuple-element.58), channel_id=1, source_target_pairs={{0,160},{4,164},{8,168},{12,172},{16,176},{20,180},{24,184},{28,18... | collective-permute-start | bytes 196616 | tf_op jit(solution)/shard_map/ppermute | solution.py:406
  174.7 3.4 %collective-permute-start.18 = (bf16[128,256]{1,0:T(8,128)(2,1)}, bf16[128,256]{1,0:T(8,128)(2,1)}, u32[]{:S(2)}, u32[]{:S(2)}) collective-permute-start(bf16[128,256]{1,0:T(8,128)(2,1)} %get-tuple-element.59), channel_id=1, source_target_pairs={{0,192},{4,196},{8,200},{12,204},{16,208},{20,212},{24,216},{28,22... | collective-permute-start | bytes 196616 | tf_op jit(solution)/shard_map/ppermute | solution.py:406
  182.4 2.2 %copy-done.2 = bf16[4,2048,256]{2,1,0:T(8,128)(2,1)S(1)} copy-done((bf16[4,2048,256]{2,1,0:T(8,128)(2,1)S(1)}, bf16[4,2048,256]{2,1,0:T(8,128)(2,1)}, u32[]{:S(2)}) %copy-start.2) | copy-done | bytes 4194328
  189.0 8.7 %shard_map.129 = (bf16[64,128]{1,0:T(8,128)(2,1)S(1)}, bf16[64,128]{1,0:T(8,128)(2,1)}, bf16[64,128]{1,0:T(8,128)(2,1)}, bf16[64,128]{1,0:T(8,128)(2,1)}) custom-call(s32[4]{0:T(128)S(1)} %copy-done.30, bf16[8192,128]{1,0:T(8,128)(2,1)S(1)} %bitcast.27, s32[1,128]{1,0:T(1,128)S(1)} %copy-done.40, s32[1,128]{1,0:T(1,128)S(1)} %copy-done.41, ...), custom_call_target="tpu_custom_call" | custom-call | tf_op jit(solution)/shard_map/pallas_call | solution.py:504
  198.4 3.3 %collective-permute-start.21 = (bf16[64,128]{1,0:T(8,128)(2,1)}, bf16[64,128]{1,0:T(8,128)(2,1)S(1)}, u32[]{:S(2)}, u32[]{:S(2)}) collective-permute-start(bf16[64,128]{1,0:T(8,128)(2,1)} %get-tuple-element.66), channel_id=1, source_target_pairs={{0,2},{1,3},{2,0},{3,1},{4,6},{5,7},{6,4},{7,5},{8,10},{9,11},{10,... | collective-permute-start | bytes 49160 | tf_op jit(solution)/shard_map/ppermute | solution.py:396
  203.4 1.7 shard_map.128
  (142 shorter events, 41.7 us)
Async XLA Ops:
  7.2 73.0 %all-gather.2.cloned.1.call-start = ((), (), s32[]{:S(2)}) async-start(), calls=%async_computation.2 | async-start | bytes 5242880 | tf_op jit(solution)/shard_map/all_gather | solution.py:420
  14.6 65.6 %copy-start.12 = (bf16[512,256]{1,0:T(8,128)(2,1)S(1)}, bf16[512,256]{1,0:T(8,128)(2,1)}, u32[]{:S(2)}) copy-start(bf16[512,256]{1,0:T(8,128)(2,1)} %ent_ref.3) | copy-start | bytes 786436
  14.6 65.6 %copy-start.13 = (bf16[256,256]{1,0:T(8,128)(2,1)S(1)}, bf16[256,256]{1,0:T(8,128)(2,1)}, u32[]{:S(2)}) copy-start(bf16[256,256]{1,0:T(8,128)(2,1)} %sw_ref.3) | copy-start | bytes 393220
  14.6 65.6 %all-to-all-start = ((bf16[64,136,128]{2,1,0:T(8,128)(2,1)}), bf16[64,136,128]{2,1,0:T(8,128)(2,1)S(1)}, u32[]{:S(2)}, u32[]{:S(2)}) async-start(bf16[64,136,128]{2,1,0:T(8,128)(2,1)} %copy-done.3), calls=%async_computation | async-start | bytes 4456448 | tf_op jit(solution)/shard_map/all_to_all | solution.py:418
  27.9 6.4 %collective-permute-start = (bf16[96,256]{1,0:T(8,128)(2,1)S(1)}, bf16[96,256]{1,0:T(8,128)(2,1)S(1)}, u32[]{:S(2)}, u32[]{:S(2)}) collective-permute-start(bf16[96,256]{1,0:T(8,128)(2,1)S(1)} %bitcast.28), channel_id=1, source_target_pairs={{0,1},{1,2},{2,3},{3,0},{4,5},{5,6},{6,7},{7,4},{8,9},{9,10},{10,1... | collective-permute-start | bytes 147464 | tf_op jit(solution)/shard_map/ppermute | solution.py:396
  29.2 7.7 %collective-permute-start.1 = (bf16[96,256]{1,0:T(8,128)(2,1)S(1)}, bf16[96,256]{1,0:T(8,128)(2,1)S(1)}, u32[]{:S(2)}, u32[]{:S(2)}) collective-permute-start(bf16[96,256]{1,0:T(8,128)(2,1)S(1)} %bitcast.29), channel_id=1, source_target_pairs={{0,2},{1,3},{2,0},{3,1},{4,6},{5,7},{6,4},{7,5},{8,10},{9,11},{10,... | collective-permute-start | bytes 147464 | tf_op jit(solution)/shard_map/ppermute | solution.py:396
  31.9 5.1 %collective-permute-start.2 = (bf16[96,256]{1,0:T(8,128)(2,1)S(1)}, bf16[96,256]{1,0:T(8,128)(2,1)S(1)}, u32[]{:S(2)}, u32[]{:S(2)}) collective-permute-start(bf16[96,256]{1,0:T(8,128)(2,1)S(1)} %bitcast.30), channel_id=1, source_target_pairs={{0,3},{1,0},{2,1},{3,2},{4,7},{5,4},{6,5},{7,6},{8,11},{9,8},{10,9... | collective-permute-start | bytes 147464 | tf_op jit(solution)/shard_map/ppermute | solution.py:396
  34.3 59.6 %copy-start.15 = (bf16[96,256]{1,0:T(8,128)(2,1)}, bf16[96,256]{1,0:T(8,128)(2,1)S(1)}, u32[]{:S(2)}) copy-start(bf16[96,256]{1,0:T(8,128)(2,1)S(1)} %collective-permute-done.c1) | copy-start | bytes 147460
  37.0 57.0 %copy-start.17 = (bf16[96,256]{1,0:T(8,128)(2,1)}, bf16[96,256]{1,0:T(8,128)(2,1)S(1)}, u32[]{:S(2)}) copy-start(bf16[96,256]{1,0:T(8,128)(2,1)S(1)} %collective-permute-done.1.c2) | copy-start | bytes 147460
  37.0 57.0 %copy-start.19 = (bf16[96,256]{1,0:T(8,128)(2,1)}, bf16[96,256]{1,0:T(8,128)(2,1)S(1)}, u32[]{:S(2)}) copy-start(bf16[96,256]{1,0:T(8,128)(2,1)S(1)} %collective-permute-done.2.c3) | copy-start | bytes 147460
  99.8 82.7 %all-to-all-start.1 = ((bf16[64,128,128]{2,1,0:T(8,128)(2,1)}), bf16[64,128,128]{2,1,0:T(8,128)(2,1)S(1)}, u32[]{:S(2)}, u32[]{:S(2)}) async-start(bf16[64,128,128]{2,1,0:T(8,128)(2,1)} %copy-done.8), calls=%async_computation.1 | async-start | bytes 4194304 | tf_op jit(solution)/shard_map/all_to_all | solution.py:448
  106.8 31.9 %collective-permute-start.3 = (bf16[1184,256]{1,0:T(8,128)(2,1)}, bf16[1184,256]{1,0:T(8,128)(2,1)S(1)}, u32[]{:S(2)}, u32[]{:S(2)}) collective-permute-start(bf16[1184,256]{1,0:T(8,128)(2,1)} %copy-done.44), channel_id=1, source_target_pairs={{0,1},{1,2},{2,3},{3,0},{4,5},{5,6},{6,7},{7,4},{8,9},{9,10},{10,1... | collective-permute-start | bytes 1818632 | tf_op jit(solution)/shard_map/ppermute | solution.py:396
  108.2 30.6 %collective-permute-start.4 = (bf16[1184,256]{1,0:T(8,128)(2,1)}, bf16[1184,256]{1,0:T(8,128)(2,1)S(1)}, u32[]{:S(2)}, u32[]{:S(2)}) collective-permute-start(bf16[1184,256]{1,0:T(8,128)(2,1)} %copy-done.43), channel_id=1, source_target_pairs={{0,2},{1,3},{2,0},{3,1},{4,6},{5,7},{6,4},{7,5},{8,10},{9,11},{10,... | collective-permute-start | bytes 1818632 | tf_op jit(solution)/shard_map/ppermute | solution.py:396
  110.8 27.9 %collective-permute-start.5 = (bf16[1184,256]{1,0:T(8,128)(2,1)}, bf16[1184,256]{1,0:T(8,128)(2,1)S(1)}, u32[]{:S(2)}, u32[]{:S(2)}) collective-permute-start(bf16[1184,256]{1,0:T(8,128)(2,1)} %copy-done.42), channel_id=1, source_target_pairs={{0,3},{1,0},{2,1},{3,2},{4,7},{5,4},{6,5},{7,6},{8,11},{9,8},{10,9... | collective-permute-start | bytes 1818632 | tf_op jit(solution)/shard_map/ppermute | solution.py:396
  117.7 20.9 %copy-start.39 = (s32[1,128]{1,0:T(1,128)S(1)}, s32[1,128]{1,0:T(1,128)}, u32[]{:S(2)}) copy-start(s32[1,128]{1,0:T(1,128)} %copy-done.38) | copy-start | bytes 1540
  123.0 11.2 %collective-permute-start.6 = (f32[8,128]{1,0:T(8,128)S(1)}, f32[8,128]{1,0:T(8,128)S(1)}, u32[]{:S(2)}, u32[]{:S(2)}) collective-permute-start(f32[8,128]{1,0:T(8,128)S(1)} %get-tuple-element.44), channel_id=1, source_target_pairs={{0,1},{1,2},{2,3},{3,0},{4,5},{5,6},{6,7},{7,4},{8,9},{9,10},{10,1... | collective-permute-start | bytes 12296 | tf_op jit(solution)/shard_map/ppermute | solution.py:396
  123.5 14.3 %collective-permute-start.7 = (f32[8,128]{1,0:T(8,128)S(1)}, f32[8,128]{1,0:T(8,128)S(1)}, u32[]{:S(2)}, u32[]{:S(2)}) collective-permute-start(f32[8,128]{1,0:T(8,128)S(1)} %get-tuple-element.45), channel_id=1, source_target_pairs={{0,2},{1,3},{2,0},{3,1},{4,6},{5,7},{6,4},{7,5},{8,10},{9,11},{10,... | collective-permute-start | bytes 12296 | tf_op jit(solution)/shard_map/ppermute | solution.py:396
  134.2 4.4 %collective-permute-start.8 = (f32[8,128]{1,0:T(8,128)S(1)}, f32[8,128]{1,0:T(8,128)S(1)}, u32[]{:S(2)}, u32[]{:S(2)}) collective-permute-start(f32[8,128]{1,0:T(8,128)S(1)} %get-tuple-element.46), channel_id=1, source_target_pairs={{0,3},{1,0},{2,1},{3,2},{4,7},{5,4},{6,5},{7,6},{8,11},{9,8},{10,9... | collective-permute-start | bytes 12296 | tf_op jit(solution)/shard_map/ppermute | solution.py:396
  143.8 3.8 %collective-permute-start.9 = (bf16[1120,256]{1,0:T(8,128)(2,1)S(1)}, bf16[1120,256]{1,0:T(8,128)(2,1)S(1)}, u32[]{:S(2)}, u32[]{:S(2)}) collective-permute-start(bf16[1120,256]{1,0:T(8,128)(2,1)S(1)} %get-tuple-element.48), channel_id=1, source_target_pairs={{0,4},{4,0},{8,12},{12,8},{16,20},{20,16},{24,28},{28,24},{32,36},... | collective-permute-start | bytes 1720328 | tf_op jit(solution)/shard_map/ppermute | solution.py:399
  148.4 8.5 %collective-permute-start.10 = (bf16[352,256]{1,0:T(8,128)(2,1)S(1)}, bf16[352,256]{1,0:T(8,128)(2,1)S(1)}, u32[]{:S(2)}, u32[]{:S(2)}) collective-permute-start(bf16[352,256]{1,0:T(8,128)(2,1)S(1)} %get-tuple-element.50), channel_id=1, source_target_pairs={{0,8},{4,12},{8,16},{12,20},{16,24},{20,28},{24,0},{28,4},{32,40},... | collective-permute-start | bytes 540680 | tf_op jit(solution)/shard_map/ppermute | solution.py:403
  149.9 12.6 %collective-permute-start.11 = (bf16[352,256]{1,0:T(8,128)(2,1)S(1)}, bf16[352,256]{1,0:T(8,128)(2,1)S(1)}, u32[]{:S(2)}, u32[]{:S(2)}) collective-permute-start(bf16[352,256]{1,0:T(8,128)(2,1)S(1)} %get-tuple-element.51), channel_id=1, source_target_pairs={{0,16},{4,20},{8,24},{12,28},{16,0},{20,4},{24,8},{28,12},{32,48},... | collective-permute-start | bytes 540680 | tf_op jit(solution)/shard_map/ppermute | solution.py:403
  152.3 10.2 %collective-permute-start.12 = (bf16[352,256]{1,0:T(8,128)(2,1)S(1)}, bf16[352,256]{1,0:T(8,128)(2,1)S(1)}, u32[]{:S(2)}, u32[]{:S(2)}) collective-permute-start(bf16[352,256]{1,0:T(8,128)(2,1)S(1)} %get-tuple-element.52), channel_id=1, source_target_pairs={{0,24},{4,28},{8,0},{12,4},{16,8},{20,12},{24,16},{28,20},{32,56},... | collective-permute-start | bytes 540680 | tf_op jit(solution)/shard_map/ppermute | solution.py:403
  164.5 9.6 %collective-permute-start.13 = (bf16[128,256]{1,0:T(8,128)(2,1)S(1)}, bf16[128,256]{1,0:T(8,128)(2,1)S(1)}, u32[]{:S(2)}, u32[]{:S(2)}) collective-permute-start(bf16[128,256]{1,0:T(8,128)(2,1)S(1)} %get-tuple-element.54), channel_id=1, source_target_pairs={{0,32},{4,36},{8,40},{12,44},{16,48},{20,52},{24,56},{28,60},{32,6... | collective-permute-start | bytes 196616 | tf_op jit(solution)/shard_map/ppermute | solution.py:406
  165.4 12.8 %collective-permute-start.14 = (bf16[128,256]{1,0:T(8,128)(2,1)S(1)}, bf16[128,256]{1,0:T(8,128)(2,1)S(1)}, u32[]{:S(2)}, u32[]{:S(2)}) collective-permute-start(bf16[128,256]{1,0:T(8,128)(2,1)S(1)} %get-tuple-element.55), channel_id=1, source_target_pairs={{0,64},{4,68},{8,72},{12,76},{16,80},{20,84},{24,88},{28,92},{32,9... | collective-permute-start | bytes 196616 | tf_op jit(solution)/shard_map/ppermute | solution.py:406
  167.2 30.6 %collective-permute-start.15 = (bf16[128,256]{1,0:T(8,128)(2,1)}, bf16[128,256]{1,0:T(8,128)(2,1)}, u32[]{:S(2)}, u32[]{:S(2)}) collective-permute-start(bf16[128,256]{1,0:T(8,128)(2,1)} %get-tuple-element.56), channel_id=1, source_target_pairs={{0,96},{4,100},{8,104},{12,108},{16,112},{20,116},{24,120},{28,124... | collective-permute-start | bytes 196616 | tf_op jit(solution)/shard_map/ppermute | solution.py:406
  169.5 29.0 %collective-permute-start.16 = (bf16[128,256]{1,0:T(8,128)(2,1)}, bf16[128,256]{1,0:T(8,128)(2,1)}, u32[]{:S(2)}, u32[]{:S(2)}) collective-permute-start(bf16[128,256]{1,0:T(8,128)(2,1)} %get-tuple-element.57), channel_id=1, source_target_pairs={{0,128},{4,132},{8,136},{12,140},{16,144},{20,148},{24,152},{28,15... | collective-permute-start | bytes 196616 | tf_op jit(solution)/shard_map/ppermute | solution.py:406
  171.5 30.2 %collective-permute-start.17 = (bf16[128,256]{1,0:T(8,128)(2,1)}, bf16[128,256]{1,0:T(8,128)(2,1)}, u32[]{:S(2)}, u32[]{:S(2)}) collective-permute-start(bf16[128,256]{1,0:T(8,128)(2,1)} %get-tuple-element.58), channel_id=1, source_target_pairs={{0,160},{4,164},{8,168},{12,172},{16,176},{20,180},{24,184},{28,18... | collective-permute-start | bytes 196616 | tf_op jit(solution)/shard_map/ppermute | solution.py:406
  174.7 28.7 %collective-permute-start.18 = (bf16[128,256]{1,0:T(8,128)(2,1)}, bf16[128,256]{1,0:T(8,128)(2,1)}, u32[]{:S(2)}, u32[]{:S(2)}) collective-permute-start(bf16[128,256]{1,0:T(8,128)(2,1)} %get-tuple-element.59), channel_id=1, source_target_pairs={{0,192},{4,196},{8,200},{12,204},{16,208},{20,212},{24,216},{28,22... | collective-permute-start | bytes 196616 | tf_op jit(solution)/shard_map/ppermute | solution.py:406
  178.8 24.6 %collective-permute-start.19 = (bf16[128,256]{1,0:T(8,128)(2,1)}, bf16[128,256]{1,0:T(8,128)(2,1)}, u32[]{:S(2)}, u32[]{:S(2)}) collective-permute-start(bf16[128,256]{1,0:T(8,128)(2,1)} %get-tuple-element.60), channel_id=1, source_target_pairs={{0,224},{4,228},{8,232},{12,236},{16,240},{20,244},{24,248},{28,25... | collective-permute-start | bytes 196616 | tf_op jit(solution)/shard_map/ppermute | solution.py:406
  197.8 8.0 %collective-permute-start.20 = (bf16[64,128]{1,0:T(8,128)(2,1)}, bf16[64,128]{1,0:T(8,128)(2,1)S(1)}, u32[]{:S(2)}, u32[]{:S(2)}) collective-permute-start(bf16[64,128]{1,0:T(8,128)(2,1)} %get-tuple-element.65), channel_id=1, source_target_pairs={{0,1},{1,2},{2,3},{3,0},{4,5},{5,6},{6,7},{7,4},{8,9},{9,10},{10,1... | collective-permute-start | bytes 49160 | tf_op jit(solution)/shard_map/ppermute | solution.py:396
  198.4 7.3 %collective-permute-start.21 = (bf16[64,128]{1,0:T(8,128)(2,1)}, bf16[64,128]{1,0:T(8,128)(2,1)S(1)}, u32[]{:S(2)}, u32[]{:S(2)}) collective-permute-start(bf16[64,128]{1,0:T(8,128)(2,1)} %get-tuple-element.66), channel_id=1, source_target_pairs={{0,2},{1,3},{2,0},{3,1},{4,6},{5,7},{6,4},{7,5},{8,10},{9,11},{10,... | collective-permute-start | bytes 49160 | tf_op jit(solution)/shard_map/ppermute | solution.py:396
  201.7 4.0 %collective-permute-start.22 = (bf16[64,128]{1,0:T(8,128)(2,1)}, bf16[64,128]{1,0:T(8,128)(2,1)S(1)}, u32[]{:S(2)}, u32[]{:S(2)}) collective-permute-start(bf16[64,128]{1,0:T(8,128)(2,1)} %get-tuple-element.67), channel_id=1, source_target_pairs={{0,3},{1,0},{2,1},{3,2},{4,7},{5,4},{6,5},{7,6},{8,11},{9,8},{10,9... | collective-permute-start | bytes 49160 | tf_op jit(solution)/shard_map/ppermute | solution.py:396
  (42 other events, 142.9 us)
Sparse Core Ops, SparseCore 0:
  9.8 56.7 all-gather.1

commit v3 on v2

v3 whole, which is shorter than its diff:
```python
import functools

import jax
import jax.numpy as jnp
from jax import lax
from jax.experimental import pallas as pl
from jax.experimental.pallas import tpu as pltpu
from jax.sharding import Mesh
from jax.sharding import PartitionSpec as P

BLK = 128
LANES = 128
NX = 4
NC = 2
ENT = ("z", "x", "c")
BF = jnp.bfloat16
F32 = jnp.float32
NT = (((1,), (1,)), ((), ()))
TN = (((0,), (0,)), ((), ()))
MIB = 1024 * 1024
VM = pl.BlockSpec(memory_space=pltpu.VMEM)
SM = pl.BlockSpec(memory_space=pltpu.SMEM)
HB = pl.BlockSpec(memory_space=pltpu.HBM)


def call(body, outs, ins, scratch=(), limit=16, outs_in=None):
    return pl.pallas_call(
        body,
        out_shape=outs,
        in_specs=ins,
        out_specs=outs_in or jax.tree.map(lambda _: VM, outs),
        scratch_shapes=list(scratch),
        compiler_params=pltpu.CompilerParams(vmem_limit_bytes=limit * MIB),
    )


def bf(*shape):
    return jax.ShapeDtypeStruct(shape, BF)


def get(ref, at):
    return jnp.concatenate([ref[h, at, :] for h in range(ref.shape[0])], axis=1)


def put(ref, at, value):
    for h in range(ref.shape[0]):
        ref[h, at, :] = value[:, h * LANES : (h + 1) * LANES]


def rows_scratch(rows, width):
    return pltpu.VMEM((width // LANES, rows, LANES), F32)


def turn(i, r, n):
    return lax.rem(i + r + n, n)


def aligned(i, size):
    return pl.ds(pl.multiple_of(i * size, size), size)


def digits(value):
    high = value.astype(BF)
    return high, (value - high.astype(F32)).astype(BF)


def start_all(copies):
    for copy in copies:
        copy.start()
    return copies


def wait_all(copies):
    for copy in copies:
        copy.wait()


def own_row_copies(ref, scr, sem, share):
    first = lax.axis_index("basis") * share
    return [
        pltpu.make_async_copy(
            ref.at[pl.ds(pl.multiple_of(n * BLK + first, share), share), :],
            scr.at[pl.ds(n * share, share), :],
            sem.at[n],
        )
        for n in range(scr.shape[0] // share)
    ]


def line(ref):
    return jnp.concatenate([ref[c : c + 1, :] for c in range(ref.shape[0])], axis=1)


def take_body(share, idx_ref, rel_ref, ent_ref, out_ref, own, outs, sem, osem):
    wait_all(start_all(own_row_copies(ent_ref, own, sem, share)))
    cap, peers = idx_ref.shape
    halves = own.shape[1] // LANES
    lane = lax.broadcasted_iota(jnp.int32, (8, LANES), 1)
    lots = osem.shape[0]
    lot = peers // lots
    copies = []
    for q in range(peers):
        note = jnp.zeros((8, LANES), jnp.int32)
        for c in range(cap):
            block = own[aligned(idx_ref[c, q], share), :]
            for h in range(halves):
                outs[q, pl.ds((c * halves + h) * share, share), :] = block[:, h * LANES : (h + 1) * LANES]
            rel = rel_ref[c, q]
            note = jnp.where(lane == 2 * c, rel >> 8, note)
            note = jnp.where(lane == 2 * c + 1, rel & 255, note)
        outs[q, pl.ds(cap * halves * share, 8), :] = note.astype(F32).astype(BF)
        if (q + 1) % lot == 0:
            i = q // lot
            at = pl.ds(i * lot, lot)
            copies += start_all([pltpu.make_async_copy(outs.at[at], out_ref.at[at], osem.at[i])])
    wait_all(copies)


def slot_weights(own, coef_refs, rel, blk, nblk, cs):
    groups = len(coef_refs)
    rows, width = coef_refs[0].shape
    chunks = rows // 16
    slots = rel.shape[1]
    parts = [jnp.zeros((16, slots), F32) for _ in coef_refs]
    for j in range(chunks):
        ids = lax.broadcasted_iota(jnp.int32, (width, slots), 0) + j * width
        hot = jnp.where(ids == rel, 1.0, 0.0).astype(BF)
        for r, ref in enumerate(coef_refs):
            parts[r] += jnp.dot(ref[pl.ds(j * 16, 16), :], hot, preferred_element_type=F32)
    for r in range(groups):
        cs[turn(lax.axis_index("basis"), -r, groups)] = parts[r][:own]
    coef = cs[...].reshape(groups * own, slots)
    return jnp.concatenate([jnp.where(blk == n, coef, 0.0) for n in range(nblk)], axis=0)


def weights_body(nblk, own, rel_ref, src_ref, c0, c1, c2, c3, out_ref, cs):
    out_ref[...] = slot_weights(own, (c0, c1, c2, c3), line(rel_ref), line(src_ref), nblk, cs).astype(BF)


def widen(x_ref, xf):
    step = 512

    def some(i, c):
        at = aligned(i, step)
        xf[at, :] = x_ref[at, :].astype(F32)
        return c

    lax.fori_loop(0, x_ref.shape[0] // step, some, 0)


def slot_rows(xf, peers, cap, halves, share, k):
    per = xf.shape[0] // peers
    return jnp.concatenate(
        [
            jnp.concatenate(
                [xf[pl.ds((c * halves + h) * share + k, peers, stride=per), :] for h in range(halves)], axis=1
            )
            for c in range(cap)
        ],
        axis=0,
    )


def rows_of(mf, base, nbase, nblk, share):
    return jnp.concatenate([get(mf, aligned(n * nbase + base, share)) for n in range(nblk)], axis=0)


def table_copies(table_ref, tab, sem):
    return [pltpu.make_async_copy(table_ref.at[g], tab.at[g], sem.at[g]) for g in range(tab.shape[0])]


def fwd_body(
    cap, nblk, own, dst_ref, count_ref, x_ref, dstv_ref, cnt_ref, c0, c1, c2, c3, sw_ref, table_ref, ent_ref,
    cot_ref, y0, y1, y2, y3, back_ref, xr_ref, pg_ref, rel_ref, act_ref,
    xf, mf, cs, at_ref, tab, ent, cot, ysc, back, xr, tsem, esem, csem, ysem, bsem, xsem,
):
    groups = tab.shape[0]
    nbase = groups * own
    width = tab.shape[2]
    halves = width // LANES
    share = BLK // groups
    peers = back.shape[0]
    per = xf.shape[0] // peers
    group0 = lax.axis_index("basis")
    first = group0 * share
    ecopies = start_all(own_row_copies(ent_ref, ent, esem, share))
    tcopies = start_all(table_copies(table_ref, tab, tsem))
    ccopies = start_all(own_row_copies(cot_ref, cot, csem, share))
    widen(x_ref, xf)
    notes = xf[pl.ds(cap * halves * share, peers, stride=per), :].astype(BF)
    lane = lax.broadcasted_iota(jnp.int32, (8, LANES), 1)
    row = lax.broadcasted_iota(jnp.int32, (8, LANES), 0)
    pick = jnp.where(lane == 2 * row, 256.0, jnp.where(lane == 2 * row + 1, 1.0, 0.0)).astype(BF)
    rels = lax.dot_general(pick, notes, NT, preferred_element_type=F32).astype(jnp.int32)
    rel = jnp.concatenate([rels[c : c + 1] for c in range(cap)], axis=1)
    rel_ref[...] = rel
    w = slot_weights(own, (c0, c1, c2, c3), rel, line(dstv_ref), nblk, cs)
    cnt = line(cnt_ref)

    def one(k, c):
        xk = slot_rows(xf, peers, cap, halves, share, k).astype(BF)
        xr[k] = xk
        wk = jnp.where(cnt > first + k, w, 0.0).astype(BF)
        put(mf, pl.ds(k, w.shape[0], stride=share), jnp.dot(wk, xk, preferred_element_type=F32))
        return c

    lax.fori_loop(0, share, one, 0, unroll=4)
    copies = start_all([pltpu.make_async_copy(xr, xr_ref, xsem)])
    wait_all(ecopies)
    acc = jnp.dot(ent[...], sw_ref[...], preferred_element_type=F32)
    rows = nblk * share
    wait_all(tcopies)
    for r in range(groups):
        group = turn(group0, r, groups)
        for b in range(own):
            mb = rows_of(mf, group * own + b, nbase, nblk, share).astype(BF)
            ysc[r, pl.ds(b * rows, rows), :] = mb
            acc += jnp.dot(mb, tab[group, pl.ds(b * width, width), :], preferred_element_type=F32)
    s = jax.nn.sigmoid(acc)
    at_ref[...] = (acc * s).T
    wait_all(ccopies)
    pg = (cot[...].astype(F32) * (s * (1.0 + acc * (1.0 - s)))).astype(BF)
    pg_ref[...] = pg
    k_of = lax.broadcasted_iota(jnp.int32, (share, width), 0) + first
    lots = bsem.shape[0]
    lot = peers // lots
    for q in range(peers):
        for c in range(cap):
            block = pg_ref[aligned(dst_ref[c, q], share), :]
            block = jnp.where(k_of < count_ref[c, q], block.astype(F32), 0.0).astype(BF)
            for h in range(halves):
                back[q, pl.ds((c * halves + h) * share, share), :] = block[:, h * LANES : (h + 1) * LANES]
        if (q + 1) % lot == 0:
            i = q // lot
            at = pl.ds(i * lot, lot)
            copies += start_all([pltpu.make_async_copy(back.at[at], back_ref.at[at], bsem.at[i])])
    cols = width // groups
    for r, y in enumerate((y0, y1, y2, y3)):
        ysc[r, pl.ds(own * rows, rows), :] = pg
        copies += start_all([pltpu.make_async_copy(ysc.at[r], y, ysem.at[r])])
        act_ref[r] = at_ref[aligned(turn(group0, r, groups), cols), :].astype(BF)
    wait_all(copies)


def score_body(nblk, own, pg_ref, dstv_ref, cnt_ref, xr_ref, table_ref, s0, s1, s2, s3, pf, ts, tab, xr, tsem, xsem):
    groups = tab.shape[0]
    nbase = groups * own
    width = tab.shape[2]
    share, slots = xr.shape[:2]
    group0 = lax.axis_index("basis")
    first = group0 * share
    tcopies = start_all(table_copies(table_ref, tab, tsem))
    xcopies = start_all([pltpu.make_async_copy(xr_ref, xr, xsem)])
    pg = pg_ref[...]
    for b in range(nbase):
        if b % own == 0:
            tcopies[b // own].wait()
        base = tab[b // own, pl.ds((b % own) * width, width), :]
        p = lax.dot_general(pg, base, NT, preferred_element_type=F32)
        for n in range(nblk):
            put(pf, pl.ds((n * nbase + b) * share, share), p[n * share : (n + 1) * share])
    cnt = line(cnt_ref)
    wait_all(xcopies)

    def one(k, acc):
        pk = get(pf, pl.ds(k, nblk * nbase, stride=share)).astype(BF)
        t = lax.dot_general(pk, xr[k], NT, preferred_element_type=F32)
        return acc + jnp.where(cnt > first + k, t, 0.0)

    acc = lax.fori_loop(0, share, one, jnp.zeros((nblk * nbase, slots), F32), unroll=4)
    blk = line(dstv_ref)
    total = jnp.zeros((nbase, slots), F32)
    for n in range(nblk):
        total += jnp.where(blk == n, acc[n * nbase : (n + 1) * nbase], 0.0)
    ts[...] = total
    for r, out in enumerate((s0, s1, s2, s3)):
        out[...] = ts[aligned(turn(group0, r, groups), own), :]


def coef_body(rel_ref, s0, s1, s2, s3, out_ref):
    own, slots = s0.shape
    width = out_ref.shape[1]
    chunks = out_ref.shape[0] // (2 * own)
    high, low = digits((s0[...] + s1[...]) + (s2[...] + s3[...]))
    both = jnp.concatenate([high.astype(F32), low.astype(F32)], axis=0).astype(BF)
    rel = rel_ref[...]
    parts = []
    for j in range(chunks):
        ids = lax.broadcasted_iota(jnp.int32, (width, slots), 0) + j * width
        hot = jnp.where(ids == rel, 1.0, 0.0).astype(BF)
        t = lax.dot_general(both, hot, NT, preferred_element_type=F32)
        parts.append(t[:own] + t[own:])
    pack(out_ref, 0, jnp.concatenate(parts, axis=0))


def pack(ref, at, value):
    high, low = digits(value)
    n = value.shape[0]
    ref[pl.ds(at, n), :] = high
    ref[pl.ds(at + n, n), :] = low


def unpack(value, at, n):
    return value[at : at + n].astype(F32) + value[at + n : at + 2 * n].astype(F32)


def basis_body(own, rows, peers, y0, y1, y2, y3, coef_ref, keep_ref, send_ref, tmp, outf):
    ys = (y0, y1, y2, y3)
    width = y0.shape[1]
    part = keep_ref.shape[0]
    each = part // NX
    deep = part * NC // (own * peers)
    nz = each // (own * deep)
    pg = jnp.concatenate([y[pl.ds(own * rows, rows), :] for y in ys], axis=0)
    for b in range(own):
        m = jnp.concatenate([y[pl.ds(b * rows, rows), :] for y in ys], axis=0)
        put(tmp, pl.ds(0, width), lax.dot_general(m, pg, TN, preferred_element_type=F32))
        for c in range(NC):
            for x in range(NX):
                for d in range(deep):
                    put(
                        outf,
                        pl.ds((c * NX + x) * each + b * deep + d, nz, stride=own * deep),
                        get(tmp, pl.ds((x * NC + c) * deep + d, nz, stride=NX * NC * deep)),
                    )
    core = lax.axis_index("c")
    keep_ref[...] = get(outf, aligned(core, part)).astype(BF)
    send_ref[pl.ds(0, part), :] = get(outf, aligned(1 - core, part)).astype(BF)
    send_ref[pl.ds(part, coef_ref.shape[0]), :] = coef_ref[...]


def core_body(keep_ref, got_ref, coef_ref, o0, o1, o2, o3, sums):
    part = keep_ref.shape[0]
    each = part // NX
    n = coef_ref.shape[0] // 2
    sums[...] = keep_ref[...].astype(F32) + got_ref[pl.ds(0, part), :].astype(F32)
    coef = unpack(coef_ref[...], 0, n) + unpack(got_ref[pl.ds(part, 2 * n), :], 0, n)
    for r, out in enumerate((o0, o1, o2, o3)):
        out[pl.ds(0, each), :] = sums[aligned(turn(lax.axis_index("x"), r, NX), each), :].astype(BF)
        pack(out, each, coef)


def x_body(i0, i1, i2, i3, out_ref, order):
    n = order.shape[1]
    each = i0.shape[0] - 2 * n
    nz = out_ref.shape[0]
    last = each // nz
    sums = sum(i[pl.ds(0, each), :].astype(F32) for i in (i0, i1, i2, i3))
    for r, i in enumerate((i0, i1, i2, i3)):
        order[turn(lax.axis_index("x"), -r, NX)] = unpack(i[pl.ds(each, 2 * n), :], 0, n)
    high, low = digits((order[0] + order[1]) + (order[2] + order[3]))
    for z in range(nz):
        out_ref[z, pl.ds(0, last), :] = sums[z * last : (z + 1) * last].astype(BF)
        out_ref[z, pl.ds(last, n), :] = high
        out_ref[z, pl.ds(last + n, n), :] = low


def z_body(own, in_ref, basis_ref, coef_ref):
    nz, rows, width = in_ref.shape
    last = basis_ref.shape[0]
    n = (rows - last) // 2
    basis = jnp.zeros((last, width), F32)
    coef = jnp.zeros((n, width), F32)
    for z in range(nz):
        basis += in_ref[z, pl.ds(0, last), :].astype(F32)
        coef += unpack(in_ref[z, pl.ds(last, 2 * n), :], 0, n)
    basis_ref[...] = basis
    relations = coef_ref.shape[1]
    for j in range(n // own):
        size = min(width, relations - j * width)
        coef_ref[:, pl.ds(j * width, size)] = coef[j * own : (j + 1) * own, :size]


def bwd_body(
    cap, own, x_ref, w_ref, act_ref, pg_ref, sw_ref, table_ref, o0, o1, o2, o3, xf, mf, at_ref, tab, tsem
):
    groups = tab.shape[0]
    nbase = groups * own
    width = tab.shape[2]
    halves = width // LANES
    share = BLK // groups
    slots = w_ref.shape[1]
    peers = slots // cap
    nblk = w_ref.shape[0] // nbase
    tcopies = start_all(table_copies(table_ref, tab, tsem))
    widen(x_ref, xf)
    w = w_ref[...]

    def one(k, c):
        xk = slot_rows(xf, peers, cap, halves, share, k).astype(BF)
        put(mf, pl.ds(k, w.shape[0], stride=share), jnp.dot(w, xk, preferred_element_type=F32))
        return c

    lax.fori_loop(0, share, one, 0, unroll=4)
    acc = lax.dot_general(pg_ref[...], sw_ref[...], NT, preferred_element_type=F32)
    wait_all(tcopies)
    for b in range(nbase):
        mb = rows_of(mf, b, nbase, nblk, share).astype(BF)
        base = tab[b // own, pl.ds((b % own) * width, width), :]
        acc += lax.dot_general(mb, base, NT, preferred_element_type=F32)
    at_ref[...] = acc.T
    cols = width // groups
    for r, out in enumerate((o0, o1, o2, o3)):
        out[0] = at_ref[aligned(turn(lax.axis_index("basis"), r, groups), cols), :].astype(BF)
        out[1] = act_ref[r]


def join_body(nblk, i0, i1, i2, i3, grad_ref, act_ref, order):
    groups = order.shape[0]
    share = BLK // groups
    for r, i in enumerate((i0, i1, i2, i3)):
        order[turn(lax.axis_index("basis"), -r, groups)] = i[...].astype(F32)
    for j, out in enumerate((grad_ref, act_ref)):
        for n in range(nblk):
            whole = jnp.concatenate([order[g, j, :, n * share : (n + 1) * share] for g in range(groups)], axis=1)
            out[:, n * BLK : (n + 1) * BLK] = whole.astype(BF)


def local(
    entity_rows,
    self_weight,
    bases,
    coefficients,
    send_block,
    edge_rel,
    edge_dst,
    edge_count,
    cotangent,
):
    peers = lax.axis_size(ENT)
    groups = lax.axis_size("basis")
    ent_dev, width = entity_rows.shape
    nblk = ent_dev // BLK
    own = bases.shape[0]
    nbase = own * groups
    relations = coefficients.shape[0]
    cap = send_block.shape[2]
    slots = peers * cap
    share = BLK // groups
    halves = width // LANES
    nz = lax.axis_size("z")
    rows = nblk * share
    dma = pltpu.SemaphoreType.DMA

    def over(axis, r, value):
        n = lax.axis_size(axis)
        return lax.ppermute(value, axis, [(i, (i + r) % n) for i in range(n)])

    src, rel_out = send_block[0].T, edge_rel[0].T
    dst, cnt = edge_dst[:, 0, :].T, edge_count[:, 0, :].T

    per = cap * halves * share
    outgoing = call(
        functools.partial(take_body, share),
        bf(peers, per + 8, LANES),
        [SM, SM, HB],
        [
            pltpu.VMEM((rows, width), BF),
            pltpu.VMEM((peers, per + 8, LANES), BF),
            dma((nblk,)),
            dma((4,)),
        ],
        outs_in=HB,
    )(src, rel_out, entity_rows)
    incoming = lax.all_to_all(outgoing, ENT, split_axis=0, concat_axis=0, tiled=True)

    table = lax.all_gather(bases.reshape(own * width, width), "basis")
    chunks = -(-relations // width)
    coef = jnp.pad(coefficients.astype(BF).T, ((0, 16 - own), (0, chunks * width - relations)))
    coef = coef.reshape(16, chunks, width).transpose(1, 0, 2).reshape(chunks * 16, width)
    coefs = [coef] + [over("basis", r, coef) for r in range(1, groups)]
    w_out = call(
        functools.partial(weights_body, nblk, own),
        bf(nblk * nbase, slots),
        [VM] * 6,
        [pltpu.VMEM((groups, own, slots), F32)],
        limit=4,
    )(rel_out, src, *coefs)

    tables = pltpu.VMEM((groups, own * width, width), BF)
    *ys, back, xr, pg, rel_in, act = call(
        functools.partial(fwd_body, cap, nblk, own),
        (
            *[bf((own + 1) * rows, width) for _ in range(groups)],
            bf(peers, per, LANES),
            bf(share, slots, width),
            bf(rows, width),
            jax.ShapeDtypeStruct((1, slots), jnp.int32),
            bf(groups, width // groups, rows),
        ),
        [SM] * 2 + [VM] * 8 + [HB] * 3,
        [
            pltpu.VMEM((peers * (per + 8), LANES), F32),
            rows_scratch(nbase * rows, width),
            pltpu.VMEM((groups, own, slots), F32),
            pltpu.VMEM((width, rows), F32),
            tables,
            pltpu.VMEM((rows, width), BF),
            pltpu.VMEM((rows, width), BF),
            pltpu.VMEM((groups, (own + 1) * rows, width), BF),
            pltpu.VMEM((peers, per, LANES), BF),
            pltpu.VMEM((share, slots, width), BF),
            dma((groups,)),
            dma((nblk,)),
            dma((nblk,)),
            dma((groups,)),
            dma((4,)),
            dma,
        ],
        limit=28,
        outs_in=(HB,) * (groups + 2) + (VM,) * 3,
    )(
        dst, cnt, incoming.reshape(peers * (per + 8), LANES), dst, cnt, *coefs, self_weight, table,
        entity_rows, cotangent,
    )

    returned = lax.all_to_all(back, ENT, split_axis=0, concat_axis=0, tiled=True)
    ys = [ys[0]] + [over("basis", r, ys[r]) for r in range(1, groups)]

    scores = call(
        functools.partial(score_body, nblk, own),
        tuple(jax.ShapeDtypeStruct((own, slots), F32) for _ in range(groups)),
        [VM] * 3 + [HB] * 2,
        [
            rows_scratch(nbase * rows, width),
            pltpu.VMEM((nbase, slots), F32),
            tables,
            pltpu.VMEM((share, slots, width), BF),
            dma((groups,)),
            dma,
        ],
    )(pg, dst, cnt, xr, table)
    scores = [scores[0]] + [over("basis", r, scores[r]) for r in range(1, groups)]
    lot = chunks * own
    coef_part = call(coef_body, bf(2 * lot, width), [VM] * 5, limit=4)(rel_in, *scores)

    part = own * width // NC
    keep, send = call(
        functools.partial(basis_body, own, rows, peers),
        (bf(part, width), bf(part + 2 * lot, width)),
        [VM] * 5,
        [rows_scratch(width, width), rows_scratch(NC * part, width)],
        limit=8,
    )(*ys, coef_part)
    got = over("c", 1, send)
    each = part // NX
    outs = call(
        core_body,
        tuple(bf(each + 2 * lot, width) for _ in range(NX)),
        [VM] * 3,
        [pltpu.VMEM((part, width), F32)],
        limit=8,
    )(keep, got, coef_part)
    ins = [outs[0]] + [over("x", r, outs[r]) for r in range(1, NX)]

    grads = call(
        functools.partial(bwd_body, cap, own),
        tuple(bf(2, width // groups, rows) for _ in range(groups)),
        [VM] * 5 + [HB],
        [
            pltpu.VMEM((peers * per, LANES), F32),
            rows_scratch(nbase * rows, width),
            pltpu.VMEM((width, rows), F32),
            tables,
            dma((groups,)),
        ],
        limit=18,
    )(returned.reshape(peers * per, LANES), w_out, act, pg, self_weight, table)

    ins = lax.optimization_barrier((*ins, grads[0]))[:NX]
    last = each // nz
    out = call(
        x_body,
        bf(nz, last + 2 * lot, width),
        [VM] * NX,
        [pltpu.VMEM((NX, lot, width), F32)],
        limit=4,
    )(*ins)
    out = lax.all_to_all(out, "z", split_axis=0, concat_axis=0, tiled=True)
    basis_grad, coef_grad = call(
        functools.partial(z_body, own),
        (jax.ShapeDtypeStruct((last, width), F32), jax.ShapeDtypeStruct((own, relations), F32)),
        [VM],
        limit=4,
    )(out)

    grads = [grads[0]] + [over("basis", r, grads[r]) for r in range(1, groups)]
    cols = width // groups
    entity_grad, activation = call(
        functools.partial(join_body, nblk),
        (bf(cols, ent_dev), bf(cols, ent_dev)),
        [VM] * groups,
        [pltpu.VMEM((groups, 2, cols, rows), F32)],
        limit=4,
    )(*grads)
    return (activation.T, basis_grad.reshape(own, width // peers, width), coef_grad.T, entity_grad.T)


def solution(mesh):
    nz = mesh.devices.shape[0] // (NX * NC)
    fine = Mesh(mesh.devices.reshape(nz, NX, NC, mesh.devices.shape[1]), (*ENT, "basis"))
    placed = (
        P(ENT, None),
        P(),
        P("basis", None, None),
        P(None, "basis"),
        P(ENT, None, None),
        P(ENT, None, None),
        P(None, ENT, None),
        P(None, ENT, None),
        P(ENT, None),
    )
    return jax.shard_map(
        local,
        mesh=fine,
        in_specs=placed,
        out_specs=(P(ENT, "basis"), P("basis", ENT, None), P(None, "basis"), P(ENT, "basis")),
        check_vma=False,
    )
```

time: 218 us -> 195 us (0.89); the launches traced: 215 us -> 194 us
  local copies, waits for them, and re-layouts: 35.8 us -> 18.8 us
  waiting for transfers between devices: 67.9 us -> 77.4 us
  starting transfers between devices: 60.9 us -> 52 us
  Pallas kernels: 35.7 us -> 31.7 us
    ppermute x23 -> x16, starting transfers between devices: 40.6 us -> 26.6 us  [over(): return lax.ppermute(value, axis, [(i, (i + r) % n) for i in range(n)])]
    unnamed x100 -> x42, local copies, waits for them, and re-layouts: 31.3 us -> 18.1 us
    all_to_all x2 -> x3, waiting for transfers between devices: 43.2 us -> 54.2 us  [the longest x1 43.6 us: local(): lax.all_to_all(outgoing, ENT, split_axis=0, concat_axis=0, tiled=True)]
    all_to_all x2 -> x3, starting transfers between devices: 20.2 us -> 25.3 us  [the longest x1 13.1 us: local(): lax.all_to_all(outgoing, ENT, split_axis=0, concat_axis=0, tiled=True)]
    reshape x4 -> x0, local copies, waits for them, and re-layouts: 3.72 us -> none  [lines(): return value.reshape(peers, cap).T.reshape(1, slots)]
    pallas_call x8, Pallas kernels: 24.1 us -> 20.8 us  [the longest x1 9.16 us: local(): call(functools.partial(fwd_body, cap, nblk, own), (*[bf((own + 1) * rows,...]
    ppermute x23 -> x16, waiting for transfers between devices: 24.1 us -> 22.5 us  [over(): return lax.ppermute(value, axis, [(i, (i + r) % n) for i in range(n)])]
  transfers between devices with their start and end apart: 26 -> 20, of which waited for: 7 -> 10; matrix products, arithmetic and copies ran while one was open for 3% -> 0% of each run, Pallas kernels for 12% -> 11%
where the time goes in v3:
time: 195 us; the launch traced here: 194 us
  waiting for transfers between devices  77.4 us (40%)
  starting transfers between devices  52 us (27%)
  Pallas kernels  31.7 us (16%)
  local copies, waits for them, and re-layouts  18.8 us (10%)
  between operations  14.3 us (7%)
    all_to_all x1, waiting for transfers between devices, local(): lax.all_to_all(outgoing, ENT, split_axis=0, concat_axis=0, tiled=True)  43.6 us
    ppermute x16, starting transfers between devices, over(): return lax.ppermute(value, axis, [(i, (i + r) % n) for i in range(n)])  26.6 us
    ppermute x16, waiting for transfers between devices, over(): return lax.ppermute(value, axis, [(i, (i + r) % n) for i in range(n)])  22.5 us
    unnamed x42, local copies, waits for them, and re-layouts  18.1 us
    all_to_all x1, starting transfers between devices, local(): lax.all_to_all(outgoing, ENT, split_axis=0, concat_axis=0, tiled=True)  13.1 us
    pallas_call x1, Pallas kernels, local(): call(functools.partial(fwd_body, cap, nblk, own), (*[bf((own + 1) * rows,...  9.16 us
    all_to_all x1, waiting for transfers between devices, local(): out = lax.all_to_all(out, 'z', split_axis=0, concat_axis=0, tiled=True)  9.03 us
    pallas_call x1, Pallas kernels, local(): call(functools.partial(bwd_body, cap, own), tuple((bf(2, width // groups,...  7.62 us
  transfers between devices with their start and end apart: 20, of which 10 were waited for; matrix products, arithmetic and copies ran while one was open for 0% of the time, Pallas kernels for 11%

profile of v3, /device:TPU:1, one launch (start us, length us, event | category | flops | bytes accessed | tf_op | source)
XLA Modules:
  0.0 194.1 jit_solution(13477644091796617201)
XLA Ops:
  10.2 1.5 shard_map.120
  11.7 1.4 copy-done.3
  13.1 13.1 %all-to-all-start = ((bf16[64,136,128]{2,1,0:T(8,128)(2,1)}), bf16[64,136,128]{2,1,0:T(8,128)(2,1)S(1)}, u32[]{:S(2)}, u32[]{:S(2)}) async-start(bf16[64,136,128]{2,1,0:T(8,128)(2,1)} %copy-done.3), calls=%async_computation | async-start | bytes 4456448 | tf_op jit(solution)/shard_map/all_to_all | solution.py:465
  26.4 1.4 collective-permute-start
  27.8 2.6 %collective-permute-start.1 = (bf16[96,256]{1,0:T(8,128)(2,1)S(1)}, bf16[96,256]{1,0:T(8,128)(2,1)S(1)}, u32[]{:S(2)}, u32[]{:S(2)}) collective-permute-start(bf16[96,256]{1,0:T(8,128)(2,1)S(1)} %bitcast.25), channel_id=1, source_target_pairs={{0,2},{1,3},{2,0},{3,1},{4,6},{5,7},{6,4},{7,5},{8,10},{9,11},{10,... | collective-permute-start | bytes 147464 | tf_op jit(solution)/shard_map/ppermute | solution.py:447
  32.0 3.0 %collective-permute-done.1.c2 = bf16[96,256]{1,0:T(8,128)(2,1)S(1)} collective-permute-done((bf16[96,256]{1,0:T(8,128)(2,1)S(1)}, bf16[96,256]{1,0:T(8,128)(2,1)S(1)}, u32[]{:S(2)}, u32[]{:S(2)}) %collective-permute-start.1) | collective-permute-done | bytes 49184 | tf_op jit(solution)/shard_map/ppermute | solution.py:447
  35.1 43.6 %all-to-all-done = bf16[64,136,128]{2,1,0:T(8,128)(2,1)S(1)} async-done(((bf16[64,136,128]{2,1,0:T(8,128)(2,1)}), bf16[64,136,128]{2,1,0:T(8,128)(2,1)S(1)}, u32[]{:S(2)}, u32[]{:S(2)}) %all-to-all-start) | async-done | bytes 2228256 | tf_op jit(solution)/shard_map/all_to_all | solution.py:465
  78.7 2.2 %copy-done = bf16[4,2048,256]{2,1,0:T(8,128)(2,1)S(1)} copy-done((bf16[4,2048,256]{2,1,0:T(8,128)(2,1)S(1)}, bf16[4,2048,256]{2,1,0:T(8,128)(2,1)}, u32[]{:S(2)}) %copy-start) | copy-done | bytes 4194328
  81.8 9.2 %shard_map.121 = (bf16[1152,256]{1,0:T(8,128)(2,1)S(1)}, bf16[1152,256]{1,0:T(8,128)(2,1)S(1)}, bf16[1152,256]{1,0:T(8,128)(2,1)S(1)}, bf16[1152,256]{1,0:T(8,12...) custom-call(s32[2,64]{1,0:T(2,128)S(1)} %bitcast.29, ...), custom_call_target="tpu_custom_call" | custom-call | tf_op jit(solution)/shard_map/pallas_call | solution.py:481
  92.4 1.4 copy-done.5
  96.3 7.1 %all-to-all-start.1 = ((bf16[64,128,128]{2,1,0:T(8,128)(2,1)}), bf16[64,128,128]{2,1,0:T(8,128)(2,1)S(1)}, u32[]{:S(2)}, u32[]{:S(2)}) async-start(bf16[64,128,128]{2,1,0:T(8,128)(2,1)} %copy-done.4), calls=%async_computation.1 | async-start | bytes 4194304 | tf_op jit(solution)/shard_map/all_to_all | solution.py:517
  103.4 1.4 collective-permute-start.6
  104.8 2.6 %collective-permute-start.7 = (bf16[1152,256]{1,0:T(8,128)(2,1)}, bf16[1152,256]{1,0:T(8,128)(2,1)S(1)}, u32[]{:S(2)}, u32[]{:S(2)}) collective-permute-start(bf16[1152,256]{1,0:T(8,128)(2,1)} %copy-done.18), channel_id=1, source_target_pairs={{0,2},{1,3},{2,0},{3,1},{4,6},{5,7},{6,4},{7,5},{8,10},{9,11},{10,... | collective-permute-start | bytes 1769480 | tf_op jit(solution)/shard_map/ppermute | solution.py:447
  108.4 2.2 %copy-done.1 = bf16[4,2048,256]{2,1,0:T(8,128)(2,1)S(1)} copy-done((bf16[4,2048,256]{2,1,0:T(8,128)(2,1)S(1)}, bf16[4,2048,256]{2,1,0:T(8,128)(2,1)}, u32[]{:S(2)}) %copy-start.1) | copy-done | bytes 4194328
  110.6 1.6 copy-done.6
  112.2 5.7 %shard_map.125 = (f32[8,128]{1,0:T(8,128)S(1)}, f32[8,128]{1,0:T(8,128)S(1)}, f32[8,128]{1,0:T(8,128)S(1)}, f32[8,128]{1,0:T(8,128)S(1)}) custom-call(bf16[128,256]{1,0:T(8,128)(2,1)S(1)} %get-tuple-element.37.pg_ref, s32[2,64]{1,0:T(2,128)S(1)} %bitcast.31, s32[2,64]{1,0:T(2,128)S(1)} %bitcast.34, bf16[32,128,256]{2,1,0:T(8,128)(2,1)S(1)} %copy-done.6, ...), custom_call_target="tpu_custom_call" | custom-call | tf_op jit(solution)/shard_map/pallas_call | solution.py:520
  118.3 2.6 %collective-permute-start.11 = (f32[8,128]{1,0:T(8,128)S(1)}, f32[8,128]{1,0:T(8,128)S(1)}, u32[]{:S(2)}, u32[]{:S(2)}) collective-permute-start(f32[8,128]{1,0:T(8,128)S(1)} %get-tuple-element.52), channel_id=1, source_target_pairs={{0,3},{1,0},{2,1},{3,2},{4,7},{5,4},{6,5},{7,6},{8,11},{9,8},{10,9... | collective-permute-start | bytes 12296 | tf_op jit(solution)/shard_map/ppermute | solution.py:447
  120.8 12.5 %collective-permute-done.10.s2 = f32[8,128]{1,0:T(8,128)S(1)} collective-permute-done((f32[8,128]{1,0:T(8,128)S(1)}, f32[8,128]{1,0:T(8,128)S(1)}, u32[]{:S(2)}, u32[]{:S(2)}) %collective-permute-start.10) | collective-permute-done | bytes 4128 | tf_op jit(solution)/shard_map/ppermute | solution.py:447
  133.3 1.4 collective-permute-start.9
  134.7 2.5 %collective-permute-done.9.s1 = f32[8,128]{1,0:T(8,128)S(1)} collective-permute-done((f32[8,128]{1,0:T(8,128)S(1)}, f32[8,128]{1,0:T(8,128)S(1)}, u32[]{:S(2)}, u32[]{:S(2)}) %collective-permute-start.9) | collective-permute-done | bytes 4128 | tf_op jit(solution)/shard_map/ppermute | solution.py:447
  137.5 3.7 %shard_map.127 = (bf16[1024,256]{1,0:T(8,128)(2,1)S(1)}, bf16[1120,256]{1,0:T(8,128)(2,1)S(1)}) custom-call(bf16[1152,256]{1,0:T(8,128)(2,1)S(1)} %get-tuple-element.43.y0, bf16[1152,256]{1,0:T(8,128)(2,1)S(1)} %collective-permute-done.6.y1, bf16[1152,256]{1,0:T(8,128)(2,1)S(1)} %collective-permute-done.7.y2, ...), custom_call_target="tpu_custom_call" | custom-call | tf_op jit(solution)/shard_map/pallas_call | solution.py:538
  141.2 2.2 %collective-permute-start.12 = (bf16[1120,256]{1,0:T(8,128)(2,1)S(1)}, bf16[1120,256]{1,0:T(8,128)(2,1)S(1)}, u32[]{:S(2)}, u32[]{:S(2)}) collective-permute-start(bf16[1120,256]{1,0:T(8,128)(2,1)S(1)} %get-tuple-element.54), channel_id=1, source_target_pairs={{0,4},{4,0},{1,5},{5,1},{2,6},{6,2},{3,7},{7,3},{8,12},{12,8},{9,1... | collective-permute-start | bytes 1720328 | tf_op jit(solution)/shard_map/ppermute | solution.py:447
  143.5 1.6 collective-permute-done.12.got_ref
  146.0 1.4 collective-permute-start.13
  147.4 2.4 %collective-permute-start.14 = (bf16[352,256]{1,0:T(8,128)(2,1)}, bf16[352,256]{1,0:T(8,128)(2,1)S(1)}, u32[]{:S(2)}, u32[]{:S(2)}) collective-permute-start(bf16[352,256]{1,0:T(8,128)(2,1)} %get-tuple-element.57), channel_id=1, source_target_pairs={{0,16},{8,24},{16,0},{24,8},{1,17},{9,25},{17,1},{25,9},{2,18},{10... | collective-permute-start | bytes 540680 | tf_op jit(solution)/shard_map/ppermute | solution.py:447
  151.4 1.6 all-to-all-done.1
  153.1 2.2 %copy-done.2 = bf16[4,2048,256]{2,1,0:T(8,128)(2,1)S(1)} copy-done((bf16[4,2048,256]{2,1,0:T(8,128)(2,1)S(1)}, bf16[4,2048,256]{2,1,0:T(8,128)(2,1)}, u32[]{:S(2)}) %copy-start.2) | copy-done | bytes 4194328
  155.2 7.6 %shard_map.123 = (bf16[2,64,128]{2,1,0:T(8,128)(2,1)S(1)}, bf16[2,64,128]{2,1,0:T(8,128)(2,1)S(1)}, bf16[2,64,128]{2,1,0:T(8,128)(2,1)S(1)}, bf16[2,64,128]{2,1,0:T(8,128)(2,1)S(1)}) custom-call(bf16[8192,128]{1,0:T(8,128)(2,1)S(1)} %bitcast.23, bf16[128,128]{1,0:T(8,128)(2,1)S(1)} %shard_map.122.w_ref, bf16[4,64,128]{2,1,0:T(8,128)(2,1)S(1)} %get-tuple-element.36.act_ref, ...), custom_call_target="tpu_custom_call" | custom-call | tf_op jit(solution)/shard_map/pallas_call | solution.py:556
  163.8 5.1 %all-to-all-start.2 = ((bf16[8,128,256]{2,1,0:T(8,128)(2,1)}), bf16[8,128,256]{2,1,0:T(8,128)(2,1)S(1)}, u32[]{:S(2)}, u32[]{:S(2)}) async-start(bf16[8,128,256]{2,1,0:T(8,128)(2,1)} %shard_map.129), calls=%async_computation.2 | async-start | bytes 1048576 | tf_op jit(solution)/shard_map/all_to_all | solution.py:579
  170.3 2.6 %collective-permute-start.4 = (bf16[2,64,128]{2,1,0:T(8,128)(2,1)S(1)}, bf16[2,64,128]{2,1,0:T(8,128)(2,1)S(1)}, u32[]{:S(2)}, u32[]{:S(2)}) collective-permute-start(bf16[2,64,128]{2,1,0:T(8,128)(2,1)S(1)} %get-tuple-element.40), channel_id=1, source_target_pairs={{0,2},{1,3},{2,0},{3,1},{4,6},{5,7},{6,4},{7,5},{8,10},{9,11},{10,... | collective-permute-start | bytes 98312 | tf_op jit(solution)/shard_map/ppermute | solution.py:447
  174.6 1.6 collective-permute-done.5.i3
  177.0 9.0 %all-to-all-done.2.in_ref = bf16[8,128,256]{2,1,0:T(8,128)(2,1)S(1)} async-done(((bf16[8,128,256]{2,1,0:T(8,128)(2,1)}), bf16[8,128,256]{2,1,0:T(8,128)(2,1)S(1)}, u32[]{:S(2)}, u32[]{:S(2)}) %all-to-all-start.2) | async-done | bytes 524320 | tf_op jit(solution)/shard_map/all_to_all | solution.py:579
  (67 shorter events, 19.8 us)
Async XLA Ops:
  7.2 71.5 %all-gather.2.cloned.1.call-start = ((), (), s32[]{:S(2)}) async-start(), calls=%async_computation.3 | async-start | bytes 5242880 | tf_op jit(solution)/shard_map/all_gather | solution.py:467
  11.7 1.4 copy-start.3
  13.1 13.2 %copy-start.20 = (f32[1315,8]{0,1:T(8,128)S(1)}, f32[1315,8]{0,1:T(8,128)}, u32[]{:S(2)}) copy-start(f32[1315,8]{0,1:T(8,128)} %param.12) | copy-start | bytes 126244
  13.1 65.6 %copy-start.8 = (bf16[512,256]{1,0:T(8,128)(2,1)S(1)}, bf16[512,256]{1,0:T(8,128)(2,1)}, u32[]{:S(2)}) copy-start(bf16[512,256]{1,0:T(8,128)(2,1)} %ent_ref.3) | copy-start | bytes 786436
  13.1 65.6 %copy-start.9 = (bf16[256,256]{1,0:T(8,128)(2,1)S(1)}, bf16[256,256]{1,0:T(8,128)(2,1)}, u32[]{:S(2)}) copy-start(bf16[256,256]{1,0:T(8,128)(2,1)} %sw_ref.3) | copy-start | bytes 393220
  13.1 65.6 %copy-start.11 = (s32[64,1,2]{0,2,1:T(2,128)S(1)}, s32[64,1,2]{0,2,1:T(2,128)}, u32[]{:S(2)}) copy-start(s32[64,1,2]{0,2,1:T(2,128)} %param.15) | copy-start | bytes 1540
  13.1 65.6 %copy-start.12 = (s32[64,1,2]{0,2,1:T(2,128)S(1)}, s32[64,1,2]{0,2,1:T(2,128)}, u32[]{:S(2)}) copy-start(s32[64,1,2]{0,2,1:T(2,128)} %param.16) | copy-start | bytes 1540
  13.1 65.5 %all-to-all-start = ((bf16[64,136,128]{2,1,0:T(8,128)(2,1)}), bf16[64,136,128]{2,1,0:T(8,128)(2,1)S(1)}, u32[]{:S(2)}, u32[]{:S(2)}) async-start(bf16[64,136,128]{2,1,0:T(8,128)(2,1)} %copy-done.3), calls=%async_computation | async-start | bytes 4456448 | tf_op jit(solution)/shard_map/all_to_all | solution.py:465
  26.4 5.6 %collective-permute-start = (bf16[96,256]{1,0:T(8,128)(2,1)S(1)}, bf16[96,256]{1,0:T(8,128)(2,1)S(1)}, u32[]{:S(2)}, u32[]{:S(2)}) collective-permute-start(bf16[96,256]{1,0:T(8,128)(2,1)S(1)} %bitcast.24), channel_id=1, source_target_pairs={{0,1},{1,2},{2,3},{3,0},{4,5},{5,6},{6,7},{7,4},{8,9},{9,10},{10,1... | collective-permute-start | bytes 147464 | tf_op jit(solution)/shard_map/ppermute | solution.py:447
  27.8 7.3 %collective-permute-start.1 = (bf16[96,256]{1,0:T(8,128)(2,1)S(1)}, bf16[96,256]{1,0:T(8,128)(2,1)S(1)}, u32[]{:S(2)}, u32[]{:S(2)}) collective-permute-start(bf16[96,256]{1,0:T(8,128)(2,1)S(1)} %bitcast.25), channel_id=1, source_target_pairs={{0,2},{1,3},{2,0},{3,1},{4,6},{5,7},{6,4},{7,5},{8,10},{9,11},{10,... | collective-permute-start | bytes 147464 | tf_op jit(solution)/shard_map/ppermute | solution.py:447
  30.4 4.7 %collective-permute-start.2 = (bf16[96,256]{1,0:T(8,128)(2,1)S(1)}, bf16[96,256]{1,0:T(8,128)(2,1)S(1)}, u32[]{:S(2)}, u32[]{:S(2)}) collective-permute-start(bf16[96,256]{1,0:T(8,128)(2,1)S(1)} %bitcast.26), channel_id=1, source_target_pairs={{0,3},{1,0},{2,1},{3,2},{4,7},{5,4},{6,5},{7,6},{8,11},{9,8},{10,9... | collective-permute-start | bytes 147464 | tf_op jit(solution)/shard_map/ppermute | solution.py:447
  78.7 2.2 %copy-start = (bf16[4,2048,256]{2,1,0:T(8,128)(2,1)S(1)}, bf16[4,2048,256]{2,1,0:T(8,128)(2,1)}, u32[]{:S(2)}) copy-start(bf16[4,2048,256]{2,1,0:T(8,128)(2,1)} %all-gather.2.cloned.1.call-done.table_ref) | copy-start | bytes 12582916
  96.3 56.8 %all-to-all-start.1 = ((bf16[64,128,128]{2,1,0:T(8,128)(2,1)}), bf16[64,128,128]{2,1,0:T(8,128)(2,1)S(1)}, u32[]{:S(2)}, u32[]{:S(2)}) async-start(bf16[64,128,128]{2,1,0:T(8,128)(2,1)} %copy-done.4), calls=%async_computation.1 | async-start | bytes 4194304 | tf_op jit(solution)/shard_map/all_to_all | solution.py:517
  103.4 34.1 %collective-permute-start.6 = (bf16[1152,256]{1,0:T(8,128)(2,1)}, bf16[1152,256]{1,0:T(8,128)(2,1)S(1)}, u32[]{:S(2)}, u32[]{:S(2)}) collective-permute-start(bf16[1152,256]{1,0:T(8,128)(2,1)} %copy-done.19), channel_id=1, source_target_pairs={{0,1},{1,2},{2,3},{3,0},{4,5},{5,6},{6,7},{7,4},{8,9},{9,10},{10,1... | collective-permute-start | bytes 1769480 | tf_op jit(solution)/shard_map/ppermute | solution.py:447
  104.8 32.7 %collective-permute-start.7 = (bf16[1152,256]{1,0:T(8,128)(2,1)}, bf16[1152,256]{1,0:T(8,128)(2,1)S(1)}, u32[]{:S(2)}, u32[]{:S(2)}) collective-permute-start(bf16[1152,256]{1,0:T(8,128)(2,1)} %copy-done.18), channel_id=1, source_target_pairs={{0,2},{1,3},{2,0},{3,1},{4,6},{5,7},{6,4},{7,5},{8,10},{9,11},{10,... | collective-permute-start | bytes 1769480 | tf_op jit(solution)/shard_map/ppermute | solution.py:447
  107.4 30.1 %collective-permute-start.8 = (bf16[1152,256]{1,0:T(8,128)(2,1)}, bf16[1152,256]{1,0:T(8,128)(2,1)S(1)}, u32[]{:S(2)}, u32[]{:S(2)}) collective-permute-start(bf16[1152,256]{1,0:T(8,128)(2,1)} %copy-done.17), channel_id=1, source_target_pairs={{0,3},{1,0},{2,1},{3,2},{4,7},{5,4},{6,5},{7,6},{8,11},{9,8},{10,9... | collective-permute-start | bytes 1769480 | tf_op jit(solution)/shard_map/ppermute | solution.py:447
  108.4 2.2 %copy-start.1 = (bf16[4,2048,256]{2,1,0:T(8,128)(2,1)S(1)}, bf16[4,2048,256]{2,1,0:T(8,128)(2,1)}, u32[]{:S(2)}) copy-start(bf16[4,2048,256]{2,1,0:T(8,128)(2,1)} %all-gather.2.cloned.1.call-done.table_ref) | copy-start | bytes 12582916
  110.6 1.6 copy-start.6
  117.9 33.1 %copy-start.14 = (s32[1,64,2]{1,2,0:T(2,128)S(1)}, s32[1,64,2]{1,2,0:T(2,128)}, u32[]{:S(2)}) copy-start(s32[1,64,2]{1,2,0:T(2,128)} %param.13) | copy-start | bytes 1540
  118.0 33.1 %copy-start.16 = (s32[1,64,2]{1,2,0:T(2,128)S(1)}, s32[1,64,2]{1,2,0:T(2,128)}, u32[]{:S(2)}) copy-start(s32[1,64,2]{1,2,0:T(2,128)} %param.14) | copy-start | bytes 1540
  118.0 15.3 %collective-permute-start.10 = (f32[8,128]{1,0:T(8,128)S(1)}, f32[8,128]{1,0:T(8,128)S(1)}, u32[]{:S(2)}, u32[]{:S(2)}) collective-permute-start(f32[8,128]{1,0:T(8,128)S(1)} %get-tuple-element.51), channel_id=1, source_target_pairs={{0,2},{1,3},{2,0},{3,1},{4,6},{5,7},{6,4},{7,5},{8,10},{9,11},{10,... | collective-permute-start | bytes 12296 | tf_op jit(solution)/shard_map/ppermute | solution.py:447
  118.3 16.4 %collective-permute-start.11 = (f32[8,128]{1,0:T(8,128)S(1)}, f32[8,128]{1,0:T(8,128)S(1)}, u32[]{:S(2)}, u32[]{:S(2)}) collective-permute-start(f32[8,128]{1,0:T(8,128)S(1)} %get-tuple-element.52), channel_id=1, source_target_pairs={{0,3},{1,0},{2,1},{3,2},{4,7},{5,4},{6,5},{7,6},{8,11},{9,8},{10,9... | collective-permute-start | bytes 12296 | tf_op jit(solution)/shard_map/ppermute | solution.py:447
  133.3 4.0 %collective-permute-start.9 = (f32[8,128]{1,0:T(8,128)S(1)}, f32[8,128]{1,0:T(8,128)S(1)}, u32[]{:S(2)}, u32[]{:S(2)}) collective-permute-start(f32[8,128]{1,0:T(8,128)S(1)} %get-tuple-element.50), channel_id=1, source_target_pairs={{0,1},{1,2},{2,3},{3,0},{4,5},{5,6},{6,7},{7,4},{8,9},{9,10},{10,1... | collective-permute-start | bytes 12296 | tf_op jit(solution)/shard_map/ppermute | solution.py:447
  141.2 3.8 %collective-permute-start.12 = (bf16[1120,256]{1,0:T(8,128)(2,1)S(1)}, bf16[1120,256]{1,0:T(8,128)(2,1)S(1)}, u32[]{:S(2)}, u32[]{:S(2)}) collective-permute-start(bf16[1120,256]{1,0:T(8,128)(2,1)S(1)} %get-tuple-element.54), channel_id=1, source_target_pairs={{0,4},{4,0},{1,5},{5,1},{2,6},{6,2},{3,7},{7,3},{8,12},{12,8},{9,1... | collective-permute-start | bytes 1720328 | tf_op jit(solution)/shard_map/ppermute | solution.py:447
  146.0 16.8 %collective-permute-start.13 = (bf16[352,256]{1,0:T(8,128)(2,1)}, bf16[352,256]{1,0:T(8,128)(2,1)S(1)}, u32[]{:S(2)}, u32[]{:S(2)}) collective-permute-start(bf16[352,256]{1,0:T(8,128)(2,1)} %get-tuple-element.56), channel_id=1, source_target_pairs={{0,8},{8,16},{16,24},{24,0},{1,9},{9,17},{17,25},{25,1},{2,10},{10... | collective-permute-start | bytes 540680 | tf_op jit(solution)/shard_map/ppermute | solution.py:447
  147.4 15.5 %collective-permute-start.14 = (bf16[352,256]{1,0:T(8,128)(2,1)}, bf16[352,256]{1,0:T(8,128)(2,1)S(1)}, u32[]{:S(2)}, u32[]{:S(2)}) collective-permute-start(bf16[352,256]{1,0:T(8,128)(2,1)} %get-tuple-element.57), channel_id=1, source_target_pairs={{0,16},{8,24},{16,0},{24,8},{1,17},{9,25},{17,1},{25,9},{2,18},{10... | collective-permute-start | bytes 540680 | tf_op jit(solution)/shard_map/ppermute | solution.py:447
  149.8 13.1 %collective-permute-start.15 = (bf16[352,256]{1,0:T(8,128)(2,1)S(1)}, bf16[352,256]{1,0:T(8,128)(2,1)S(1)}, u32[]{:S(2)}, u32[]{:S(2)}) collective-permute-start(bf16[352,256]{1,0:T(8,128)(2,1)S(1)} %get-tuple-element.58), channel_id=1, source_target_pairs={{0,24},{8,0},{16,8},{24,16},{1,25},{9,1},{17,9},{25,17},{2,26},{10... | collective-permute-start | bytes 540680 | tf_op jit(solution)/shard_map/ppermute | solution.py:447
  153.1 2.2 %copy-start.2 = (bf16[4,2048,256]{2,1,0:T(8,128)(2,1)S(1)}, bf16[4,2048,256]{2,1,0:T(8,128)(2,1)}, u32[]{:S(2)}) copy-start(bf16[4,2048,256]{2,1,0:T(8,128)(2,1)} %all-gather.2.cloned.1.call-done.table_ref) | copy-start | bytes 12582916
  163.8 22.2 %all-to-all-start.2 = ((bf16[8,128,256]{2,1,0:T(8,128)(2,1)}), bf16[8,128,256]{2,1,0:T(8,128)(2,1)S(1)}, u32[]{:S(2)}, u32[]{:S(2)}) async-start(bf16[8,128,256]{2,1,0:T(8,128)(2,1)} %shard_map.129), calls=%async_computation.2 | async-start | bytes 1048576 | tf_op jit(solution)/shard_map/all_to_all | solution.py:579
  169.0 5.0 %collective-permute-start.3 = (bf16[2,64,128]{2,1,0:T(8,128)(2,1)S(1)}, bf16[2,64,128]{2,1,0:T(8,128)(2,1)S(1)}, u32[]{:S(2)}, u32[]{:S(2)}) collective-permute-start(bf16[2,64,128]{2,1,0:T(8,128)(2,1)S(1)} %get-tuple-element.39), channel_id=1, source_target_pairs={{0,1},{1,2},{2,3},{3,0},{4,5},{5,6},{6,7},{7,4},{8,9},{9,10},{10,1... | collective-permute-start | bytes 98312 | tf_op jit(solution)/shard_map/ppermute | solution.py:447
  170.3 4.3 %collective-permute-start.4 = (bf16[2,64,128]{2,1,0:T(8,128)(2,1)S(1)}, bf16[2,64,128]{2,1,0:T(8,128)(2,1)S(1)}, u32[]{:S(2)}, u32[]{:S(2)}) collective-permute-start(bf16[2,64,128]{2,1,0:T(8,128)(2,1)S(1)} %get-tuple-element.40), channel_id=1, source_target_pairs={{0,2},{1,3},{2,0},{3,1},{4,6},{5,7},{6,4},{7,5},{8,10},{9,11},{10,... | collective-permute-start | bytes 98312 | tf_op jit(solution)/shard_map/ppermute | solution.py:447
  172.9 3.3 %collective-permute-start.5 = (bf16[2,64,128]{2,1,0:T(8,128)(2,1)S(1)}, bf16[2,64,128]{2,1,0:T(8,128)(2,1)S(1)}, u32[]{:S(2)}, u32[]{:S(2)}) collective-permute-start(bf16[2,64,128]{2,1,0:T(8,128)(2,1)S(1)} %get-tuple-element.41), channel_id=1, source_target_pairs={{0,3},{1,0},{2,1},{3,2},{4,7},{5,4},{6,5},{7,6},{8,11},{9,8},{10,9... | collective-permute-start | bytes 98312 | tf_op jit(solution)/shard_map/ppermute | solution.py:447
  (9 other events, 8.5 us)
Sparse Core Ops, SparseCore 0:
  9.8 56.7 all-gather.1

commit v4 on v3

--- a/solution.py
+++ b/solution.py
@@ -36,6 +36,14 @@
 
 def bf(*shape):
     return jax.ShapeDtypeStruct(shape, BF)
+
+
+def hbm(*shape):
+    return pltpu.HBM(shape, BF)
+
+
+def far(value):
+    return pltpu.with_memory_space_constraint(value, pltpu.HBM)
 
 
 def get(ref, at):
@@ -452,7 +460,7 @@
     per = cap * halves * share
     outgoing = call(
         functools.partial(take_body, share),
-        bf(peers, per + 8, LANES),
+        hbm(peers, per + 8, LANES),
         [SM, SM, HB],
         [
             pltpu.VMEM((rows, width), BF),
@@ -461,7 +469,7 @@
             dma((4,)),
         ],
         outs_in=HB,
-    )(src, rel_out, entity_rows)
+    )(src, rel_out, far(entity_rows))
     incoming = lax.all_to_all(outgoing, ENT, split_axis=0, concat_axis=0, tiled=True)
 
     table = lax.all_gather(bases.reshape(own * width, width), "basis")
@@ -481,9 +489,9 @@
     *ys, back, xr, pg, rel_in, act = call(
         functools.partial(fwd_body, cap, nblk, own),
         (
-            *[bf((own + 1) * rows, width) for _ in range(groups)],
-            bf(peers, per, LANES),
-            bf(share, slots, width),
+            *[hbm((own + 1) * rows, width) for _ in range(groups)],
+            hbm(peers, per, LANES),
+            hbm(share, slots, width),
             bf(rows, width),
             jax.ShapeDtypeStruct((1, slots), jnp.int32),
             bf(groups, width // groups, rows),
@@ -510,8 +518,8 @@
         limit=28,
         outs_in=(HB,) * (groups + 2) + (VM,) * 3,
     )(
-        dst, cnt, incoming.reshape(peers * (per + 8), LANES), dst, cnt, *coefs, self_weight, table,
-        entity_rows, cotangent,
+        dst, cnt, incoming.reshape(peers * (per + 8), LANES), dst, cnt, *coefs, self_weight, far(table),
+        far(entity_rows), far(cotangent),
     )
 
     returned = lax.all_to_all(back, ENT, split_axis=0, concat_axis=0, tiled=True)
@@ -529,7 +537,7 @@
             dma((groups,)),
             dma,
         ],
-    )(pg, dst, cnt, xr, table)
+    )(pg, dst, cnt, far(xr), far(table))
     scores = [scores[0]] + [over("basis", r, scores[r]) for r in range(1, groups)]
     lot = chunks * own
     coef_part = call(coef_body, bf(2 * lot, width), [VM] * 5, limit=4)(rel_in, *scores)
@@ -565,7 +573,7 @@
             dma((groups,)),
         ],
         limit=18,
-    )(returned.reshape(peers * per, LANES), w_out, act, pg, self_weight, table)
+    )(returned.reshape(peers * per, LANES), w_out, act, pg, self_weight, far(table))
 
     ins = lax.optimization_barrier((*ins, grads[0]))[:NX]
     last = each // nz

time: 195 us -> 184 us (0.944)
  local copies, waits for them, and re-layouts: 18.8 us -> 2.12 us
  waiting for transfers between devices: 77.4 us -> 80 us
  Pallas kernels: 31.7 us -> 34.2 us
    unnamed x42 -> x20, local copies, waits for them, and re-layouts: 18.1 us -> 1.4 us
    ppermute x16, waiting for transfers between devices: 22.5 us -> 25.5 us  [over(): return lax.ppermute(value, axis, [(i, (i + r) % n) for i in range(n)])]
  transfers between devices with their start and end apart: 20 -> 20, of which waited for: 10 -> 9; matrix products, arithmetic and copies ran while one was open for 0% -> 0% of each run, Pallas kernels for 11% -> 13%
where the time goes in v4:
time: 184 us; the launch traced here: 183 us
  waiting for transfers between devices  80 us (43%)
  starting transfers between devices  52.1 us (28%)
  Pallas kernels  34.2 us (19%)
  between operations  14.3 us (8%)
  local copies, waits for them, and re-layouts  2.12 us (1%)
    all_to_all x1, waiting for transfers between devices, local(): lax.all_to_all(outgoing, ENT, split_axis=0, concat_axis=0, tiled=True)  43.5 us
    ppermute x16, starting transfers between devices, over(): return lax.ppermute(value, axis, [(i, (i + r) % n) for i in range(n)])  26.6 us
    ppermute x16, waiting for transfers between devices, over(): return lax.ppermute(value, axis, [(i, (i + r) % n) for i in range(n)])  25.5 us
    all_to_all x1, starting transfers between devices, local(): lax.all_to_all(outgoing, ENT, split_axis=0, concat_axis=0, tiled=True)  13.1 us
    pallas_call x1, Pallas kernels, local(): call(functools.partial(fwd_body, cap, nblk, own), (*[hbm((own + 1) * rows...  9.61 us
    all_to_all x1, waiting for transfers between devices, local(): out = lax.all_to_all(out, 'z', split_axis=0, concat_axis=0, tiled=True)  8.67 us
    pallas_call x1, Pallas kernels, local(): call(functools.partial(bwd_body, cap, own), tuple((bf(2, width // groups,...  7.36 us
    all_to_all x1, starting transfers between devices, local(): lax.all_to_all(back, ENT, split_axis=0, concat_axis=0, tiled=True)  7.23 us
  transfers between devices with their start and end apart: 20, of which 9 were waited for; matrix products, arithmetic and copies ran while one was open for 0% of the time, Pallas kernels for 13%

profile of v4, /device:TPU:1, one launch (start us, length us, event | category | flops | bytes accessed | tf_op | source)
XLA Modules:
  0.0 182.7 jit_solution(6456826431791603847)
XLA Ops:
  9.3 2.9 %shard_map.120 = bf16[64,136,128]{2,1,0:T(8,128)(2,1)} custom-call(s32[2,64]{1,0:T(2,128)S(1)} %bitcast.35, s32[2,64]{1,0:T(2,128)S(1)} %bitcast.37, bf16[512,256]{1,0:T(8,128)(2,1)} %ent_ref.3), custom_call_target="tpu_custom_call" | custom-call | tf_op jit(solution)/shard_map/pallas_call | solution.py:461
  12.2 13.1 %all-to-all-start = ((bf16[64,136,128]{2,1,0:T(8,128)(2,1)}), bf16[64,136,128]{2,1,0:T(8,128)(2,1)S(1)}, u32[]{:S(2)}, u32[]{:S(2)}) async-start(bf16[64,136,128]{2,1,0:T(8,128)(2,1)} %shard_map.120), calls=%async_computation | async-start | bytes 4456448 | tf_op jit(solution)/shard_map/all_to_all | solution.py:473
  25.5 1.4 collective-permute-start
  26.9 2.6 %collective-permute-start.1 = (bf16[96,256]{1,0:T(8,128)(2,1)S(1)}, bf16[96,256]{1,0:T(8,128)(2,1)S(1)}, u32[]{:S(2)}, u32[]{:S(2)}) collective-permute-start(bf16[96,256]{1,0:T(8,128)(2,1)S(1)} %bitcast.25), channel_id=1, source_target_pairs={{0,2},{1,3},{2,0},{3,1},{4,6},{5,7},{6,4},{7,5},{8,10},{9,11},{10,... | collective-permute-start | bytes 147464 | tf_op jit(solution)/shard_map/ppermute | solution.py:455
  29.5 1.1 collective-permute-start.2
  30.6 3.7 %collective-permute-done.1.c2 = bf16[96,256]{1,0:T(8,128)(2,1)S(1)} collective-permute-done((bf16[96,256]{1,0:T(8,128)(2,1)S(1)}, bf16[96,256]{1,0:T(8,128)(2,1)S(1)}, u32[]{:S(2)}, u32[]{:S(2)}) %collective-permute-start.1) | collective-permute-done | bytes 49184 | tf_op jit(solution)/shard_map/ppermute | solution.py:455
  34.2 43.5 %all-to-all-done = bf16[64,136,128]{2,1,0:T(8,128)(2,1)S(1)} async-done(((bf16[64,136,128]{2,1,0:T(8,128)(2,1)}), bf16[64,136,128]{2,1,0:T(8,128)(2,1)S(1)}, u32[]{:S(2)}, u32[]{:S(2)}) %all-to-all-start) | async-done | bytes 2228256 | tf_op jit(solution)/shard_map/all_to_all | solution.py:473
  77.8 9.6 %shard_map.121 = (bf16[1152,256]{1,0:T(8,128)(2,1)}, bf16[1152,256]{1,0:T(8,128)(2,1)}, bf16[1152,256]{1,0:T(8,128)(2,1)}, bf16[1152,256]{1,0:T(8,128)(2,1)}, bf...) custom-call(s32[2,64]{1,0:T(2,128)S(1)} %bitcast.29, ...), custom_call_target="tpu_custom_call" | custom-call | tf_op jit(solution)/shard_map/pallas_call | solution.py:489
  87.4 7.2 %all-to-all-start.1 = ((bf16[64,128,128]{2,1,0:T(8,128)(2,1)}), bf16[64,128,128]{2,1,0:T(8,128)(2,1)S(1)}, u32[]{:S(2)}, u32[]{:S(2)}) async-start(bf16[64,128,128]{2,1,0:T(8,128)(2,1)} %get-tuple-element.35), calls=%async_computation.1 | async-start | bytes 4194304 | tf_op jit(solution)/shard_map/all_to_all | solution.py:525
  94.6 1.4 collective-permute-start.6
  96.0 2.6 %collective-permute-start.7 = (bf16[1152,256]{1,0:T(8,128)(2,1)}, bf16[1152,256]{1,0:T(8,128)(2,1)S(1)}, u32[]{:S(2)}, u32[]{:S(2)}) collective-permute-start(bf16[1152,256]{1,0:T(8,128)(2,1)} %get-tuple-element.45), channel_id=1, source_target_pairs={{0,2},{1,3},{2,0},{3,1},{4,6},{5,7},{6,4},{7,5},{8,10},{9,11},{10,... | collective-permute-start | bytes 1769480 | tf_op jit(solution)/shard_map/ppermute | solution.py:455
  98.6 1.1 collective-permute-start.8
  99.7 6.6 %shard_map.125 = (f32[8,128]{1,0:T(8,128)S(1)}, f32[8,128]{1,0:T(8,128)S(1)}, f32[8,128]{1,0:T(8,128)S(1)}, f32[8,128]{1,0:T(8,128)S(1)}) custom-call(bf16[128,256]{1,0:T(8,128)(2,1)S(1)} %get-tuple-element.37.pg_ref, s32[2,64]{1,0:T(2,128)S(1)} %bitcast.31, s32[2,64]{1,0:T(2,128)S(1)} %bitcast.34, bf16[32,128,256]{2,1,0:T(8,128)(2,1)} %get-tuple-element.48.xr_ref, ...), custom_call_target="tpu_custom_call" | custom-call | tf_op jit(solution)/shard_map/pallas_call | solution.py:528
  106.6 2.6 %collective-permute-start.11 = (f32[8,128]{1,0:T(8,128)S(1)}, f32[8,128]{1,0:T(8,128)S(1)}, u32[]{:S(2)}, u32[]{:S(2)}) collective-permute-start(f32[8,128]{1,0:T(8,128)S(1)} %get-tuple-element.52), channel_id=1, source_target_pairs={{0,3},{1,0},{2,1},{3,2},{4,7},{5,4},{6,5},{7,6},{8,11},{9,8},{10,9... | collective-permute-start | bytes 12296 | tf_op jit(solution)/shard_map/ppermute | solution.py:455
  109.2 15.4 %collective-permute-done.10.s2 = f32[8,128]{1,0:T(8,128)S(1)} collective-permute-done((f32[8,128]{1,0:T(8,128)S(1)}, f32[8,128]{1,0:T(8,128)S(1)}, u32[]{:S(2)}, u32[]{:S(2)}) %collective-permute-start.10) | collective-permute-done | bytes 4128 | tf_op jit(solution)/shard_map/ppermute | solution.py:455
  124.6 1.4 collective-permute-start.9
  126.0 2.5 %collective-permute-done.9.s1 = f32[8,128]{1,0:T(8,128)S(1)} collective-permute-done((f32[8,128]{1,0:T(8,128)S(1)}, f32[8,128]{1,0:T(8,128)S(1)}, u32[]{:S(2)}, u32[]{:S(2)}) %collective-permute-start.9) | collective-permute-done | bytes 4128 | tf_op jit(solution)/shard_map/ppermute | solution.py:455
  128.8 3.7 %shard_map.127 = (bf16[1024,256]{1,0:T(8,128)(2,1)S(1)}, bf16[1120,256]{1,0:T(8,128)(2,1)S(1)}) custom-call(bf16[1152,256]{1,0:T(8,128)(2,1)S(1)} %copy-done, bf16[1152,256]{1,0:T(8,128)(2,1)S(1)} %collective-permute-done.6.y1, bf16[1152,256]{1,0:T(8,128)(2,1)S(1)} %collective-permute-done.7.y2, bf16[1152,256]{1,0:T(8,128)(2,1)S(1)} %collective-permute-done.8.y3, ...), custom_call_target="tpu_custom_call" | custom-call | tf_op jit(solution)/shard_map/pallas_call | solution.py:546
  132.5 2.2 %collective-permute-start.12 = (bf16[1120,256]{1,0:T(8,128)(2,1)S(1)}, bf16[1120,256]{1,0:T(8,128)(2,1)S(1)}, u32[]{:S(2)}, u32[]{:S(2)}) collective-permute-start(bf16[1120,256]{1,0:T(8,128)(2,1)S(1)} %get-tuple-element.54), channel_id=1, source_target_pairs={{0,4},{4,0},{1,5},{5,1},{2,6},{6,2},{3,7},{7,3},{8,12},{12,8},{9,1... | collective-permute-start | bytes 1720328 | tf_op jit(solution)/shard_map/ppermute | solution.py:455
  134.8 1.6 collective-permute-done.12.got_ref
  136.4 1.0 shard_map.128
  137.4 1.4 collective-permute-start.13
  138.8 2.4 %collective-permute-start.14 = (bf16[352,256]{1,0:T(8,128)(2,1)}, bf16[352,256]{1,0:T(8,128)(2,1)S(1)}, u32[]{:S(2)}, u32[]{:S(2)}) collective-permute-start(bf16[352,256]{1,0:T(8,128)(2,1)} %get-tuple-element.57), channel_id=1, source_target_pairs={{0,16},{8,24},{16,0},{24,8},{1,17},{9,25},{17,1},{25,9},{2,18},{10... | collective-permute-start | bytes 540680 | tf_op jit(solution)/shard_map/ppermute | solution.py:455
  141.1 1.2 collective-permute-start.15
  142.7 1.6 all-to-all-done.1
  144.3 7.4 %shard_map.123 = (bf16[2,64,128]{2,1,0:T(8,128)(2,1)S(1)}, bf16[2,64,128]{2,1,0:T(8,128)(2,1)S(1)}, bf16[2,64,128]{2,1,0:T(8,128)(2,1)S(1)}, bf16[2,64,128]{2,1,0:T(8,128)(2,1)S(1)}) custom-call(bf16[8192,128]{1,0:T(8,128)(2,1)S(1)} %bitcast.23, bf16[128,128]{1,0:T(8,128)(2,1)S(1)} %shard_map.122.w_ref, bf16[4,64,128]{2,1,0:T(8,128)(2,1)S(1)} %get-tuple-element.36.act_ref, ...), custom_call_target="tpu_custom_call" | custom-call | tf_op jit(solution)/shard_map/pallas_call | solution.py:564
  152.6 5.1 %all-to-all-start.2 = ((bf16[8,128,256]{2,1,0:T(8,128)(2,1)}), bf16[8,128,256]{2,1,0:T(8,128)(2,1)S(1)}, u32[]{:S(2)}, u32[]{:S(2)}) async-start(bf16[8,128,256]{2,1,0:T(8,128)(2,1)} %shard_map.129), calls=%async_computation.2 | async-start | bytes 1048576 | tf_op jit(solution)/shard_map/all_to_all | solution.py:587
  157.8 1.3 collective-permute-start.3
  159.1 2.6 %collective-permute-start.4 = (bf16[2,64,128]{2,1,0:T(8,128)(2,1)S(1)}, bf16[2,64,128]{2,1,0:T(8,128)(2,1)S(1)}, u32[]{:S(2)}, u32[]{:S(2)}) collective-permute-start(bf16[2,64,128]{2,1,0:T(8,128)(2,1)S(1)} %get-tuple-element.40), channel_id=1, source_target_pairs={{0,2},{1,3},{2,0},{3,1},{4,6},{5,7},{6,4},{7,5},{8,10},{9,11},{10,... | collective-permute-start | bytes 98312 | tf_op jit(solution)/shard_map/ppermute | solution.py:455
  161.7 1.1 collective-permute-start.5
  163.4 1.7 collective-permute-done.5.i3
  165.8 8.7 %all-to-all-done.2.in_ref = bf16[8,128,256]{2,1,0:T(8,128)(2,1)S(1)} async-done(((bf16[8,128,256]{2,1,0:T(8,128)(2,1)}), bf16[8,128,256]{2,1,0:T(8,128)(2,1)S(1)}, u32[]{:S(2)}, u32[]{:S(2)}) %all-to-all-start.2) | async-done | bytes 524320 | tf_op jit(solution)/shard_map/all_to_all | solution.py:587
  (45 shorter events, 6.8 us)
Async XLA Ops:
  7.2 70.6 %all-gather.2.cloned.1.call-start = ((), (), s32[]{:S(2)}) async-start(), calls=%async_computation.3 | async-start | bytes 5242880 | tf_op jit(solution)/shard_map/all_gather | solution.py:475
  7.9 0.7 copy-start.4
  8.6 0.7 copy-start.6
  12.2 13.2 %copy-start.8 = (f32[1315,8]{0,1:T(8,128)S(1)}, f32[1315,8]{0,1:T(8,128)}, u32[]{:S(2)}) copy-start(f32[1315,8]{0,1:T(8,128)} %param.12) | copy-start | bytes 126244
  12.2 65.6 %copy-start.1 = (bf16[256,256]{1,0:T(8,128)(2,1)S(1)}, bf16[256,256]{1,0:T(8,128)(2,1)}, u32[]{:S(2)}) copy-start(bf16[256,256]{1,0:T(8,128)(2,1)} %sw_ref.3) | copy-start | bytes 393220
  12.2 65.6 %copy-start.2 = (s32[64,1,2]{0,2,1:T(2,128)S(1)}, s32[64,1,2]{0,2,1:T(2,128)}, u32[]{:S(2)}) copy-start(s32[64,1,2]{0,2,1:T(2,128)} %param.15) | copy-start | bytes 1540
  12.2 65.6 %copy-start.3 = (s32[64,1,2]{0,2,1:T(2,128)S(1)}, s32[64,1,2]{0,2,1:T(2,128)}, u32[]{:S(2)}) copy-start(s32[64,1,2]{0,2,1:T(2,128)} %param.16) | copy-start | bytes 1540
  12.2 65.5 %all-to-all-start = ((bf16[64,136,128]{2,1,0:T(8,128)(2,1)}), bf16[64,136,128]{2,1,0:T(8,128)(2,1)S(1)}, u32[]{:S(2)}, u32[]{:S(2)}) async-start(bf16[64,136,128]{2,1,0:T(8,128)(2,1)} %shard_map.120), calls=%async_computation | async-start | bytes 4456448 | tf_op jit(solution)/shard_map/all_to_all | solution.py:473
  25.5 5.1 %collective-permute-start = (bf16[96,256]{1,0:T(8,128)(2,1)S(1)}, bf16[96,256]{1,0:T(8,128)(2,1)S(1)}, u32[]{:S(2)}, u32[]{:S(2)}) collective-permute-start(bf16[96,256]{1,0:T(8,128)(2,1)S(1)} %bitcast.24), channel_id=1, source_target_pairs={{0,1},{1,2},{2,3},{3,0},{4,5},{5,6},{6,7},{7,4},{8,9},{9,10},{10,1... | collective-permute-start | bytes 147464 | tf_op jit(solution)/shard_map/ppermute | solution.py:455
  26.9 7.4 %collective-permute-start.1 = (bf16[96,256]{1,0:T(8,128)(2,1)S(1)}, bf16[96,256]{1,0:T(8,128)(2,1)S(1)}, u32[]{:S(2)}, u32[]{:S(2)}) collective-permute-start(bf16[96,256]{1,0:T(8,128)(2,1)S(1)} %bitcast.25), channel_id=1, source_target_pairs={{0,2},{1,3},{2,0},{3,1},{4,6},{5,7},{6,4},{7,5},{8,10},{9,11},{10,... | collective-permute-start | bytes 147464 | tf_op jit(solution)/shard_map/ppermute | solution.py:455
  29.5 4.8 %collective-permute-start.2 = (bf16[96,256]{1,0:T(8,128)(2,1)S(1)}, bf16[96,256]{1,0:T(8,128)(2,1)S(1)}, u32[]{:S(2)}, u32[]{:S(2)}) collective-permute-start(bf16[96,256]{1,0:T(8,128)(2,1)S(1)} %bitcast.26), channel_id=1, source_target_pairs={{0,3},{1,0},{2,1},{3,2},{4,7},{5,4},{6,5},{7,6},{8,11},{9,8},{10,9... | collective-permute-start | bytes 147464 | tf_op jit(solution)/shard_map/ppermute | solution.py:455
  87.4 11.2 %copy-start.9 = (bf16[1152,256]{1,0:T(8,128)(2,1)S(1)}, bf16[1152,256]{1,0:T(8,128)(2,1)}, u32[]{:S(2)}) copy-start(bf16[1152,256]{1,0:T(8,128)(2,1)} %get-tuple-element.46) | copy-start | bytes 1769476
  87.4 56.9 %all-to-all-start.1 = ((bf16[64,128,128]{2,1,0:T(8,128)(2,1)}), bf16[64,128,128]{2,1,0:T(8,128)(2,1)S(1)}, u32[]{:S(2)}, u32[]{:S(2)}) async-start(bf16[64,128,128]{2,1,0:T(8,128)(2,1)} %get-tuple-element.35), calls=%async_computation.1 | async-start | bytes 4194304 | tf_op jit(solution)/shard_map/all_to_all | solution.py:525
  94.6 34.1 %collective-permute-start.6 = (bf16[1152,256]{1,0:T(8,128)(2,1)}, bf16[1152,256]{1,0:T(8,128)(2,1)S(1)}, u32[]{:S(2)}, u32[]{:S(2)}) collective-permute-start(bf16[1152,256]{1,0:T(8,128)(2,1)} %get-tuple-element.44), channel_id=1, source_target_pairs={{0,1},{1,2},{2,3},{3,0},{4,5},{5,6},{6,7},{7,4},{8,9},{9,10},{10,1... | collective-permute-start | bytes 1769480 | tf_op jit(solution)/shard_map/ppermute | solution.py:455
  96.0 32.7 %collective-permute-start.7 = (bf16[1152,256]{1,0:T(8,128)(2,1)}, bf16[1152,256]{1,0:T(8,128)(2,1)S(1)}, u32[]{:S(2)}, u32[]{:S(2)}) collective-permute-start(bf16[1152,256]{1,0:T(8,128)(2,1)} %get-tuple-element.45), channel_id=1, source_target_pairs={{0,2},{1,3},{2,0},{3,1},{4,6},{5,7},{6,4},{7,5},{8,10},{9,11},{10,... | collective-permute-start | bytes 1769480 | tf_op jit(solution)/shard_map/ppermute | solution.py:455
  98.6 30.1 %collective-permute-start.8 = (bf16[1152,256]{1,0:T(8,128)(2,1)S(1)}, bf16[1152,256]{1,0:T(8,128)(2,1)S(1)}, u32[]{:S(2)}, u32[]{:S(2)}) collective-permute-start(bf16[1152,256]{1,0:T(8,128)(2,1)S(1)} %copy-done.9), channel_id=1, source_target_pairs={{0,3},{1,0},{2,1},{3,2},{4,7},{5,4},{6,5},{7,6},{8,11},{9,8},{10,9... | collective-permute-start | bytes 1769480 | tf_op jit(solution)/shard_map/ppermute | solution.py:455
  99.7 29.1 %copy-start = (bf16[1152,256]{1,0:T(8,128)(2,1)S(1)}, bf16[1152,256]{1,0:T(8,128)(2,1)}, u32[]{:S(2)}) copy-start(bf16[1152,256]{1,0:T(8,128)(2,1)} %get-tuple-element.43.y0) | copy-start | bytes 1769476
  106.3 36.0 %copy-start.5 = (s32[1,64,2]{1,2,0:T(2,128)S(1)}, s32[1,64,2]{1,2,0:T(2,128)}, u32[]{:S(2)}) copy-start(s32[1,64,2]{1,2,0:T(2,128)} %param.13) | copy-start | bytes 1540
  106.3 36.0 %copy-start.7 = (s32[1,64,2]{1,2,0:T(2,128)S(1)}, s32[1,64,2]{1,2,0:T(2,128)}, u32[]{:S(2)}) copy-start(s32[1,64,2]{1,2,0:T(2,128)} %param.14) | copy-start | bytes 1540
  106.3 18.2 %collective-permute-start.10 = (f32[8,128]{1,0:T(8,128)S(1)}, f32[8,128]{1,0:T(8,128)S(1)}, u32[]{:S(2)}, u32[]{:S(2)}) collective-permute-start(f32[8,128]{1,0:T(8,128)S(1)} %get-tuple-element.51), channel_id=1, source_target_pairs={{0,2},{1,3},{2,0},{3,1},{4,6},{5,7},{6,4},{7,5},{8,10},{9,11},{10,... | collective-permute-start | bytes 12296 | tf_op jit(solution)/shard_map/ppermute | solution.py:455
  106.6 19.3 %collective-permute-start.11 = (f32[8,128]{1,0:T(8,128)S(1)}, f32[8,128]{1,0:T(8,128)S(1)}, u32[]{:S(2)}, u32[]{:S(2)}) collective-permute-start(f32[8,128]{1,0:T(8,128)S(1)} %get-tuple-element.52), channel_id=1, source_target_pairs={{0,3},{1,0},{2,1},{3,2},{4,7},{5,4},{6,5},{7,6},{8,11},{9,8},{10,9... | collective-permute-start | bytes 12296 | tf_op jit(solution)/shard_map/ppermute | solution.py:455
  124.6 4.0 %collective-permute-start.9 = (f32[8,128]{1,0:T(8,128)S(1)}, f32[8,128]{1,0:T(8,128)S(1)}, u32[]{:S(2)}, u32[]{:S(2)}) collective-permute-start(f32[8,128]{1,0:T(8,128)S(1)} %get-tuple-element.50), channel_id=1, source_target_pairs={{0,1},{1,2},{2,3},{3,0},{4,5},{5,6},{6,7},{7,4},{8,9},{9,10},{10,1... | collective-permute-start | bytes 12296 | tf_op jit(solution)/shard_map/ppermute | solution.py:455
  132.5 3.8 %collective-permute-start.12 = (bf16[1120,256]{1,0:T(8,128)(2,1)S(1)}, bf16[1120,256]{1,0:T(8,128)(2,1)S(1)}, u32[]{:S(2)}, u32[]{:S(2)}) collective-permute-start(bf16[1120,256]{1,0:T(8,128)(2,1)S(1)} %get-tuple-element.54), channel_id=1, source_target_pairs={{0,4},{4,0},{1,5},{5,1},{2,6},{6,2},{3,7},{7,3},{8,12},{12,8},{9,1... | collective-permute-start | bytes 1720328 | tf_op jit(solution)/shard_map/ppermute | solution.py:455
  137.4 14.3 %collective-permute-start.13 = (bf16[352,256]{1,0:T(8,128)(2,1)}, bf16[352,256]{1,0:T(8,128)(2,1)S(1)}, u32[]{:S(2)}, u32[]{:S(2)}) collective-permute-start(bf16[352,256]{1,0:T(8,128)(2,1)} %get-tuple-element.56), channel_id=1, source_target_pairs={{0,8},{8,16},{16,24},{24,0},{1,9},{9,17},{17,25},{25,1},{2,10},{10... | collective-permute-start | bytes 540680 | tf_op jit(solution)/shard_map/ppermute | solution.py:455
  138.8 12.9 %collective-permute-start.14 = (bf16[352,256]{1,0:T(8,128)(2,1)}, bf16[352,256]{1,0:T(8,128)(2,1)S(1)}, u32[]{:S(2)}, u32[]{:S(2)}) collective-permute-start(bf16[352,256]{1,0:T(8,128)(2,1)} %get-tuple-element.57), channel_id=1, source_target_pairs={{0,16},{8,24},{16,0},{24,8},{1,17},{9,25},{17,1},{25,9},{2,18},{10... | collective-permute-start | bytes 540680 | tf_op jit(solution)/shard_map/ppermute | solution.py:455
  141.1 10.6 %collective-permute-start.15 = (bf16[352,256]{1,0:T(8,128)(2,1)}, bf16[352,256]{1,0:T(8,128)(2,1)S(1)}, u32[]{:S(2)}, u32[]{:S(2)}) collective-permute-start(bf16[352,256]{1,0:T(8,128)(2,1)} %get-tuple-element.58), channel_id=1, source_target_pairs={{0,24},{8,0},{16,8},{24,16},{1,25},{9,1},{17,9},{25,17},{2,26},{10... | collective-permute-start | bytes 540680 | tf_op jit(solution)/shard_map/ppermute | solution.py:455
  152.6 21.9 %all-to-all-start.2 = ((bf16[8,128,256]{2,1,0:T(8,128)(2,1)}), bf16[8,128,256]{2,1,0:T(8,128)(2,1)S(1)}, u32[]{:S(2)}, u32[]{:S(2)}) async-start(bf16[8,128,256]{2,1,0:T(8,128)(2,1)} %shard_map.129), calls=%async_computation.2 | async-start | bytes 1048576 | tf_op jit(solution)/shard_map/all_to_all | solution.py:587
  157.8 5.0 %collective-permute-start.3 = (bf16[2,64,128]{2,1,0:T(8,128)(2,1)S(1)}, bf16[2,64,128]{2,1,0:T(8,128)(2,1)S(1)}, u32[]{:S(2)}, u32[]{:S(2)}) collective-permute-start(bf16[2,64,128]{2,1,0:T(8,128)(2,1)S(1)} %get-tuple-element.39), channel_id=1, source_target_pairs={{0,1},{1,2},{2,3},{3,0},{4,5},{5,6},{6,7},{7,4},{8,9},{9,10},{10,1... | collective-permute-start | bytes 98312 | tf_op jit(solution)/shard_map/ppermute | solution.py:455
  159.1 4.3 %collective-permute-start.4 = (bf16[2,64,128]{2,1,0:T(8,128)(2,1)S(1)}, bf16[2,64,128]{2,1,0:T(8,128)(2,1)S(1)}, u32[]{:S(2)}, u32[]{:S(2)}) collective-permute-start(bf16[2,64,128]{2,1,0:T(8,128)(2,1)S(1)} %get-tuple-element.40), channel_id=1, source_target_pairs={{0,2},{1,3},{2,0},{3,1},{4,6},{5,7},{6,4},{7,5},{8,10},{9,11},{10,... | collective-permute-start | bytes 98312 | tf_op jit(solution)/shard_map/ppermute | solution.py:455
  161.7 3.3 %collective-permute-start.5 = (bf16[2,64,128]{2,1,0:T(8,128)(2,1)S(1)}, bf16[2,64,128]{2,1,0:T(8,128)(2,1)S(1)}, u32[]{:S(2)}, u32[]{:S(2)}) collective-permute-start(bf16[2,64,128]{2,1,0:T(8,128)(2,1)S(1)} %get-tuple-element.41), channel_id=1, source_target_pairs={{0,3},{1,0},{2,1},{3,2},{4,7},{5,4},{6,5},{7,6},{8,11},{9,8},{10,9... | collective-permute-start | bytes 98312 | tf_op jit(solution)/shard_map/ppermute | solution.py:455
Sparse Core Ops, SparseCore 0:
  9.8 56.2 all-gather.1

commit v5 on v4

--- a/solution.py
+++ b/solution.py
@@ -20,16 +20,18 @@
 MIB = 1024 * 1024
 VM = pl.BlockSpec(memory_space=pltpu.VMEM)
 SM = pl.BlockSpec(memory_space=pltpu.SMEM)
+COST = pl.CostEstimate(flops=8 * 10**9, transcendentals=0, bytes_accessed=20 * 10**6)
 HB = pl.BlockSpec(memory_space=pltpu.HBM)
 
 
-def call(body, outs, ins, scratch=(), limit=16, outs_in=None):
+def call(body, outs, ins, scratch=(), limit=16, outs_in=None, cost=None):
     return pl.pallas_call(
         body,
         out_shape=outs,
         in_specs=ins,
         out_specs=outs_in or jax.tree.map(lambda _: VM, outs),
         scratch_shapes=list(scratch),
+        cost_estimate=cost,
         compiler_params=pltpu.CompilerParams(vmem_limit_bytes=limit * MIB),
     )
 
@@ -99,8 +101,10 @@
     return jnp.concatenate([ref[c : c + 1, :] for c in range(ref.shape[0])], axis=1)
 
 
-def take_body(share, idx_ref, rel_ref, ent_ref, out_ref, own, outs, sem, osem):
-    wait_all(start_all(own_row_copies(ent_ref, own, sem, share)))
+def take_body(share, src_ref, edge_ref, ent_ref, out_ref, idx_ref, rel_ref, own, outs, isem, sem, osem):
+    copies = own_row_copies(ent_ref, own, sem, share)
+    copies += [pltpu.make_async_copy(src_ref, idx_ref, isem.at[0]), pltpu.make_async_copy(edge_ref, rel_ref, isem.at[1])]
+    wait_all(start_all(copies))
     cap, peers = idx_ref.shape
     halves = own.shape[1] // LANES
     lane = lax.broadcasted_iota(jnp.int32, (8, LANES), 1)
@@ -141,10 +145,6 @@
     return jnp.concatenate([jnp.where(blk == n, coef, 0.0) for n in range(nblk)], axis=0)
 
 
-def weights_body(nblk, own, rel_ref, src_ref, c0, c1, c2, c3, out_ref, cs):
-    out_ref[...] = slot_weights(own, (c0, c1, c2, c3), line(rel_ref), line(src_ref), nblk, cs).astype(BF)
-
-
 def widen(x_ref, xf):
     step = 512
 
@@ -179,8 +179,8 @@
 
 def fwd_body(
     cap, nblk, own, dst_ref, count_ref, x_ref, dstv_ref, cnt_ref, c0, c1, c2, c3, sw_ref, table_ref, ent_ref,
-    cot_ref, y0, y1, y2, y3, back_ref, xr_ref, pg_ref, rel_ref, act_ref,
-    xf, mf, cs, at_ref, tab, ent, cot, ysc, back, xr, tsem, esem, csem, ysem, bsem, xsem,
+    cot_ref, y0, y1, y2, y3, back_ref, pg_ref, rel_ref, act_ref,
+    xf, mf, cs, at_ref, tab, ent, cot, ysc, back, tsem, esem, csem, ysem, psem, bsem,
 ):
     groups = tab.shape[0]
     nbase = groups * own
@@ -207,16 +207,16 @@
 
     def one(k, c):
         xk = slot_rows(xf, peers, cap, halves, share, k).astype(BF)
-        xr[k] = xk
         wk = jnp.where(cnt > first + k, w, 0.0).astype(BF)
         put(mf, pl.ds(k, w.shape[0], stride=share), jnp.dot(wk, xk, preferred_element_type=F32))
         return c
 
-    lax.fori_loop(0, share, one, 0, unroll=4)
-    copies = start_all([pltpu.make_async_copy(xr, xr_ref, xsem)])
+    lax.fori_loop(0, share, one, 0, unroll=8)
+    copies = []
     wait_all(ecopies)
     acc = jnp.dot(ent[...], sw_ref[...], preferred_element_type=F32)
     rows = nblk * share
+    ys = (y0, y1, y2, y3)
     wait_all(tcopies)
     for r in range(groups):
         group = turn(group0, r, groups)
@@ -224,6 +224,9 @@
             mb = rows_of(mf, group * own + b, nbase, nblk, share).astype(BF)
             ysc[r, pl.ds(b * rows, rows), :] = mb
             acc += jnp.dot(mb, tab[group, pl.ds(b * width, width), :], preferred_element_type=F32)
+        if r:
+            at = pl.ds(0, own * rows)
+            copies += start_all([pltpu.make_async_copy(ysc.at[r, at], ys[r].at[at], ysem.at[r])])
     s = jax.nn.sigmoid(acc)
     at_ref[...] = (acc * s).T
     wait_all(ccopies)
@@ -243,22 +246,29 @@
             at = pl.ds(i * lot, lot)
             copies += start_all([pltpu.make_async_copy(back.at[at], back_ref.at[at], bsem.at[i])])
     cols = width // groups
-    for r, y in enumerate((y0, y1, y2, y3)):
-        ysc[r, pl.ds(own * rows, rows), :] = pg
-        copies += start_all([pltpu.make_async_copy(ysc.at[r], y, ysem.at[r])])
+    at = pl.ds(own * rows, rows)
+    for r in range(groups):
+        ysc[r, at, :] = pg
+        copies += start_all([pltpu.make_async_copy(ysc.at[r, at] if r else ysc.at[r], ys[r].at[at] if r else ys[r], psem.at[r])])
         act_ref[r] = at_ref[aligned(turn(group0, r, groups), cols), :].astype(BF)
     wait_all(copies)
 
 
-def score_body(nblk, own, pg_ref, dstv_ref, cnt_ref, xr_ref, table_ref, s0, s1, s2, s3, pf, ts, tab, xr, tsem, xsem):
+def score_body(
+    cap, nblk, own, halves, pg_ref, dstv_ref, cnt_ref, x_ref, rel_ref, src_ref, c0, c1, c2, c3, table_ref,
+    s0, s1, s2, s3, w_ref, xf, pf, ts, tab, cs, tsem,
+):
     groups = tab.shape[0]
     nbase = groups * own
     width = tab.shape[2]
-    share, slots = xr.shape[:2]
+    peers = cnt_ref.shape[1]
+    slots = cap * peers
+    share = BLK // groups
     group0 = lax.axis_index("basis")
     first = group0 * share
     tcopies = start_all(table_copies(table_ref, tab, tsem))
-    xcopies = start_all([pltpu.make_async_copy(xr_ref, xr, xsem)])
+    w_ref[...] = slot_weights(own, (c0, c1, c2, c3), line(rel_ref), line(src_ref), nblk, cs).astype(BF)
+    widen(x_ref, xf)
     pg = pg_ref[...]
     for b in range(nbase):
         if b % own == 0:
@@ -268,11 +278,11 @@
         for n in range(nblk):
             put(pf, pl.ds((n * nbase + b) * share, share), p[n * share : (n + 1) * share])
     cnt = line(cnt_ref)
-    wait_all(xcopies)
 
     def one(k, acc):
         pk = get(pf, pl.ds(k, nblk * nbase, stride=share)).astype(BF)
-        t = lax.dot_general(pk, xr[k], NT, preferred_element_type=F32)
+        xk = slot_rows(xf, peers, cap, halves, share, k).astype(BF)
+        t = lax.dot_general(pk, xk, NT, preferred_element_type=F32)
         return acc + jnp.where(cnt > first + k, t, 0.0)
 
     acc = lax.fori_loop(0, share, one, jnp.zeros((nblk * nbase, slots), F32), unroll=4)
@@ -312,7 +322,7 @@
     return value[at : at + n].astype(F32) + value[at + n : at + 2 * n].astype(F32)
 
 
-def basis_body(own, rows, peers, y0, y1, y2, y3, coef_ref, keep_ref, send_ref, tmp, outf):
+def basis_body(own, rows, peers, y0, y1, y2, y3, keep_ref, send_ref, tmp, outf):
     ys = (y0, y1, y2, y3)
     width = y0.shape[1]
     part = keep_ref.shape[0]
@@ -333,16 +343,15 @@
                     )
     core = lax.axis_index("c")
     keep_ref[...] = get(outf, aligned(core, part)).astype(BF)
-    send_ref[pl.ds(0, part), :] = get(outf, aligned(1 - core, part)).astype(BF)
-    send_ref[pl.ds(part, coef_ref.shape[0]), :] = coef_ref[...]
-
-
-def core_body(keep_ref, got_ref, coef_ref, o0, o1, o2, o3, sums):
+    send_ref[...] = get(outf, aligned(1 - core, part)).astype(BF)
+
+
+def core_body(keep_ref, got_ref, coef_ref, other_ref, o0, o1, o2, o3, sums):
     part = keep_ref.shape[0]
     each = part // NX
     n = coef_ref.shape[0] // 2
-    sums[...] = keep_ref[...].astype(F32) + got_ref[pl.ds(0, part), :].astype(F32)
-    coef = unpack(coef_ref[...], 0, n) + unpack(got_ref[pl.ds(part, 2 * n), :], 0, n)
+    sums[...] = keep_ref[...].astype(F32) + got_ref[...].astype(F32)
+    coef = unpack(coef_ref[...], 0, n) + unpack(other_ref[...], 0, n)
     for r, out in enumerate((o0, o1, o2, o3)):
         out[pl.ds(0, each), :] = sums[aligned(turn(lax.axis_index("x"), r, NX), each), :].astype(BF)
         pack(out, each, coef)
@@ -399,7 +408,7 @@
         put(mf, pl.ds(k, w.shape[0], stride=share), jnp.dot(w, xk, preferred_element_type=F32))
         return c
 
-    lax.fori_loop(0, share, one, 0, unroll=4)
+    lax.fori_loop(0, share, one, 0, unroll=8)
     acc = lax.dot_general(pg_ref[...], sw_ref[...], NT, preferred_element_type=F32)
     wait_all(tcopies)
     for b in range(nbase):
@@ -461,37 +470,33 @@
     outgoing = call(
         functools.partial(take_body, share),
         hbm(peers, per + 8, LANES),
-        [SM, SM, HB],
+        [HB] * 3,
         [
+            pltpu.SMEM((cap, peers), jnp.int32),
+            pltpu.SMEM((cap, peers), jnp.int32),
             pltpu.VMEM((rows, width), BF),
             pltpu.VMEM((peers, per + 8, LANES), BF),
+            dma((2,)),
             dma((nblk,)),
             dma((4,)),
         ],
         outs_in=HB,
-    )(src, rel_out, far(entity_rows))
+    )(far(src), far(rel_out), far(entity_rows))
     incoming = lax.all_to_all(outgoing, ENT, split_axis=0, concat_axis=0, tiled=True)
 
+    bases, _ = lax.optimization_barrier((bases, outgoing))
     table = lax.all_gather(bases.reshape(own * width, width), "basis")
     chunks = -(-relations // width)
     coef = jnp.pad(coefficients.astype(BF).T, ((0, 16 - own), (0, chunks * width - relations)))
     coef = coef.reshape(16, chunks, width).transpose(1, 0, 2).reshape(chunks * 16, width)
     coefs = [coef] + [over("basis", r, coef) for r in range(1, groups)]
-    w_out = call(
-        functools.partial(weights_body, nblk, own),
-        bf(nblk * nbase, slots),
-        [VM] * 6,
-        [pltpu.VMEM((groups, own, slots), F32)],
-        limit=4,
-    )(rel_out, src, *coefs)
-
     tables = pltpu.VMEM((groups, own * width, width), BF)
-    *ys, back, xr, pg, rel_in, act = call(
+    incoming = incoming.reshape(peers * (per + 8), LANES)
+    *ys, back, pg, rel_in, act = call(
         functools.partial(fwd_body, cap, nblk, own),
         (
             *[hbm((own + 1) * rows, width) for _ in range(groups)],
             hbm(peers, per, LANES),
-            hbm(share, slots, width),
             bf(rows, width),
             jax.ShapeDtypeStruct((1, slots), jnp.int32),
             bf(groups, width // groups, rows),
@@ -507,58 +512,60 @@
             pltpu.VMEM((rows, width), BF),
             pltpu.VMEM((groups, (own + 1) * rows, width), BF),
             pltpu.VMEM((peers, per, LANES), BF),
-            pltpu.VMEM((share, slots, width), BF),
             dma((groups,)),
             dma((nblk,)),
             dma((nblk,)),
             dma((groups,)),
+            dma((groups,)),
             dma((4,)),
-            dma,
         ],
         limit=28,
-        outs_in=(HB,) * (groups + 2) + (VM,) * 3,
+        outs_in=(HB,) * (groups + 1) + (VM,) * 3,
     )(
-        dst, cnt, incoming.reshape(peers * (per + 8), LANES), dst, cnt, *coefs, self_weight, far(table),
+        dst, cnt, incoming, dst, cnt, *coefs, self_weight, far(table),
         far(entity_rows), far(cotangent),
     )
 
     returned = lax.all_to_all(back, ENT, split_axis=0, concat_axis=0, tiled=True)
     ys = [ys[0]] + [over("basis", r, ys[r]) for r in range(1, groups)]
 
-    scores = call(
-        functools.partial(score_body, nblk, own),
-        tuple(jax.ShapeDtypeStruct((own, slots), F32) for _ in range(groups)),
-        [VM] * 3 + [HB] * 2,
+    *scores, w_out = call(
+        functools.partial(score_body, cap, nblk, own, halves),
+        (*[jax.ShapeDtypeStruct((own, slots), F32) for _ in range(groups)], bf(nblk * nbase, slots)),
+        [VM] * 10 + [HB],
         [
+            pltpu.VMEM((peers * (per + 8), LANES), F32),
             rows_scratch(nbase * rows, width),
             pltpu.VMEM((nbase, slots), F32),
             tables,
-            pltpu.VMEM((share, slots, width), BF),
+            pltpu.VMEM((groups, own, slots), F32),
             dma((groups,)),
-            dma,
         ],
-    )(pg, dst, cnt, far(xr), far(table))
+        limit=18,
+        cost=COST,
+    )(pg, dst, cnt, incoming, rel_out, src, *coefs, far(table))
     scores = [scores[0]] + [over("basis", r, scores[r]) for r in range(1, groups)]
     lot = chunks * own
     coef_part = call(coef_body, bf(2 * lot, width), [VM] * 5, limit=4)(rel_in, *scores)
 
+    ys = lax.optimization_barrier((*ys, scores[1], scores[3]))[:groups]
     part = own * width // NC
     keep, send = call(
         functools.partial(basis_body, own, rows, peers),
-        (bf(part, width), bf(part + 2 * lot, width)),
-        [VM] * 5,
+        (bf(part, width), bf(part, width)),
+        [VM] * 4,
         [rows_scratch(width, width), rows_scratch(NC * part, width)],
         limit=8,
-    )(*ys, coef_part)
+    )(*ys)
     got = over("c", 1, send)
     each = part // NX
     outs = call(
         core_body,
         tuple(bf(each + 2 * lot, width) for _ in range(NX)),
-        [VM] * 3,
+        [VM] * 4,
         [pltpu.VMEM((part, width), F32)],
         limit=8,
-    )(keep, got, coef_part)
+    )(keep, got, coef_part, over("c", 1, coef_part))
     ins = [outs[0]] + [over("x", r, outs[r]) for r in range(1, NX)]
 
     grads = call(
@@ -575,7 +582,6 @@
         limit=18,
     )(returned.reshape(peers * per, LANES), w_out, act, pg, self_weight, far(table))
 
-    ins = lax.optimization_barrier((*ins, grads[0]))[:NX]
     last = each // nz
     out = call(
         x_body,

time: 184 us -> 181 us (0.984)
    ppermute x16 -> x17, waiting for transfers between devices: 25.5 us -> 33 us  [over(): return lax.ppermute(value, axis, [(i, (i + r) % n) for i in range(n)])]
    all_to_all x1, waiting for transfers between devices: 8.67 us -> 4.08 us  [local(): out = lax.all_to_all(out, 'z', split_axis=0, concat_axis=0, tiled=True)]
    pallas_call x3 -> x2, Pallas kernels: 9.87 us -> 9.37 us  [the longest x1 6.93 us: local(): call(functools.partial(score_body, cap, nblk, own, halves), (*[jax.ShapeD...]
    ppermute x16 -> x17, starting transfers between devices: 26.6 us -> 26.2 us  [over(): return lax.ppermute(value, axis, [(i, (i + r) % n) for i in range(n)])]
  transfers between devices with their start and end apart: 20 -> 21, of which waited for: 9 -> 12; matrix products, arithmetic and copies ran while one was open for 0% -> 0% of each run, Pallas kernels for 13% -> 12%
where the time goes in v5:
time: 181 us
  waiting for transfers between devices  79.5 us (44%)
  starting transfers between devices  52.6 us (29%)
  Pallas kernels  33.6 us (19%)
  between operations  14.2 us (8%)
    all_to_all x1, waiting for transfers between devices, local(): lax.all_to_all(outgoing, ENT, split_axis=0, concat_axis=0, tiled=True)  42.4 us
    ppermute x17, waiting for transfers between devices, over(): return lax.ppermute(value, axis, [(i, (i + r) % n) for i in range(n)])  33 us
    ppermute x17, starting transfers between devices, over(): return lax.ppermute(value, axis, [(i, (i + r) % n) for i in range(n)])  26.2 us
    all_to_all x1, starting transfers between devices, local(): lax.all_to_all(outgoing, ENT, split_axis=0, concat_axis=0, tiled=True)  13.1 us
    pallas_call x1, Pallas kernels, local(): call(functools.partial(bwd_body, cap, own), tuple((bf(2, width // groups,...  9.01 us
    pallas_call x1, Pallas kernels, local(): call(functools.partial(fwd_body, cap, nblk, own), (*[hbm((own + 1) * rows...  8.54 us
    all_to_all x1, starting transfers between devices, local(): lax.all_to_all(back, ENT, split_axis=0, concat_axis=0, tiled=True)  7.43 us
    pallas_call x1, Pallas kernels, local(): call(functools.partial(score_body, cap, nblk, own, halves), (*[jax.ShapeD...  6.93 us
  transfers between devices with their start and end apart: 21, of which 12 were waited for; matrix products, arithmetic and copies ran while one was open for 0% of the time, Pallas kernels for 12%

profile of v5, /device:TPU:1, one launch (start us, length us, event | category | flops | bytes accessed | tf_op | source)
XLA Modules:
  0.0 180.6 jit_solution(3973434946840148594)
XLA Ops:
  7.2 2.4 %shard_map.120 = bf16[64,136,128]{2,1,0:T(8,128)(2,1)} custom-call(s32[2,64]{1,0:T(2,128)} %bitcast.35, s32[2,64]{1,0:T(2,128)} %bitcast.37, bf16[512,256]{1,0:T(8,128)(2,1)} %ent_ref.3), custom_call_target="tpu_custom_call" | custom-call | tf_op jit(solution)/shard_map/pallas_call | solution.py:470
  9.7 13.1 %all-to-all-start = ((bf16[64,136,128]{2,1,0:T(8,128)(2,1)}), bf16[64,136,128]{2,1,0:T(8,128)(2,1)S(1)}, u32[]{:S(2)}, u32[]{:S(2)}) async-start(bf16[64,136,128]{2,1,0:T(8,128)(2,1)} %shard_map.120), calls=%async_computation | async-start | bytes 4456448 | tf_op jit(solution)/shard_map/all_to_all | solution.py:485
  23.0 2.8 %collective-permute-start.2 = (bf16[96,256]{1,0:T(8,128)(2,1)S(1)}, bf16[96,256]{1,0:T(8,128)(2,1)S(1)}, u32[]{:S(2)}, u32[]{:S(2)}) collective-permute-start(bf16[96,256]{1,0:T(8,128)(2,1)S(1)} %bitcast.24), channel_id=1, source_target_pairs={{0,3},{1,0},{2,1},{3,2},{4,7},{5,4},{6,5},{7,6},{8,11},{9,8},{10,9... | collective-permute-start | bytes 147464 | tf_op jit(solution)/shard_map/ppermute | solution.py:464
  27.0 3.4 %collective-permute-done.1.c2 = bf16[96,256]{1,0:T(8,128)(2,1)S(1)} collective-permute-done((bf16[96,256]{1,0:T(8,128)(2,1)S(1)}, bf16[96,256]{1,0:T(8,128)(2,1)S(1)}, u32[]{:S(2)}, u32[]{:S(2)}) %collective-permute-start.1) | collective-permute-done | bytes 49184 | tf_op jit(solution)/shard_map/ppermute | solution.py:464
  30.4 2.5 %collective-permute-done.c1 = bf16[96,256]{1,0:T(8,128)(2,1)S(1)} collective-permute-done((bf16[96,256]{1,0:T(8,128)(2,1)S(1)}, bf16[96,256]{1,0:T(8,128)(2,1)S(1)}, u32[]{:S(2)}, u32[]{:S(2)}) %collective-permute-start) | collective-permute-done | bytes 49184 | tf_op jit(solution)/shard_map/ppermute | solution.py:464
  32.9 42.4 %all-to-all-done = bf16[64,136,128]{2,1,0:T(8,128)(2,1)S(1)} async-done(((bf16[64,136,128]{2,1,0:T(8,128)(2,1)}), bf16[64,136,128]{2,1,0:T(8,128)(2,1)S(1)}, u32[]{:S(2)}, u32[]{:S(2)}) %all-to-all-start) | async-done | bytes 2228256 | tf_op jit(solution)/shard_map/all_to_all | solution.py:485
  75.3 8.5 %shard_map.121 = (bf16[1152,256]{1,0:T(8,128)(2,1)}, bf16[1152,256]{1,0:T(8,128)(2,1)}, bf16[1152,256]{1,0:T(8,128)(2,1)}, bf16[1152,256]{1,0:T(8,128)(2,1)}, bf...) custom-call(s32[2,64]{1,0:T(2,128)S(1)} %bitcast.29, ...), custom_call_target="tpu_custom_call" | custom-call | tf_op jit(solution)/shard_map/pallas_call | solution.py:495
  83.9 7.4 %all-to-all-start.1 = ((bf16[64,128,128]{2,1,0:T(8,128)(2,1)}), bf16[64,128,128]{2,1,0:T(8,128)(2,1)}, u32[]{:S(2)}, u32[]{:S(2)}) async-start(bf16[64,128,128]{2,1,0:T(8,128)(2,1)} %get-tuple-element.37), calls=%async_computation.1 | async-start | bytes 4194304 | tf_op jit(solution)/shard_map/all_to_all | solution.py:529
  91.3 1.4 collective-permute-start.6
  92.7 2.6 %collective-permute-start.7 = (bf16[1152,256]{1,0:T(8,128)(2,1)}, bf16[1152,256]{1,0:T(8,128)(2,1)S(1)}, u32[]{:S(2)}, u32[]{:S(2)}) collective-permute-start(bf16[1152,256]{1,0:T(8,128)(2,1)} %get-tuple-element.48), channel_id=1, source_target_pairs={{0,2},{1,3},{2,0},{3,1},{4,6},{5,7},{6,4},{7,5},{8,10},{9,11},{10,... | collective-permute-start | bytes 1769480 | tf_op jit(solution)/shard_map/ppermute | solution.py:464
  95.3 1.1 collective-permute-start.8
  96.4 6.9 %shard_map.122 = (f32[8,128]{1,0:T(8,128)S(1)}, f32[8,128]{1,0:T(8,128)S(1)}, f32[8,128]{1,0:T(8,128)S(1)}, f32[8,128]{1,0:T(8,128)S(1)}, bf16[128,128]{1,0:T(8,128)(2,1)S(1)}) custom-call(bf16[128,256]{1,0:T(8,128)(2,1)S(1)} %get-tuple-element.38.pg_ref, s32[2,64]{1,0:T(2,128)S(1)} %bitcast.31, s32[2,64]{1,0:T(2,128)S(1)} %bitcast.34, ...), custom_call_target="tpu_custom_call" | custom-call | flops 8000000000 | bytes 20000000 | tf_op jit(solution)/shard_map/pallas_call | solution.py:532
  103.8 2.3 %collective-permute-start.10 = (f32[8,128]{1,0:T(8,128)S(1)}, f32[8,128]{1,0:T(8,128)S(1)}, u32[]{:S(2)}, u32[]{:S(2)}) collective-permute-start(f32[8,128]{1,0:T(8,128)S(1)} %get-tuple-element.51), channel_id=1, source_target_pairs={{0,3},{1,0},{2,1},{3,2},{4,7},{5,4},{6,5},{7,6},{8,11},{9,8},{10,9... | collective-permute-start | bytes 12296 | tf_op jit(solution)/shard_map/ppermute | solution.py:464
  106.1 11.8 %collective-permute-done.9.s1 = f32[8,128]{1,0:T(8,128)S(1)} collective-permute-done((f32[8,128]{1,0:T(8,128)S(1)}, f32[8,128]{1,0:T(8,128)S(1)}, u32[]{:S(2)}, u32[]{:S(2)}) %collective-permute-start.9) | collective-permute-done | bytes 4128 | tf_op jit(solution)/shard_map/ppermute | solution.py:464
  117.8 2.8 %collective-permute-done.10.s3 = f32[8,128]{1,0:T(8,128)S(1)} collective-permute-done((f32[8,128]{1,0:T(8,128)S(1)}, f32[8,128]{1,0:T(8,128)S(1)}, u32[]{:S(2)}, u32[]{:S(2)}) %collective-permute-start.10) | collective-permute-done | bytes 4128 | tf_op jit(solution)/shard_map/ppermute | solution.py:464
  121.2 3.7 %shard_map.125 = (bf16[1024,256]{1,0:T(8,128)(2,1)S(1)}, bf16[1024,256]{1,0:T(8,128)(2,1)S(1)}) custom-call(bf16[1152,256]{1,0:T(8,128)(2,1)S(1)} %copy-done, bf16[1152,256]{1,0:T(8,128)(2,1)S(1)} %collective-permute-done.6.y1, bf16[1152,256]{1,0:T(8,128)(2,1)S(1)} %collective-permute-done.7.y2, bf16[1152,256]{1,0:T(8,128)(2,1)S(1)} %collective-permute-done.8.y3), custom_call_target="tpu_custom_call" | custom-call | tf_op jit(solution)/shard_map/pallas_call | solution.py:553
  124.9 1.4 collective-permute-start.11
  126.3 2.4 %collective-permute-start.12 = (f32[8,128]{1,0:T(8,128)S(1)}, f32[8,128]{1,0:T(8,128)S(1)}, u32[]{:S(2)}, u32[]{:S(2)}) collective-permute-start(f32[8,128]{1,0:T(8,128)S(1)} %get-tuple-element.60), channel_id=1, source_target_pairs={{0,2},{1,3},{2,0},{3,1},{4,6},{5,7},{6,4},{7,5},{8,10},{9,11},{10,... | collective-permute-start | bytes 12296 | tf_op jit(solution)/shard_map/ppermute | solution.py:464
  128.7 2.0 %collective-permute-done.12.s2 = f32[8,128]{1,0:T(8,128)S(1)} collective-permute-done((f32[8,128]{1,0:T(8,128)S(1)}, f32[8,128]{1,0:T(8,128)S(1)}, u32[]{:S(2)}, u32[]{:S(2)}) %collective-permute-start.12) | collective-permute-done | bytes 4128 | tf_op jit(solution)/shard_map/ppermute | solution.py:464
  130.9 0.9 collective-permute-start.13
  132.9 1.5 collective-permute-start.14
  134.4 2.4 %collective-permute-start.15 = (bf16[352,256]{1,0:T(8,128)(2,1)S(1)}, bf16[352,256]{1,0:T(8,128)(2,1)S(1)}, u32[]{:S(2)}, u32[]{:S(2)}) collective-permute-start(bf16[352,256]{1,0:T(8,128)(2,1)S(1)} %get-tuple-element.63), channel_id=1, source_target_pairs={{0,16},{8,24},{16,0},{24,8},{1,17},{9,25},{17,1},{25,9},{2,18},{10... | collective-permute-start | bytes 540680 | tf_op jit(solution)/shard_map/ppermute | solution.py:464
  136.8 1.2 collective-permute-start.16
  138.0 3.5 %collective-permute-done.14.i1 = bf16[352,256]{1,0:T(8,128)(2,1)S(1)} collective-permute-done((bf16[352,256]{1,0:T(8,128)(2,1)S(1)}, bf16[352,256]{1,0:T(8,128)(2,1)S(1)}, u32[]{:S(2)}, u32[]{:S(2)}) %collective-permute-start.14) | collective-permute-done | bytes 180256 | tf_op jit(solution)/shard_map/ppermute | solution.py:464
  141.5 5.5 %collective-permute-done.15.i2 = bf16[352,256]{1,0:T(8,128)(2,1)S(1)} collective-permute-done((bf16[352,256]{1,0:T(8,128)(2,1)S(1)}, bf16[352,256]{1,0:T(8,128)(2,1)S(1)}, u32[]{:S(2)}, u32[]{:S(2)}) %collective-permute-start.15) | collective-permute-done | bytes 180256 | tf_op jit(solution)/shard_map/ppermute | solution.py:464
  146.9 1.0 shard_map.128
  147.9 5.8 %all-to-all-start.2 = ((bf16[8,128,256]{2,1,0:T(8,128)(2,1)}), bf16[8,128,256]{2,1,0:T(8,128)(2,1)S(1)}, u32[]{:S(2)}, u32[]{:S(2)}) async-start(bf16[8,128,256]{2,1,0:T(8,128)(2,1)} %shard_map.128), calls=%async_computation.2 | async-start | bytes 1048576 | tf_op jit(solution)/shard_map/all_to_all | solution.py:593
  153.7 9.0 %shard_map.123 = (bf16[2,64,128]{2,1,0:T(8,128)(2,1)S(1)}, bf16[2,64,128]{2,1,0:T(8,128)(2,1)S(1)}, bf16[2,64,128]{2,1,0:T(8,128)(2,1)S(1)}, bf16[2,64,128]{2,1,0:T(8,128)(2,1)S(1)}) custom-call(bf16[8192,128]{1,0:T(8,128)(2,1)} %bitcast.13.x_ref, bf16[128,128]{1,0:T(8,128)(2,1)S(1)} %get-tuple-element.39.w_ref, ...), custom_call_target="tpu_custom_call" | custom-call | tf_op jit(solution)/shard_map/pallas_call | solution.py:571
  162.7 1.2 collective-permute-start.3
  163.9 2.4 %collective-permute-start.4 = (bf16[2,64,128]{2,1,0:T(8,128)(2,1)S(1)}, bf16[2,64,128]{2,1,0:T(8,128)(2,1)S(1)}, u32[]{:S(2)}, u32[]{:S(2)}) collective-permute-start(bf16[2,64,128]{2,1,0:T(8,128)(2,1)S(1)} %get-tuple-element.43), channel_id=1, source_target_pairs={{0,2},{1,3},{2,0},{3,1},{4,6},{5,7},{6,4},{7,5},{8,10},{9,11},{10,... | collective-permute-start | bytes 98312 | tf_op jit(solution)/shard_map/ppermute | solution.py:464
  166.3 1.3 collective-permute-start.5
  167.5 4.1 %all-to-all-done.2.in_ref = bf16[8,128,256]{2,1,0:T(8,128)(2,1)S(1)} async-done(((bf16[8,128,256]{2,1,0:T(8,128)(2,1)}), bf16[8,128,256]{2,1,0:T(8,128)(2,1)S(1)}, u32[]{:S(2)}, u32[]{:S(2)}) %all-to-all-start.2) | async-done | bytes 524320 | tf_op jit(solution)/shard_map/all_to_all | solution.py:593
  (42 shorter events, 5.8 us)
Async XLA Ops:
  7.2 68.1 %all-gather.2.cloned.1.call-start = ((), (), s32[]{:S(2)}) async-start(), calls=%async_computation.3 | async-start | bytes 5242880 | tf_op jit(solution)/shard_map/all_gather | solution.py:488
  9.7 13.2 %copy-start.6 = (f32[1315,8]{0,1:T(8,128)S(1)}, f32[1315,8]{0,1:T(8,128)}, u32[]{:S(2)}) copy-start(f32[1315,8]{0,1:T(8,128)} %param.12) | copy-start | bytes 126244
  9.7 65.6 %copy-start.1 = (bf16[256,256]{1,0:T(8,128)(2,1)S(1)}, bf16[256,256]{1,0:T(8,128)(2,1)}, u32[]{:S(2)}) copy-start(bf16[256,256]{1,0:T(8,128)(2,1)} %sw_ref.3) | copy-start | bytes 393220
  9.7 65.6 %copy-start.2 = (s32[64,1,2]{0,2,1:T(2,128)S(1)}, s32[64,1,2]{0,2,1:T(2,128)}, u32[]{:S(2)}) copy-start(s32[64,1,2]{0,2,1:T(2,128)} %param.15) | copy-start | bytes 1540
  9.7 65.6 %copy-start.3 = (s32[64,1,2]{0,2,1:T(2,128)S(1)}, s32[64,1,2]{0,2,1:T(2,128)}, u32[]{:S(2)}) copy-start(s32[64,1,2]{0,2,1:T(2,128)} %param.16) | copy-start | bytes 1540
  9.7 65.5 %all-to-all-start = ((bf16[64,136,128]{2,1,0:T(8,128)(2,1)}), bf16[64,136,128]{2,1,0:T(8,128)(2,1)S(1)}, u32[]{:S(2)}, u32[]{:S(2)}) async-start(bf16[64,136,128]{2,1,0:T(8,128)(2,1)} %shard_map.120), calls=%async_computation | async-start | bytes 4456448 | tf_op jit(solution)/shard_map/all_to_all | solution.py:485
  23.0 4.0 %collective-permute-start.2 = (bf16[96,256]{1,0:T(8,128)(2,1)S(1)}, bf16[96,256]{1,0:T(8,128)(2,1)S(1)}, u32[]{:S(2)}, u32[]{:S(2)}) collective-permute-start(bf16[96,256]{1,0:T(8,128)(2,1)S(1)} %bitcast.24), channel_id=1, source_target_pairs={{0,3},{1,0},{2,1},{3,2},{4,7},{5,4},{6,5},{7,6},{8,11},{9,8},{10,9... | collective-permute-start | bytes 147464 | tf_op jit(solution)/shard_map/ppermute | solution.py:464
  25.8 4.6 %collective-permute-start.1 = (bf16[96,256]{1,0:T(8,128)(2,1)S(1)}, bf16[96,256]{1,0:T(8,128)(2,1)S(1)}, u32[]{:S(2)}, u32[]{:S(2)}) collective-permute-start(bf16[96,256]{1,0:T(8,128)(2,1)S(1)} %bitcast.25), channel_id=1, source_target_pairs={{0,2},{1,3},{2,0},{3,1},{4,6},{5,7},{6,4},{7,5},{8,10},{9,11},{10,... | collective-permute-start | bytes 147464 | tf_op jit(solution)/shard_map/ppermute | solution.py:464
  26.2 6.7 %collective-permute-start = (bf16[96,256]{1,0:T(8,128)(2,1)S(1)}, bf16[96,256]{1,0:T(8,128)(2,1)S(1)}, u32[]{:S(2)}, u32[]{:S(2)}) collective-permute-start(bf16[96,256]{1,0:T(8,128)(2,1)S(1)} %bitcast.26), channel_id=1, source_target_pairs={{0,1},{1,2},{2,3},{3,0},{4,5},{5,6},{6,7},{7,4},{8,9},{9,10},{10,1... | collective-permute-start | bytes 147464 | tf_op jit(solution)/shard_map/ppermute | solution.py:464
  83.8 11.5 %copy-start.7 = (bf16[1152,256]{1,0:T(8,128)(2,1)S(1)}, bf16[1152,256]{1,0:T(8,128)(2,1)}, u32[]{:S(2)}) copy-start(bf16[1152,256]{1,0:T(8,128)(2,1)} %get-tuple-element.49) | copy-start | bytes 1769476
  83.8 12.5 %copy-start.4 = (s32[1,64,2]{1,2,0:T(2,128)S(1)}, s32[1,64,2]{1,2,0:T(2,128)}, u32[]{:S(2)}) copy-start(s32[1,64,2]{1,2,0:T(2,128)} %param.13) | copy-start | bytes 1540
  83.9 12.5 %copy-start.5 = (s32[1,64,2]{1,2,0:T(2,128)S(1)}, s32[1,64,2]{1,2,0:T(2,128)}, u32[]{:S(2)}) copy-start(s32[1,64,2]{1,2,0:T(2,128)} %param.14) | copy-start | bytes 1540
  83.9 64.0 %all-to-all-start.1 = ((bf16[64,128,128]{2,1,0:T(8,128)(2,1)}), bf16[64,128,128]{2,1,0:T(8,128)(2,1)}, u32[]{:S(2)}, u32[]{:S(2)}) async-start(bf16[64,128,128]{2,1,0:T(8,128)(2,1)} %get-tuple-element.37), calls=%async_computation.1 | async-start | bytes 4194304 | tf_op jit(solution)/shard_map/all_to_all | solution.py:529
  91.3 29.3 %collective-permute-start.6 = (bf16[1152,256]{1,0:T(8,128)(2,1)}, bf16[1152,256]{1,0:T(8,128)(2,1)S(1)}, u32[]{:S(2)}, u32[]{:S(2)}) collective-permute-start(bf16[1152,256]{1,0:T(8,128)(2,1)} %get-tuple-element.47), channel_id=1, source_target_pairs={{0,1},{1,2},{2,3},{3,0},{4,5},{5,6},{6,7},{7,4},{8,9},{9,10},{10,1... | collective-permute-start | bytes 1769480 | tf_op jit(solution)/shard_map/ppermute | solution.py:464
  92.7 28.5 %collective-permute-start.7 = (bf16[1152,256]{1,0:T(8,128)(2,1)}, bf16[1152,256]{1,0:T(8,128)(2,1)S(1)}, u32[]{:S(2)}, u32[]{:S(2)}) collective-permute-start(bf16[1152,256]{1,0:T(8,128)(2,1)} %get-tuple-element.48), channel_id=1, source_target_pairs={{0,2},{1,3},{2,0},{3,1},{4,6},{5,7},{6,4},{7,5},{8,10},{9,11},{10,... | collective-permute-start | bytes 1769480 | tf_op jit(solution)/shard_map/ppermute | solution.py:464
  95.3 25.9 %collective-permute-start.8 = (bf16[1152,256]{1,0:T(8,128)(2,1)S(1)}, bf16[1152,256]{1,0:T(8,128)(2,1)S(1)}, u32[]{:S(2)}, u32[]{:S(2)}) collective-permute-start(bf16[1152,256]{1,0:T(8,128)(2,1)S(1)} %copy-done.7), channel_id=1, source_target_pairs={{0,3},{1,0},{2,1},{3,2},{4,7},{5,4},{6,5},{7,6},{8,11},{9,8},{10,9... | collective-permute-start | bytes 1769480 | tf_op jit(solution)/shard_map/ppermute | solution.py:464
  96.4 24.8 %copy-start = (bf16[1152,256]{1,0:T(8,128)(2,1)S(1)}, bf16[1152,256]{1,0:T(8,128)(2,1)}, u32[]{:S(2)}) copy-start(bf16[1152,256]{1,0:T(8,128)(2,1)} %get-tuple-element.52.y0) | copy-start | bytes 1769476
  103.3 14.5 %collective-permute-start.9 = (f32[8,128]{1,0:T(8,128)S(1)}, f32[8,128]{1,0:T(8,128)S(1)}, u32[]{:S(2)}, u32[]{:S(2)}) collective-permute-start(f32[8,128]{1,0:T(8,128)S(1)} %get-tuple-element.50), channel_id=1, source_target_pairs={{0,1},{1,2},{2,3},{3,0},{4,5},{5,6},{6,7},{7,4},{8,9},{9,10},{10,1... | collective-permute-start | bytes 12296 | tf_op jit(solution)/shard_map/ppermute | solution.py:464
  103.8 16.9 %collective-permute-start.10 = (f32[8,128]{1,0:T(8,128)S(1)}, f32[8,128]{1,0:T(8,128)S(1)}, u32[]{:S(2)}, u32[]{:S(2)}) collective-permute-start(f32[8,128]{1,0:T(8,128)S(1)} %get-tuple-element.51), channel_id=1, source_target_pairs={{0,3},{1,0},{2,1},{3,2},{4,7},{5,4},{6,5},{7,6},{8,11},{9,8},{10,9... | collective-permute-start | bytes 12296 | tf_op jit(solution)/shard_map/ppermute | solution.py:464
  124.9 7.8 %collective-permute-start.11 = (bf16[1024,256]{1,0:T(8,128)(2,1)S(1)}, bf16[1024,256]{1,0:T(8,128)(2,1)S(1)}, u32[]{:S(2)}, u32[]{:S(2)}) collective-permute-start(bf16[1024,256]{1,0:T(8,128)(2,1)S(1)} %get-tuple-element.57), channel_id=1, source_target_pairs={{0,4},{4,0},{1,5},{5,1},{2,6},{6,2},{3,7},{7,3},{8,12},{12,8},{9,1... | collective-permute-start | bytes 1572872 | tf_op jit(solution)/shard_map/ppermute | solution.py:464
  126.3 4.4 %collective-permute-start.12 = (f32[8,128]{1,0:T(8,128)S(1)}, f32[8,128]{1,0:T(8,128)S(1)}, u32[]{:S(2)}, u32[]{:S(2)}) collective-permute-start(f32[8,128]{1,0:T(8,128)S(1)} %get-tuple-element.60), channel_id=1, source_target_pairs={{0,2},{1,3},{2,0},{3,1},{4,6},{5,7},{6,4},{7,5},{8,10},{9,11},{10,... | collective-permute-start | bytes 12296 | tf_op jit(solution)/shard_map/ppermute | solution.py:464
  130.9 1.8 collective-permute-start.13
  132.9 8.5 %collective-permute-start.14 = (bf16[352,256]{1,0:T(8,128)(2,1)S(1)}, bf16[352,256]{1,0:T(8,128)(2,1)S(1)}, u32[]{:S(2)}, u32[]{:S(2)}) collective-permute-start(bf16[352,256]{1,0:T(8,128)(2,1)S(1)} %get-tuple-element.62), channel_id=1, source_target_pairs={{0,8},{8,16},{16,24},{24,0},{1,9},{9,17},{17,25},{25,1},{2,10},{10... | collective-permute-start | bytes 540680 | tf_op jit(solution)/shard_map/ppermute | solution.py:464
  134.4 12.5 %collective-permute-start.15 = (bf16[352,256]{1,0:T(8,128)(2,1)S(1)}, bf16[352,256]{1,0:T(8,128)(2,1)S(1)}, u32[]{:S(2)}, u32[]{:S(2)}) collective-permute-start(bf16[352,256]{1,0:T(8,128)(2,1)S(1)} %get-tuple-element.63), channel_id=1, source_target_pairs={{0,16},{8,24},{16,0},{24,8},{1,17},{9,25},{17,1},{25,9},{2,18},{10... | collective-permute-start | bytes 540680 | tf_op jit(solution)/shard_map/ppermute | solution.py:464
  136.8 10.1 %collective-permute-start.16 = (bf16[352,256]{1,0:T(8,128)(2,1)S(1)}, bf16[352,256]{1,0:T(8,128)(2,1)S(1)}, u32[]{:S(2)}, u32[]{:S(2)}) collective-permute-start(bf16[352,256]{1,0:T(8,128)(2,1)S(1)} %get-tuple-element.64), channel_id=1, source_target_pairs={{0,24},{8,0},{16,8},{24,16},{1,25},{9,1},{17,9},{25,17},{2,26},{10... | collective-permute-start | bytes 540680 | tf_op jit(solution)/shard_map/ppermute | solution.py:464
  147.9 23.7 %all-to-all-start.2 = ((bf16[8,128,256]{2,1,0:T(8,128)(2,1)}), bf16[8,128,256]{2,1,0:T(8,128)(2,1)S(1)}, u32[]{:S(2)}, u32[]{:S(2)}) async-start(bf16[8,128,256]{2,1,0:T(8,128)(2,1)} %shard_map.128), calls=%async_computation.2 | async-start | bytes 1048576 | tf_op jit(solution)/shard_map/all_to_all | solution.py:593
  162.7 10.2 %collective-permute-start.3 = (bf16[2,64,128]{2,1,0:T(8,128)(2,1)S(1)}, bf16[2,64,128]{2,1,0:T(8,128)(2,1)S(1)}, u32[]{:S(2)}, u32[]{:S(2)}) collective-permute-start(bf16[2,64,128]{2,1,0:T(8,128)(2,1)S(1)} %get-tuple-element.42), channel_id=1, source_target_pairs={{0,1},{1,2},{2,3},{3,0},{4,5},{5,6},{6,7},{7,4},{8,9},{9,10},{10,1... | collective-permute-start | bytes 98312 | tf_op jit(solution)/shard_map/ppermute | solution.py:464
  163.9 9.0 %collective-permute-start.4 = (bf16[2,64,128]{2,1,0:T(8,128)(2,1)S(1)}, bf16[2,64,128]{2,1,0:T(8,128)(2,1)S(1)}, u32[]{:S(2)}, u32[]{:S(2)}) collective-permute-start(bf16[2,64,128]{2,1,0:T(8,128)(2,1)S(1)} %get-tuple-element.43), channel_id=1, source_target_pairs={{0,2},{1,3},{2,0},{3,1},{4,6},{5,7},{6,4},{7,5},{8,10},{9,11},{10,... | collective-permute-start | bytes 98312 | tf_op jit(solution)/shard_map/ppermute | solution.py:464
  166.3 6.7 %collective-permute-start.5 = (bf16[2,64,128]{2,1,0:T(8,128)(2,1)S(1)}, bf16[2,64,128]{2,1,0:T(8,128)(2,1)S(1)}, u32[]{:S(2)}, u32[]{:S(2)}) collective-permute-start(bf16[2,64,128]{2,1,0:T(8,128)(2,1)S(1)} %get-tuple-element.44), channel_id=1, source_target_pairs={{0,3},{1,0},{2,1},{3,2},{4,7},{5,4},{6,5},{7,6},{8,11},{9,8},{10,9... | collective-permute-start | bytes 98312 | tf_op jit(solution)/shard_map/ppermute | solution.py:464
Sparse Core Ops, SparseCore 0:
  9.8 56.3 all-gather.1

commit v6 on v5

--- a/solution.py
+++ b/solution.py
@@ -298,7 +298,7 @@
 def coef_body(rel_ref, s0, s1, s2, s3, out_ref):
     own, slots = s0.shape
     width = out_ref.shape[1]
-    chunks = out_ref.shape[0] // (2 * own)
+    chunks = out_ref.shape[0] // own
     high, low = digits((s0[...] + s1[...]) + (s2[...] + s3[...]))
     both = jnp.concatenate([high.astype(F32), low.astype(F32)], axis=0).astype(BF)
     rel = rel_ref[...]
@@ -308,18 +308,7 @@
         hot = jnp.where(ids == rel, 1.0, 0.0).astype(BF)
         t = lax.dot_general(both, hot, NT, preferred_element_type=F32)
         parts.append(t[:own] + t[own:])
-    pack(out_ref, 0, jnp.concatenate(parts, axis=0))
-
-
-def pack(ref, at, value):
-    high, low = digits(value)
-    n = value.shape[0]
-    ref[pl.ds(at, n), :] = high
-    ref[pl.ds(at + n, n), :] = low
-
-
-def unpack(value, at, n):
-    return value[at : at + n].astype(F32) + value[at + n : at + 2 * n].astype(F32)
+    out_ref[...] = jnp.concatenate(parts, axis=0).astype(BF)
 
 
 def basis_body(own, rows, peers, y0, y1, y2, y3, keep_ref, send_ref, tmp, outf):
@@ -349,38 +338,36 @@
 def core_body(keep_ref, got_ref, coef_ref, other_ref, o0, o1, o2, o3, sums):
     part = keep_ref.shape[0]
     each = part // NX
-    n = coef_ref.shape[0] // 2
     sums[...] = keep_ref[...].astype(F32) + got_ref[...].astype(F32)
-    coef = unpack(coef_ref[...], 0, n) + unpack(other_ref[...], 0, n)
+    coef = (coef_ref[...].astype(F32) + other_ref[...].astype(F32)).astype(BF)
     for r, out in enumerate((o0, o1, o2, o3)):
         out[pl.ds(0, each), :] = sums[aligned(turn(lax.axis_index("x"), r, NX), each), :].astype(BF)
-        pack(out, each, coef)
+        out[pl.ds(each, coef.shape[0]), :] = coef
 
 
 def x_body(i0, i1, i2, i3, out_ref, order):
     n = order.shape[1]
-    each = i0.shape[0] - 2 * n
+    each = i0.shape[0] - n
     nz = out_ref.shape[0]
     last = each // nz
     sums = sum(i[pl.ds(0, each), :].astype(F32) for i in (i0, i1, i2, i3))
     for r, i in enumerate((i0, i1, i2, i3)):
-        order[turn(lax.axis_index("x"), -r, NX)] = unpack(i[pl.ds(each, 2 * n), :], 0, n)
-    high, low = digits((order[0] + order[1]) + (order[2] + order[3]))
+        order[turn(lax.axis_index("x"), -r, NX)] = i[pl.ds(each, n), :].astype(F32)
+    coef = ((order[0] + order[1]) + (order[2] + order[3])).astype(BF)
     for z in range(nz):
         out_ref[z, pl.ds(0, last), :] = sums[z * last : (z + 1) * last].astype(BF)
-        out_ref[z, pl.ds(last, n), :] = high
-        out_ref[z, pl.ds(last + n, n), :] = low
+        out_ref[z, pl.ds(last, n), :] = coef
 
 
 def z_body(own, in_ref, basis_ref, coef_ref):
     nz, rows, width = in_ref.shape
     last = basis_ref.shape[0]
-    n = (rows - last) // 2
+    n = rows - last
     basis = jnp.zeros((last, width), F32)
     coef = jnp.zeros((n, width), F32)
     for z in range(nz):
         basis += in_ref[z, pl.ds(0, last), :].astype(F32)
-        coef += unpack(in_ref[z, pl.ds(last, 2 * n), :], 0, n)
+        coef += in_ref[z, pl.ds(last, n), :].astype(F32)
     basis_ref[...] = basis
     relations = coef_ref.shape[1]
     for j in range(n // own):
@@ -546,7 +533,7 @@
     )(pg, dst, cnt, incoming, rel_out, src, *coefs, far(table))
     scores = [scores[0]] + [over("basis", r, scores[r]) for r in range(1, groups)]
     lot = chunks * own
-    coef_part = call(coef_body, bf(2 * lot, width), [VM] * 5, limit=4)(rel_in, *scores)
+    coef_part = call(coef_body, bf(lot, width), [VM] * 5, limit=4)(rel_in, *scores)
 
     ys = lax.optimization_barrier((*ys, scores[1], scores[3]))[:groups]
     part = own * width // NC
@@ -561,7 +548,7 @@
     each = part // NX
     outs = call(
         core_body,
-        tuple(bf(each + 2 * lot, width) for _ in range(NX)),
+        tuple(bf(each + lot, width) for _ in range(NX)),
         [VM] * 4,
         [pltpu.VMEM((part, width), F32)],
         limit=8,
@@ -582,10 +569,11 @@
         limit=18,
     )(returned.reshape(peers * per, LANES), w_out, act, pg, self_weight, far(table))
 
+    ins = lax.optimization_barrier((*ins, grads[0]))[:NX]
     last = each // nz
     out = call(
         x_body,
-        bf(nz, last + 2 * lot, width),
+        bf(nz, last + lot, width),
         [VM] * NX,
         [pltpu.VMEM((NX, lot, width), F32)],
         limit=4,

time: 181 us -> 178 us (0.983)
  waiting for transfers between devices: 79.5 us -> 77.3 us
    ppermute x17, waiting for transfers between devices: 33 us -> 26 us  [over(): return lax.ppermute(value, axis, [(i, (i + r) % n) for i in range(n)])]
    all_to_all x1, waiting for transfers between devices: 0.01 us -> 2.98 us  [local(): lax.all_to_all(back, ENT, split_axis=0, concat_axis=0, tiled=True)]
    all_to_all x1, waiting for transfers between devices: 4.08 us -> 5.92 us  [local(): out = lax.all_to_all(out, 'z', split_axis=0, concat_axis=0, tiled=True)]
  transfers between devices with their start and end apart: 21 -> 21, of which waited for: 12 -> 13; matrix products, arithmetic and copies ran while one was open for 0% -> 0% of each run, Pallas kernels for 12% -> 12%
where the time goes in v6:
time: 178 us
  waiting for transfers between devices  77.3 us (43%)
  starting transfers between devices  52.1 us (29%)
  Pallas kernels  33.4 us (19%)
  between operations  14.2 us (8%)
    all_to_all x1, waiting for transfers between devices, local(): lax.all_to_all(outgoing, ENT, split_axis=0, concat_axis=0, tiled=True)  42.4 us
    ppermute x17, starting transfers between devices, over(): return lax.ppermute(value, axis, [(i, (i + r) % n) for i in range(n)])  26.4 us
    ppermute x17, waiting for transfers between devices, over(): return lax.ppermute(value, axis, [(i, (i + r) % n) for i in range(n)])  26 us
    all_to_all x1, starting transfers between devices, local(): lax.all_to_all(outgoing, ENT, split_axis=0, concat_axis=0, tiled=True)  13.1 us
    pallas_call x1, Pallas kernels, local(): call(functools.partial(bwd_body, cap, own), tuple((bf(2, width // groups,...  9.01 us
    pallas_call x1, Pallas kernels, local(): call(functools.partial(fwd_body, cap, nblk, own), (*[hbm((own + 1) * rows...  8.54 us
    all_to_all x1, starting transfers between devices, local(): lax.all_to_all(back, ENT, split_axis=0, concat_axis=0, tiled=True)  7.43 us
    pallas_call x1, Pallas kernels, local(): call(functools.partial(score_body, cap, nblk, own, halves), (*[jax.ShapeD...  6.93 us
  transfers between devices with their start and end apart: 21, of which 13 were waited for; matrix products, arithmetic and copies ran while one was open for 0% of the time, Pallas kernels for 12%

profile of v6, /device:TPU:1, one launch (start us, length us, event | category | flops | bytes accessed | tf_op | source)
XLA Modules:
  0.0 177.8 jit_solution(17054894726676818761)
XLA Ops:
  7.2 2.4 %shard_map.120 = bf16[64,136,128]{2,1,0:T(8,128)(2,1)} custom-call(s32[2,64]{1,0:T(2,128)} %bitcast.35, s32[2,64]{1,0:T(2,128)} %bitcast.37, bf16[512,256]{1,0:T(8,128)(2,1)} %ent_ref.3), custom_call_target="tpu_custom_call" | custom-call | tf_op jit(solution)/shard_map/pallas_call | solution.py:457
  9.7 13.1 %all-to-all-start = ((bf16[64,136,128]{2,1,0:T(8,128)(2,1)}), bf16[64,136,128]{2,1,0:T(8,128)(2,1)S(1)}, u32[]{:S(2)}, u32[]{:S(2)}) async-start(bf16[64,136,128]{2,1,0:T(8,128)(2,1)} %shard_map.120), calls=%async_computation | async-start | bytes 4456448 | tf_op jit(solution)/shard_map/all_to_all | solution.py:472
  23.0 2.8 %collective-permute-start.2 = (bf16[96,256]{1,0:T(8,128)(2,1)S(1)}, bf16[96,256]{1,0:T(8,128)(2,1)S(1)}, u32[]{:S(2)}, u32[]{:S(2)}) collective-permute-start(bf16[96,256]{1,0:T(8,128)(2,1)S(1)} %bitcast.24), channel_id=1, source_target_pairs={{0,3},{1,0},{2,1},{3,2},{4,7},{5,4},{6,5},{7,6},{8,11},{9,8},{10,9... | collective-permute-start | bytes 147464 | tf_op jit(solution)/shard_map/ppermute | solution.py:451
  27.0 3.4 %collective-permute-done.1.c2 = bf16[96,256]{1,0:T(8,128)(2,1)S(1)} collective-permute-done((bf16[96,256]{1,0:T(8,128)(2,1)S(1)}, bf16[96,256]{1,0:T(8,128)(2,1)S(1)}, u32[]{:S(2)}, u32[]{:S(2)}) %collective-permute-start.1) | collective-permute-done | bytes 49184 | tf_op jit(solution)/shard_map/ppermute | solution.py:451
  30.4 2.5 %collective-permute-done.c1 = bf16[96,256]{1,0:T(8,128)(2,1)S(1)} collective-permute-done((bf16[96,256]{1,0:T(8,128)(2,1)S(1)}, bf16[96,256]{1,0:T(8,128)(2,1)S(1)}, u32[]{:S(2)}, u32[]{:S(2)}) %collective-permute-start) | collective-permute-done | bytes 49184 | tf_op jit(solution)/shard_map/ppermute | solution.py:451
  32.9 42.4 %all-to-all-done = bf16[64,136,128]{2,1,0:T(8,128)(2,1)S(1)} async-done(((bf16[64,136,128]{2,1,0:T(8,128)(2,1)}), bf16[64,136,128]{2,1,0:T(8,128)(2,1)S(1)}, u32[]{:S(2)}, u32[]{:S(2)}) %all-to-all-start) | async-done | bytes 2228256 | tf_op jit(solution)/shard_map/all_to_all | solution.py:472
  75.3 8.5 %shard_map.121 = (bf16[1152,256]{1,0:T(8,128)(2,1)}, bf16[1152,256]{1,0:T(8,128)(2,1)}, bf16[1152,256]{1,0:T(8,128)(2,1)}, bf16[1152,256]{1,0:T(8,128)(2,1)}, bf...) custom-call(s32[2,64]{1,0:T(2,128)S(1)} %bitcast.29, ...), custom_call_target="tpu_custom_call" | custom-call | tf_op jit(solution)/shard_map/pallas_call | solution.py:482
  83.9 7.4 %all-to-all-start.1 = ((bf16[64,128,128]{2,1,0:T(8,128)(2,1)}), bf16[64,128,128]{2,1,0:T(8,128)(2,1)}, u32[]{:S(2)}, u32[]{:S(2)}) async-start(bf16[64,128,128]{2,1,0:T(8,128)(2,1)} %get-tuple-element.41), calls=%async_computation.1 | async-start | bytes 4194304 | tf_op jit(solution)/shard_map/all_to_all | solution.py:516
  91.3 1.4 collective-permute-start.6
  92.7 2.6 %collective-permute-start.7 = (bf16[1152,256]{1,0:T(8,128)(2,1)}, bf16[1152,256]{1,0:T(8,128)(2,1)S(1)}, u32[]{:S(2)}, u32[]{:S(2)}) collective-permute-start(bf16[1152,256]{1,0:T(8,128)(2,1)} %get-tuple-element.52), channel_id=1, source_target_pairs={{0,2},{1,3},{2,0},{3,1},{4,6},{5,7},{6,4},{7,5},{8,10},{9,11},{10,... | collective-permute-start | bytes 1769480 | tf_op jit(solution)/shard_map/ppermute | solution.py:451
  95.3 1.1 collective-permute-start.8
  96.4 6.9 %shard_map.122 = (f32[8,128]{1,0:T(8,128)S(1)}, f32[8,128]{1,0:T(8,128)S(1)}, f32[8,128]{1,0:T(8,128)S(1)}, f32[8,128]{1,0:T(8,128)S(1)}, bf16[128,128]{1,0:T(8,128)(2,1)S(1)}) custom-call(bf16[128,256]{1,0:T(8,128)(2,1)S(1)} %get-tuple-element.42.pg_ref, s32[2,64]{1,0:T(2,128)S(1)} %bitcast.31, s32[2,64]{1,0:T(2,128)S(1)} %bitcast.34, ...), custom_call_target="tpu_custom_call" | custom-call | flops 8000000000 | bytes 20000000 | tf_op jit(solution)/shard_map/pallas_call | solution.py:519
  103.8 2.3 %collective-permute-start.10 = (f32[8,128]{1,0:T(8,128)S(1)}, f32[8,128]{1,0:T(8,128)S(1)}, u32[]{:S(2)}, u32[]{:S(2)}) collective-permute-start(f32[8,128]{1,0:T(8,128)S(1)} %get-tuple-element.55), channel_id=1, source_target_pairs={{0,3},{1,0},{2,1},{3,2},{4,7},{5,4},{6,5},{7,6},{8,11},{9,8},{10,9... | collective-permute-start | bytes 12296 | tf_op jit(solution)/shard_map/ppermute | solution.py:451
  106.1 11.8 %collective-permute-done.9.s1 = f32[8,128]{1,0:T(8,128)S(1)} collective-permute-done((f32[8,128]{1,0:T(8,128)S(1)}, f32[8,128]{1,0:T(8,128)S(1)}, u32[]{:S(2)}, u32[]{:S(2)}) %collective-permute-start.9) | collective-permute-done | bytes 4128 | tf_op jit(solution)/shard_map/ppermute | solution.py:451
  117.8 2.8 %collective-permute-done.10.s3 = f32[8,128]{1,0:T(8,128)S(1)} collective-permute-done((f32[8,128]{1,0:T(8,128)S(1)}, f32[8,128]{1,0:T(8,128)S(1)}, u32[]{:S(2)}, u32[]{:S(2)}) %collective-permute-start.10) | collective-permute-done | bytes 4128 | tf_op jit(solution)/shard_map/ppermute | solution.py:451
  121.2 3.7 %shard_map.125 = (bf16[1024,256]{1,0:T(8,128)(2,1)S(1)}, bf16[1024,256]{1,0:T(8,128)(2,1)S(1)}) custom-call(bf16[1152,256]{1,0:T(8,128)(2,1)S(1)} %copy-done, bf16[1152,256]{1,0:T(8,128)(2,1)S(1)} %collective-permute-done.6.y1, bf16[1152,256]{1,0:T(8,128)(2,1)S(1)} %collective-permute-done.7.y2, bf16[1152,256]{1,0:T(8,128)(2,1)S(1)} %collective-permute-done.8.y3), custom_call_target="tpu_custom_call" | custom-call | tf_op jit(solution)/shard_map/pallas_call | solution.py:540
  124.9 1.4 collective-permute-start.11
  126.3 2.4 %collective-permute-start.12 = (f32[8,128]{1,0:T(8,128)S(1)}, f32[8,128]{1,0:T(8,128)S(1)}, u32[]{:S(2)}, u32[]{:S(2)}) collective-permute-start(f32[8,128]{1,0:T(8,128)S(1)} %get-tuple-element.64), channel_id=1, source_target_pairs={{0,2},{1,3},{2,0},{3,1},{4,6},{5,7},{6,4},{7,5},{8,10},{9,11},{10,... | collective-permute-start | bytes 12296 | tf_op jit(solution)/shard_map/ppermute | solution.py:451
  128.7 2.0 %collective-permute-done.12.s2 = f32[8,128]{1,0:T(8,128)S(1)} collective-permute-done((f32[8,128]{1,0:T(8,128)S(1)}, f32[8,128]{1,0:T(8,128)S(1)}, u32[]{:S(2)}, u32[]{:S(2)}) %collective-permute-start.12) | collective-permute-done | bytes 4128 | tf_op jit(solution)/shard_map/ppermute | solution.py:451
  130.9 0.9 collective-permute-start.13
  132.9 1.5 collective-permute-start.14
  134.3 2.4 %collective-permute-start.15 = (bf16[304,256]{1,0:T(8,128)(2,1)S(1)}, bf16[304,256]{1,0:T(8,128)(2,1)S(1)}, u32[]{:S(2)}, u32[]{:S(2)}) collective-permute-start(bf16[304,256]{1,0:T(8,128)(2,1)S(1)} %get-tuple-element.67), channel_id=1, source_target_pairs={{0,16},{8,24},{16,0},{24,8},{1,17},{9,25},{17,1},{25,9},{2,18},{10... | collective-permute-start | bytes 466952 | tf_op jit(solution)/shard_map/ppermute | solution.py:451
  136.7 1.2 collective-permute-start.16
  137.9 3.0 %all-to-all-done.1 = bf16[64,128,128]{2,1,0:T(8,128)(2,1)} async-done(((bf16[64,128,128]{2,1,0:T(8,128)(2,1)}), bf16[64,128,128]{2,1,0:T(8,128)(2,1)}, u32[]{:S(2)}, u32[]{:S(2)}) %all-to-all-start.1) | async-done | bytes 2097184 | tf_op jit(solution)/shard_map/all_to_all | solution.py:516
  140.9 9.0 %shard_map.123 = (bf16[2,64,128]{2,1,0:T(8,128)(2,1)S(1)}, bf16[2,64,128]{2,1,0:T(8,128)(2,1)S(1)}, bf16[2,64,128]{2,1,0:T(8,128)(2,1)S(1)}, bf16[2,64,128]{2,1,0:T(8,128)(2,1)S(1)}) custom-call(bf16[8192,128]{1,0:T(8,128)(2,1)} %bitcast.13.x_ref, bf16[128,128]{1,0:T(8,128)(2,1)S(1)} %get-tuple-element.43.w_ref, ...), custom_call_target="tpu_custom_call" | custom-call | tf_op jit(solution)/shard_map/pallas_call | solution.py:558
  150.0 0.9 shard_map.128
  150.8 5.1 %all-to-all-start.2 = ((bf16[8,80,256]{2,1,0:T(8,128)(2,1)}), bf16[8,80,256]{2,1,0:T(8,128)(2,1)S(1)}, u32[]{:S(2)}, u32[]{:S(2)}) async-start(bf16[8,80,256]{2,1,0:T(8,128)(2,1)} %shard_map.128), calls=%async_computation.2 | async-start | bytes 655360 | tf_op jit(solution)/shard_map/all_to_all | solution.py:581
  155.9 1.3 collective-permute-start.3
  157.2 2.6 %collective-permute-start.4 = (bf16[2,64,128]{2,1,0:T(8,128)(2,1)S(1)}, bf16[2,64,128]{2,1,0:T(8,128)(2,1)S(1)}, u32[]{:S(2)}, u32[]{:S(2)}) collective-permute-start(bf16[2,64,128]{2,1,0:T(8,128)(2,1)S(1)} %get-tuple-element.47), channel_id=1, source_target_pairs={{0,2},{1,3},{2,0},{3,1},{4,6},{5,7},{6,4},{7,5},{8,10},{9,11},{10,... | collective-permute-start | bytes 98312 | tf_op jit(solution)/shard_map/ppermute | solution.py:451
  159.9 1.1 collective-permute-start.5
  161.5 1.4 collective-permute-done.5.i3
  163.8 5.9 %all-to-all-done.2.in_ref = bf16[8,80,256]{2,1,0:T(8,128)(2,1)S(1)} async-done(((bf16[8,80,256]{2,1,0:T(8,128)(2,1)}), bf16[8,80,256]{2,1,0:T(8,128)(2,1)S(1)}, u32[]{:S(2)}, u32[]{:S(2)}) %all-to-all-start.2) | async-done | bytes 327712 | tf_op jit(solution)/shard_map/all_to_all | solution.py:581
  (42 shorter events, 6.4 us)
Async XLA Ops:
  7.2 68.1 %all-gather.2.cloned.1.call-start = ((), (), s32[]{:S(2)}) async-start(), calls=%async_computation.3 | async-start | bytes 5242880 | tf_op jit(solution)/shard_map/all_gather | solution.py:475
  9.7 13.2 %copy-start.6 = (f32[1315,8]{0,1:T(8,128)S(1)}, f32[1315,8]{0,1:T(8,128)}, u32[]{:S(2)}) copy-start(f32[1315,8]{0,1:T(8,128)} %param.12) | copy-start | bytes 126244
  9.7 65.6 %copy-start.1 = (bf16[256,256]{1,0:T(8,128)(2,1)S(1)}, bf16[256,256]{1,0:T(8,128)(2,1)}, u32[]{:S(2)}) copy-start(bf16[256,256]{1,0:T(8,128)(2,1)} %sw_ref.3) | copy-start | bytes 393220
  9.7 65.6 %copy-start.2 = (s32[64,1,2]{0,2,1:T(2,128)S(1)}, s32[64,1,2]{0,2,1:T(2,128)}, u32[]{:S(2)}) copy-start(s32[64,1,2]{0,2,1:T(2,128)} %param.15) | copy-start | bytes 1540
  9.7 65.6 %copy-start.3 = (s32[64,1,2]{0,2,1:T(2,128)S(1)}, s32[64,1,2]{0,2,1:T(2,128)}, u32[]{:S(2)}) copy-start(s32[64,1,2]{0,2,1:T(2,128)} %param.16) | copy-start | bytes 1540
  9.7 65.5 %all-to-all-start = ((bf16[64,136,128]{2,1,0:T(8,128)(2,1)}), bf16[64,136,128]{2,1,0:T(8,128)(2,1)S(1)}, u32[]{:S(2)}, u32[]{:S(2)}) async-start(bf16[64,136,128]{2,1,0:T(8,128)(2,1)} %shard_map.120), calls=%async_computation | async-start | bytes 4456448 | tf_op jit(solution)/shard_map/all_to_all | solution.py:472
  23.0 4.0 %collective-permute-start.2 = (bf16[96,256]{1,0:T(8,128)(2,1)S(1)}, bf16[96,256]{1,0:T(8,128)(2,1)S(1)}, u32[]{:S(2)}, u32[]{:S(2)}) collective-permute-start(bf16[96,256]{1,0:T(8,128)(2,1)S(1)} %bitcast.24), channel_id=1, source_target_pairs={{0,3},{1,0},{2,1},{3,2},{4,7},{5,4},{6,5},{7,6},{8,11},{9,8},{10,9... | collective-permute-start | bytes 147464 | tf_op jit(solution)/shard_map/ppermute | solution.py:451
  25.8 4.6 %collective-permute-start.1 = (bf16[96,256]{1,0:T(8,128)(2,1)S(1)}, bf16[96,256]{1,0:T(8,128)(2,1)S(1)}, u32[]{:S(2)}, u32[]{:S(2)}) collective-permute-start(bf16[96,256]{1,0:T(8,128)(2,1)S(1)} %bitcast.25), channel_id=1, source_target_pairs={{0,2},{1,3},{2,0},{3,1},{4,6},{5,7},{6,4},{7,5},{8,10},{9,11},{10,... | collective-permute-start | bytes 147464 | tf_op jit(solution)/shard_map/ppermute | solution.py:451
  26.2 6.7 %collective-permute-start = (bf16[96,256]{1,0:T(8,128)(2,1)S(1)}, bf16[96,256]{1,0:T(8,128)(2,1)S(1)}, u32[]{:S(2)}, u32[]{:S(2)}) collective-permute-start(bf16[96,256]{1,0:T(8,128)(2,1)S(1)} %bitcast.26), channel_id=1, source_target_pairs={{0,1},{1,2},{2,3},{3,0},{4,5},{5,6},{6,7},{7,4},{8,9},{9,10},{10,1... | collective-permute-start | bytes 147464 | tf_op jit(solution)/shard_map/ppermute | solution.py:451
  83.8 11.5 %copy-start.7 = (bf16[1152,256]{1,0:T(8,128)(2,1)S(1)}, bf16[1152,256]{1,0:T(8,128)(2,1)}, u32[]{:S(2)}) copy-start(bf16[1152,256]{1,0:T(8,128)(2,1)} %get-tuple-element.53) | copy-start | bytes 1769476
  83.8 12.5 %copy-start.4 = (s32[1,64,2]{1,2,0:T(2,128)S(1)}, s32[1,64,2]{1,2,0:T(2,128)}, u32[]{:S(2)}) copy-start(s32[1,64,2]{1,2,0:T(2,128)} %param.13) | copy-start | bytes 1540
  83.9 12.5 %copy-start.5 = (s32[1,64,2]{1,2,0:T(2,128)S(1)}, s32[1,64,2]{1,2,0:T(2,128)}, u32[]{:S(2)}) copy-start(s32[1,64,2]{1,2,0:T(2,128)} %param.14) | copy-start | bytes 1540
  83.9 57.0 %all-to-all-start.1 = ((bf16[64,128,128]{2,1,0:T(8,128)(2,1)}), bf16[64,128,128]{2,1,0:T(8,128)(2,1)}, u32[]{:S(2)}, u32[]{:S(2)}) async-start(bf16[64,128,128]{2,1,0:T(8,128)(2,1)} %get-tuple-element.41), calls=%async_computation.1 | async-start | bytes 4194304 | tf_op jit(solution)/shard_map/all_to_all | solution.py:516
  91.3 29.3 %collective-permute-start.6 = (bf16[1152,256]{1,0:T(8,128)(2,1)}, bf16[1152,256]{1,0:T(8,128)(2,1)S(1)}, u32[]{:S(2)}, u32[]{:S(2)}) collective-permute-start(bf16[1152,256]{1,0:T(8,128)(2,1)} %get-tuple-element.51), channel_id=1, source_target_pairs={{0,1},{1,2},{2,3},{3,0},{4,5},{5,6},{6,7},{7,4},{8,9},{9,10},{10,1... | collective-permute-start | bytes 1769480 | tf_op jit(solution)/shard_map/ppermute | solution.py:451
  92.7 28.5 %collective-permute-start.7 = (bf16[1152,256]{1,0:T(8,128)(2,1)}, bf16[1152,256]{1,0:T(8,128)(2,1)S(1)}, u32[]{:S(2)}, u32[]{:S(2)}) collective-permute-start(bf16[1152,256]{1,0:T(8,128)(2,1)} %get-tuple-element.52), channel_id=1, source_target_pairs={{0,2},{1,3},{2,0},{3,1},{4,6},{5,7},{6,4},{7,5},{8,10},{9,11},{10,... | collective-permute-start | bytes 1769480 | tf_op jit(solution)/shard_map/ppermute | solution.py:451
  95.3 25.9 %collective-permute-start.8 = (bf16[1152,256]{1,0:T(8,128)(2,1)S(1)}, bf16[1152,256]{1,0:T(8,128)(2,1)S(1)}, u32[]{:S(2)}, u32[]{:S(2)}) collective-permute-start(bf16[1152,256]{1,0:T(8,128)(2,1)S(1)} %copy-done.7), channel_id=1, source_target_pairs={{0,3},{1,0},{2,1},{3,2},{4,7},{5,4},{6,5},{7,6},{8,11},{9,8},{10,9... | collective-permute-start | bytes 1769480 | tf_op jit(solution)/shard_map/ppermute | solution.py:451
  96.4 24.8 %copy-start = (bf16[1152,256]{1,0:T(8,128)(2,1)S(1)}, bf16[1152,256]{1,0:T(8,128)(2,1)}, u32[]{:S(2)}) copy-start(bf16[1152,256]{1,0:T(8,128)(2,1)} %get-tuple-element.56.y0) | copy-start | bytes 1769476
  103.3 14.5 %collective-permute-start.9 = (f32[8,128]{1,0:T(8,128)S(1)}, f32[8,128]{1,0:T(8,128)S(1)}, u32[]{:S(2)}, u32[]{:S(2)}) collective-permute-start(f32[8,128]{1,0:T(8,128)S(1)} %get-tuple-element.54), channel_id=1, source_target_pairs={{0,1},{1,2},{2,3},{3,0},{4,5},{5,6},{6,7},{7,4},{8,9},{9,10},{10,1... | collective-permute-start | bytes 12296 | tf_op jit(solution)/shard_map/ppermute | solution.py:451
  103.8 16.9 %collective-permute-start.10 = (f32[8,128]{1,0:T(8,128)S(1)}, f32[8,128]{1,0:T(8,128)S(1)}, u32[]{:S(2)}, u32[]{:S(2)}) collective-permute-start(f32[8,128]{1,0:T(8,128)S(1)} %get-tuple-element.55), channel_id=1, source_target_pairs={{0,3},{1,0},{2,1},{3,2},{4,7},{5,4},{6,5},{7,6},{8,11},{9,8},{10,9... | collective-permute-start | bytes 12296 | tf_op jit(solution)/shard_map/ppermute | solution.py:451
  124.9 7.8 %collective-permute-start.11 = (bf16[1024,256]{1,0:T(8,128)(2,1)S(1)}, bf16[1024,256]{1,0:T(8,128)(2,1)S(1)}, u32[]{:S(2)}, u32[]{:S(2)}) collective-permute-start(bf16[1024,256]{1,0:T(8,128)(2,1)S(1)} %get-tuple-element.61), channel_id=1, source_target_pairs={{0,4},{4,0},{1,5},{5,1},{2,6},{6,2},{3,7},{7,3},{8,12},{12,8},{9,1... | collective-permute-start | bytes 1572872 | tf_op jit(solution)/shard_map/ppermute | solution.py:451
  126.3 4.4 %collective-permute-start.12 = (f32[8,128]{1,0:T(8,128)S(1)}, f32[8,128]{1,0:T(8,128)S(1)}, u32[]{:S(2)}, u32[]{:S(2)}) collective-permute-start(f32[8,128]{1,0:T(8,128)S(1)} %get-tuple-element.64), channel_id=1, source_target_pairs={{0,2},{1,3},{2,0},{3,1},{4,6},{5,7},{6,4},{7,5},{8,10},{9,11},{10,... | collective-permute-start | bytes 12296 | tf_op jit(solution)/shard_map/ppermute | solution.py:451
  130.9 1.8 collective-permute-start.13
  132.9 17.0 %collective-permute-start.14 = (bf16[304,256]{1,0:T(8,128)(2,1)S(1)}, bf16[304,256]{1,0:T(8,128)(2,1)S(1)}, u32[]{:S(2)}, u32[]{:S(2)}) collective-permute-start(bf16[304,256]{1,0:T(8,128)(2,1)S(1)} %get-tuple-element.66), channel_id=1, source_target_pairs={{0,8},{8,16},{16,24},{24,0},{1,9},{9,17},{17,25},{25,1},{2,10},{10... | collective-permute-start | bytes 466952 | tf_op jit(solution)/shard_map/ppermute | solution.py:451
  134.3 15.6 %collective-permute-start.15 = (bf16[304,256]{1,0:T(8,128)(2,1)S(1)}, bf16[304,256]{1,0:T(8,128)(2,1)S(1)}, u32[]{:S(2)}, u32[]{:S(2)}) collective-permute-start(bf16[304,256]{1,0:T(8,128)(2,1)S(1)} %get-tuple-element.67), channel_id=1, source_target_pairs={{0,16},{8,24},{16,0},{24,8},{1,17},{9,25},{17,1},{25,9},{2,18},{10... | collective-permute-start | bytes 466952 | tf_op jit(solution)/shard_map/ppermute | solution.py:451
  136.7 13.2 %collective-permute-start.16 = (bf16[304,256]{1,0:T(8,128)(2,1)S(1)}, bf16[304,256]{1,0:T(8,128)(2,1)S(1)}, u32[]{:S(2)}, u32[]{:S(2)}) collective-permute-start(bf16[304,256]{1,0:T(8,128)(2,1)S(1)} %get-tuple-element.68), channel_id=1, source_target_pairs={{0,24},{8,0},{16,8},{24,16},{1,25},{9,1},{17,9},{25,17},{2,26},{10... | collective-permute-start | bytes 466952 | tf_op jit(solution)/shard_map/ppermute | solution.py:451
  150.8 18.9 %all-to-all-start.2 = ((bf16[8,80,256]{2,1,0:T(8,128)(2,1)}), bf16[8,80,256]{2,1,0:T(8,128)(2,1)S(1)}, u32[]{:S(2)}, u32[]{:S(2)}) async-start(bf16[8,80,256]{2,1,0:T(8,128)(2,1)} %shard_map.128), calls=%async_computation.2 | async-start | bytes 655360 | tf_op jit(solution)/shard_map/all_to_all | solution.py:581
  155.9 5.0 %collective-permute-start.3 = (bf16[2,64,128]{2,1,0:T(8,128)(2,1)S(1)}, bf16[2,64,128]{2,1,0:T(8,128)(2,1)S(1)}, u32[]{:S(2)}, u32[]{:S(2)}) collective-permute-start(bf16[2,64,128]{2,1,0:T(8,128)(2,1)S(1)} %get-tuple-element.46), channel_id=1, source_target_pairs={{0,1},{1,2},{2,3},{3,0},{4,5},{5,6},{6,7},{7,4},{8,9},{9,10},{10,1... | collective-permute-start | bytes 98312 | tf_op jit(solution)/shard_map/ppermute | solution.py:451
  157.2 4.3 %collective-permute-start.4 = (bf16[2,64,128]{2,1,0:T(8,128)(2,1)S(1)}, bf16[2,64,128]{2,1,0:T(8,128)(2,1)S(1)}, u32[]{:S(2)}, u32[]{:S(2)}) collective-permute-start(bf16[2,64,128]{2,1,0:T(8,128)(2,1)S(1)} %get-tuple-element.47), channel_id=1, source_target_pairs={{0,2},{1,3},{2,0},{3,1},{4,6},{5,7},{6,4},{7,5},{8,10},{9,11},{10,... | collective-permute-start | bytes 98312 | tf_op jit(solution)/shard_map/ppermute | solution.py:451
  159.9 3.1 %collective-permute-start.5 = (bf16[2,64,128]{2,1,0:T(8,128)(2,1)S(1)}, bf16[2,64,128]{2,1,0:T(8,128)(2,1)S(1)}, u32[]{:S(2)}, u32[]{:S(2)}) collective-permute-start(bf16[2,64,128]{2,1,0:T(8,128)(2,1)S(1)} %get-tuple-element.48), channel_id=1, source_target_pairs={{0,3},{1,0},{2,1},{3,2},{4,7},{5,4},{6,5},{7,6},{8,11},{9,8},{10,9... | collective-permute-start | bytes 98312 | tf_op jit(solution)/shard_map/ppermute | solution.py:451
Sparse Core Ops, SparseCore 0:
  9.8 56.3 all-gather.1

commit v7 on v6

--- a/solution.py
+++ b/solution.py
@@ -361,14 +361,16 @@
 
 def z_body(own, in_ref, basis_ref, coef_ref):
     nz, rows, width = in_ref.shape
-    last = basis_ref.shape[0]
+    deep = basis_ref.shape[1]
+    last = own * deep
     n = rows - last
     basis = jnp.zeros((last, width), F32)
     coef = jnp.zeros((n, width), F32)
     for z in range(nz):
         basis += in_ref[z, pl.ds(0, last), :].astype(F32)
         coef += in_ref[z, pl.ds(last, n), :].astype(F32)
-    basis_ref[...] = basis
+    for b in range(own):
+        basis_ref[b] = basis[b * deep : (b + 1) * deep]
     relations = coef_ref.shape[1]
     for j in range(n // own):
         size = min(width, relations - j * width)
@@ -376,7 +378,7 @@
 
 
 def bwd_body(
-    cap, own, x_ref, w_ref, act_ref, pg_ref, sw_ref, table_ref, o0, o1, o2, o3, xf, mf, at_ref, tab, tsem
+    cap, own, w_ref, act_ref, pg_ref, sw_ref, x_ref, table_ref, o0, o1, o2, o3, xb, xf, mf, at_ref, tab, xsem, tsem
 ):
     groups = tab.shape[0]
     nbase = groups * own
@@ -386,9 +388,15 @@
     slots = w_ref.shape[1]
     peers = slots // cap
     nblk = w_ref.shape[0] // nbase
+    lots = xsem.shape[0]
+    lot = xb.shape[0] // lots
+    lots_at = [pl.ds(i * lot, lot) for i in range(lots)]
+    xcopies = start_all([pltpu.make_async_copy(x_ref.at[at], xb.at[at], xsem.at[i]) for i, at in enumerate(lots_at)])
     tcopies = start_all(table_copies(table_ref, tab, tsem))
-    widen(x_ref, xf)
     w = w_ref[...]
+    for copy, at in zip(xcopies, lots_at):
+        copy.wait()
+        widen(xb.at[at], xf.at[at])
 
     def one(k, c):
         xk = slot_rows(xf, peers, cap, halves, share, k).astype(BF)
@@ -558,16 +566,18 @@
     grads = call(
         functools.partial(bwd_body, cap, own),
         tuple(bf(2, width // groups, rows) for _ in range(groups)),
-        [VM] * 5 + [HB],
+        [VM] * 4 + [HB] * 2,
         [
+            pltpu.VMEM((peers * per, LANES), BF),
             pltpu.VMEM((peers * per, LANES), F32),
             rows_scratch(nbase * rows, width),
             pltpu.VMEM((width, rows), F32),
             tables,
+            dma((8,)),
             dma((groups,)),
         ],
         limit=18,
-    )(returned.reshape(peers * per, LANES), w_out, act, pg, self_weight, far(table))
+    )(w_out, act, pg, self_weight, far(returned.reshape(peers * per, LANES)), far(table))
 
     ins = lax.optimization_barrier((*ins, grads[0]))[:NX]
     last = each // nz
@@ -581,7 +591,7 @@
     out = lax.all_to_all(out, "z", split_axis=0, concat_axis=0, tiled=True)
     basis_grad, coef_grad = call(
         functools.partial(z_body, own),
-        (jax.ShapeDtypeStruct((last, width), F32), jax.ShapeDtypeStruct((own, relations), F32)),
+        (jax.ShapeDtypeStruct((own, width // peers, width), F32), jax.ShapeDtypeStruct((own, relations), F32)),
         [VM],
         limit=4,
     )(out)
@@ -595,7 +605,7 @@
         [pltpu.VMEM((groups, 2, cols, rows), F32)],
         limit=4,
     )(*grads)
-    return (activation.T, basis_grad.reshape(own, width // peers, width), coef_grad.T, entity_grad.T)
+    return (activation.T, basis_grad, coef_grad.T, entity_grad.T)
 
 
 def solution(mesh):

time: 178 us -> 178 us (level)
  no operation moved by 1% of the time
where the time goes in v7:
time: 178 us
  waiting for transfers between devices  77.3 us (43%)
  starting transfers between devices  52.1 us (29%)
  Pallas kernels  34 us (19%)
  between operations  14.2 us (8%)
    all_to_all x1, waiting for transfers between devices, local(): lax.all_to_all(outgoing, ENT, split_axis=0, concat_axis=0, tiled=True)  42.4 us
    ppermute x17, starting transfers between devices, over(): return lax.ppermute(value, axis, [(i, (i + r) % n) for i in range(n)])  26.4 us
    ppermute x17, waiting for transfers between devices, over(): return lax.ppermute(value, axis, [(i, (i + r) % n) for i in range(n)])  26 us
    all_to_all x1, starting transfers between devices, local(): lax.all_to_all(outgoing, ENT, split_axis=0, concat_axis=0, tiled=True)  13.1 us
    pallas_call x1, Pallas kernels, local(): call(functools.partial(bwd_body, cap, own), tuple((bf(2, width // groups,...  9.62 us
    pallas_call x1, Pallas kernels, local(): call(functools.partial(fwd_body, cap, nblk, own), (*[hbm((own + 1) * rows...  8.54 us
    all_to_all x1, starting transfers between devices, local(): lax.all_to_all(back, ENT, split_axis=0, concat_axis=0, tiled=True)  7.43 us
    pallas_call x1, Pallas kernels, local(): call(functools.partial(score_body, cap, nblk, own, halves), (*[jax.ShapeD...  6.93 us
  transfers between devices with their start and end apart: 21, of which 13 were waited for; matrix products, arithmetic and copies ran while one was open for 0% of the time, Pallas kernels for 12%

profile of v7, /device:TPU:1, one launch (start us, length us, event | category | flops | bytes accessed | tf_op | source)
XLA Modules:
  0.0 177.8 jit_solution(10691817075791048320)
XLA Ops:
  7.2 2.4 %shard_map.120 = bf16[64,136,128]{2,1,0:T(8,128)(2,1)} custom-call(s32[2,64]{1,0:T(2,128)} %bitcast.35, s32[2,64]{1,0:T(2,128)} %bitcast.37, bf16[512,256]{1,0:T(8,128)(2,1)} %ent_ref.3), custom_call_target="tpu_custom_call" | custom-call | tf_op jit(solution)/shard_map/pallas_call | solution.py:465
  9.7 13.1 %all-to-all-start = ((bf16[64,136,128]{2,1,0:T(8,128)(2,1)}), bf16[64,136,128]{2,1,0:T(8,128)(2,1)S(1)}, u32[]{:S(2)}, u32[]{:S(2)}) async-start(bf16[64,136,128]{2,1,0:T(8,128)(2,1)} %shard_map.120), calls=%async_computation | async-start | bytes 4456448 | tf_op jit(solution)/shard_map/all_to_all | solution.py:480
  23.0 2.8 %collective-permute-start.2 = (bf16[96,256]{1,0:T(8,128)(2,1)S(1)}, bf16[96,256]{1,0:T(8,128)(2,1)S(1)}, u32[]{:S(2)}, u32[]{:S(2)}) collective-permute-start(bf16[96,256]{1,0:T(8,128)(2,1)S(1)} %bitcast.24), channel_id=1, source_target_pairs={{0,3},{1,0},{2,1},{3,2},{4,7},{5,4},{6,5},{7,6},{8,11},{9,8},{10,9... | collective-permute-start | bytes 147464 | tf_op jit(solution)/shard_map/ppermute | solution.py:459
  27.0 3.4 %collective-permute-done.1.c2 = bf16[96,256]{1,0:T(8,128)(2,1)S(1)} collective-permute-done((bf16[96,256]{1,0:T(8,128)(2,1)S(1)}, bf16[96,256]{1,0:T(8,128)(2,1)S(1)}, u32[]{:S(2)}, u32[]{:S(2)}) %collective-permute-start.1) | collective-permute-done | bytes 49184 | tf_op jit(solution)/shard_map/ppermute | solution.py:459
  30.4 2.5 %collective-permute-done.c1 = bf16[96,256]{1,0:T(8,128)(2,1)S(1)} collective-permute-done((bf16[96,256]{1,0:T(8,128)(2,1)S(1)}, bf16[96,256]{1,0:T(8,128)(2,1)S(1)}, u32[]{:S(2)}, u32[]{:S(2)}) %collective-permute-start) | collective-permute-done | bytes 49184 | tf_op jit(solution)/shard_map/ppermute | solution.py:459
  32.9 42.4 %all-to-all-done = bf16[64,136,128]{2,1,0:T(8,128)(2,1)S(1)} async-done(((bf16[64,136,128]{2,1,0:T(8,128)(2,1)}), bf16[64,136,128]{2,1,0:T(8,128)(2,1)S(1)}, u32[]{:S(2)}, u32[]{:S(2)}) %all-to-all-start) | async-done | bytes 2228256 | tf_op jit(solution)/shard_map/all_to_all | solution.py:480
  75.3 8.5 %shard_map.121 = (bf16[1152,256]{1,0:T(8,128)(2,1)}, bf16[1152,256]{1,0:T(8,128)(2,1)}, bf16[1152,256]{1,0:T(8,128)(2,1)}, bf16[1152,256]{1,0:T(8,128)(2,1)}, bf...) custom-call(s32[2,64]{1,0:T(2,128)S(1)} %bitcast.29, ...), custom_call_target="tpu_custom_call" | custom-call | tf_op jit(solution)/shard_map/pallas_call | solution.py:490
  83.9 7.4 %all-to-all-start.1 = ((bf16[64,128,128]{2,1,0:T(8,128)(2,1)}), bf16[64,128,128]{2,1,0:T(8,128)(2,1)}, u32[]{:S(2)}, u32[]{:S(2)}) async-start(bf16[64,128,128]{2,1,0:T(8,128)(2,1)} %get-tuple-element.44), calls=%async_computation.1 | async-start | bytes 4194304 | tf_op jit(solution)/shard_map/all_to_all | solution.py:524
  91.3 1.4 collective-permute-start.6
  92.7 2.6 %collective-permute-start.7 = (bf16[1152,256]{1,0:T(8,128)(2,1)}, bf16[1152,256]{1,0:T(8,128)(2,1)S(1)}, u32[]{:S(2)}, u32[]{:S(2)}) collective-permute-start(bf16[1152,256]{1,0:T(8,128)(2,1)} %get-tuple-element.52), channel_id=1, source_target_pairs={{0,2},{1,3},{2,0},{3,1},{4,6},{5,7},{6,4},{7,5},{8,10},{9,11},{10,... | collective-permute-start | bytes 1769480 | tf_op jit(solution)/shard_map/ppermute | solution.py:459
  95.3 1.1 collective-permute-start.8
  96.4 6.9 %shard_map.122 = (f32[8,128]{1,0:T(8,128)S(1)}, f32[8,128]{1,0:T(8,128)S(1)}, f32[8,128]{1,0:T(8,128)S(1)}, f32[8,128]{1,0:T(8,128)S(1)}, bf16[128,128]{1,0:T(8,128)(2,1)S(1)}) custom-call(bf16[128,256]{1,0:T(8,128)(2,1)S(1)} %get-tuple-element.41.pg_ref, s32[2,64]{1,0:T(2,128)S(1)} %bitcast.31, s32[2,64]{1,0:T(2,128)S(1)} %bitcast.34, ...), custom_call_target="tpu_custom_call" | custom-call | flops 8000000000 | bytes 20000000 | tf_op jit(solution)/shard_map/pallas_call | solution.py:527
  103.8 2.3 %collective-permute-start.10 = (f32[8,128]{1,0:T(8,128)S(1)}, f32[8,128]{1,0:T(8,128)S(1)}, u32[]{:S(2)}, u32[]{:S(2)}) collective-permute-start(f32[8,128]{1,0:T(8,128)S(1)} %get-tuple-element.55), channel_id=1, source_target_pairs={{0,3},{1,0},{2,1},{3,2},{4,7},{5,4},{6,5},{7,6},{8,11},{9,8},{10,9... | collective-permute-start | bytes 12296 | tf_op jit(solution)/shard_map/ppermute | solution.py:459
  106.1 11.8 %collective-permute-done.9.s1 = f32[8,128]{1,0:T(8,128)S(1)} collective-permute-done((f32[8,128]{1,0:T(8,128)S(1)}, f32[8,128]{1,0:T(8,128)S(1)}, u32[]{:S(2)}, u32[]{:S(2)}) %collective-permute-start.9) | collective-permute-done | bytes 4128 | tf_op jit(solution)/shard_map/ppermute | solution.py:459
  117.8 2.8 %collective-permute-done.10.s3 = f32[8,128]{1,0:T(8,128)S(1)} collective-permute-done((f32[8,128]{1,0:T(8,128)S(1)}, f32[8,128]{1,0:T(8,128)S(1)}, u32[]{:S(2)}, u32[]{:S(2)}) %collective-permute-start.10) | collective-permute-done | bytes 4128 | tf_op jit(solution)/shard_map/ppermute | solution.py:459
  121.2 3.7 %shard_map.125 = (bf16[1024,256]{1,0:T(8,128)(2,1)S(1)}, bf16[1024,256]{1,0:T(8,128)(2,1)S(1)}) custom-call(bf16[1152,256]{1,0:T(8,128)(2,1)S(1)} %copy-done, bf16[1152,256]{1,0:T(8,128)(2,1)S(1)} %collective-permute-done.6.y1, bf16[1152,256]{1,0:T(8,128)(2,1)S(1)} %collective-permute-done.7.y2, bf16[1152,256]{1,0:T(8,128)(2,1)S(1)} %collective-permute-done.8.y3), custom_call_target="tpu_custom_call" | custom-call | tf_op jit(solution)/shard_map/pallas_call | solution.py:548
  124.9 1.4 collective-permute-start.11
  126.3 2.4 %collective-permute-start.12 = (f32[8,128]{1,0:T(8,128)S(1)}, f32[8,128]{1,0:T(8,128)S(1)}, u32[]{:S(2)}, u32[]{:S(2)}) collective-permute-start(f32[8,128]{1,0:T(8,128)S(1)} %get-tuple-element.64), channel_id=1, source_target_pairs={{0,2},{1,3},{2,0},{3,1},{4,6},{5,7},{6,4},{7,5},{8,10},{9,11},{10,... | collective-permute-start | bytes 12296 | tf_op jit(solution)/shard_map/ppermute | solution.py:459
  128.7 2.0 %collective-permute-done.12.s2 = f32[8,128]{1,0:T(8,128)S(1)} collective-permute-done((f32[8,128]{1,0:T(8,128)S(1)}, f32[8,128]{1,0:T(8,128)S(1)}, u32[]{:S(2)}, u32[]{:S(2)}) %collective-permute-start.12) | collective-permute-done | bytes 4128 | tf_op jit(solution)/shard_map/ppermute | solution.py:459
  130.9 0.9 collective-permute-start.13
  132.9 1.5 collective-permute-start.14
  134.3 2.4 %collective-permute-start.15 = (bf16[304,256]{1,0:T(8,128)(2,1)S(1)}, bf16[304,256]{1,0:T(8,128)(2,1)S(1)}, u32[]{:S(2)}, u32[]{:S(2)}) collective-permute-start(bf16[304,256]{1,0:T(8,128)(2,1)S(1)} %get-tuple-element.67), channel_id=1, source_target_pairs={{0,16},{8,24},{16,0},{24,8},{1,17},{9,25},{17,1},{25,9},{2,18},{10... | collective-permute-start | bytes 466952 | tf_op jit(solution)/shard_map/ppermute | solution.py:459
  136.7 1.2 collective-permute-start.16
  137.9 3.0 %all-to-all-done.1 = bf16[64,128,128]{2,1,0:T(8,128)(2,1)} async-done(((bf16[64,128,128]{2,1,0:T(8,128)(2,1)}), bf16[64,128,128]{2,1,0:T(8,128)(2,1)}, u32[]{:S(2)}, u32[]{:S(2)}) %all-to-all-start.1) | async-done | bytes 2097184 | tf_op jit(solution)/shard_map/all_to_all | solution.py:524
  140.9 9.6 %shard_map.123 = (bf16[2,64,128]{2,1,0:T(8,128)(2,1)S(1)}, bf16[2,64,128]{2,1,0:T(8,128)(2,1)S(1)}, bf16[2,64,128]{2,1,0:T(8,128)(2,1)S(1)}, bf16[2,64,128]{2,1,0:T(8,128)(2,1)S(1)}) custom-call(bf16[128,128]{1,0:T(8,128)(2,1)S(1)} %get-tuple-element.42.w_ref, bf16[4,64,128]{2,1,0:T(8,128)(2,1)S(1)} %get-tuple-element.43.act_ref, ...), custom_call_target="tpu_custom_call" | custom-call | tf_op jit(solution)/shard_map/pallas_call | solution.py:566
  150.6 0.9 shard_map.128
  151.4 5.1 %all-to-all-start.2 = ((bf16[8,80,256]{2,1,0:T(8,128)(2,1)}), bf16[8,80,256]{2,1,0:T(8,128)(2,1)S(1)}, u32[]{:S(2)}, u32[]{:S(2)}) async-start(bf16[8,80,256]{2,1,0:T(8,128)(2,1)} %shard_map.128), calls=%async_computation.2 | async-start | bytes 655360 | tf_op jit(solution)/shard_map/all_to_all | solution.py:591
  156.5 1.3 collective-permute-start.3
  157.8 2.6 %collective-permute-start.4 = (bf16[2,64,128]{2,1,0:T(8,128)(2,1)S(1)}, bf16[2,64,128]{2,1,0:T(8,128)(2,1)S(1)}, u32[]{:S(2)}, u32[]{:S(2)}) collective-permute-start(bf16[2,64,128]{2,1,0:T(8,128)(2,1)S(1)} %get-tuple-element.47), channel_id=1, source_target_pairs={{0,2},{1,3},{2,0},{3,1},{4,6},{5,7},{6,4},{7,5},{8,10},{9,11},{10,... | collective-permute-start | bytes 98312 | tf_op jit(solution)/shard_map/ppermute | solution.py:459
  160.5 1.1 collective-permute-start.5
  162.1 1.4 collective-permute-done.5.i3
  164.4 5.9 %all-to-all-done.2.in_ref = bf16[8,80,256]{2,1,0:T(8,128)(2,1)S(1)} async-done(((bf16[8,80,256]{2,1,0:T(8,128)(2,1)}), bf16[8,80,256]{2,1,0:T(8,128)(2,1)S(1)}, u32[]{:S(2)}, u32[]{:S(2)}) %all-to-all-start.2) | async-done | bytes 327712 | tf_op jit(solution)/shard_map/all_to_all | solution.py:591
  (41 shorter events, 5.7 us)
Async XLA Ops:
  7.2 68.1 %all-gather.2.cloned.1.call-start = ((), (), s32[]{:S(2)}) async-start(), calls=%async_computation.3 | async-start | bytes 5242880 | tf_op jit(solution)/shard_map/all_gather | solution.py:483
  9.7 13.2 %copy-start.6 = (f32[1315,8]{0,1:T(8,128)S(1)}, f32[1315,8]{0,1:T(8,128)}, u32[]{:S(2)}) copy-start(f32[1315,8]{0,1:T(8,128)} %param.12) | copy-start | bytes 126244
  9.7 65.6 %copy-start.1 = (bf16[256,256]{1,0:T(8,128)(2,1)S(1)}, bf16[256,256]{1,0:T(8,128)(2,1)}, u32[]{:S(2)}) copy-start(bf16[256,256]{1,0:T(8,128)(2,1)} %sw_ref.3) | copy-start | bytes 393220
  9.7 65.6 %copy-start.2 = (s32[64,1,2]{0,2,1:T(2,128)S(1)}, s32[64,1,2]{0,2,1:T(2,128)}, u32[]{:S(2)}) copy-start(s32[64,1,2]{0,2,1:T(2,128)} %param.15) | copy-start | bytes 1540
  9.7 65.6 %copy-start.3 = (s32[64,1,2]{0,2,1:T(2,128)S(1)}, s32[64,1,2]{0,2,1:T(2,128)}, u32[]{:S(2)}) copy-start(s32[64,1,2]{0,2,1:T(2,128)} %param.16) | copy-start | bytes 1540
  9.7 65.5 %all-to-all-start = ((bf16[64,136,128]{2,1,0:T(8,128)(2,1)}), bf16[64,136,128]{2,1,0:T(8,128)(2,1)S(1)}, u32[]{:S(2)}, u32[]{:S(2)}) async-start(bf16[64,136,128]{2,1,0:T(8,128)(2,1)} %shard_map.120), calls=%async_computation | async-start | bytes 4456448 | tf_op jit(solution)/shard_map/all_to_all | solution.py:480
  23.0 4.0 %collective-permute-start.2 = (bf16[96,256]{1,0:T(8,128)(2,1)S(1)}, bf16[96,256]{1,0:T(8,128)(2,1)S(1)}, u32[]{:S(2)}, u32[]{:S(2)}) collective-permute-start(bf16[96,256]{1,0:T(8,128)(2,1)S(1)} %bitcast.24), channel_id=1, source_target_pairs={{0,3},{1,0},{2,1},{3,2},{4,7},{5,4},{6,5},{7,6},{8,11},{9,8},{10,9... | collective-permute-start | bytes 147464 | tf_op jit(solution)/shard_map/ppermute | solution.py:459
  25.8 4.6 %collective-permute-start.1 = (bf16[96,256]{1,0:T(8,128)(2,1)S(1)}, bf16[96,256]{1,0:T(8,128)(2,1)S(1)}, u32[]{:S(2)}, u32[]{:S(2)}) collective-permute-start(bf16[96,256]{1,0:T(8,128)(2,1)S(1)} %bitcast.25), channel_id=1, source_target_pairs={{0,2},{1,3},{2,0},{3,1},{4,6},{5,7},{6,4},{7,5},{8,10},{9,11},{10,... | collective-permute-start | bytes 147464 | tf_op jit(solution)/shard_map/ppermute | solution.py:459
  26.2 6.7 %collective-permute-start = (bf16[96,256]{1,0:T(8,128)(2,1)S(1)}, bf16[96,256]{1,0:T(8,128)(2,1)S(1)}, u32[]{:S(2)}, u32[]{:S(2)}) collective-permute-start(bf16[96,256]{1,0:T(8,128)(2,1)S(1)} %bitcast.26), channel_id=1, source_target_pairs={{0,1},{1,2},{2,3},{3,0},{4,5},{5,6},{6,7},{7,4},{8,9},{9,10},{10,1... | collective-permute-start | bytes 147464 | tf_op jit(solution)/shard_map/ppermute | solution.py:459
  83.8 11.5 %copy-start.7 = (bf16[1152,256]{1,0:T(8,128)(2,1)S(1)}, bf16[1152,256]{1,0:T(8,128)(2,1)}, u32[]{:S(2)}) copy-start(bf16[1152,256]{1,0:T(8,128)(2,1)} %get-tuple-element.53) | copy-start | bytes 1769476
  83.8 12.5 %copy-start.4 = (s32[1,64,2]{1,2,0:T(2,128)S(1)}, s32[1,64,2]{1,2,0:T(2,128)}, u32[]{:S(2)}) copy-start(s32[1,64,2]{1,2,0:T(2,128)} %param.13) | copy-start | bytes 1540
  83.9 12.5 %copy-start.5 = (s32[1,64,2]{1,2,0:T(2,128)S(1)}, s32[1,64,2]{1,2,0:T(2,128)}, u32[]{:S(2)}) copy-start(s32[1,64,2]{1,2,0:T(2,128)} %param.14) | copy-start | bytes 1540
  83.9 57.0 %all-to-all-start.1 = ((bf16[64,128,128]{2,1,0:T(8,128)(2,1)}), bf16[64,128,128]{2,1,0:T(8,128)(2,1)}, u32[]{:S(2)}, u32[]{:S(2)}) async-start(bf16[64,128,128]{2,1,0:T(8,128)(2,1)} %get-tuple-element.44), calls=%async_computation.1 | async-start | bytes 4194304 | tf_op jit(solution)/shard_map/all_to_all | solution.py:524
  91.3 29.3 %collective-permute-start.6 = (bf16[1152,256]{1,0:T(8,128)(2,1)}, bf16[1152,256]{1,0:T(8,128)(2,1)S(1)}, u32[]{:S(2)}, u32[]{:S(2)}) collective-permute-start(bf16[1152,256]{1,0:T(8,128)(2,1)} %get-tuple-element.51), channel_id=1, source_target_pairs={{0,1},{1,2},{2,3},{3,0},{4,5},{5,6},{6,7},{7,4},{8,9},{9,10},{10,1... | collective-permute-start | bytes 1769480 | tf_op jit(solution)/shard_map/ppermute | solution.py:459
  92.7 28.5 %collective-permute-start.7 = (bf16[1152,256]{1,0:T(8,128)(2,1)}, bf16[1152,256]{1,0:T(8,128)(2,1)S(1)}, u32[]{:S(2)}, u32[]{:S(2)}) collective-permute-start(bf16[1152,256]{1,0:T(8,128)(2,1)} %get-tuple-element.52), channel_id=1, source_target_pairs={{0,2},{1,3},{2,0},{3,1},{4,6},{5,7},{6,4},{7,5},{8,10},{9,11},{10,... | collective-permute-start | bytes 1769480 | tf_op jit(solution)/shard_map/ppermute | solution.py:459
  95.3 25.9 %collective-permute-start.8 = (bf16[1152,256]{1,0:T(8,128)(2,1)S(1)}, bf16[1152,256]{1,0:T(8,128)(2,1)S(1)}, u32[]{:S(2)}, u32[]{:S(2)}) collective-permute-start(bf16[1152,256]{1,0:T(8,128)(2,1)S(1)} %copy-done.7), channel_id=1, source_target_pairs={{0,3},{1,0},{2,1},{3,2},{4,7},{5,4},{6,5},{7,6},{8,11},{9,8},{10,9... | collective-permute-start | bytes 1769480 | tf_op jit(solution)/shard_map/ppermute | solution.py:459
  96.4 24.8 %copy-start = (bf16[1152,256]{1,0:T(8,128)(2,1)S(1)}, bf16[1152,256]{1,0:T(8,128)(2,1)}, u32[]{:S(2)}) copy-start(bf16[1152,256]{1,0:T(8,128)(2,1)} %get-tuple-element.56.y0) | copy-start | bytes 1769476
  103.3 14.5 %collective-permute-start.9 = (f32[8,128]{1,0:T(8,128)S(1)}, f32[8,128]{1,0:T(8,128)S(1)}, u32[]{:S(2)}, u32[]{:S(2)}) collective-permute-start(f32[8,128]{1,0:T(8,128)S(1)} %get-tuple-element.54), channel_id=1, source_target_pairs={{0,1},{1,2},{2,3},{3,0},{4,5},{5,6},{6,7},{7,4},{8,9},{9,10},{10,1... | collective-permute-start | bytes 12296 | tf_op jit(solution)/shard_map/ppermute | solution.py:459
  103.8 16.9 %collective-permute-start.10 = (f32[8,128]{1,0:T(8,128)S(1)}, f32[8,128]{1,0:T(8,128)S(1)}, u32[]{:S(2)}, u32[]{:S(2)}) collective-permute-start(f32[8,128]{1,0:T(8,128)S(1)} %get-tuple-element.55), channel_id=1, source_target_pairs={{0,3},{1,0},{2,1},{3,2},{4,7},{5,4},{6,5},{7,6},{8,11},{9,8},{10,9... | collective-permute-start | bytes 12296 | tf_op jit(solution)/shard_map/ppermute | solution.py:459
  124.9 7.8 %collective-permute-start.11 = (bf16[1024,256]{1,0:T(8,128)(2,1)S(1)}, bf16[1024,256]{1,0:T(8,128)(2,1)S(1)}, u32[]{:S(2)}, u32[]{:S(2)}) collective-permute-start(bf16[1024,256]{1,0:T(8,128)(2,1)S(1)} %get-tuple-element.61), channel_id=1, source_target_pairs={{0,4},{4,0},{1,5},{5,1},{2,6},{6,2},{3,7},{7,3},{8,12},{12,8},{9,1... | collective-permute-start | bytes 1572872 | tf_op jit(solution)/shard_map/ppermute | solution.py:459
  126.3 4.4 %collective-permute-start.12 = (f32[8,128]{1,0:T(8,128)S(1)}, f32[8,128]{1,0:T(8,128)S(1)}, u32[]{:S(2)}, u32[]{:S(2)}) collective-permute-start(f32[8,128]{1,0:T(8,128)S(1)} %get-tuple-element.64), channel_id=1, source_target_pairs={{0,2},{1,3},{2,0},{3,1},{4,6},{5,7},{6,4},{7,5},{8,10},{9,11},{10,... | collective-permute-start | bytes 12296 | tf_op jit(solution)/shard_map/ppermute | solution.py:459
  130.9 1.8 collective-permute-start.13
  132.9 17.7 %collective-permute-start.14 = (bf16[304,256]{1,0:T(8,128)(2,1)S(1)}, bf16[304,256]{1,0:T(8,128)(2,1)S(1)}, u32[]{:S(2)}, u32[]{:S(2)}) collective-permute-start(bf16[304,256]{1,0:T(8,128)(2,1)S(1)} %get-tuple-element.66), channel_id=1, source_target_pairs={{0,8},{8,16},{16,24},{24,0},{1,9},{9,17},{17,25},{25,1},{2,10},{10... | collective-permute-start | bytes 466952 | tf_op jit(solution)/shard_map/ppermute | solution.py:459
  134.3 16.2 %collective-permute-start.15 = (bf16[304,256]{1,0:T(8,128)(2,1)S(1)}, bf16[304,256]{1,0:T(8,128)(2,1)S(1)}, u32[]{:S(2)}, u32[]{:S(2)}) collective-permute-start(bf16[304,256]{1,0:T(8,128)(2,1)S(1)} %get-tuple-element.67), channel_id=1, source_target_pairs={{0,16},{8,24},{16,0},{24,8},{1,17},{9,25},{17,1},{25,9},{2,18},{10... | collective-permute-start | bytes 466952 | tf_op jit(solution)/shard_map/ppermute | solution.py:459
  136.7 13.8 %collective-permute-start.16 = (bf16[304,256]{1,0:T(8,128)(2,1)S(1)}, bf16[304,256]{1,0:T(8,128)(2,1)S(1)}, u32[]{:S(2)}, u32[]{:S(2)}) collective-permute-start(bf16[304,256]{1,0:T(8,128)(2,1)S(1)} %get-tuple-element.68), channel_id=1, source_target_pairs={{0,24},{8,0},{16,8},{24,16},{1,25},{9,1},{17,9},{25,17},{2,26},{10... | collective-permute-start | bytes 466952 | tf_op jit(solution)/shard_map/ppermute | solution.py:459
  151.4 18.9 %all-to-all-start.2 = ((bf16[8,80,256]{2,1,0:T(8,128)(2,1)}), bf16[8,80,256]{2,1,0:T(8,128)(2,1)S(1)}, u32[]{:S(2)}, u32[]{:S(2)}) async-start(bf16[8,80,256]{2,1,0:T(8,128)(2,1)} %shard_map.128), calls=%async_computation.2 | async-start | bytes 655360 | tf_op jit(solution)/shard_map/all_to_all | solution.py:591
  156.5 5.0 %collective-permute-start.3 = (bf16[2,64,128]{2,1,0:T(8,128)(2,1)S(1)}, bf16[2,64,128]{2,1,0:T(8,128)(2,1)S(1)}, u32[]{:S(2)}, u32[]{:S(2)}) collective-permute-start(bf16[2,64,128]{2,1,0:T(8,128)(2,1)S(1)} %get-tuple-element.46), channel_id=1, source_target_pairs={{0,1},{1,2},{2,3},{3,0},{4,5},{5,6},{6,7},{7,4},{8,9},{9,10},{10,1... | collective-permute-start | bytes 98312 | tf_op jit(solution)/shard_map/ppermute | solution.py:459
  157.8 4.3 %collective-permute-start.4 = (bf16[2,64,128]{2,1,0:T(8,128)(2,1)S(1)}, bf16[2,64,128]{2,1,0:T(8,128)(2,1)S(1)}, u32[]{:S(2)}, u32[]{:S(2)}) collective-permute-start(bf16[2,64,128]{2,1,0:T(8,128)(2,1)S(1)} %get-tuple-element.47), channel_id=1, source_target_pairs={{0,2},{1,3},{2,0},{3,1},{4,6},{5,7},{6,4},{7,5},{8,10},{9,11},{10,... | collective-permute-start | bytes 98312 | tf_op jit(solution)/shard_map/ppermute | solution.py:459
  160.5 3.1 %collective-permute-start.5 = (bf16[2,64,128]{2,1,0:T(8,128)(2,1)S(1)}, bf16[2,64,128]{2,1,0:T(8,128)(2,1)S(1)}, u32[]{:S(2)}, u32[]{:S(2)}) collective-permute-start(bf16[2,64,128]{2,1,0:T(8,128)(2,1)S(1)} %get-tuple-element.48), channel_id=1, source_target_pairs={{0,3},{1,0},{2,1},{3,2},{4,7},{5,4},{6,5},{7,6},{8,11},{9,8},{10,9... | collective-permute-start | bytes 98312 | tf_op jit(solution)/shard_map/ppermute | solution.py:459
Sparse Core Ops, SparseCore 0:
  9.8 56.3 all-gather.1

commit v8 on v6

--- a/solution.py
+++ b/solution.py
@@ -10,6 +10,7 @@
 
 BLK = 128
 LANES = 128
+GAP = 8
 NX = 4
 NC = 2
 ENT = ("z", "x", "c")
@@ -63,6 +64,10 @@
 
 def turn(i, r, n):
     return lax.rem(i + r + n, n)
+
+
+def spaced(i, size):
+    return pl.ds(pl.multiple_of(i * (size + GAP), 8), size)
 
 
 def aligned(i, size):
@@ -145,15 +150,23 @@
     return jnp.concatenate([jnp.where(blk == n, coef, 0.0) for n in range(nblk)], axis=0)
 
 
-def widen(x_ref, xf):
-    step = 512
-
-    def some(i, c):
-        at = aligned(i, step)
+def widen(x_ref, xf, peers):
+    per = x_ref.shape[0] // peers
+    space = xf.shape[0] // peers
+
+    def some(p, c):
+        xf[pl.ds(pl.multiple_of(p * space, 8), per), :] = x_ref[aligned(p, per), :].astype(F32)
+        return c
+
+    def straight(i, c):
+        at = aligned(i, 4 * LANES)
         xf[at, :] = x_ref[at, :].astype(F32)
         return c
 
-    lax.fori_loop(0, x_ref.shape[0] // step, some, 0)
+    if space == per:
+        lax.fori_loop(0, x_ref.shape[0] // (4 * LANES), straight, 0)
+    else:
+        lax.fori_loop(0, peers, some, 0, unroll=4)
 
 
 def slot_rows(xf, peers, cap, halves, share, k):
@@ -170,7 +183,7 @@
 
 
 def rows_of(mf, base, nbase, nblk, share):
-    return jnp.concatenate([get(mf, aligned(n * nbase + base, share)) for n in range(nblk)], axis=0)
+    return jnp.concatenate([get(mf, spaced(n * nbase + base, share)) for n in range(nblk)], axis=0)
 
 
 def table_copies(table_ref, tab, sem):
@@ -194,7 +207,7 @@
     ecopies = start_all(own_row_copies(ent_ref, ent, esem, share))
     tcopies = start_all(table_copies(table_ref, tab, tsem))
     ccopies = start_all(own_row_copies(cot_ref, cot, csem, share))
-    widen(x_ref, xf)
+    widen(x_ref, xf, peers)
     notes = xf[pl.ds(cap * halves * share, peers, stride=per), :].astype(BF)
     lane = lax.broadcasted_iota(jnp.int32, (8, LANES), 1)
     row = lax.broadcasted_iota(jnp.int32, (8, LANES), 0)
@@ -208,7 +221,7 @@
     def one(k, c):
         xk = slot_rows(xf, peers, cap, halves, share, k).astype(BF)
         wk = jnp.where(cnt > first + k, w, 0.0).astype(BF)
-        put(mf, pl.ds(k, w.shape[0], stride=share), jnp.dot(wk, xk, preferred_element_type=F32))
+        put(mf, pl.ds(k, w.shape[0], stride=share + GAP), jnp.dot(wk, xk, preferred_element_type=F32))
         return c
 
     lax.fori_loop(0, share, one, 0, unroll=8)
@@ -268,7 +281,7 @@
     first = group0 * share
     tcopies = start_all(table_copies(table_ref, tab, tsem))
     w_ref[...] = slot_weights(own, (c0, c1, c2, c3), line(rel_ref), line(src_ref), nblk, cs).astype(BF)
-    widen(x_ref, xf)
+    widen(x_ref, xf, peers)
     pg = pg_ref[...]
     for b in range(nbase):
         if b % own == 0:
@@ -276,11 +289,11 @@
         base = tab[b // own, pl.ds((b % own) * width, width), :]
         p = lax.dot_general(pg, base, NT, preferred_element_type=F32)
         for n in range(nblk):
-            put(pf, pl.ds((n * nbase + b) * share, share), p[n * share : (n + 1) * share])
+            put(pf, spaced(n * nbase + b, share), p[n * share : (n + 1) * share])
     cnt = line(cnt_ref)
 
     def one(k, acc):
-        pk = get(pf, pl.ds(k, nblk * nbase, stride=share)).astype(BF)
+        pk = get(pf, pl.ds(k, nblk * nbase, stride=share + GAP)).astype(BF)
         xk = slot_rows(xf, peers, cap, halves, share, k).astype(BF)
         t = lax.dot_general(pk, xk, NT, preferred_element_type=F32)
         return acc + jnp.where(cnt > first + k, t, 0.0)
@@ -317,22 +330,27 @@
     part = keep_ref.shape[0]
     each = part // NX
     deep = part * NC // (own * peers)
-    nz = each // (own * deep)
+    lines = own * deep
+    nz = each // lines
+    plane = NX * NC * deep
     pg = jnp.concatenate([y[pl.ds(own * rows, rows), :] for y in ys], axis=0)
     for b in range(own):
         m = jnp.concatenate([y[pl.ds(b * rows, rows), :] for y in ys], axis=0)
-        put(tmp, pl.ds(0, width), lax.dot_general(m, pg, TN, preferred_element_type=F32))
+        t = lax.dot_general(m, pg, TN, preferred_element_type=F32)
+        for z in range(nz):
+            put(tmp, spaced(z, plane), t[z * plane : (z + 1) * plane])
         for c in range(NC):
             for x in range(NX):
                 for d in range(deep):
                     put(
                         outf,
-                        pl.ds((c * NX + x) * each + b * deep + d, nz, stride=own * deep),
-                        get(tmp, pl.ds((x * NC + c) * deep + d, nz, stride=NX * NC * deep)),
+                        pl.ds((c * NX + x) * nz * (lines + GAP) + b * deep + d, nz, stride=lines + GAP),
+                        get(tmp, pl.ds((x * NC + c) * deep + d, nz, stride=plane + GAP)),
                     )
     core = lax.axis_index("c")
-    keep_ref[...] = get(outf, aligned(core, part)).astype(BF)
-    send_ref[...] = get(outf, aligned(1 - core, part)).astype(BF)
+    for i in range(NX * nz):
+        keep_ref[pl.ds(i * lines, lines), :] = get(outf, spaced(core * (NX * nz) + i, lines)).astype(BF)
+        send_ref[pl.ds(i * lines, lines), :] = get(outf, spaced((1 - core) * (NX * nz) + i, lines)).astype(BF)
 
 
 def core_body(keep_ref, got_ref, coef_ref, other_ref, o0, o1, o2, o3, sums):
@@ -361,14 +379,16 @@
 
 def z_body(own, in_ref, basis_ref, coef_ref):
     nz, rows, width = in_ref.shape
-    last = basis_ref.shape[0]
+    deep = basis_ref.shape[1]
+    last = own * deep
     n = rows - last
     basis = jnp.zeros((last, width), F32)
     coef = jnp.zeros((n, width), F32)
     for z in range(nz):
         basis += in_ref[z, pl.ds(0, last), :].astype(F32)
         coef += in_ref[z, pl.ds(last, n), :].astype(F32)
-    basis_ref[...] = basis
+    for b in range(own):
+        basis_ref[b] = basis[b * deep : (b + 1) * deep]
     relations = coef_ref.shape[1]
     for j in range(n // own):
         size = min(width, relations - j * width)
@@ -387,22 +407,22 @@
     peers = slots // cap
     nblk = w_ref.shape[0] // nbase
     tcopies = start_all(table_copies(table_ref, tab, tsem))
-    widen(x_ref, xf)
+    widen(x_ref, xf, peers)
     w = w_ref[...]
 
     def one(k, c):
         xk = slot_rows(xf, peers, cap, halves, share, k).astype(BF)
-        put(mf, pl.ds(k, w.shape[0], stride=share), jnp.dot(w, xk, preferred_element_type=F32))
+        put(mf, pl.ds(k, w.shape[0], stride=share + GAP), jnp.dot(w, xk, preferred_element_type=F32))
         return c
 
     lax.fori_loop(0, share, one, 0, unroll=8)
-    acc = lax.dot_general(pg_ref[...], sw_ref[...], NT, preferred_element_type=F32)
+    acc = lax.dot_general(sw_ref[...], pg_ref[...], NT, preferred_element_type=F32)
     wait_all(tcopies)
     for b in range(nbase):
         mb = rows_of(mf, b, nbase, nblk, share).astype(BF)
         base = tab[b // own, pl.ds((b % own) * width, width), :]
-        acc += lax.dot_general(mb, base, NT, preferred_element_type=F32)
-    at_ref[...] = acc.T
+        acc += lax.dot_general(base, mb, NT, preferred_element_type=F32)
+    at_ref[...] = acc
     cols = width // groups
     for r, out in enumerate((o0, o1, o2, o3)):
         out[0] = at_ref[aligned(turn(lax.axis_index("basis"), r, groups), cols), :].astype(BF)
@@ -491,7 +511,7 @@
         [SM] * 2 + [VM] * 8 + [HB] * 3,
         [
             pltpu.VMEM((peers * (per + 8), LANES), F32),
-            rows_scratch(nbase * rows, width),
+            rows_scratch(nbase * nblk * (share + GAP), width),
             pltpu.VMEM((groups, own, slots), F32),
             pltpu.VMEM((width, rows), F32),
             tables,
@@ -506,7 +526,7 @@
             dma((groups,)),
             dma((4,)),
         ],
-        limit=28,
+        limit=30,
         outs_in=(HB,) * (groups + 1) + (VM,) * 3,
     )(
         dst, cnt, incoming, dst, cnt, *coefs, self_weight, far(table),
@@ -522,13 +542,13 @@
         [VM] * 10 + [HB],
         [
             pltpu.VMEM((peers * (per + 8), LANES), F32),
-            rows_scratch(nbase * rows, width),
+            rows_scratch(nbase * nblk * (share + GAP), width),
             pltpu.VMEM((nbase, slots), F32),
             tables,
             pltpu.VMEM((groups, own, slots), F32),
             dma((groups,)),
         ],
-        limit=18,
+        limit=20,
         cost=COST,
     )(pg, dst, cnt, incoming, rel_out, src, *coefs, far(table))
     scores = [scores[0]] + [over("basis", r, scores[r]) for r in range(1, groups)]
@@ -541,8 +561,8 @@
         functools.partial(basis_body, own, rows, peers),
         (bf(part, width), bf(part, width)),
         [VM] * 4,
-        [rows_scratch(width, width), rows_scratch(NC * part, width)],
-        limit=8,
+        [rows_scratch(2 * width, width), rows_scratch(2 * NC * part, width)],
+        limit=12,
     )(*ys)
     got = over("c", 1, send)
     each = part // NX
@@ -560,13 +580,13 @@
         tuple(bf(2, width // groups, rows) for _ in range(groups)),
         [VM] * 5 + [HB],
         [
-            pltpu.VMEM((peers * per, LANES), F32),
-            rows_scratch(nbase * rows, width),
+            pltpu.VMEM((peers * (per + GAP), LANES), F32),
+            rows_scratch(nbase * nblk * (share + GAP), width),
             pltpu.VMEM((width, rows), F32),
             tables,
             dma((groups,)),
         ],
-        limit=18,
+        limit=20,
     )(returned.reshape(peers * per, LANES), w_out, act, pg, self_weight, far(table))
 
     ins = lax.optimization_barrier((*ins, grads[0]))[:NX]
@@ -581,7 +601,7 @@
     out = lax.all_to_all(out, "z", split_axis=0, concat_axis=0, tiled=True)
     basis_grad, coef_grad = call(
         functools.partial(z_body, own),
-        (jax.ShapeDtypeStruct((last, width), F32), jax.ShapeDtypeStruct((own, relations), F32)),
+        (jax.ShapeDtypeStruct((own, width // peers, width), F32), jax.ShapeDtypeStruct((own, relations), F32)),
         [VM],
         limit=4,
     )(out)
@@ -595,7 +615,7 @@
         [pltpu.VMEM((groups, 2, cols, rows), F32)],
         limit=4,
     )(*grads)
-    return (activation.T, basis_grad.reshape(own, width // peers, width), coef_grad.T, entity_grad.T)
+    return (activation.T, basis_grad, coef_grad.T, entity_grad.T)
 
 
 def solution(mesh):

time: 178 us -> 171 us (0.961)
  Pallas kernels: 33.4 us -> 23 us
  waiting for transfers between devices: 77.3 us -> 81.2 us
    pallas_call x1, Pallas kernels: 9.01 us -> 5.1 us  [local(): call(functools.partial(bwd_body, cap, own), tuple((bf(2, width // groups,...]
    pallas_call x1, Pallas kernels: 8.54 us -> 5.93 us  [local(): call(functools.partial(fwd_body, cap, nblk, own), (*[hbm((own + 1) * rows...]
    all_to_all x1, waiting for transfers between devices: 2.98 us -> 5.38 us  [local(): lax.all_to_all(back, ENT, split_axis=0, concat_axis=0, tiled=True)]
    pallas_call x1, Pallas kernels: 3.72 us -> 1.33 us  [local(): call(functools.partial(basis_body, own, rows, peers), (bf(part, width), b...]
  transfers between devices with their start and end apart: 21 -> 21, of which waited for: 13 -> 13; matrix products, arithmetic and copies ran while one was open for 0% -> 0% of each run, Pallas kernels for 12% -> 8%
where the time goes in v8:
time: 171 us
  waiting for transfers between devices  81.2 us (47%)
  starting transfers between devices  52.1 us (30%)
  Pallas kernels  23 us (13%)
  between operations  14.2 us (8%)
    all_to_all x1, waiting for transfers between devices, local(): lax.all_to_all(outgoing, ENT, split_axis=0, concat_axis=0, tiled=True)  42.4 us
    ppermute x17, waiting for transfers between devices, over(): return lax.ppermute(value, axis, [(i, (i + r) % n) for i in range(n)])  27.4 us
    ppermute x17, starting transfers between devices, over(): return lax.ppermute(value, axis, [(i, (i + r) % n) for i in range(n)])  26.4 us
    all_to_all x1, starting transfers between devices, local(): lax.all_to_all(outgoing, ENT, split_axis=0, concat_axis=0, tiled=True)  13.1 us
    all_to_all x1, starting transfers between devices, local(): lax.all_to_all(back, ENT, split_axis=0, concat_axis=0, tiled=True)  7.43 us
    all_to_all x1, waiting for transfers between devices, local(): out = lax.all_to_all(out, 'z', split_axis=0, concat_axis=0, tiled=True)  5.96 us
    pallas_call x1, Pallas kernels, local(): call(functools.partial(fwd_body, cap, nblk, own), (*[hbm((own + 1) * rows...  5.93 us
    pallas_call x1, Pallas kernels, local(): call(functools.partial(score_body, cap, nblk, own, halves), (*[jax.ShapeD...  5.49 us
  transfers between devices with their start and end apart: 21, of which 13 were waited for; matrix products, arithmetic and copies ran while one was open for 0% of the time, Pallas kernels for 8%

profile of v8, /device:TPU:1, one launch (start us, length us, event | category | flops | bytes accessed | tf_op | source)
XLA Modules:
  0.0 170.7 jit_solution(6953175198187692921)
XLA Ops:
  7.2 2.4 %shard_map.120 = bf16[64,136,128]{2,1,0:T(8,128)(2,1)} custom-call(s32[2,64]{1,0:T(2,128)} %bitcast.35, s32[2,64]{1,0:T(2,128)} %bitcast.37, bf16[512,256]{1,0:T(8,128)(2,1)} %ent_ref.3), custom_call_target="tpu_custom_call" | custom-call | tf_op jit(solution)/shard_map/pallas_call | solution.py:477
  9.7 13.1 %all-to-all-start = ((bf16[64,136,128]{2,1,0:T(8,128)(2,1)}), bf16[64,136,128]{2,1,0:T(8,128)(2,1)S(1)}, u32[]{:S(2)}, u32[]{:S(2)}) async-start(bf16[64,136,128]{2,1,0:T(8,128)(2,1)} %shard_map.120), calls=%async_computation | async-start | bytes 4456448 | tf_op jit(solution)/shard_map/all_to_all | solution.py:492
  23.0 2.8 %collective-permute-start.2 = (bf16[96,256]{1,0:T(8,128)(2,1)S(1)}, bf16[96,256]{1,0:T(8,128)(2,1)S(1)}, u32[]{:S(2)}, u32[]{:S(2)}) collective-permute-start(bf16[96,256]{1,0:T(8,128)(2,1)S(1)} %bitcast.24), channel_id=1, source_target_pairs={{0,3},{1,0},{2,1},{3,2},{4,7},{5,4},{6,5},{7,6},{8,11},{9,8},{10,9... | collective-permute-start | bytes 147464 | tf_op jit(solution)/shard_map/ppermute | solution.py:471
  27.0 3.4 %collective-permute-done.1.c2 = bf16[96,256]{1,0:T(8,128)(2,1)S(1)} collective-permute-done((bf16[96,256]{1,0:T(8,128)(2,1)S(1)}, bf16[96,256]{1,0:T(8,128)(2,1)S(1)}, u32[]{:S(2)}, u32[]{:S(2)}) %collective-permute-start.1) | collective-permute-done | bytes 49184 | tf_op jit(solution)/shard_map/ppermute | solution.py:471
  30.4 2.5 %collective-permute-done.c1 = bf16[96,256]{1,0:T(8,128)(2,1)S(1)} collective-permute-done((bf16[96,256]{1,0:T(8,128)(2,1)S(1)}, bf16[96,256]{1,0:T(8,128)(2,1)S(1)}, u32[]{:S(2)}, u32[]{:S(2)}) %collective-permute-start) | collective-permute-done | bytes 49184 | tf_op jit(solution)/shard_map/ppermute | solution.py:471
  32.9 42.4 %all-to-all-done = bf16[64,136,128]{2,1,0:T(8,128)(2,1)S(1)} async-done(((bf16[64,136,128]{2,1,0:T(8,128)(2,1)}), bf16[64,136,128]{2,1,0:T(8,128)(2,1)S(1)}, u32[]{:S(2)}, u32[]{:S(2)}) %all-to-all-start) | async-done | bytes 2228256 | tf_op jit(solution)/shard_map/all_to_all | solution.py:492
  75.3 5.9 %shard_map.121 = (bf16[1152,256]{1,0:T(8,128)(2,1)}, bf16[1152,256]{1,0:T(8,128)(2,1)}, bf16[1152,256]{1,0:T(8,128)(2,1)}, bf16[1152,256]{1,0:T(8,128)(2,1)}, bf...) custom-call(s32[2,64]{1,0:T(2,128)S(1)} %bitcast.29, ...), custom_call_target="tpu_custom_call" | custom-call | tf_op jit(solution)/shard_map/pallas_call | solution.py:502
  81.3 7.4 %all-to-all-start.1 = ((bf16[64,128,128]{2,1,0:T(8,128)(2,1)}), bf16[64,128,128]{2,1,0:T(8,128)(2,1)}, u32[]{:S(2)}, u32[]{:S(2)}) async-start(bf16[64,128,128]{2,1,0:T(8,128)(2,1)} %get-tuple-element.41), calls=%async_computation.1 | async-start | bytes 4194304 | tf_op jit(solution)/shard_map/all_to_all | solution.py:536
  88.7 1.4 collective-permute-start.6
  90.1 2.6 %collective-permute-start.7 = (bf16[1152,256]{1,0:T(8,128)(2,1)}, bf16[1152,256]{1,0:T(8,128)(2,1)S(1)}, u32[]{:S(2)}, u32[]{:S(2)}) collective-permute-start(bf16[1152,256]{1,0:T(8,128)(2,1)} %get-tuple-element.52), channel_id=1, source_target_pairs={{0,2},{1,3},{2,0},{3,1},{4,6},{5,7},{6,4},{7,5},{8,10},{9,11},{10,... | collective-permute-start | bytes 1769480 | tf_op jit(solution)/shard_map/ppermute | solution.py:471
  92.7 1.1 collective-permute-start.8
  93.8 5.5 %shard_map.122 = (f32[8,128]{1,0:T(8,128)S(1)}, f32[8,128]{1,0:T(8,128)S(1)}, f32[8,128]{1,0:T(8,128)S(1)}, f32[8,128]{1,0:T(8,128)S(1)}, bf16[128,128]{1,0:T(8,128)(2,1)S(1)}) custom-call(bf16[128,256]{1,0:T(8,128)(2,1)S(1)} %get-tuple-element.42.pg_ref, s32[2,64]{1,0:T(2,128)S(1)} %bitcast.31, s32[2,64]{1,0:T(2,128)S(1)} %bitcast.34, ...), custom_call_target="tpu_custom_call" | custom-call | flops 8000000000 | bytes 20000000 | tf_op jit(solution)/shard_map/pallas_call | solution.py:539
  99.7 2.3 %collective-permute-start.10 = (f32[8,128]{1,0:T(8,128)S(1)}, f32[8,128]{1,0:T(8,128)S(1)}, u32[]{:S(2)}, u32[]{:S(2)}) collective-permute-start(f32[8,128]{1,0:T(8,128)S(1)} %get-tuple-element.55), channel_id=1, source_target_pairs={{0,3},{1,0},{2,1},{3,2},{4,7},{5,4},{6,5},{7,6},{8,11},{9,8},{10,9... | collective-permute-start | bytes 12296 | tf_op jit(solution)/shard_map/ppermute | solution.py:471
  102.0 13.2 %collective-permute-done.9.s1 = f32[8,128]{1,0:T(8,128)S(1)} collective-permute-done((f32[8,128]{1,0:T(8,128)S(1)}, f32[8,128]{1,0:T(8,128)S(1)}, u32[]{:S(2)}, u32[]{:S(2)}) %collective-permute-start.9) | collective-permute-done | bytes 4128 | tf_op jit(solution)/shard_map/ppermute | solution.py:471
  115.2 2.8 %collective-permute-done.10.s3 = f32[8,128]{1,0:T(8,128)S(1)} collective-permute-done((f32[8,128]{1,0:T(8,128)S(1)}, f32[8,128]{1,0:T(8,128)S(1)}, u32[]{:S(2)}, u32[]{:S(2)}) %collective-permute-start.10) | collective-permute-done | bytes 4128 | tf_op jit(solution)/shard_map/ppermute | solution.py:471
  118.6 1.3 shard_map.125
  119.9 1.4 collective-permute-start.11
  121.3 2.4 %collective-permute-start.12 = (f32[8,128]{1,0:T(8,128)S(1)}, f32[8,128]{1,0:T(8,128)S(1)}, u32[]{:S(2)}, u32[]{:S(2)}) collective-permute-start(f32[8,128]{1,0:T(8,128)S(1)} %get-tuple-element.64), channel_id=1, source_target_pairs={{0,2},{1,3},{2,0},{3,1},{4,6},{5,7},{6,4},{7,5},{8,10},{9,11},{10,... | collective-permute-start | bytes 12296 | tf_op jit(solution)/shard_map/ppermute | solution.py:471
  123.7 2.0 %collective-permute-done.12.s2 = f32[8,128]{1,0:T(8,128)S(1)} collective-permute-done((f32[8,128]{1,0:T(8,128)S(1)}, f32[8,128]{1,0:T(8,128)S(1)}, u32[]{:S(2)}, u32[]{:S(2)}) %collective-permute-start.12) | collective-permute-done | bytes 4128 | tf_op jit(solution)/shard_map/ppermute | solution.py:471
  125.9 0.9 collective-permute-start.13
  127.9 1.5 collective-permute-start.14
  129.3 2.4 %collective-permute-start.15 = (bf16[304,256]{1,0:T(8,128)(2,1)S(1)}, bf16[304,256]{1,0:T(8,128)(2,1)S(1)}, u32[]{:S(2)}, u32[]{:S(2)}) collective-permute-start(bf16[304,256]{1,0:T(8,128)(2,1)S(1)} %get-tuple-element.67), channel_id=1, source_target_pairs={{0,16},{8,24},{16,0},{24,8},{1,17},{9,25},{17,1},{25,9},{2,18},{10... | collective-permute-start | bytes 466952 | tf_op jit(solution)/shard_map/ppermute | solution.py:471
  131.7 1.2 collective-permute-start.16
  132.9 5.4 %all-to-all-done.1 = bf16[64,128,128]{2,1,0:T(8,128)(2,1)} async-done(((bf16[64,128,128]{2,1,0:T(8,128)(2,1)}), bf16[64,128,128]{2,1,0:T(8,128)(2,1)}, u32[]{:S(2)}, u32[]{:S(2)}) %all-to-all-start.1) | async-done | bytes 2097184 | tf_op jit(solution)/shard_map/all_to_all | solution.py:536
  138.3 5.1 %shard_map.123 = (bf16[2,64,128]{2,1,0:T(8,128)(2,1)S(1)}, bf16[2,64,128]{2,1,0:T(8,128)(2,1)S(1)}, bf16[2,64,128]{2,1,0:T(8,128)(2,1)S(1)}, bf16[2,64,128]{2,1,0:T(8,128)(2,1)S(1)}) custom-call(bf16[8192,128]{1,0:T(8,128)(2,1)} %bitcast.13.x_ref, bf16[128,128]{1,0:T(8,128)(2,1)S(1)} %get-tuple-element.43.w_ref, ...), custom_call_target="tpu_custom_call" | custom-call | tf_op jit(solution)/shard_map/pallas_call | solution.py:578
  143.4 0.9 shard_map.128
  144.3 5.2 %all-to-all-start.2 = ((bf16[8,80,256]{2,1,0:T(8,128)(2,1)}), bf16[8,80,256]{2,1,0:T(8,128)(2,1)S(1)}, u32[]{:S(2)}, u32[]{:S(2)}) async-start(bf16[8,80,256]{2,1,0:T(8,128)(2,1)} %shard_map.128), calls=%async_computation.2 | async-start | bytes 655360 | tf_op jit(solution)/shard_map/all_to_all | solution.py:601
  149.4 1.3 collective-permute-start.3
  150.7 2.6 %collective-permute-start.4 = (bf16[2,64,128]{2,1,0:T(8,128)(2,1)S(1)}, bf16[2,64,128]{2,1,0:T(8,128)(2,1)S(1)}, u32[]{:S(2)}, u32[]{:S(2)}) collective-permute-start(bf16[2,64,128]{2,1,0:T(8,128)(2,1)S(1)} %get-tuple-element.47), channel_id=1, source_target_pairs={{0,2},{1,3},{2,0},{3,1},{4,6},{5,7},{6,4},{7,5},{8,10},{9,11},{10,... | collective-permute-start | bytes 98312 | tf_op jit(solution)/shard_map/ppermute | solution.py:471
  153.4 1.1 collective-permute-start.5
  155.0 1.4 collective-permute-done.5.i3
  157.2 6.0 %all-to-all-done.2.in_ref = bf16[8,80,256]{2,1,0:T(8,128)(2,1)S(1)} async-done(((bf16[8,80,256]{2,1,0:T(8,128)(2,1)}), bf16[8,80,256]{2,1,0:T(8,128)(2,1)S(1)}, u32[]{:S(2)}, u32[]{:S(2)}) %all-to-all-start.2) | async-done | bytes 327712 | tf_op jit(solution)/shard_map/all_to_all | solution.py:601
  (41 shorter events, 5.7 us)
Async XLA Ops:
  7.2 68.1 %all-gather.2.cloned.1.call-start = ((), (), s32[]{:S(2)}) async-start(), calls=%async_computation.3 | async-start | bytes 5242880 | tf_op jit(solution)/shard_map/all_gather | solution.py:495
  9.7 13.2 %copy-start.6 = (f32[1315,8]{0,1:T(8,128)S(1)}, f32[1315,8]{0,1:T(8,128)}, u32[]{:S(2)}) copy-start(f32[1315,8]{0,1:T(8,128)} %param.12) | copy-start | bytes 126244
  9.7 65.6 %copy-start.1 = (bf16[256,256]{1,0:T(8,128)(2,1)S(1)}, bf16[256,256]{1,0:T(8,128)(2,1)}, u32[]{:S(2)}) copy-start(bf16[256,256]{1,0:T(8,128)(2,1)} %sw_ref.3) | copy-start | bytes 393220
  9.7 65.6 %copy-start.2 = (s32[64,1,2]{0,2,1:T(2,128)S(1)}, s32[64,1,2]{0,2,1:T(2,128)}, u32[]{:S(2)}) copy-start(s32[64,1,2]{0,2,1:T(2,128)} %param.15) | copy-start | bytes 1540
  9.7 65.6 %copy-start.3 = (s32[64,1,2]{0,2,1:T(2,128)S(1)}, s32[64,1,2]{0,2,1:T(2,128)}, u32[]{:S(2)}) copy-start(s32[64,1,2]{0,2,1:T(2,128)} %param.16) | copy-start | bytes 1540
  9.7 65.5 %all-to-all-start = ((bf16[64,136,128]{2,1,0:T(8,128)(2,1)}), bf16[64,136,128]{2,1,0:T(8,128)(2,1)S(1)}, u32[]{:S(2)}, u32[]{:S(2)}) async-start(bf16[64,136,128]{2,1,0:T(8,128)(2,1)} %shard_map.120), calls=%async_computation | async-start | bytes 4456448 | tf_op jit(solution)/shard_map/all_to_all | solution.py:492
  23.0 4.0 %collective-permute-start.2 = (bf16[96,256]{1,0:T(8,128)(2,1)S(1)}, bf16[96,256]{1,0:T(8,128)(2,1)S(1)}, u32[]{:S(2)}, u32[]{:S(2)}) collective-permute-start(bf16[96,256]{1,0:T(8,128)(2,1)S(1)} %bitcast.24), channel_id=1, source_target_pairs={{0,3},{1,0},{2,1},{3,2},{4,7},{5,4},{6,5},{7,6},{8,11},{9,8},{10,9... | collective-permute-start | bytes 147464 | tf_op jit(solution)/shard_map/ppermute | solution.py:471
  25.8 4.6 %collective-permute-start.1 = (bf16[96,256]{1,0:T(8,128)(2,1)S(1)}, bf16[96,256]{1,0:T(8,128)(2,1)S(1)}, u32[]{:S(2)}, u32[]{:S(2)}) collective-permute-start(bf16[96,256]{1,0:T(8,128)(2,1)S(1)} %bitcast.25), channel_id=1, source_target_pairs={{0,2},{1,3},{2,0},{3,1},{4,6},{5,7},{6,4},{7,5},{8,10},{9,11},{10,... | collective-permute-start | bytes 147464 | tf_op jit(solution)/shard_map/ppermute | solution.py:471
  26.2 6.7 %collective-permute-start = (bf16[96,256]{1,0:T(8,128)(2,1)S(1)}, bf16[96,256]{1,0:T(8,128)(2,1)S(1)}, u32[]{:S(2)}, u32[]{:S(2)}) collective-permute-start(bf16[96,256]{1,0:T(8,128)(2,1)S(1)} %bitcast.26), channel_id=1, source_target_pairs={{0,1},{1,2},{2,3},{3,0},{4,5},{5,6},{6,7},{7,4},{8,9},{9,10},{10,1... | collective-permute-start | bytes 147464 | tf_op jit(solution)/shard_map/ppermute | solution.py:471
  81.2 11.5 %copy-start.7 = (bf16[1152,256]{1,0:T(8,128)(2,1)S(1)}, bf16[1152,256]{1,0:T(8,128)(2,1)}, u32[]{:S(2)}) copy-start(bf16[1152,256]{1,0:T(8,128)(2,1)} %get-tuple-element.53) | copy-start | bytes 1769476
  81.2 12.5 %copy-start.4 = (s32[1,64,2]{1,2,0:T(2,128)S(1)}, s32[1,64,2]{1,2,0:T(2,128)}, u32[]{:S(2)}) copy-start(s32[1,64,2]{1,2,0:T(2,128)} %param.13) | copy-start | bytes 1540
  81.3 12.5 %copy-start.5 = (s32[1,64,2]{1,2,0:T(2,128)S(1)}, s32[1,64,2]{1,2,0:T(2,128)}, u32[]{:S(2)}) copy-start(s32[1,64,2]{1,2,0:T(2,128)} %param.14) | copy-start | bytes 1540
  81.3 57.0 %all-to-all-start.1 = ((bf16[64,128,128]{2,1,0:T(8,128)(2,1)}), bf16[64,128,128]{2,1,0:T(8,128)(2,1)}, u32[]{:S(2)}, u32[]{:S(2)}) async-start(bf16[64,128,128]{2,1,0:T(8,128)(2,1)} %get-tuple-element.41), calls=%async_computation.1 | async-start | bytes 4194304 | tf_op jit(solution)/shard_map/all_to_all | solution.py:536
  88.7 29.3 %collective-permute-start.6 = (bf16[1152,256]{1,0:T(8,128)(2,1)}, bf16[1152,256]{1,0:T(8,128)(2,1)S(1)}, u32[]{:S(2)}, u32[]{:S(2)}) collective-permute-start(bf16[1152,256]{1,0:T(8,128)(2,1)} %get-tuple-element.51), channel_id=1, source_target_pairs={{0,1},{1,2},{2,3},{3,0},{4,5},{5,6},{6,7},{7,4},{8,9},{9,10},{10,1... | collective-permute-start | bytes 1769480 | tf_op jit(solution)/shard_map/ppermute | solution.py:471
  90.1 28.5 %collective-permute-start.7 = (bf16[1152,256]{1,0:T(8,128)(2,1)}, bf16[1152,256]{1,0:T(8,128)(2,1)S(1)}, u32[]{:S(2)}, u32[]{:S(2)}) collective-permute-start(bf16[1152,256]{1,0:T(8,128)(2,1)} %get-tuple-element.52), channel_id=1, source_target_pairs={{0,2},{1,3},{2,0},{3,1},{4,6},{5,7},{6,4},{7,5},{8,10},{9,11},{10,... | collective-permute-start | bytes 1769480 | tf_op jit(solution)/shard_map/ppermute | solution.py:471
  92.7 25.9 %collective-permute-start.8 = (bf16[1152,256]{1,0:T(8,128)(2,1)S(1)}, bf16[1152,256]{1,0:T(8,128)(2,1)S(1)}, u32[]{:S(2)}, u32[]{:S(2)}) collective-permute-start(bf16[1152,256]{1,0:T(8,128)(2,1)S(1)} %copy-done.7), channel_id=1, source_target_pairs={{0,3},{1,0},{2,1},{3,2},{4,7},{5,4},{6,5},{7,6},{8,11},{9,8},{10,9... | collective-permute-start | bytes 1769480 | tf_op jit(solution)/shard_map/ppermute | solution.py:471
  93.8 24.8 %copy-start = (bf16[1152,256]{1,0:T(8,128)(2,1)S(1)}, bf16[1152,256]{1,0:T(8,128)(2,1)}, u32[]{:S(2)}) copy-start(bf16[1152,256]{1,0:T(8,128)(2,1)} %get-tuple-element.56.y0) | copy-start | bytes 1769476
  99.3 16.0 %collective-permute-start.9 = (f32[8,128]{1,0:T(8,128)S(1)}, f32[8,128]{1,0:T(8,128)S(1)}, u32[]{:S(2)}, u32[]{:S(2)}) collective-permute-start(f32[8,128]{1,0:T(8,128)S(1)} %get-tuple-element.54), channel_id=1, source_target_pairs={{0,1},{1,2},{2,3},{3,0},{4,5},{5,6},{6,7},{7,4},{8,9},{9,10},{10,1... | collective-permute-start | bytes 12296 | tf_op jit(solution)/shard_map/ppermute | solution.py:471
  99.7 18.3 %collective-permute-start.10 = (f32[8,128]{1,0:T(8,128)S(1)}, f32[8,128]{1,0:T(8,128)S(1)}, u32[]{:S(2)}, u32[]{:S(2)}) collective-permute-start(f32[8,128]{1,0:T(8,128)S(1)} %get-tuple-element.55), channel_id=1, source_target_pairs={{0,3},{1,0},{2,1},{3,2},{4,7},{5,4},{6,5},{7,6},{8,11},{9,8},{10,9... | collective-permute-start | bytes 12296 | tf_op jit(solution)/shard_map/ppermute | solution.py:471
  119.9 7.8 %collective-permute-start.11 = (bf16[1024,256]{1,0:T(8,128)(2,1)S(1)}, bf16[1024,256]{1,0:T(8,128)(2,1)S(1)}, u32[]{:S(2)}, u32[]{:S(2)}) collective-permute-start(bf16[1024,256]{1,0:T(8,128)(2,1)S(1)} %get-tuple-element.61), channel_id=1, source_target_pairs={{0,4},{4,0},{1,5},{5,1},{2,6},{6,2},{3,7},{7,3},{8,12},{12,8},{9,1... | collective-permute-start | bytes 1572872 | tf_op jit(solution)/shard_map/ppermute | solution.py:471
  121.3 4.4 %collective-permute-start.12 = (f32[8,128]{1,0:T(8,128)S(1)}, f32[8,128]{1,0:T(8,128)S(1)}, u32[]{:S(2)}, u32[]{:S(2)}) collective-permute-start(f32[8,128]{1,0:T(8,128)S(1)} %get-tuple-element.64), channel_id=1, source_target_pairs={{0,2},{1,3},{2,0},{3,1},{4,6},{5,7},{6,4},{7,5},{8,10},{9,11},{10,... | collective-permute-start | bytes 12296 | tf_op jit(solution)/shard_map/ppermute | solution.py:471
  125.9 1.8 %collective-permute-start.13 = (bf16[48,256]{1,0:T(8,128)(2,1)S(1)}, bf16[48,256]{1,0:T(8,128)(2,1)S(1)}, u32[]{:S(2)}, u32[]{:S(2)}) collective-permute-start(bf16[48,256]{1,0:T(8,128)(2,1)S(1)} %shard_map.126.coef_ref), channel_id=1, source_target_pairs={{0,4},{4,0},{1,5},{5,1},{2,6},{6,2},{3,7},{7,3},{8,12},{12,8},{9,1... | collective-permute-start | bytes 73736 | tf_op jit(solution)/shard_map/ppermute | solution.py:471
  127.9 15.5 %collective-permute-start.14 = (bf16[304,256]{1,0:T(8,128)(2,1)S(1)}, bf16[304,256]{1,0:T(8,128)(2,1)S(1)}, u32[]{:S(2)}, u32[]{:S(2)}) collective-permute-start(bf16[304,256]{1,0:T(8,128)(2,1)S(1)} %get-tuple-element.66), channel_id=1, source_target_pairs={{0,8},{8,16},{16,24},{24,0},{1,9},{9,17},{17,25},{25,1},{2,10},{10... | collective-permute-start | bytes 466952 | tf_op jit(solution)/shard_map/ppermute | solution.py:471
  129.3 14.1 %collective-permute-start.15 = (bf16[304,256]{1,0:T(8,128)(2,1)S(1)}, bf16[304,256]{1,0:T(8,128)(2,1)S(1)}, u32[]{:S(2)}, u32[]{:S(2)}) collective-permute-start(bf16[304,256]{1,0:T(8,128)(2,1)S(1)} %get-tuple-element.67), channel_id=1, source_target_pairs={{0,16},{8,24},{16,0},{24,8},{1,17},{9,25},{17,1},{25,9},{2,18},{10... | collective-permute-start | bytes 466952 | tf_op jit(solution)/shard_map/ppermute | solution.py:471
  131.7 11.7 %collective-permute-start.16 = (bf16[304,256]{1,0:T(8,128)(2,1)S(1)}, bf16[304,256]{1,0:T(8,128)(2,1)S(1)}, u32[]{:S(2)}, u32[]{:S(2)}) collective-permute-start(bf16[304,256]{1,0:T(8,128)(2,1)S(1)} %get-tuple-element.68), channel_id=1, source_target_pairs={{0,24},{8,0},{16,8},{24,16},{1,25},{9,1},{17,9},{25,17},{2,26},{10... | collective-permute-start | bytes 466952 | tf_op jit(solution)/shard_map/ppermute | solution.py:471
  144.3 18.9 %all-to-all-start.2 = ((bf16[8,80,256]{2,1,0:T(8,128)(2,1)}), bf16[8,80,256]{2,1,0:T(8,128)(2,1)S(1)}, u32[]{:S(2)}, u32[]{:S(2)}) async-start(bf16[8,80,256]{2,1,0:T(8,128)(2,1)} %shard_map.128), calls=%async_computation.2 | async-start | bytes 655360 | tf_op jit(solution)/shard_map/all_to_all | solution.py:601
  149.4 5.0 %collective-permute-start.3 = (bf16[2,64,128]{2,1,0:T(8,128)(2,1)S(1)}, bf16[2,64,128]{2,1,0:T(8,128)(2,1)S(1)}, u32[]{:S(2)}, u32[]{:S(2)}) collective-permute-start(bf16[2,64,128]{2,1,0:T(8,128)(2,1)S(1)} %get-tuple-element.46), channel_id=1, source_target_pairs={{0,1},{1,2},{2,3},{3,0},{4,5},{5,6},{6,7},{7,4},{8,9},{9,10},{10,1... | collective-permute-start | bytes 98312 | tf_op jit(solution)/shard_map/ppermute | solution.py:471
  150.7 4.3 %collective-permute-start.4 = (bf16[2,64,128]{2,1,0:T(8,128)(2,1)S(1)}, bf16[2,64,128]{2,1,0:T(8,128)(2,1)S(1)}, u32[]{:S(2)}, u32[]{:S(2)}) collective-permute-start(bf16[2,64,128]{2,1,0:T(8,128)(2,1)S(1)} %get-tuple-element.47), channel_id=1, source_target_pairs={{0,2},{1,3},{2,0},{3,1},{4,6},{5,7},{6,4},{7,5},{8,10},{9,11},{10,... | collective-permute-start | bytes 98312 | tf_op jit(solution)/shard_map/ppermute | solution.py:471
  153.4 3.1 %collective-permute-start.5 = (bf16[2,64,128]{2,1,0:T(8,128)(2,1)S(1)}, bf16[2,64,128]{2,1,0:T(8,128)(2,1)S(1)}, u32[]{:S(2)}, u32[]{:S(2)}) collective-permute-start(bf16[2,64,128]{2,1,0:T(8,128)(2,1)S(1)} %get-tuple-element.48), channel_id=1, source_target_pairs={{0,3},{1,0},{2,1},{3,2},{4,7},{5,4},{6,5},{7,6},{8,11},{9,8},{10,9... | collective-permute-start | bytes 98312 | tf_op jit(solution)/shard_map/ppermute | solution.py:471
Sparse Core Ops, SparseCore 0:
  9.8 56.3 all-gather.1

commit v9 on v8

--- a/solution.py
+++ b/solution.py
@@ -555,7 +555,7 @@
     lot = chunks * own
     coef_part = call(coef_body, bf(lot, width), [VM] * 5, limit=4)(rel_in, *scores)
 
-    ys = lax.optimization_barrier((*ys, scores[1], scores[3]))[:groups]
+    ys = lax.optimization_barrier((*ys, scores[2], scores[3]))[:groups]
     part = own * width // NC
     keep, send = call(
         functools.partial(basis_body, own, rows, peers),
@@ -589,7 +589,6 @@
         limit=20,
     )(returned.reshape(peers * per, LANES), w_out, act, pg, self_weight, far(table))
 
-    ins = lax.optimization_barrier((*ins, grads[0]))[:NX]
     last = each // nz
     out = call(
         x_body,

time: 171 us -> 170 us (level)
  waiting for transfers between devices: 81.2 us -> 78.8 us
    ppermute x17, waiting for transfers between devices: 27.4 us -> 34.6 us  [over(): return lax.ppermute(value, axis, [(i, (i + r) % n) for i in range(n)])]
    all_to_all x1, waiting for transfers between devices: 5.38 us -> 0.01 us  [local(): lax.all_to_all(back, ENT, split_axis=0, concat_axis=0, tiled=True)]
    all_to_all x1, waiting for transfers between devices: 5.96 us -> 1.8 us  [local(): out = lax.all_to_all(out, 'z', split_axis=0, concat_axis=0, tiled=True)]
  transfers between devices with their start and end apart: 21 -> 21, of which waited for: 13 -> 10; matrix products, arithmetic and copies ran while one was open for 0% -> 0% of each run, Pallas kernels for 8% -> 8%
where the time goes in v9:
time: 170 us; the launch traced here: 168 us
  waiting for transfers between devices  78.8 us (46%)
  starting transfers between devices  52 us (31%)
  Pallas kernels  23.1 us (14%)
  between operations  14.2 us (8%)
    all_to_all x1, waiting for transfers between devices, local(): lax.all_to_all(outgoing, ENT, split_axis=0, concat_axis=0, tiled=True)  42.4 us
    ppermute x17, waiting for transfers between devices, over(): return lax.ppermute(value, axis, [(i, (i + r) % n) for i in range(n)])  34.6 us
    ppermute x17, starting transfers between devices, over(): return lax.ppermute(value, axis, [(i, (i + r) % n) for i in range(n)])  25.8 us
    all_to_all x1, starting transfers between devices, local(): lax.all_to_all(outgoing, ENT, split_axis=0, concat_axis=0, tiled=True)  13.1 us
    all_to_all x1, starting transfers between devices, local(): lax.all_to_all(back, ENT, split_axis=0, concat_axis=0, tiled=True)  7.43 us
    pallas_call x1, Pallas kernels, local(): call(functools.partial(fwd_body, cap, nblk, own), (*[hbm((own + 1) * rows...  5.93 us
    all_to_all x1, starting transfers between devices, local(): out = lax.all_to_all(out, 'z', split_axis=0, concat_axis=0, tiled=True)  5.62 us
    pallas_call x1, Pallas kernels, local(): call(functools.partial(score_body, cap, nblk, own, halves), (*[jax.ShapeD...  5.49 us
  transfers between devices with their start and end apart: 21, of which 10 were waited for; matrix products, arithmetic and copies ran while one was open for 0% of the time, Pallas kernels for 8%

profile of v9, /device:TPU:1, one launch (start us, length us, event | category | flops | bytes accessed | tf_op | source)
XLA Modules:
  0.0 168.3 jit_solution(4746794993907586154)
XLA Ops:
  7.2 2.4 %shard_map.120 = bf16[64,136,128]{2,1,0:T(8,128)(2,1)} custom-call(s32[2,64]{1,0:T(2,128)} %bitcast.35, s32[2,64]{1,0:T(2,128)} %bitcast.37, bf16[512,256]{1,0:T(8,128)(2,1)} %ent_ref.3), custom_call_target="tpu_custom_call" | custom-call | tf_op jit(solution)/shard_map/pallas_call | solution.py:477
  9.7 13.1 %all-to-all-start = ((bf16[64,136,128]{2,1,0:T(8,128)(2,1)}), bf16[64,136,128]{2,1,0:T(8,128)(2,1)S(1)}, u32[]{:S(2)}, u32[]{:S(2)}) async-start(bf16[64,136,128]{2,1,0:T(8,128)(2,1)} %shard_map.120), calls=%async_computation | async-start | bytes 4456448 | tf_op jit(solution)/shard_map/all_to_all | solution.py:492
  23.0 2.8 %collective-permute-start.2 = (bf16[96,256]{1,0:T(8,128)(2,1)S(1)}, bf16[96,256]{1,0:T(8,128)(2,1)S(1)}, u32[]{:S(2)}, u32[]{:S(2)}) collective-permute-start(bf16[96,256]{1,0:T(8,128)(2,1)S(1)} %bitcast.24), channel_id=1, source_target_pairs={{0,3},{1,0},{2,1},{3,2},{4,7},{5,4},{6,5},{7,6},{8,11},{9,8},{10,9... | collective-permute-start | bytes 147464 | tf_op jit(solution)/shard_map/ppermute | solution.py:471
  27.0 3.4 %collective-permute-done.1.c2 = bf16[96,256]{1,0:T(8,128)(2,1)S(1)} collective-permute-done((bf16[96,256]{1,0:T(8,128)(2,1)S(1)}, bf16[96,256]{1,0:T(8,128)(2,1)S(1)}, u32[]{:S(2)}, u32[]{:S(2)}) %collective-permute-start.1) | collective-permute-done | bytes 49184 | tf_op jit(solution)/shard_map/ppermute | solution.py:471
  30.4 2.5 %collective-permute-done.c1 = bf16[96,256]{1,0:T(8,128)(2,1)S(1)} collective-permute-done((bf16[96,256]{1,0:T(8,128)(2,1)S(1)}, bf16[96,256]{1,0:T(8,128)(2,1)S(1)}, u32[]{:S(2)}, u32[]{:S(2)}) %collective-permute-start) | collective-permute-done | bytes 49184 | tf_op jit(solution)/shard_map/ppermute | solution.py:471
  32.9 42.4 %all-to-all-done = bf16[64,136,128]{2,1,0:T(8,128)(2,1)S(1)} async-done(((bf16[64,136,128]{2,1,0:T(8,128)(2,1)}), bf16[64,136,128]{2,1,0:T(8,128)(2,1)S(1)}, u32[]{:S(2)}, u32[]{:S(2)}) %all-to-all-start) | async-done | bytes 2228256 | tf_op jit(solution)/shard_map/all_to_all | solution.py:492
  75.3 5.9 %shard_map.121 = (bf16[1152,256]{1,0:T(8,128)(2,1)}, bf16[1152,256]{1,0:T(8,128)(2,1)}, bf16[1152,256]{1,0:T(8,128)(2,1)}, bf16[1152,256]{1,0:T(8,128)(2,1)}, bf...) custom-call(s32[2,64]{1,0:T(2,128)S(1)} %bitcast.29, ...), custom_call_target="tpu_custom_call" | custom-call | tf_op jit(solution)/shard_map/pallas_call | solution.py:502
  81.3 7.4 %all-to-all-start.1 = ((bf16[64,128,128]{2,1,0:T(8,128)(2,1)}), bf16[64,128,128]{2,1,0:T(8,128)(2,1)}, u32[]{:S(2)}, u32[]{:S(2)}) async-start(bf16[64,128,128]{2,1,0:T(8,128)(2,1)} %get-tuple-element.37), calls=%async_computation.1 | async-start | bytes 4194304 | tf_op jit(solution)/shard_map/all_to_all | solution.py:536
  88.7 1.4 collective-permute-start.6
  90.1 2.6 %collective-permute-start.7 = (bf16[1152,256]{1,0:T(8,128)(2,1)}, bf16[1152,256]{1,0:T(8,128)(2,1)S(1)}, u32[]{:S(2)}, u32[]{:S(2)}) collective-permute-start(bf16[1152,256]{1,0:T(8,128)(2,1)} %get-tuple-element.48), channel_id=1, source_target_pairs={{0,2},{1,3},{2,0},{3,1},{4,6},{5,7},{6,4},{7,5},{8,10},{9,11},{10,... | collective-permute-start | bytes 1769480 | tf_op jit(solution)/shard_map/ppermute | solution.py:471
  92.7 1.1 collective-permute-start.8
  93.8 5.5 %shard_map.122 = (f32[8,128]{1,0:T(8,128)S(1)}, f32[8,128]{1,0:T(8,128)S(1)}, f32[8,128]{1,0:T(8,128)S(1)}, f32[8,128]{1,0:T(8,128)S(1)}, bf16[128,128]{1,0:T(8,128)(2,1)S(1)}) custom-call(bf16[128,256]{1,0:T(8,128)(2,1)S(1)} %get-tuple-element.38.pg_ref, s32[2,64]{1,0:T(2,128)S(1)} %bitcast.31, s32[2,64]{1,0:T(2,128)S(1)} %bitcast.34, ...), custom_call_target="tpu_custom_call" | custom-call | flops 8000000000 | bytes 20000000 | tf_op jit(solution)/shard_map/pallas_call | solution.py:539
  99.6 2.6 %collective-permute-start.10 = (f32[8,128]{1,0:T(8,128)S(1)}, f32[8,128]{1,0:T(8,128)S(1)}, u32[]{:S(2)}, u32[]{:S(2)}) collective-permute-start(f32[8,128]{1,0:T(8,128)S(1)} %get-tuple-element.51), channel_id=1, source_target_pairs={{0,3},{1,0},{2,1},{3,2},{4,7},{5,4},{6,5},{7,6},{8,11},{9,8},{10,9... | collective-permute-start | bytes 12296 | tf_op jit(solution)/shard_map/ppermute | solution.py:471
  102.2 16.5 %collective-permute-done.9.s2 = f32[8,128]{1,0:T(8,128)S(1)} collective-permute-done((f32[8,128]{1,0:T(8,128)S(1)}, f32[8,128]{1,0:T(8,128)S(1)}, u32[]{:S(2)}, u32[]{:S(2)}) %collective-permute-start.9) | collective-permute-done | bytes 4128 | tf_op jit(solution)/shard_map/ppermute | solution.py:471
  118.7 1.3 shard_map.125
  120.0 1.4 collective-permute-start.11
  121.4 1.8 %collective-permute-start.12 = (f32[8,128]{1,0:T(8,128)S(1)}, f32[8,128]{1,0:T(8,128)S(1)}, u32[]{:S(2)}, u32[]{:S(2)}) collective-permute-start(f32[8,128]{1,0:T(8,128)S(1)} %get-tuple-element.60), channel_id=1, source_target_pairs={{0,1},{1,2},{2,3},{3,0},{4,5},{5,6},{6,7},{7,4},{8,9},{9,10},{10,1... | collective-permute-start | bytes 12296 | tf_op jit(solution)/shard_map/ppermute | solution.py:471
  123.1 2.2 %collective-permute-done.12.s1 = f32[8,128]{1,0:T(8,128)S(1)} collective-permute-done((f32[8,128]{1,0:T(8,128)S(1)}, f32[8,128]{1,0:T(8,128)S(1)}, u32[]{:S(2)}, u32[]{:S(2)}) %collective-permute-start.12) | collective-permute-done | bytes 4128 | tf_op jit(solution)/shard_map/ppermute | solution.py:471
  125.5 1.1 collective-permute-start.13
  126.6 0.8 collective-permute-done.13.other_ref
  127.6 1.5 collective-permute-start.14
  129.1 2.4 %collective-permute-start.15 = (bf16[304,256]{1,0:T(8,128)(2,1)S(1)}, bf16[304,256]{1,0:T(8,128)(2,1)S(1)}, u32[]{:S(2)}, u32[]{:S(2)}) collective-permute-start(bf16[304,256]{1,0:T(8,128)(2,1)S(1)} %get-tuple-element.63), channel_id=1, source_target_pairs={{0,16},{8,24},{16,0},{24,8},{1,17},{9,25},{17,1},{25,9},{2,18},{10... | collective-permute-start | bytes 466952 | tf_op jit(solution)/shard_map/ppermute | solution.py:471
  131.5 1.2 collective-permute-start.16
  132.7 3.4 %collective-permute-done.14.i1 = bf16[304,256]{1,0:T(8,128)(2,1)S(1)} collective-permute-done((bf16[304,256]{1,0:T(8,128)(2,1)S(1)}, bf16[304,256]{1,0:T(8,128)(2,1)S(1)}, u32[]{:S(2)}, u32[]{:S(2)}) %collective-permute-start.14) | collective-permute-done | bytes 155680 | tf_op jit(solution)/shard_map/ppermute | solution.py:471
  136.0 5.7 %collective-permute-done.15.i2 = bf16[304,256]{1,0:T(8,128)(2,1)S(1)} collective-permute-done((bf16[304,256]{1,0:T(8,128)(2,1)S(1)}, bf16[304,256]{1,0:T(8,128)(2,1)S(1)}, u32[]{:S(2)}, u32[]{:S(2)}) %collective-permute-start.15) | collective-permute-done | bytes 155680 | tf_op jit(solution)/shard_map/ppermute | solution.py:471
  141.7 0.9 shard_map.128
  142.6 5.6 %all-to-all-start.2 = ((bf16[8,80,256]{2,1,0:T(8,128)(2,1)}), bf16[8,80,256]{2,1,0:T(8,128)(2,1)S(1)}, u32[]{:S(2)}, u32[]{:S(2)}) async-start(bf16[8,80,256]{2,1,0:T(8,128)(2,1)} %shard_map.128), calls=%async_computation.2 | async-start | bytes 655360 | tf_op jit(solution)/shard_map/all_to_all | solution.py:600
  148.2 5.1 %shard_map.123 = (bf16[2,64,128]{2,1,0:T(8,128)(2,1)S(1)}, bf16[2,64,128]{2,1,0:T(8,128)(2,1)S(1)}, bf16[2,64,128]{2,1,0:T(8,128)(2,1)S(1)}, bf16[2,64,128]{2,1,0:T(8,128)(2,1)S(1)}) custom-call(bf16[8192,128]{1,0:T(8,128)(2,1)} %bitcast.13.x_ref, bf16[128,128]{1,0:T(8,128)(2,1)S(1)} %get-tuple-element.39.w_ref, ...), custom_call_target="tpu_custom_call" | custom-call | tf_op jit(solution)/shard_map/pallas_call | solution.py:578
  154.1 2.9 %collective-permute-start.4 = (bf16[2,64,128]{2,1,0:T(8,128)(2,1)S(1)}, bf16[2,64,128]{2,1,0:T(8,128)(2,1)S(1)}, u32[]{:S(2)}, u32[]{:S(2)}) collective-permute-start(bf16[2,64,128]{2,1,0:T(8,128)(2,1)S(1)} %get-tuple-element.43), channel_id=1, source_target_pairs={{0,2},{1,3},{2,0},{3,1},{4,6},{5,7},{6,4},{7,5},{8,10},{9,11},{10,... | collective-permute-start | bytes 98312 | tf_op jit(solution)/shard_map/ppermute | solution.py:471
  157.0 1.1 collective-permute-start.5
  158.1 1.8 %all-to-all-done.2.in_ref = bf16[8,80,256]{2,1,0:T(8,128)(2,1)S(1)} async-done(((bf16[8,80,256]{2,1,0:T(8,128)(2,1)}), bf16[8,80,256]{2,1,0:T(8,128)(2,1)S(1)}, u32[]{:S(2)}, u32[]{:S(2)}) %all-to-all-start.2) | async-done | bytes 327712 | tf_op jit(solution)/shard_map/all_to_all | solution.py:600
  160.6 0.8 shard_map.124
  (41 shorter events, 3.6 us)
Async XLA Ops:
  7.2 68.1 %all-gather.2.cloned.1.call-start = ((), (), s32[]{:S(2)}) async-start(), calls=%async_computation.3 | async-start | bytes 5242880 | tf_op jit(solution)/shard_map/all_gather | solution.py:495
  9.7 13.2 %copy-start.6 = (f32[1315,8]{0,1:T(8,128)S(1)}, f32[1315,8]{0,1:T(8,128)}, u32[]{:S(2)}) copy-start(f32[1315,8]{0,1:T(8,128)} %param.12) | copy-start | bytes 126244
  9.7 65.6 %copy-start.1 = (bf16[256,256]{1,0:T(8,128)(2,1)S(1)}, bf16[256,256]{1,0:T(8,128)(2,1)}, u32[]{:S(2)}) copy-start(bf16[256,256]{1,0:T(8,128)(2,1)} %sw_ref.3) | copy-start | bytes 393220
  9.7 65.6 %copy-start.2 = (s32[64,1,2]{0,2,1:T(2,128)S(1)}, s32[64,1,2]{0,2,1:T(2,128)}, u32[]{:S(2)}) copy-start(s32[64,1,2]{0,2,1:T(2,128)} %param.15) | copy-start | bytes 1540
  9.7 65.6 %copy-start.3 = (s32[64,1,2]{0,2,1:T(2,128)S(1)}, s32[64,1,2]{0,2,1:T(2,128)}, u32[]{:S(2)}) copy-start(s32[64,1,2]{0,2,1:T(2,128)} %param.16) | copy-start | bytes 1540
  9.7 65.5 %all-to-all-start = ((bf16[64,136,128]{2,1,0:T(8,128)(2,1)}), bf16[64,136,128]{2,1,0:T(8,128)(2,1)S(1)}, u32[]{:S(2)}, u32[]{:S(2)}) async-start(bf16[64,136,128]{2,1,0:T(8,128)(2,1)} %shard_map.120), calls=%async_computation | async-start | bytes 4456448 | tf_op jit(solution)/shard_map/all_to_all | solution.py:492
  23.0 4.0 %collective-permute-start.2 = (bf16[96,256]{1,0:T(8,128)(2,1)S(1)}, bf16[96,256]{1,0:T(8,128)(2,1)S(1)}, u32[]{:S(2)}, u32[]{:S(2)}) collective-permute-start(bf16[96,256]{1,0:T(8,128)(2,1)S(1)} %bitcast.24), channel_id=1, source_target_pairs={{0,3},{1,0},{2,1},{3,2},{4,7},{5,4},{6,5},{7,6},{8,11},{9,8},{10,9... | collective-permute-start | bytes 147464 | tf_op jit(solution)/shard_map/ppermute | solution.py:471
  25.8 4.6 %collective-permute-start.1 = (bf16[96,256]{1,0:T(8,128)(2,1)S(1)}, bf16[96,256]{1,0:T(8,128)(2,1)S(1)}, u32[]{:S(2)}, u32[]{:S(2)}) collective-permute-start(bf16[96,256]{1,0:T(8,128)(2,1)S(1)} %bitcast.25), channel_id=1, source_target_pairs={{0,2},{1,3},{2,0},{3,1},{4,6},{5,7},{6,4},{7,5},{8,10},{9,11},{10,... | collective-permute-start | bytes 147464 | tf_op jit(solution)/shard_map/ppermute | solution.py:471
  26.2 6.7 %collective-permute-start = (bf16[96,256]{1,0:T(8,128)(2,1)S(1)}, bf16[96,256]{1,0:T(8,128)(2,1)S(1)}, u32[]{:S(2)}, u32[]{:S(2)}) collective-permute-start(bf16[96,256]{1,0:T(8,128)(2,1)S(1)} %bitcast.26), channel_id=1, source_target_pairs={{0,1},{1,2},{2,3},{3,0},{4,5},{5,6},{6,7},{7,4},{8,9},{9,10},{10,1... | collective-permute-start | bytes 147464 | tf_op jit(solution)/shard_map/ppermute | solution.py:471
  81.2 11.5 %copy-start.7 = (bf16[1152,256]{1,0:T(8,128)(2,1)S(1)}, bf16[1152,256]{1,0:T(8,128)(2,1)}, u32[]{:S(2)}) copy-start(bf16[1152,256]{1,0:T(8,128)(2,1)} %get-tuple-element.49) | copy-start | bytes 1769476
  81.2 12.5 %copy-start.4 = (s32[1,64,2]{1,2,0:T(2,128)S(1)}, s32[1,64,2]{1,2,0:T(2,128)}, u32[]{:S(2)}) copy-start(s32[1,64,2]{1,2,0:T(2,128)} %param.13) | copy-start | bytes 1540
  81.3 12.5 %copy-start.5 = (s32[1,64,2]{1,2,0:T(2,128)S(1)}, s32[1,64,2]{1,2,0:T(2,128)}, u32[]{:S(2)}) copy-start(s32[1,64,2]{1,2,0:T(2,128)} %param.14) | copy-start | bytes 1540
  81.3 61.3 %all-to-all-start.1 = ((bf16[64,128,128]{2,1,0:T(8,128)(2,1)}), bf16[64,128,128]{2,1,0:T(8,128)(2,1)}, u32[]{:S(2)}, u32[]{:S(2)}) async-start(bf16[64,128,128]{2,1,0:T(8,128)(2,1)} %get-tuple-element.37), calls=%async_computation.1 | async-start | bytes 4194304 | tf_op jit(solution)/shard_map/all_to_all | solution.py:536
  88.7 29.9 %collective-permute-start.6 = (bf16[1152,256]{1,0:T(8,128)(2,1)}, bf16[1152,256]{1,0:T(8,128)(2,1)S(1)}, u32[]{:S(2)}, u32[]{:S(2)}) collective-permute-start(bf16[1152,256]{1,0:T(8,128)(2,1)} %get-tuple-element.47), channel_id=1, source_target_pairs={{0,1},{1,2},{2,3},{3,0},{4,5},{5,6},{6,7},{7,4},{8,9},{9,10},{10,1... | collective-permute-start | bytes 1769480 | tf_op jit(solution)/shard_map/ppermute | solution.py:471
  90.1 28.6 %collective-permute-start.7 = (bf16[1152,256]{1,0:T(8,128)(2,1)}, bf16[1152,256]{1,0:T(8,128)(2,1)S(1)}, u32[]{:S(2)}, u32[]{:S(2)}) collective-permute-start(bf16[1152,256]{1,0:T(8,128)(2,1)} %get-tuple-element.48), channel_id=1, source_target_pairs={{0,2},{1,3},{2,0},{3,1},{4,6},{5,7},{6,4},{7,5},{8,10},{9,11},{10,... | collective-permute-start | bytes 1769480 | tf_op jit(solution)/shard_map/ppermute | solution.py:471
  92.7 26.0 %collective-permute-start.8 = (bf16[1152,256]{1,0:T(8,128)(2,1)S(1)}, bf16[1152,256]{1,0:T(8,128)(2,1)S(1)}, u32[]{:S(2)}, u32[]{:S(2)}) collective-permute-start(bf16[1152,256]{1,0:T(8,128)(2,1)S(1)} %copy-done.7), channel_id=1, source_target_pairs={{0,3},{1,0},{2,1},{3,2},{4,7},{5,4},{6,5},{7,6},{8,11},{9,8},{10,9... | collective-permute-start | bytes 1769480 | tf_op jit(solution)/shard_map/ppermute | solution.py:471
  93.8 24.9 %copy-start = (bf16[1152,256]{1,0:T(8,128)(2,1)S(1)}, bf16[1152,256]{1,0:T(8,128)(2,1)}, u32[]{:S(2)}) copy-start(bf16[1152,256]{1,0:T(8,128)(2,1)} %get-tuple-element.52.y0) | copy-start | bytes 1769476
  99.3 19.4 %collective-permute-start.9 = (f32[8,128]{1,0:T(8,128)S(1)}, f32[8,128]{1,0:T(8,128)S(1)}, u32[]{:S(2)}, u32[]{:S(2)}) collective-permute-start(f32[8,128]{1,0:T(8,128)S(1)} %get-tuple-element.50), channel_id=1, source_target_pairs={{0,2},{1,3},{2,0},{3,1},{4,6},{5,7},{6,4},{7,5},{8,10},{9,11},{10,... | collective-permute-start | bytes 12296 | tf_op jit(solution)/shard_map/ppermute | solution.py:471
  99.6 19.1 %collective-permute-start.10 = (f32[8,128]{1,0:T(8,128)S(1)}, f32[8,128]{1,0:T(8,128)S(1)}, u32[]{:S(2)}, u32[]{:S(2)}) collective-permute-start(f32[8,128]{1,0:T(8,128)S(1)} %get-tuple-element.51), channel_id=1, source_target_pairs={{0,3},{1,0},{2,1},{3,2},{4,7},{5,4},{6,5},{7,6},{8,11},{9,8},{10,9... | collective-permute-start | bytes 12296 | tf_op jit(solution)/shard_map/ppermute | solution.py:471
  120.0 7.4 %collective-permute-start.11 = (bf16[1024,256]{1,0:T(8,128)(2,1)S(1)}, bf16[1024,256]{1,0:T(8,128)(2,1)S(1)}, u32[]{:S(2)}, u32[]{:S(2)}) collective-permute-start(bf16[1024,256]{1,0:T(8,128)(2,1)S(1)} %get-tuple-element.57), channel_id=1, source_target_pairs={{0,4},{4,0},{1,5},{5,1},{2,6},{6,2},{3,7},{7,3},{8,12},{12,8},{9,1... | collective-permute-start | bytes 1572872 | tf_op jit(solution)/shard_map/ppermute | solution.py:471
  121.4 3.9 %collective-permute-start.12 = (f32[8,128]{1,0:T(8,128)S(1)}, f32[8,128]{1,0:T(8,128)S(1)}, u32[]{:S(2)}, u32[]{:S(2)}) collective-permute-start(f32[8,128]{1,0:T(8,128)S(1)} %get-tuple-element.60), channel_id=1, source_target_pairs={{0,1},{1,2},{2,3},{3,0},{4,5},{5,6},{6,7},{7,4},{8,9},{9,10},{10,1... | collective-permute-start | bytes 12296 | tf_op jit(solution)/shard_map/ppermute | solution.py:471
  125.5 1.9 %collective-permute-start.13 = (bf16[48,256]{1,0:T(8,128)(2,1)S(1)}, bf16[48,256]{1,0:T(8,128)(2,1)S(1)}, u32[]{:S(2)}, u32[]{:S(2)}) collective-permute-start(bf16[48,256]{1,0:T(8,128)(2,1)S(1)} %shard_map.126.coef_ref), channel_id=1, source_target_pairs={{0,4},{4,0},{1,5},{5,1},{2,6},{6,2},{3,7},{7,3},{8,12},{12,8},{9,1... | collective-permute-start | bytes 73736 | tf_op jit(solution)/shard_map/ppermute | solution.py:471
  127.6 8.4 %collective-permute-start.14 = (bf16[304,256]{1,0:T(8,128)(2,1)S(1)}, bf16[304,256]{1,0:T(8,128)(2,1)S(1)}, u32[]{:S(2)}, u32[]{:S(2)}) collective-permute-start(bf16[304,256]{1,0:T(8,128)(2,1)S(1)} %get-tuple-element.62), channel_id=1, source_target_pairs={{0,8},{8,16},{16,24},{24,0},{1,9},{9,17},{17,25},{25,1},{2,10},{10... | collective-permute-start | bytes 466952 | tf_op jit(solution)/shard_map/ppermute | solution.py:471
  129.1 12.6 %collective-permute-start.15 = (bf16[304,256]{1,0:T(8,128)(2,1)S(1)}, bf16[304,256]{1,0:T(8,128)(2,1)S(1)}, u32[]{:S(2)}, u32[]{:S(2)}) collective-permute-start(bf16[304,256]{1,0:T(8,128)(2,1)S(1)} %get-tuple-element.63), channel_id=1, source_target_pairs={{0,16},{8,24},{16,0},{24,8},{1,17},{9,25},{17,1},{25,9},{2,18},{10... | collective-permute-start | bytes 466952 | tf_op jit(solution)/shard_map/ppermute | solution.py:471
  131.5 10.2 %collective-permute-start.16 = (bf16[304,256]{1,0:T(8,128)(2,1)S(1)}, bf16[304,256]{1,0:T(8,128)(2,1)S(1)}, u32[]{:S(2)}, u32[]{:S(2)}) collective-permute-start(bf16[304,256]{1,0:T(8,128)(2,1)S(1)} %get-tuple-element.64), channel_id=1, source_target_pairs={{0,24},{8,0},{16,8},{24,16},{1,25},{9,1},{17,9},{25,17},{2,26},{10... | collective-permute-start | bytes 466952 | tf_op jit(solution)/shard_map/ppermute | solution.py:471
  142.6 17.3 %all-to-all-start.2 = ((bf16[8,80,256]{2,1,0:T(8,128)(2,1)}), bf16[8,80,256]{2,1,0:T(8,128)(2,1)S(1)}, u32[]{:S(2)}, u32[]{:S(2)}) async-start(bf16[8,80,256]{2,1,0:T(8,128)(2,1)} %shard_map.128), calls=%async_computation.2 | async-start | bytes 655360 | tf_op jit(solution)/shard_map/all_to_all | solution.py:600
  153.3 7.3 %collective-permute-start.3 = (bf16[2,64,128]{2,1,0:T(8,128)(2,1)S(1)}, bf16[2,64,128]{2,1,0:T(8,128)(2,1)S(1)}, u32[]{:S(2)}, u32[]{:S(2)}) collective-permute-start(bf16[2,64,128]{2,1,0:T(8,128)(2,1)S(1)} %get-tuple-element.42), channel_id=1, source_target_pairs={{0,1},{1,2},{2,3},{3,0},{4,5},{5,6},{6,7},{7,4},{8,9},{9,10},{10,1... | collective-permute-start | bytes 98312 | tf_op jit(solution)/shard_map/ppermute | solution.py:471
  154.1 6.5 %collective-permute-start.4 = (bf16[2,64,128]{2,1,0:T(8,128)(2,1)S(1)}, bf16[2,64,128]{2,1,0:T(8,128)(2,1)S(1)}, u32[]{:S(2)}, u32[]{:S(2)}) collective-permute-start(bf16[2,64,128]{2,1,0:T(8,128)(2,1)S(1)} %get-tuple-element.43), channel_id=1, source_target_pairs={{0,2},{1,3},{2,0},{3,1},{4,6},{5,7},{6,4},{7,5},{8,10},{9,11},{10,... | collective-permute-start | bytes 98312 | tf_op jit(solution)/shard_map/ppermute | solution.py:471
  157.0 3.6 %collective-permute-start.5 = (bf16[2,64,128]{2,1,0:T(8,128)(2,1)S(1)}, bf16[2,64,128]{2,1,0:T(8,128)(2,1)S(1)}, u32[]{:S(2)}, u32[]{:S(2)}) collective-permute-start(bf16[2,64,128]{2,1,0:T(8,128)(2,1)S(1)} %get-tuple-element.44), channel_id=1, source_target_pairs={{0,3},{1,0},{2,1},{3,2},{4,7},{5,4},{6,5},{7,6},{8,11},{9,8},{10,9... | collective-permute-start | bytes 98312 | tf_op jit(solution)/shard_map/ppermute | solution.py:471
Sparse Core Ops, SparseCore 0:
  9.8 56.3 all-gather.1

commit v10 on v9

--- a/solution.py
+++ b/solution.py
@@ -11,6 +11,7 @@
 BLK = 128
 LANES = 128
 GAP = 8
+ORDER = (0, 2, 1, 3)
 NX = 4
 NC = 2
 ENT = ("z", "x", "c")
@@ -369,7 +370,7 @@
     nz = out_ref.shape[0]
     last = each // nz
     sums = sum(i[pl.ds(0, each), :].astype(F32) for i in (i0, i1, i2, i3))
-    for r, i in enumerate((i0, i1, i2, i3)):
+    for r, i in zip(ORDER, (i0, i1, i2, i3)):
         order[turn(lax.axis_index("x"), -r, NX)] = i[pl.ds(each, n), :].astype(F32)
     coef = ((order[0] + order[1]) + (order[2] + order[3])).astype(BF)
     for z in range(nz):
@@ -432,7 +433,7 @@
 def join_body(nblk, i0, i1, i2, i3, grad_ref, act_ref, order):
     groups = order.shape[0]
     share = BLK // groups
-    for r, i in enumerate((i0, i1, i2, i3)):
+    for r, i in zip(ORDER, (i0, i1, i2, i3)):
         order[turn(lax.axis_index("basis"), -r, groups)] = i[...].astype(F32)
     for j, out in enumerate((grad_ref, act_ref)):
         for n in range(nblk):
@@ -469,6 +470,9 @@
     def over(axis, r, value):
         n = lax.axis_size(axis)
         return lax.ppermute(value, axis, [(i, (i + r) % n) for i in range(n)])
+
+    def exchange(axis, values):
+        return [over(axis, r, values[r]) if r else values[0] for r in ORDER]
 
     src, rel_out = send_block[0].T, edge_rel[0].T
     dst, cnt = edge_dst[:, 0, :].T, edge_count[:, 0, :].T
@@ -534,7 +538,7 @@
     )
 
     returned = lax.all_to_all(back, ENT, split_axis=0, concat_axis=0, tiled=True)
-    ys = [ys[0]] + [over("basis", r, ys[r]) for r in range(1, groups)]
+    ys = exchange("basis", ys)
 
     *scores, w_out = call(
         functools.partial(score_body, cap, nblk, own, halves),
@@ -573,7 +577,7 @@
         [pltpu.VMEM((part, width), F32)],
         limit=8,
     )(keep, got, coef_part, over("c", 1, coef_part))
-    ins = [outs[0]] + [over("x", r, outs[r]) for r in range(1, NX)]
+    ins = exchange("x", outs)
 
     grads = call(
         functools.partial(bwd_body, cap, own),
@@ -605,7 +609,7 @@
         limit=4,
     )(out)
 
-    grads = [grads[0]] + [over("basis", r, grads[r]) for r in range(1, groups)]
+    grads = exchange("basis", grads)
     cols = width // groups
     entity_grad, activation = call(
         functools.partial(join_body, nblk),

time: 170 us -> 169 us (level)
  transfers between devices with their start and end apart: 21 -> 21, of which waited for: 10 -> 12; matrix products, arithmetic and copies ran while one was open for 0% -> 0% of each run, Pallas kernels for 8% -> 8%
where the time goes in v10:
time: 169 us
  waiting for transfers between devices  80 us (47%)
  starting transfers between devices  51.4 us (30%)
  Pallas kernels  23.1 us (14%)
  between operations  14.2 us (8%)
    all_to_all x1, waiting for transfers between devices, local(): lax.all_to_all(outgoing, ENT, split_axis=0, concat_axis=0, tiled=True)  42.4 us
    ppermute x17, waiting for transfers between devices, over(): return lax.ppermute(value, axis, [(i, (i + r) % n) for i in range(n)])  34.7 us
    ppermute x17, starting transfers between devices, over(): return lax.ppermute(value, axis, [(i, (i + r) % n) for i in range(n)])  24.8 us
    all_to_all x1, starting transfers between devices, local(): lax.all_to_all(outgoing, ENT, split_axis=0, concat_axis=0, tiled=True)  13.1 us
    all_to_all x1, starting transfers between devices, local(): lax.all_to_all(back, ENT, split_axis=0, concat_axis=0, tiled=True)  7.43 us
    all_to_all x1, starting transfers between devices, local(): out = lax.all_to_all(out, 'z', split_axis=0, concat_axis=0, tiled=True)  6.03 us
    pallas_call x1, Pallas kernels, local(): call(functools.partial(fwd_body, cap, nblk, own), (*[hbm((own + 1) * rows...  5.93 us
    pallas_call x1, Pallas kernels, local(): call(functools.partial(score_body, cap, nblk, own, halves), (*[jax.ShapeD...  5.49 us
  transfers between devices with their start and end apart: 21, of which 12 were waited for; matrix products, arithmetic and copies ran while one was open for 0% of the time, Pallas kernels for 8%

profile of v10, /device:TPU:1, one launch (start us, length us, event | category | flops | bytes accessed | tf_op | source)
XLA Modules:
  0.0 168.8 jit_solution(15086479199722048199)
XLA Ops:
  7.2 2.4 %shard_map.120 = bf16[64,136,128]{2,1,0:T(8,128)(2,1)} custom-call(s32[2,64]{1,0:T(2,128)} %bitcast.35, s32[2,64]{1,0:T(2,128)} %bitcast.37, bf16[512,256]{1,0:T(8,128)(2,1)} %ent_ref.3), custom_call_target="tpu_custom_call" | custom-call | tf_op jit(solution)/shard_map/pallas_call | solution.py:481
  9.7 13.1 %all-to-all-start = ((bf16[64,136,128]{2,1,0:T(8,128)(2,1)}), bf16[64,136,128]{2,1,0:T(8,128)(2,1)S(1)}, u32[]{:S(2)}, u32[]{:S(2)}) async-start(bf16[64,136,128]{2,1,0:T(8,128)(2,1)} %shard_map.120), calls=%async_computation | async-start | bytes 4456448 | tf_op jit(solution)/shard_map/all_to_all | solution.py:496
  23.0 2.8 %collective-permute-start.2 = (bf16[96,256]{1,0:T(8,128)(2,1)S(1)}, bf16[96,256]{1,0:T(8,128)(2,1)S(1)}, u32[]{:S(2)}, u32[]{:S(2)}) collective-permute-start(bf16[96,256]{1,0:T(8,128)(2,1)S(1)} %bitcast.24), channel_id=1, source_target_pairs={{0,3},{1,0},{2,1},{3,2},{4,7},{5,4},{6,5},{7,6},{8,11},{9,8},{10,9... | collective-permute-start | bytes 147464 | tf_op jit(solution)/shard_map/ppermute | solution.py:472
  26.2 0.7 collective-permute-start
  27.0 3.4 %collective-permute-done.1.c2 = bf16[96,256]{1,0:T(8,128)(2,1)S(1)} collective-permute-done((bf16[96,256]{1,0:T(8,128)(2,1)S(1)}, bf16[96,256]{1,0:T(8,128)(2,1)S(1)}, u32[]{:S(2)}, u32[]{:S(2)}) %collective-permute-start.1) | collective-permute-done | bytes 49184 | tf_op jit(solution)/shard_map/ppermute | solution.py:472
  30.4 2.5 %collective-permute-done.c1 = bf16[96,256]{1,0:T(8,128)(2,1)S(1)} collective-permute-done((bf16[96,256]{1,0:T(8,128)(2,1)S(1)}, bf16[96,256]{1,0:T(8,128)(2,1)S(1)}, u32[]{:S(2)}, u32[]{:S(2)}) %collective-permute-start) | collective-permute-done | bytes 49184 | tf_op jit(solution)/shard_map/ppermute | solution.py:472
  32.9 42.4 %all-to-all-done = bf16[64,136,128]{2,1,0:T(8,128)(2,1)S(1)} async-done(((bf16[64,136,128]{2,1,0:T(8,128)(2,1)}), bf16[64,136,128]{2,1,0:T(8,128)(2,1)S(1)}, u32[]{:S(2)}, u32[]{:S(2)}) %all-to-all-start) | async-done | bytes 2228256 | tf_op jit(solution)/shard_map/all_to_all | solution.py:496
  75.3 5.9 %shard_map.121 = (bf16[1152,256]{1,0:T(8,128)(2,1)}, bf16[1152,256]{1,0:T(8,128)(2,1)}, bf16[1152,256]{1,0:T(8,128)(2,1)}, bf16[1152,256]{1,0:T(8,128)(2,1)}, bf...) custom-call(s32[2,64]{1,0:T(2,128)S(1)} %bitcast.29, ...), custom_call_target="tpu_custom_call" | custom-call | tf_op jit(solution)/shard_map/pallas_call | solution.py:506
  81.3 7.4 %all-to-all-start.1 = ((bf16[64,128,128]{2,1,0:T(8,128)(2,1)}), bf16[64,128,128]{2,1,0:T(8,128)(2,1)}, u32[]{:S(2)}, u32[]{:S(2)}) async-start(bf16[64,128,128]{2,1,0:T(8,128)(2,1)} %get-tuple-element.37), calls=%async_computation.1 | async-start | bytes 4194304 | tf_op jit(solution)/shard_map/all_to_all | solution.py:540
  88.7 3.0 %collective-permute-start.6 = (bf16[1152,256]{1,0:T(8,128)(2,1)}, bf16[1152,256]{1,0:T(8,128)(2,1)S(1)}, u32[]{:S(2)}, u32[]{:S(2)}) collective-permute-start(bf16[1152,256]{1,0:T(8,128)(2,1)} %get-tuple-element.47), channel_id=1, source_target_pairs={{0,2},{1,3},{2,0},{3,1},{4,6},{5,7},{6,4},{7,5},{8,10},{9,11},{10,... | collective-permute-start | bytes 1769480 | tf_op jit(solution)/shard_map/ppermute | solution.py:472
  92.1 2.3 %collective-permute-start.8 = (bf16[1152,256]{1,0:T(8,128)(2,1)S(1)}, bf16[1152,256]{1,0:T(8,128)(2,1)S(1)}, u32[]{:S(2)}, u32[]{:S(2)}) collective-permute-start(bf16[1152,256]{1,0:T(8,128)(2,1)S(1)} %copy-done.7), channel_id=1, source_target_pairs={{0,3},{1,0},{2,1},{3,2},{4,7},{5,4},{6,5},{7,6},{8,11},{9,8},{10,9... | collective-permute-start | bytes 1769480 | tf_op jit(solution)/shard_map/ppermute | solution.py:472
  94.4 5.5 %shard_map.122 = (f32[8,128]{1,0:T(8,128)S(1)}, f32[8,128]{1,0:T(8,128)S(1)}, f32[8,128]{1,0:T(8,128)S(1)}, f32[8,128]{1,0:T(8,128)S(1)}, bf16[128,128]{1,0:T(8,128)(2,1)S(1)}) custom-call(bf16[128,256]{1,0:T(8,128)(2,1)S(1)} %get-tuple-element.38.pg_ref, s32[2,64]{1,0:T(2,128)S(1)} %bitcast.31, s32[2,64]{1,0:T(2,128)S(1)} %bitcast.34, ...), custom_call_target="tpu_custom_call" | custom-call | flops 8000000000 | bytes 20000000 | tf_op jit(solution)/shard_map/pallas_call | solution.py:543
  100.0 1.6 collective-permute-start.10
  101.5 15.8 %collective-permute-done.9.s2 = f32[8,128]{1,0:T(8,128)S(1)} collective-permute-done((f32[8,128]{1,0:T(8,128)S(1)}, f32[8,128]{1,0:T(8,128)S(1)}, u32[]{:S(2)}, u32[]{:S(2)}) %collective-permute-start.9) | collective-permute-done | bytes 4128 | tf_op jit(solution)/shard_map/ppermute | solution.py:472
  117.3 0.8 collective-permute-done.10.s3
  118.5 1.3 shard_map.125
  119.9 1.0 collective-permute-start.11
  120.9 0.9 collective-permute-start.12
  121.8 3.0 %collective-permute-done.12.s1 = f32[8,128]{1,0:T(8,128)S(1)} collective-permute-done((f32[8,128]{1,0:T(8,128)S(1)}, f32[8,128]{1,0:T(8,128)S(1)}, u32[]{:S(2)}, u32[]{:S(2)}) %collective-permute-start.12) | collective-permute-done | bytes 4128 | tf_op jit(solution)/shard_map/ppermute | solution.py:472
  125.0 1.1 collective-permute-start.13
  126.1 0.8 collective-permute-done.13.other_ref
  127.2 3.0 %collective-permute-start.14 = (bf16[304,256]{1,0:T(8,128)(2,1)S(1)}, bf16[304,256]{1,0:T(8,128)(2,1)S(1)}, u32[]{:S(2)}, u32[]{:S(2)}) collective-permute-start(bf16[304,256]{1,0:T(8,128)(2,1)S(1)} %get-tuple-element.62), channel_id=1, source_target_pairs={{0,16},{8,24},{16,0},{24,8},{1,17},{9,25},{17,1},{25,9},{2,18},{10... | collective-permute-start | bytes 466952 | tf_op jit(solution)/shard_map/ppermute | solution.py:472
  130.4 2.4 %collective-permute-start.16 = (bf16[304,256]{1,0:T(8,128)(2,1)S(1)}, bf16[304,256]{1,0:T(8,128)(2,1)S(1)}, u32[]{:S(2)}, u32[]{:S(2)}) collective-permute-start(bf16[304,256]{1,0:T(8,128)(2,1)S(1)} %get-tuple-element.64), channel_id=1, source_target_pairs={{0,24},{8,0},{16,8},{24,16},{1,25},{9,1},{17,9},{25,17},{2,26},{10... | collective-permute-start | bytes 466952 | tf_op jit(solution)/shard_map/ppermute | solution.py:472
  132.8 4.0 %collective-permute-done.14.i1 = bf16[304,256]{1,0:T(8,128)(2,1)S(1)} collective-permute-done((bf16[304,256]{1,0:T(8,128)(2,1)S(1)}, bf16[304,256]{1,0:T(8,128)(2,1)S(1)}, u32[]{:S(2)}, u32[]{:S(2)}) %collective-permute-start.14) | collective-permute-done | bytes 155680 | tf_op jit(solution)/shard_map/ppermute | solution.py:472
  136.9 3.8 %collective-permute-done.15.i2 = bf16[304,256]{1,0:T(8,128)(2,1)S(1)} collective-permute-done((bf16[304,256]{1,0:T(8,128)(2,1)S(1)}, bf16[304,256]{1,0:T(8,128)(2,1)S(1)}, u32[]{:S(2)}, u32[]{:S(2)}) %collective-permute-start.15) | collective-permute-done | bytes 155680 | tf_op jit(solution)/shard_map/ppermute | solution.py:472
  140.7 0.9 shard_map.128
  141.5 6.0 %all-to-all-start.2 = ((bf16[8,80,256]{2,1,0:T(8,128)(2,1)}), bf16[8,80,256]{2,1,0:T(8,128)(2,1)S(1)}, u32[]{:S(2)}, u32[]{:S(2)}) async-start(bf16[8,80,256]{2,1,0:T(8,128)(2,1)} %shard_map.128), calls=%async_computation.2 | async-start | bytes 655360 | tf_op jit(solution)/shard_map/all_to_all | solution.py:604
  147.6 5.1 %shard_map.123 = (bf16[2,64,128]{2,1,0:T(8,128)(2,1)S(1)}, bf16[2,64,128]{2,1,0:T(8,128)(2,1)S(1)}, bf16[2,64,128]{2,1,0:T(8,128)(2,1)S(1)}, bf16[2,64,128]{2,1,0:T(8,128)(2,1)S(1)}) custom-call(bf16[8192,128]{1,0:T(8,128)(2,1)} %bitcast.13.x_ref, bf16[128,128]{1,0:T(8,128)(2,1)S(1)} %get-tuple-element.39.w_ref, ...), custom_call_target="tpu_custom_call" | custom-call | tf_op jit(solution)/shard_map/pallas_call | solution.py:582
  152.7 2.3 %collective-permute-start.3 = (bf16[2,64,128]{2,1,0:T(8,128)(2,1)S(1)}, bf16[2,64,128]{2,1,0:T(8,128)(2,1)S(1)}, u32[]{:S(2)}, u32[]{:S(2)}) collective-permute-start(bf16[2,64,128]{2,1,0:T(8,128)(2,1)S(1)} %get-tuple-element.42), channel_id=1, source_target_pairs={{0,2},{1,3},{2,0},{3,1},{4,6},{5,7},{6,4},{7,5},{8,10},{9,11},{10,... | collective-permute-start | bytes 98312 | tf_op jit(solution)/shard_map/ppermute | solution.py:472
  155.4 2.2 %collective-permute-start.5 = (bf16[2,64,128]{2,1,0:T(8,128)(2,1)S(1)}, bf16[2,64,128]{2,1,0:T(8,128)(2,1)S(1)}, u32[]{:S(2)}, u32[]{:S(2)}) collective-permute-start(bf16[2,64,128]{2,1,0:T(8,128)(2,1)S(1)} %get-tuple-element.44), channel_id=1, source_target_pairs={{0,3},{1,0},{2,1},{3,2},{4,7},{5,4},{6,5},{7,6},{8,11},{9,8},{10,9... | collective-permute-start | bytes 98312 | tf_op jit(solution)/shard_map/ppermute | solution.py:472
  157.6 2.9 %all-to-all-done.2.in_ref = bf16[8,80,256]{2,1,0:T(8,128)(2,1)S(1)} async-done(((bf16[8,80,256]{2,1,0:T(8,128)(2,1)}), bf16[8,80,256]{2,1,0:T(8,128)(2,1)S(1)}, u32[]{:S(2)}, u32[]{:S(2)}) %all-to-all-start.2) | async-done | bytes 327712 | tf_op jit(solution)/shard_map/all_to_all | solution.py:604
  161.2 0.8 shard_map.124
  (41 shorter events, 3.4 us)
Async XLA Ops:
  7.2 68.1 %all-gather.2.cloned.1.call-start = ((), (), s32[]{:S(2)}) async-start(), calls=%async_computation.3 | async-start | bytes 5242880 | tf_op jit(solution)/shard_map/all_gather | solution.py:499
  9.7 13.2 %copy-start.6 = (f32[1315,8]{0,1:T(8,128)S(1)}, f32[1315,8]{0,1:T(8,128)}, u32[]{:S(2)}) copy-start(f32[1315,8]{0,1:T(8,128)} %param.12) | copy-start | bytes 126244
  9.7 65.6 %copy-start.1 = (bf16[256,256]{1,0:T(8,128)(2,1)S(1)}, bf16[256,256]{1,0:T(8,128)(2,1)}, u32[]{:S(2)}) copy-start(bf16[256,256]{1,0:T(8,128)(2,1)} %sw_ref.3) | copy-start | bytes 393220
  9.7 65.6 %copy-start.2 = (s32[64,1,2]{0,2,1:T(2,128)S(1)}, s32[64,1,2]{0,2,1:T(2,128)}, u32[]{:S(2)}) copy-start(s32[64,1,2]{0,2,1:T(2,128)} %param.15) | copy-start | bytes 1540
  9.7 65.6 %copy-start.3 = (s32[64,1,2]{0,2,1:T(2,128)S(1)}, s32[64,1,2]{0,2,1:T(2,128)}, u32[]{:S(2)}) copy-start(s32[64,1,2]{0,2,1:T(2,128)} %param.16) | copy-start | bytes 1540
  9.7 65.5 %all-to-all-start = ((bf16[64,136,128]{2,1,0:T(8,128)(2,1)}), bf16[64,136,128]{2,1,0:T(8,128)(2,1)S(1)}, u32[]{:S(2)}, u32[]{:S(2)}) async-start(bf16[64,136,128]{2,1,0:T(8,128)(2,1)} %shard_map.120), calls=%async_computation | async-start | bytes 4456448 | tf_op jit(solution)/shard_map/all_to_all | solution.py:496
  23.0 4.0 %collective-permute-start.2 = (bf16[96,256]{1,0:T(8,128)(2,1)S(1)}, bf16[96,256]{1,0:T(8,128)(2,1)S(1)}, u32[]{:S(2)}, u32[]{:S(2)}) collective-permute-start(bf16[96,256]{1,0:T(8,128)(2,1)S(1)} %bitcast.24), channel_id=1, source_target_pairs={{0,3},{1,0},{2,1},{3,2},{4,7},{5,4},{6,5},{7,6},{8,11},{9,8},{10,9... | collective-permute-start | bytes 147464 | tf_op jit(solution)/shard_map/ppermute | solution.py:472
  25.8 4.6 %collective-permute-start.1 = (bf16[96,256]{1,0:T(8,128)(2,1)S(1)}, bf16[96,256]{1,0:T(8,128)(2,1)S(1)}, u32[]{:S(2)}, u32[]{:S(2)}) collective-permute-start(bf16[96,256]{1,0:T(8,128)(2,1)S(1)} %bitcast.25), channel_id=1, source_target_pairs={{0,2},{1,3},{2,0},{3,1},{4,6},{5,7},{6,4},{7,5},{8,10},{9,11},{10,... | collective-permute-start | bytes 147464 | tf_op jit(solution)/shard_map/ppermute | solution.py:472
  26.2 6.7 %collective-permute-start = (bf16[96,256]{1,0:T(8,128)(2,1)S(1)}, bf16[96,256]{1,0:T(8,128)(2,1)S(1)}, u32[]{:S(2)}, u32[]{:S(2)}) collective-permute-start(bf16[96,256]{1,0:T(8,128)(2,1)S(1)} %bitcast.26), channel_id=1, source_target_pairs={{0,1},{1,2},{2,3},{3,0},{4,5},{5,6},{6,7},{7,4},{8,9},{9,10},{10,1... | collective-permute-start | bytes 147464 | tf_op jit(solution)/shard_map/ppermute | solution.py:472
  81.2 10.9 %copy-start.7 = (bf16[1152,256]{1,0:T(8,128)(2,1)S(1)}, bf16[1152,256]{1,0:T(8,128)(2,1)}, u32[]{:S(2)}) copy-start(bf16[1152,256]{1,0:T(8,128)(2,1)} %get-tuple-element.49) | copy-start | bytes 1769476
  81.2 13.1 %copy-start.4 = (s32[1,64,2]{1,2,0:T(2,128)S(1)}, s32[1,64,2]{1,2,0:T(2,128)}, u32[]{:S(2)}) copy-start(s32[1,64,2]{1,2,0:T(2,128)} %param.13) | copy-start | bytes 1540
  81.3 13.1 %copy-start.5 = (s32[1,64,2]{1,2,0:T(2,128)S(1)}, s32[1,64,2]{1,2,0:T(2,128)}, u32[]{:S(2)}) copy-start(s32[1,64,2]{1,2,0:T(2,128)} %param.14) | copy-start | bytes 1540
  81.3 60.3 %all-to-all-start.1 = ((bf16[64,128,128]{2,1,0:T(8,128)(2,1)}), bf16[64,128,128]{2,1,0:T(8,128)(2,1)}, u32[]{:S(2)}, u32[]{:S(2)}) async-start(bf16[64,128,128]{2,1,0:T(8,128)(2,1)} %get-tuple-element.37), calls=%async_computation.1 | async-start | bytes 4194304 | tf_op jit(solution)/shard_map/all_to_all | solution.py:540
  88.7 29.5 %collective-permute-start.6 = (bf16[1152,256]{1,0:T(8,128)(2,1)}, bf16[1152,256]{1,0:T(8,128)(2,1)S(1)}, u32[]{:S(2)}, u32[]{:S(2)}) collective-permute-start(bf16[1152,256]{1,0:T(8,128)(2,1)} %get-tuple-element.47), channel_id=1, source_target_pairs={{0,2},{1,3},{2,0},{3,1},{4,6},{5,7},{6,4},{7,5},{8,10},{9,11},{10,... | collective-permute-start | bytes 1769480 | tf_op jit(solution)/shard_map/ppermute | solution.py:472
  91.7 26.8 %collective-permute-start.7 = (bf16[1152,256]{1,0:T(8,128)(2,1)}, bf16[1152,256]{1,0:T(8,128)(2,1)S(1)}, u32[]{:S(2)}, u32[]{:S(2)}) collective-permute-start(bf16[1152,256]{1,0:T(8,128)(2,1)} %get-tuple-element.48), channel_id=1, source_target_pairs={{0,1},{1,2},{2,3},{3,0},{4,5},{5,6},{6,7},{7,4},{8,9},{9,10},{10,1... | collective-permute-start | bytes 1769480 | tf_op jit(solution)/shard_map/ppermute | solution.py:472
  92.1 26.4 %collective-permute-start.8 = (bf16[1152,256]{1,0:T(8,128)(2,1)S(1)}, bf16[1152,256]{1,0:T(8,128)(2,1)S(1)}, u32[]{:S(2)}, u32[]{:S(2)}) collective-permute-start(bf16[1152,256]{1,0:T(8,128)(2,1)S(1)} %copy-done.7), channel_id=1, source_target_pairs={{0,3},{1,0},{2,1},{3,2},{4,7},{5,4},{6,5},{7,6},{8,11},{9,8},{10,9... | collective-permute-start | bytes 1769480 | tf_op jit(solution)/shard_map/ppermute | solution.py:472
  94.4 24.2 %copy-start = (bf16[1152,256]{1,0:T(8,128)(2,1)S(1)}, bf16[1152,256]{1,0:T(8,128)(2,1)}, u32[]{:S(2)}) copy-start(bf16[1152,256]{1,0:T(8,128)(2,1)} %get-tuple-element.52.y0) | copy-start | bytes 1769476
  99.9 17.5 %collective-permute-start.9 = (f32[8,128]{1,0:T(8,128)S(1)}, f32[8,128]{1,0:T(8,128)S(1)}, u32[]{:S(2)}, u32[]{:S(2)}) collective-permute-start(f32[8,128]{1,0:T(8,128)S(1)} %get-tuple-element.50), channel_id=1, source_target_pairs={{0,2},{1,3},{2,0},{3,1},{4,6},{5,7},{6,4},{7,5},{8,10},{9,11},{10,... | collective-permute-start | bytes 12296 | tf_op jit(solution)/shard_map/ppermute | solution.py:472
  100.0 18.2 %collective-permute-start.10 = (f32[8,128]{1,0:T(8,128)S(1)}, f32[8,128]{1,0:T(8,128)S(1)}, u32[]{:S(2)}, u32[]{:S(2)}) collective-permute-start(f32[8,128]{1,0:T(8,128)S(1)} %get-tuple-element.51), channel_id=1, source_target_pairs={{0,3},{1,0},{2,1},{3,2},{4,7},{5,4},{6,5},{7,6},{8,11},{9,8},{10,9... | collective-permute-start | bytes 12296 | tf_op jit(solution)/shard_map/ppermute | solution.py:472
  119.9 7.1 %collective-permute-start.11 = (bf16[1024,256]{1,0:T(8,128)(2,1)S(1)}, bf16[1024,256]{1,0:T(8,128)(2,1)S(1)}, u32[]{:S(2)}, u32[]{:S(2)}) collective-permute-start(bf16[1024,256]{1,0:T(8,128)(2,1)S(1)} %get-tuple-element.57), channel_id=1, source_target_pairs={{0,4},{4,0},{1,5},{5,1},{2,6},{6,2},{3,7},{7,3},{8,12},{12,8},{9,1... | collective-permute-start | bytes 1572872 | tf_op jit(solution)/shard_map/ppermute | solution.py:472
  120.9 3.9 %collective-permute-start.12 = (f32[8,128]{1,0:T(8,128)S(1)}, f32[8,128]{1,0:T(8,128)S(1)}, u32[]{:S(2)}, u32[]{:S(2)}) collective-permute-start(f32[8,128]{1,0:T(8,128)S(1)} %get-tuple-element.60), channel_id=1, source_target_pairs={{0,1},{1,2},{2,3},{3,0},{4,5},{5,6},{6,7},{7,4},{8,9},{9,10},{10,1... | collective-permute-start | bytes 12296 | tf_op jit(solution)/shard_map/ppermute | solution.py:472
  125.0 1.9 %collective-permute-start.13 = (bf16[48,256]{1,0:T(8,128)(2,1)S(1)}, bf16[48,256]{1,0:T(8,128)(2,1)S(1)}, u32[]{:S(2)}, u32[]{:S(2)}) collective-permute-start(bf16[48,256]{1,0:T(8,128)(2,1)S(1)} %shard_map.126.coef_ref), channel_id=1, source_target_pairs={{0,4},{4,0},{1,5},{5,1},{2,6},{6,2},{3,7},{7,3},{8,12},{12,8},{9,1... | collective-permute-start | bytes 73736 | tf_op jit(solution)/shard_map/ppermute | solution.py:472
  127.2 9.7 %collective-permute-start.14 = (bf16[304,256]{1,0:T(8,128)(2,1)S(1)}, bf16[304,256]{1,0:T(8,128)(2,1)S(1)}, u32[]{:S(2)}, u32[]{:S(2)}) collective-permute-start(bf16[304,256]{1,0:T(8,128)(2,1)S(1)} %get-tuple-element.62), channel_id=1, source_target_pairs={{0,16},{8,24},{16,0},{24,8},{1,17},{9,25},{17,1},{25,9},{2,18},{10... | collective-permute-start | bytes 466952 | tf_op jit(solution)/shard_map/ppermute | solution.py:472
  130.1 10.5 %collective-permute-start.15 = (bf16[304,256]{1,0:T(8,128)(2,1)S(1)}, bf16[304,256]{1,0:T(8,128)(2,1)S(1)}, u32[]{:S(2)}, u32[]{:S(2)}) collective-permute-start(bf16[304,256]{1,0:T(8,128)(2,1)S(1)} %get-tuple-element.63), channel_id=1, source_target_pairs={{0,8},{8,16},{16,24},{24,0},{1,9},{9,17},{17,25},{25,1},{2,10},{10... | collective-permute-start | bytes 466952 | tf_op jit(solution)/shard_map/ppermute | solution.py:472
  130.4 10.2 %collective-permute-start.16 = (bf16[304,256]{1,0:T(8,128)(2,1)S(1)}, bf16[304,256]{1,0:T(8,128)(2,1)S(1)}, u32[]{:S(2)}, u32[]{:S(2)}) collective-permute-start(bf16[304,256]{1,0:T(8,128)(2,1)S(1)} %get-tuple-element.64), channel_id=1, source_target_pairs={{0,24},{8,0},{16,8},{24,16},{1,25},{9,1},{17,9},{25,17},{2,26},{10... | collective-permute-start | bytes 466952 | tf_op jit(solution)/shard_map/ppermute | solution.py:472
  141.5 18.9 %all-to-all-start.2 = ((bf16[8,80,256]{2,1,0:T(8,128)(2,1)}), bf16[8,80,256]{2,1,0:T(8,128)(2,1)S(1)}, u32[]{:S(2)}, u32[]{:S(2)}) async-start(bf16[8,80,256]{2,1,0:T(8,128)(2,1)} %shard_map.128), calls=%async_computation.2 | async-start | bytes 655360 | tf_op jit(solution)/shard_map/all_to_all | solution.py:604
  152.7 8.5 %collective-permute-start.3 = (bf16[2,64,128]{2,1,0:T(8,128)(2,1)S(1)}, bf16[2,64,128]{2,1,0:T(8,128)(2,1)S(1)}, u32[]{:S(2)}, u32[]{:S(2)}) collective-permute-start(bf16[2,64,128]{2,1,0:T(8,128)(2,1)S(1)} %get-tuple-element.42), channel_id=1, source_target_pairs={{0,2},{1,3},{2,0},{3,1},{4,6},{5,7},{6,4},{7,5},{8,10},{9,11},{10,... | collective-permute-start | bytes 98312 | tf_op jit(solution)/shard_map/ppermute | solution.py:472
  154.9 6.2 %collective-permute-start.4 = (bf16[2,64,128]{2,1,0:T(8,128)(2,1)S(1)}, bf16[2,64,128]{2,1,0:T(8,128)(2,1)S(1)}, u32[]{:S(2)}, u32[]{:S(2)}) collective-permute-start(bf16[2,64,128]{2,1,0:T(8,128)(2,1)S(1)} %get-tuple-element.43), channel_id=1, source_target_pairs={{0,1},{1,2},{2,3},{3,0},{4,5},{5,6},{6,7},{7,4},{8,9},{9,10},{10,1... | collective-permute-start | bytes 98312 | tf_op jit(solution)/shard_map/ppermute | solution.py:472
  155.4 5.8 %collective-permute-start.5 = (bf16[2,64,128]{2,1,0:T(8,128)(2,1)S(1)}, bf16[2,64,128]{2,1,0:T(8,128)(2,1)S(1)}, u32[]{:S(2)}, u32[]{:S(2)}) collective-permute-start(bf16[2,64,128]{2,1,0:T(8,128)(2,1)S(1)} %get-tuple-element.44), channel_id=1, source_target_pairs={{0,3},{1,0},{2,1},{3,2},{4,7},{5,4},{6,5},{7,6},{8,11},{9,8},{10,9... | collective-permute-start | bytes 98312 | tf_op jit(solution)/shard_map/ppermute | solution.py:472
Sparse Core Ops, SparseCore 0:
  9.8 56.3 all-gather.1

commit v11 on v10

--- a/solution.py
+++ b/solution.py
@@ -602,13 +602,6 @@
         limit=4,
     )(*ins)
     out = lax.all_to_all(out, "z", split_axis=0, concat_axis=0, tiled=True)
-    basis_grad, coef_grad = call(
-        functools.partial(z_body, own),
-        (jax.ShapeDtypeStruct((own, width // peers, width), F32), jax.ShapeDtypeStruct((own, relations), F32)),
-        [VM],
-        limit=4,
-    )(out)
-
     grads = exchange("basis", grads)
     cols = width // groups
     entity_grad, activation = call(
@@ -618,6 +611,13 @@
         [pltpu.VMEM((groups, 2, cols, rows), F32)],
         limit=4,
     )(*grads)
+    out, _ = lax.optimization_barrier((out, entity_grad))
+    basis_grad, coef_grad = call(
+        functools.partial(z_body, own),
+        (jax.ShapeDtypeStruct((own, width // peers, width), F32), jax.ShapeDtypeStruct((own, relations), F32)),
+        [VM],
+        limit=4,
+    )(out)
     return (activation.T, basis_grad, coef_grad.T, entity_grad.T)
 
 

time: 169 us -> 169 us (level)
    all_to_all x1, waiting for transfers between devices: 2.86 us -> 0.72 us  [local(): out = lax.all_to_all(out, 'z', split_axis=0, concat_axis=0, tiled=True)]
  transfers between devices with their start and end apart: 21 -> 21, of which waited for: 12 -> 13; matrix products, arithmetic and copies ran while one was open for 0% -> 0% of each run, Pallas kernels for 8% -> 8%
where the time goes in v11:
time: 169 us; the launch traced here: 168 us
  waiting for transfers between devices  79.1 us (47%)
  starting transfers between devices  51.4 us (30%)
  Pallas kernels  23.1 us (14%)
  between operations  14.2 us (8%)
    all_to_all x1, waiting for transfers between devices, local(): lax.all_to_all(outgoing, ENT, split_axis=0, concat_axis=0, tiled=True)  42.4 us
    ppermute x17, waiting for transfers between devices, over(): return lax.ppermute(value, axis, [(i, (i + r) % n) for i in range(n)])  36 us
    ppermute x17, starting transfers between devices, over(): return lax.ppermute(value, axis, [(i, (i + r) % n) for i in range(n)])  24.8 us
    all_to_all x1, starting transfers between devices, local(): lax.all_to_all(outgoing, ENT, split_axis=0, concat_axis=0, tiled=True)  13.1 us
    all_to_all x1, starting transfers between devices, local(): lax.all_to_all(back, ENT, split_axis=0, concat_axis=0, tiled=True)  7.43 us
    all_to_all x1, starting transfers between devices, local(): out = lax.all_to_all(out, 'z', split_axis=0, concat_axis=0, tiled=True)  6.03 us
    pallas_call x1, Pallas kernels, local(): call(functools.partial(fwd_body, cap, nblk, own), (*[hbm((own + 1) * rows...  5.93 us
    pallas_call x1, Pallas kernels, local(): call(functools.partial(score_body, cap, nblk, own, halves), (*[jax.ShapeD...  5.49 us
  transfers between devices with their start and end apart: 21, of which 13 were waited for; matrix products, arithmetic and copies ran while one was open for 0% of the time, Pallas kernels for 8%

profile of v11, /device:TPU:1, one launch (start us, length us, event | category | flops | bytes accessed | tf_op | source)
XLA Modules:
  0.0 168.0 jit_solution(3032634113720229030)
XLA Ops:
  7.2 2.4 %shard_map.120 = bf16[64,136,128]{2,1,0:T(8,128)(2,1)} custom-call(s32[2,64]{1,0:T(2,128)} %bitcast.35, s32[2,64]{1,0:T(2,128)} %bitcast.37, bf16[512,256]{1,0:T(8,128)(2,1)} %ent_ref.3), custom_call_target="tpu_custom_call" | custom-call | tf_op jit(solution)/shard_map/pallas_call | solution.py:481
  9.7 13.1 %all-to-all-start = ((bf16[64,136,128]{2,1,0:T(8,128)(2,1)}), bf16[64,136,128]{2,1,0:T(8,128)(2,1)S(1)}, u32[]{:S(2)}, u32[]{:S(2)}) async-start(bf16[64,136,128]{2,1,0:T(8,128)(2,1)} %shard_map.120), calls=%async_computation | async-start | bytes 4456448 | tf_op jit(solution)/shard_map/all_to_all | solution.py:496
  23.0 2.8 %collective-permute-start.2 = (bf16[96,256]{1,0:T(8,128)(2,1)S(1)}, bf16[96,256]{1,0:T(8,128)(2,1)S(1)}, u32[]{:S(2)}, u32[]{:S(2)}) collective-permute-start(bf16[96,256]{1,0:T(8,128)(2,1)S(1)} %bitcast.24), channel_id=1, source_target_pairs={{0,3},{1,0},{2,1},{3,2},{4,7},{5,4},{6,5},{7,6},{8,11},{9,8},{10,9... | collective-permute-start | bytes 147464 | tf_op jit(solution)/shard_map/ppermute | solution.py:472
  27.0 3.4 %collective-permute-done.1.c2 = bf16[96,256]{1,0:T(8,128)(2,1)S(1)} collective-permute-done((bf16[96,256]{1,0:T(8,128)(2,1)S(1)}, bf16[96,256]{1,0:T(8,128)(2,1)S(1)}, u32[]{:S(2)}, u32[]{:S(2)}) %collective-permute-start.1) | collective-permute-done | bytes 49184 | tf_op jit(solution)/shard_map/ppermute | solution.py:472
  30.4 2.5 %collective-permute-done.c1 = bf16[96,256]{1,0:T(8,128)(2,1)S(1)} collective-permute-done((bf16[96,256]{1,0:T(8,128)(2,1)S(1)}, bf16[96,256]{1,0:T(8,128)(2,1)S(1)}, u32[]{:S(2)}, u32[]{:S(2)}) %collective-permute-start) | collective-permute-done | bytes 49184 | tf_op jit(solution)/shard_map/ppermute | solution.py:472
  32.9 42.4 %all-to-all-done = bf16[64,136,128]{2,1,0:T(8,128)(2,1)S(1)} async-done(((bf16[64,136,128]{2,1,0:T(8,128)(2,1)}), bf16[64,136,128]{2,1,0:T(8,128)(2,1)S(1)}, u32[]{:S(2)}, u32[]{:S(2)}) %all-to-all-start) | async-done | bytes 2228256 | tf_op jit(solution)/shard_map/all_to_all | solution.py:496
  75.3 5.9 %shard_map.121 = (bf16[1152,256]{1,0:T(8,128)(2,1)}, bf16[1152,256]{1,0:T(8,128)(2,1)}, bf16[1152,256]{1,0:T(8,128)(2,1)}, bf16[1152,256]{1,0:T(8,128)(2,1)}, bf...) custom-call(s32[2,64]{1,0:T(2,128)S(1)} %bitcast.29, ...), custom_call_target="tpu_custom_call" | custom-call | tf_op jit(solution)/shard_map/pallas_call | solution.py:506
  81.3 7.4 %all-to-all-start.1 = ((bf16[64,128,128]{2,1,0:T(8,128)(2,1)}), bf16[64,128,128]{2,1,0:T(8,128)(2,1)}, u32[]{:S(2)}, u32[]{:S(2)}) async-start(bf16[64,128,128]{2,1,0:T(8,128)(2,1)} %get-tuple-element.38), calls=%async_computation.1 | async-start | bytes 4194304 | tf_op jit(solution)/shard_map/all_to_all | solution.py:540
  88.7 3.0 %collective-permute-start.6 = (bf16[1152,256]{1,0:T(8,128)(2,1)}, bf16[1152,256]{1,0:T(8,128)(2,1)S(1)}, u32[]{:S(2)}, u32[]{:S(2)}) collective-permute-start(bf16[1152,256]{1,0:T(8,128)(2,1)} %get-tuple-element.48), channel_id=1, source_target_pairs={{0,2},{1,3},{2,0},{3,1},{4,6},{5,7},{6,4},{7,5},{8,10},{9,11},{10,... | collective-permute-start | bytes 1769480 | tf_op jit(solution)/shard_map/ppermute | solution.py:472
  92.1 2.3 %collective-permute-start.8 = (bf16[1152,256]{1,0:T(8,128)(2,1)S(1)}, bf16[1152,256]{1,0:T(8,128)(2,1)S(1)}, u32[]{:S(2)}, u32[]{:S(2)}) collective-permute-start(bf16[1152,256]{1,0:T(8,128)(2,1)S(1)} %copy-done.7), channel_id=1, source_target_pairs={{0,3},{1,0},{2,1},{3,2},{4,7},{5,4},{6,5},{7,6},{8,11},{9,8},{10,9... | collective-permute-start | bytes 1769480 | tf_op jit(solution)/shard_map/ppermute | solution.py:472
  94.4 5.5 %shard_map.122 = (f32[8,128]{1,0:T(8,128)S(1)}, f32[8,128]{1,0:T(8,128)S(1)}, f32[8,128]{1,0:T(8,128)S(1)}, f32[8,128]{1,0:T(8,128)S(1)}, bf16[128,128]{1,0:T(8,128)(2,1)S(1)}) custom-call(bf16[128,256]{1,0:T(8,128)(2,1)S(1)} %get-tuple-element.39.pg_ref, s32[2,64]{1,0:T(2,128)S(1)} %bitcast.31, s32[2,64]{1,0:T(2,128)S(1)} %bitcast.34, ...), custom_call_target="tpu_custom_call" | custom-call | flops 8000000000 | bytes 20000000 | tf_op jit(solution)/shard_map/pallas_call | solution.py:543
  100.0 1.6 collective-permute-start.10
  101.5 15.8 %collective-permute-done.9.s2 = f32[8,128]{1,0:T(8,128)S(1)} collective-permute-done((f32[8,128]{1,0:T(8,128)S(1)}, f32[8,128]{1,0:T(8,128)S(1)}, u32[]{:S(2)}, u32[]{:S(2)}) %collective-permute-start.9) | collective-permute-done | bytes 4128 | tf_op jit(solution)/shard_map/ppermute | solution.py:472
  117.3 0.8 collective-permute-done.10.s3
  118.5 1.3 shard_map.125
  119.9 1.0 collective-permute-start.11
  120.9 0.9 collective-permute-start.12
  121.8 3.0 %collective-permute-done.12.s1 = f32[8,128]{1,0:T(8,128)S(1)} collective-permute-done((f32[8,128]{1,0:T(8,128)S(1)}, f32[8,128]{1,0:T(8,128)S(1)}, u32[]{:S(2)}, u32[]{:S(2)}) %collective-permute-start.12) | collective-permute-done | bytes 4128 | tf_op jit(solution)/shard_map/ppermute | solution.py:472
  125.0 1.1 collective-permute-start.13
  126.1 0.8 collective-permute-done.13.other_ref
  127.2 3.0 %collective-permute-start.14 = (bf16[304,256]{1,0:T(8,128)(2,1)S(1)}, bf16[304,256]{1,0:T(8,128)(2,1)S(1)}, u32[]{:S(2)}, u32[]{:S(2)}) collective-permute-start(bf16[304,256]{1,0:T(8,128)(2,1)S(1)} %get-tuple-element.63), channel_id=1, source_target_pairs={{0,16},{8,24},{16,0},{24,8},{1,17},{9,25},{17,1},{25,9},{2,18},{10... | collective-permute-start | bytes 466952 | tf_op jit(solution)/shard_map/ppermute | solution.py:472
  130.4 2.4 %collective-permute-start.16 = (bf16[304,256]{1,0:T(8,128)(2,1)S(1)}, bf16[304,256]{1,0:T(8,128)(2,1)S(1)}, u32[]{:S(2)}, u32[]{:S(2)}) collective-permute-start(bf16[304,256]{1,0:T(8,128)(2,1)S(1)} %get-tuple-element.65), channel_id=1, source_target_pairs={{0,24},{8,0},{16,8},{24,16},{1,25},{9,1},{17,9},{25,17},{2,26},{10... | collective-permute-start | bytes 466952 | tf_op jit(solution)/shard_map/ppermute | solution.py:472
  132.8 4.0 %collective-permute-done.14.i1 = bf16[304,256]{1,0:T(8,128)(2,1)S(1)} collective-permute-done((bf16[304,256]{1,0:T(8,128)(2,1)S(1)}, bf16[304,256]{1,0:T(8,128)(2,1)S(1)}, u32[]{:S(2)}, u32[]{:S(2)}) %collective-permute-start.14) | collective-permute-done | bytes 155680 | tf_op jit(solution)/shard_map/ppermute | solution.py:472
  136.9 3.8 %collective-permute-done.15.i2 = bf16[304,256]{1,0:T(8,128)(2,1)S(1)} collective-permute-done((bf16[304,256]{1,0:T(8,128)(2,1)S(1)}, bf16[304,256]{1,0:T(8,128)(2,1)S(1)}, u32[]{:S(2)}, u32[]{:S(2)}) %collective-permute-start.15) | collective-permute-done | bytes 155680 | tf_op jit(solution)/shard_map/ppermute | solution.py:472
  140.7 0.9 shard_map.128
  141.5 6.0 %all-to-all-start.2 = ((bf16[8,80,256]{2,1,0:T(8,128)(2,1)}), bf16[8,80,256]{2,1,0:T(8,128)(2,1)S(1)}, u32[]{:S(2)}, u32[]{:S(2)}) async-start(bf16[8,80,256]{2,1,0:T(8,128)(2,1)} %shard_map.128), calls=%async_computation.2 | async-start | bytes 655360 | tf_op jit(solution)/shard_map/all_to_all | solution.py:604
  147.6 5.1 %shard_map.123 = (bf16[2,64,128]{2,1,0:T(8,128)(2,1)S(1)}, bf16[2,64,128]{2,1,0:T(8,128)(2,1)S(1)}, bf16[2,64,128]{2,1,0:T(8,128)(2,1)S(1)}, bf16[2,64,128]{2,1,0:T(8,128)(2,1)S(1)}) custom-call(bf16[8192,128]{1,0:T(8,128)(2,1)} %bitcast.13.x_ref, bf16[128,128]{1,0:T(8,128)(2,1)S(1)} %get-tuple-element.40.w_ref, ...), custom_call_target="tpu_custom_call" | custom-call | tf_op jit(solution)/shard_map/pallas_call | solution.py:582
  152.7 2.3 %collective-permute-start.3 = (bf16[2,64,128]{2,1,0:T(8,128)(2,1)S(1)}, bf16[2,64,128]{2,1,0:T(8,128)(2,1)S(1)}, u32[]{:S(2)}, u32[]{:S(2)}) collective-permute-start(bf16[2,64,128]{2,1,0:T(8,128)(2,1)S(1)} %get-tuple-element.43), channel_id=1, source_target_pairs={{0,2},{1,3},{2,0},{3,1},{4,6},{5,7},{6,4},{7,5},{8,10},{9,11},{10,... | collective-permute-start | bytes 98312 | tf_op jit(solution)/shard_map/ppermute | solution.py:472
  155.4 2.2 %collective-permute-start.5 = (bf16[2,64,128]{2,1,0:T(8,128)(2,1)S(1)}, bf16[2,64,128]{2,1,0:T(8,128)(2,1)S(1)}, u32[]{:S(2)}, u32[]{:S(2)}) collective-permute-start(bf16[2,64,128]{2,1,0:T(8,128)(2,1)S(1)} %get-tuple-element.45), channel_id=1, source_target_pairs={{0,3},{1,0},{2,1},{3,2},{4,7},{5,4},{6,5},{7,6},{8,11},{9,8},{10,9... | collective-permute-start | bytes 98312 | tf_op jit(solution)/shard_map/ppermute | solution.py:472
  157.6 1.3 collective-permute-done.4.i2
  158.9 0.8 shard_map.124
  159.8 0.7 all-to-all-done.2.in_ref
  (41 shorter events, 4.1 us)
Async XLA Ops:
  7.2 68.1 %all-gather.2.cloned.1.call-start = ((), (), s32[]{:S(2)}) async-start(), calls=%async_computation.3 | async-start | bytes 5242880 | tf_op jit(solution)/shard_map/all_gather | solution.py:499
  9.7 13.2 %copy-start.6 = (f32[1315,8]{0,1:T(8,128)S(1)}, f32[1315,8]{0,1:T(8,128)}, u32[]{:S(2)}) copy-start(f32[1315,8]{0,1:T(8,128)} %param.12) | copy-start | bytes 126244
  9.7 65.6 %copy-start.1 = (bf16[256,256]{1,0:T(8,128)(2,1)S(1)}, bf16[256,256]{1,0:T(8,128)(2,1)}, u32[]{:S(2)}) copy-start(bf16[256,256]{1,0:T(8,128)(2,1)} %sw_ref.3) | copy-start | bytes 393220
  9.7 65.6 %copy-start.2 = (s32[64,1,2]{0,2,1:T(2,128)S(1)}, s32[64,1,2]{0,2,1:T(2,128)}, u32[]{:S(2)}) copy-start(s32[64,1,2]{0,2,1:T(2,128)} %param.15) | copy-start | bytes 1540
  9.7 65.6 %copy-start.3 = (s32[64,1,2]{0,2,1:T(2,128)S(1)}, s32[64,1,2]{0,2,1:T(2,128)}, u32[]{:S(2)}) copy-start(s32[64,1,2]{0,2,1:T(2,128)} %param.16) | copy-start | bytes 1540
  9.7 65.5 %all-to-all-start = ((bf16[64,136,128]{2,1,0:T(8,128)(2,1)}), bf16[64,136,128]{2,1,0:T(8,128)(2,1)S(1)}, u32[]{:S(2)}, u32[]{:S(2)}) async-start(bf16[64,136,128]{2,1,0:T(8,128)(2,1)} %shard_map.120), calls=%async_computation | async-start | bytes 4456448 | tf_op jit(solution)/shard_map/all_to_all | solution.py:496
  23.0 4.0 %collective-permute-start.2 = (bf16[96,256]{1,0:T(8,128)(2,1)S(1)}, bf16[96,256]{1,0:T(8,128)(2,1)S(1)}, u32[]{:S(2)}, u32[]{:S(2)}) collective-permute-start(bf16[96,256]{1,0:T(8,128)(2,1)S(1)} %bitcast.24), channel_id=1, source_target_pairs={{0,3},{1,0},{2,1},{3,2},{4,7},{5,4},{6,5},{7,6},{8,11},{9,8},{10,9... | collective-permute-start | bytes 147464 | tf_op jit(solution)/shard_map/ppermute | solution.py:472
  25.8 4.6 %collective-permute-start.1 = (bf16[96,256]{1,0:T(8,128)(2,1)S(1)}, bf16[96,256]{1,0:T(8,128)(2,1)S(1)}, u32[]{:S(2)}, u32[]{:S(2)}) collective-permute-start(bf16[96,256]{1,0:T(8,128)(2,1)S(1)} %bitcast.25), channel_id=1, source_target_pairs={{0,2},{1,3},{2,0},{3,1},{4,6},{5,7},{6,4},{7,5},{8,10},{9,11},{10,... | collective-permute-start | bytes 147464 | tf_op jit(solution)/shard_map/ppermute | solution.py:472
  26.2 6.7 %collective-permute-start = (bf16[96,256]{1,0:T(8,128)(2,1)S(1)}, bf16[96,256]{1,0:T(8,128)(2,1)S(1)}, u32[]{:S(2)}, u32[]{:S(2)}) collective-permute-start(bf16[96,256]{1,0:T(8,128)(2,1)S(1)} %bitcast.26), channel_id=1, source_target_pairs={{0,1},{1,2},{2,3},{3,0},{4,5},{5,6},{6,7},{7,4},{8,9},{9,10},{10,1... | collective-permute-start | bytes 147464 | tf_op jit(solution)/shard_map/ppermute | solution.py:472
  81.2 10.9 %copy-start.7 = (bf16[1152,256]{1,0:T(8,128)(2,1)S(1)}, bf16[1152,256]{1,0:T(8,128)(2,1)}, u32[]{:S(2)}) copy-start(bf16[1152,256]{1,0:T(8,128)(2,1)} %get-tuple-element.50) | copy-start | bytes 1769476
  81.2 13.1 %copy-start.4 = (s32[1,64,2]{1,2,0:T(2,128)S(1)}, s32[1,64,2]{1,2,0:T(2,128)}, u32[]{:S(2)}) copy-start(s32[1,64,2]{1,2,0:T(2,128)} %param.13) | copy-start | bytes 1540
  81.3 13.1 %copy-start.5 = (s32[1,64,2]{1,2,0:T(2,128)S(1)}, s32[1,64,2]{1,2,0:T(2,128)}, u32[]{:S(2)}) copy-start(s32[1,64,2]{1,2,0:T(2,128)} %param.14) | copy-start | bytes 1540
  81.3 60.3 %all-to-all-start.1 = ((bf16[64,128,128]{2,1,0:T(8,128)(2,1)}), bf16[64,128,128]{2,1,0:T(8,128)(2,1)}, u32[]{:S(2)}, u32[]{:S(2)}) async-start(bf16[64,128,128]{2,1,0:T(8,128)(2,1)} %get-tuple-element.38), calls=%async_computation.1 | async-start | bytes 4194304 | tf_op jit(solution)/shard_map/all_to_all | solution.py:540
  88.7 29.5 %collective-permute-start.6 = (bf16[1152,256]{1,0:T(8,128)(2,1)}, bf16[1152,256]{1,0:T(8,128)(2,1)S(1)}, u32[]{:S(2)}, u32[]{:S(2)}) collective-permute-start(bf16[1152,256]{1,0:T(8,128)(2,1)} %get-tuple-element.48), channel_id=1, source_target_pairs={{0,2},{1,3},{2,0},{3,1},{4,6},{5,7},{6,4},{7,5},{8,10},{9,11},{10,... | collective-permute-start | bytes 1769480 | tf_op jit(solution)/shard_map/ppermute | solution.py:472
  91.7 26.8 %collective-permute-start.7 = (bf16[1152,256]{1,0:T(8,128)(2,1)}, bf16[1152,256]{1,0:T(8,128)(2,1)S(1)}, u32[]{:S(2)}, u32[]{:S(2)}) collective-permute-start(bf16[1152,256]{1,0:T(8,128)(2,1)} %get-tuple-element.49), channel_id=1, source_target_pairs={{0,1},{1,2},{2,3},{3,0},{4,5},{5,6},{6,7},{7,4},{8,9},{9,10},{10,1... | collective-permute-start | bytes 1769480 | tf_op jit(solution)/shard_map/ppermute | solution.py:472
  92.1 26.4 %collective-permute-start.8 = (bf16[1152,256]{1,0:T(8,128)(2,1)S(1)}, bf16[1152,256]{1,0:T(8,128)(2,1)S(1)}, u32[]{:S(2)}, u32[]{:S(2)}) collective-permute-start(bf16[1152,256]{1,0:T(8,128)(2,1)S(1)} %copy-done.7), channel_id=1, source_target_pairs={{0,3},{1,0},{2,1},{3,2},{4,7},{5,4},{6,5},{7,6},{8,11},{9,8},{10,9... | collective-permute-start | bytes 1769480 | tf_op jit(solution)/shard_map/ppermute | solution.py:472
  94.4 24.2 %copy-start = (bf16[1152,256]{1,0:T(8,128)(2,1)S(1)}, bf16[1152,256]{1,0:T(8,128)(2,1)}, u32[]{:S(2)}) copy-start(bf16[1152,256]{1,0:T(8,128)(2,1)} %get-tuple-element.53.y0) | copy-start | bytes 1769476
  99.9 17.5 %collective-permute-start.9 = (f32[8,128]{1,0:T(8,128)S(1)}, f32[8,128]{1,0:T(8,128)S(1)}, u32[]{:S(2)}, u32[]{:S(2)}) collective-permute-start(f32[8,128]{1,0:T(8,128)S(1)} %get-tuple-element.51), channel_id=1, source_target_pairs={{0,2},{1,3},{2,0},{3,1},{4,6},{5,7},{6,4},{7,5},{8,10},{9,11},{10,... | collective-permute-start | bytes 12296 | tf_op jit(solution)/shard_map/ppermute | solution.py:472
  100.0 18.2 %collective-permute-start.10 = (f32[8,128]{1,0:T(8,128)S(1)}, f32[8,128]{1,0:T(8,128)S(1)}, u32[]{:S(2)}, u32[]{:S(2)}) collective-permute-start(f32[8,128]{1,0:T(8,128)S(1)} %get-tuple-element.52), channel_id=1, source_target_pairs={{0,3},{1,0},{2,1},{3,2},{4,7},{5,4},{6,5},{7,6},{8,11},{9,8},{10,9... | collective-permute-start | bytes 12296 | tf_op jit(solution)/shard_map/ppermute | solution.py:472
  119.9 7.1 %collective-permute-start.11 = (bf16[1024,256]{1,0:T(8,128)(2,1)S(1)}, bf16[1024,256]{1,0:T(8,128)(2,1)S(1)}, u32[]{:S(2)}, u32[]{:S(2)}) collective-permute-start(bf16[1024,256]{1,0:T(8,128)(2,1)S(1)} %get-tuple-element.58), channel_id=1, source_target_pairs={{0,4},{4,0},{1,5},{5,1},{2,6},{6,2},{3,7},{7,3},{8,12},{12,8},{9,1... | collective-permute-start | bytes 1572872 | tf_op jit(solution)/shard_map/ppermute | solution.py:472
  120.9 3.9 %collective-permute-start.12 = (f32[8,128]{1,0:T(8,128)S(1)}, f32[8,128]{1,0:T(8,128)S(1)}, u32[]{:S(2)}, u32[]{:S(2)}) collective-permute-start(f32[8,128]{1,0:T(8,128)S(1)} %get-tuple-element.61), channel_id=1, source_target_pairs={{0,1},{1,2},{2,3},{3,0},{4,5},{5,6},{6,7},{7,4},{8,9},{9,10},{10,1... | collective-permute-start | bytes 12296 | tf_op jit(solution)/shard_map/ppermute | solution.py:472
  125.0 1.9 %collective-permute-start.13 = (bf16[48,256]{1,0:T(8,128)(2,1)S(1)}, bf16[48,256]{1,0:T(8,128)(2,1)S(1)}, u32[]{:S(2)}, u32[]{:S(2)}) collective-permute-start(bf16[48,256]{1,0:T(8,128)(2,1)S(1)} %shard_map.126.coef_ref), channel_id=1, source_target_pairs={{0,4},{4,0},{1,5},{5,1},{2,6},{6,2},{3,7},{7,3},{8,12},{12,8},{9,1... | collective-permute-start | bytes 73736 | tf_op jit(solution)/shard_map/ppermute | solution.py:472
  127.2 9.7 %collective-permute-start.14 = (bf16[304,256]{1,0:T(8,128)(2,1)S(1)}, bf16[304,256]{1,0:T(8,128)(2,1)S(1)}, u32[]{:S(2)}, u32[]{:S(2)}) collective-permute-start(bf16[304,256]{1,0:T(8,128)(2,1)S(1)} %get-tuple-element.63), channel_id=1, source_target_pairs={{0,16},{8,24},{16,0},{24,8},{1,17},{9,25},{17,1},{25,9},{2,18},{10... | collective-permute-start | bytes 466952 | tf_op jit(solution)/shard_map/ppermute | solution.py:472
  130.1 10.5 %collective-permute-start.15 = (bf16[304,256]{1,0:T(8,128)(2,1)S(1)}, bf16[304,256]{1,0:T(8,128)(2,1)S(1)}, u32[]{:S(2)}, u32[]{:S(2)}) collective-permute-start(bf16[304,256]{1,0:T(8,128)(2,1)S(1)} %get-tuple-element.64), channel_id=1, source_target_pairs={{0,8},{8,16},{16,24},{24,0},{1,9},{9,17},{17,25},{25,1},{2,10},{10... | collective-permute-start | bytes 466952 | tf_op jit(solution)/shard_map/ppermute | solution.py:472
  130.4 10.2 %collective-permute-start.16 = (bf16[304,256]{1,0:T(8,128)(2,1)S(1)}, bf16[304,256]{1,0:T(8,128)(2,1)S(1)}, u32[]{:S(2)}, u32[]{:S(2)}) collective-permute-start(bf16[304,256]{1,0:T(8,128)(2,1)S(1)} %get-tuple-element.65), channel_id=1, source_target_pairs={{0,24},{8,0},{16,8},{24,16},{1,25},{9,1},{17,9},{25,17},{2,26},{10... | collective-permute-start | bytes 466952 | tf_op jit(solution)/shard_map/ppermute | solution.py:472
  141.5 18.9 %all-to-all-start.2 = ((bf16[8,80,256]{2,1,0:T(8,128)(2,1)}), bf16[8,80,256]{2,1,0:T(8,128)(2,1)S(1)}, u32[]{:S(2)}, u32[]{:S(2)}) async-start(bf16[8,80,256]{2,1,0:T(8,128)(2,1)} %shard_map.128), calls=%async_computation.2 | async-start | bytes 655360 | tf_op jit(solution)/shard_map/all_to_all | solution.py:604
  152.7 5.0 %collective-permute-start.3 = (bf16[2,64,128]{2,1,0:T(8,128)(2,1)S(1)}, bf16[2,64,128]{2,1,0:T(8,128)(2,1)S(1)}, u32[]{:S(2)}, u32[]{:S(2)}) collective-permute-start(bf16[2,64,128]{2,1,0:T(8,128)(2,1)S(1)} %get-tuple-element.43), channel_id=1, source_target_pairs={{0,2},{1,3},{2,0},{3,1},{4,6},{5,7},{6,4},{7,5},{8,10},{9,11},{10,... | collective-permute-start | bytes 98312 | tf_op jit(solution)/shard_map/ppermute | solution.py:472
  154.9 4.0 %collective-permute-start.4 = (bf16[2,64,128]{2,1,0:T(8,128)(2,1)S(1)}, bf16[2,64,128]{2,1,0:T(8,128)(2,1)S(1)}, u32[]{:S(2)}, u32[]{:S(2)}) collective-permute-start(bf16[2,64,128]{2,1,0:T(8,128)(2,1)S(1)} %get-tuple-element.44), channel_id=1, source_target_pairs={{0,1},{1,2},{2,3},{3,0},{4,5},{5,6},{6,7},{7,4},{8,9},{9,10},{10,1... | collective-permute-start | bytes 98312 | tf_op jit(solution)/shard_map/ppermute | solution.py:472
  155.4 3.6 %collective-permute-start.5 = (bf16[2,64,128]{2,1,0:T(8,128)(2,1)S(1)}, bf16[2,64,128]{2,1,0:T(8,128)(2,1)S(1)}, u32[]{:S(2)}, u32[]{:S(2)}) collective-permute-start(bf16[2,64,128]{2,1,0:T(8,128)(2,1)S(1)} %get-tuple-element.45), channel_id=1, source_target_pairs={{0,3},{1,0},{2,1},{3,2},{4,7},{5,4},{6,5},{7,6},{8,11},{9,8},{10,9... | collective-permute-start | bytes 98312 | tf_op jit(solution)/shard_map/ppermute | solution.py:472
Sparse Core Ops, SparseCore 0:
  9.8 56.3 all-gather.1
